TPU v7x, 32 devices: a whole 2x2x4 slice. The times are simulated.
32 devices in a mesh: section: 8 (over y, x, core), rep: 4 (over z).
Axes of the slice: x: 2, y: 2, z: 4, core: 2. Of those that a mesh axis runs over, the one named last changes fastest.
Arguments:
- features: bfloat16 [16384, 128], P('section'), may hold values from -6 to 6
- order: int32 [16384], P('section'), may hold values from 0 to 2047, as said below
- tiles: bfloat16 [8, 4, 2, 96, 128, 128], P('section', 'rep'), may hold values from -0.125 to 0.125
- tile_rows: int32 [8, 4, 2, 96], P('section', 'rep'), may hold values from 0 to 15, as said below
- tile_cols: int32 [8, 4, 2, 96], P('section', 'rep'), may hold values from 0 to 15, as said below
- live: int32 [8, 4, 2], P('section', 'rep'), may hold values from 1 to 96, as said below
- weight: bfloat16 [128, 128], replicated, may hold values from -0.5 to 0.5
- cotangent: bfloat16 [16384, 128], P('section'), may hold values from -6 to 6
Outputs:
- hidden: bfloat16 [16384, 128], P('section')
- weight_grad: float32 [128, 128], replicated
- feature_grad: bfloat16 [16384, 128], P('section')
Inputs may be any that keep to these rules, and one draw needn't show every extreme that they name: `order`: within each panel of 2048 rows, a permutation of the local row numbers. For one section, replica and round, the 96 pairs (tile_rows, tile_cols) are distinct. `tile_cols`: block column within the panel j * 4 + r for replica r and round j. Some section, replica and round has all 96 slots live.
All inputs are finite; a program needn't handle non-finite values.
Results may differ from a plain program's by a relative error of at most 0.012.
Values may be sent and summed in bfloat16 or wider, within the bound.
No kernel may reach another device: no remote copies, remote signals or barrier semaphores. Data moves between devices by JAX's collectives and lax.ppermute only.
A program may use at most 192 MiB of HBM per device.

v0:
```python
import math

import jax
import jax.numpy as jnp
from jax import lax
from jax.sharding import PartitionSpec as P


def spread(value, axis, source):
    kept = jnp.where(lax.axis_index(axis) == source, value, 0).astype(value.dtype)
    return lax.psum(kept, axis)


def shards(features, order, tiles, tile_rows, tile_cols, live, weight, cotangent):
    rep_count = lax.axis_size("rep")
    section_count = lax.axis_size("section")
    rep_index = lax.axis_index("rep")
    section_index = lax.axis_index("section")
    panel_rows, width = features.shape
    block_rows = tiles.shape[-1]
    blocks = panel_rows // block_rows
    rounds = tiles.shape[2]
    slot_count = tiles.shape[3]
    own_tiles = tiles[0, 0]
    row_table = tile_rows[0, 0]
    col_table = tile_cols[0, 0]
    live_counts = live[0, 0]
    slot_ids = jnp.arange(slot_count, dtype=jnp.int32)
    block_ids = jnp.arange(blocks, dtype=jnp.int32)
    grad_scale = 1.0 / math.sqrt(panel_rows * section_count)
    reordered = jnp.take(features, order, axis=0)

    def forward_round(round_no, running):
        root = round_no * rep_count + rep_index
        panel = spread(reordered, "section", root)
        tile_set = lax.dynamic_index_in_dim(own_tiles, round_no, 0, keepdims=False)
        row_ids = lax.dynamic_index_in_dim(row_table, round_no, 0, keepdims=False)
        col_ids = lax.dynamic_index_in_dim(col_table, round_no, 0, keepdims=False)
        count_now = lax.dynamic_index_in_dim(live_counts, round_no, 0, keepdims=False)
        picked = jnp.take(panel.reshape(blocks, block_rows, width), col_ids, axis=0)
        products = jnp.einsum("kab,kbf->kaf", tile_set, picked, preferred_element_type=jnp.float32)
        select = (
            (row_ids[None, :] == block_ids[:, None]) & (slot_ids < count_now)[None, :]
        ).astype(jnp.float32)
        return running + jnp.einsum(
            "pk,kaf->paf", select, products, precision=lax.Precision.HIGHEST
        )

    partial_sum = lax.fori_loop(
        0, rounds, forward_round, jnp.zeros((blocks, block_rows, width), jnp.float32)
    )
    partial_sum = partial_sum.reshape(panel_rows, width)
    share_rows = panel_rows // rep_count
    row_share = lax.psum_scatter(partial_sum, "rep", scatter_dimension=0, tiled=True)
    co_share = lax.dynamic_slice_in_dim(cotangent, rep_index * share_rows, share_rows, 0)
    aggregated = row_share.astype(jnp.bfloat16)
    preact = jnp.dot(aggregated, weight, preferred_element_type=jnp.float32)
    out_rows = jax.nn.silu(preact).astype(jnp.bfloat16)
    sigmoid_part = jax.nn.sigmoid(preact)
    grad_pre = (
        co_share.astype(jnp.float32) * sigmoid_part * (1.0 + preact * (1.0 - sigmoid_part))
    ).astype(jnp.bfloat16)
    grad_part = jnp.einsum("nf,ng->fg", aggregated, grad_pre, preferred_element_type=jnp.float32)
    up_rows = jnp.einsum("ng,fg->nf", grad_pre, weight, preferred_element_type=jnp.float32).astype(
        jnp.bfloat16
    )
    hidden_share, grad_part, upstream_share = (out_rows, grad_part, up_rows)
    weight_grad = lax.psum(grad_part, ("section", "rep")) * grad_scale
    hidden, upstream = (
        lax.all_gather(hidden_share, "rep", axis=0, tiled=True),
        lax.all_gather(upstream_share, "rep", axis=0, tiled=True),
    )
    up_blocks = upstream.reshape(blocks, block_rows, width)
    picked_up = jnp.take(up_blocks, row_table.reshape(-1), axis=0).reshape(
        rounds, slot_count, block_rows, width
    )
    products_back = jnp.einsum(
        "jkab,jkaf->jkbf", own_tiles, picked_up, preferred_element_type=jnp.float32
    )
    alive_mask = slot_ids[None, None, :] < live_counts[:, None, None]
    select_back = ((col_table[:, None, :] == block_ids[None, :, None]) & alive_mask).astype(
        jnp.float32
    )
    contrib = jnp.einsum(
        "jpk,jkbf->jpbf", select_back, products_back, precision=lax.Precision.HIGHEST
    )
    contrib = lax.optimization_barrier(contrib.astype(jnp.bfloat16)).astype(jnp.float32)
    contrib = contrib.reshape(rounds, panel_rows, width)
    totals = lax.psum(contrib.astype(jnp.bfloat16), "section").astype(jnp.float32)
    own_panel = lax.dynamic_index_in_dim(
        totals, section_index // rep_count, 0, keepdims=False
    ).astype(jnp.bfloat16)
    grad_rows = spread(own_panel, "rep", section_index % rep_count)
    feature_grad = jnp.zeros_like(features).at[order].set(grad_rows)
    return (hidden, weight_grad, feature_grad)


def solution(mesh):
    placed = (
        P("section", None),
        P("section"),
        P("section", "rep", None, None, None, None),
        P("section", "rep", None, None),
        P("section", "rep", None, None),
        P("section", "rep", None),
        P(),
        P("section", None),
    )
    return jax.shard_map(
        shards,
        mesh=mesh,
        in_specs=placed,
        out_specs=(P("section", None), P(), P("section", None)),
        check_vma=False,
    )
```

profile of v0, /device:TPU:0, one launch (start us, length us, event | category | flops | bytes accessed | tf_op | source)
XLA Modules:
  0.0 487.0 jit_solution(13288153377587932532)
XLA Ops:
  9.5 6.2 %gather_fusion.1 = bf16[2048,128]{1,0:T(8,128)(2,1)S(1)} fusion(bf16[2048,128]{1,0:T(8,128)(2,1)S(1)} %copy-done, s32[2048]{0:T(1024)S(1)} %get-tuple-element.296), kind=kCustom, calls=%fused_computation.1 | custom fusion | bytes 1056768 | tf_op jit(solution)/shard_map/jit(_take)/gather | solution.py:31
  16.0 147.6 %while.16 = (s32[]{:T(128)}, f32[16,128,128]{2,0,1:T(8,128)S(1)}, s32[2,96]{1,0:T(2,128)}, s32[2]{0:T(128)}, bf16[2,96,128,128]{3,2,1,0:T(8,128)(2,1)}, /*index=...) while((s32[]{:T(128)}, f32[16,128,128]{2,0,1:T(8,128)S(1)}, ...), condition=%wide.region_2.3_spmd.clone, body=%wide.region_0.0_spmd.clone.sunk | while | flops 707269568 | bytes 31465112 | solution.py:49
  20.9 57.2 %all-reduce.11.cloned.1.call-done = bf16[16,128,128]{2,1,0:T(8,128)(2,1)} async-done(((bf16[16,128,128]{2,1,0:T(8,128)(2,1)}), bf16[16,128,128]{2,1,0:T(8,128)(2,1)}) %all-reduce.11.cloned.1.call-update) | async-done | bytes 524304 | tf_op jit(solution)/shard_map/while/body/eval_jaxpr/psum | solution.py:11
  78.1 3.7 gather_fusion
  81.9 3.9 fusion.65
  85.8 5.7 %fusion.67 = f32[16,128,128]{2,0,1:T(8,128)S(1)} fusion(f32[96,128,128]{2,1,0:T(8,128)S(1)} %fusion.65, f32[16,128,128]{2,0,1:T(8,128)S(1)} %get-tuple-element.360, pred[]{:T(512)S(6)} %compare.6, s32[96]{0:T(128)S(1)} %fusion.66, pred[96]{0:T(512)(128)(4,1)S(1)} %iota_compare_fusion.5), kind=kOutput, calls=%fused_computation.14.clone.1 | convolution fusion | flops 302517248 | bytes 8389089 | tf_op jit(solution)/shard_map/while/body/eval_jaxpr/pk,kaf->paf/dot_general | solution.py:45
  96.4 53.8 %all-reduce.11.cloned.1.call-done = bf16[16,128,128]{2,1,0:T(8,128)(2,1)} async-done(((bf16[16,128,128]{2,1,0:T(8,128)(2,1)}), bf16[16,128,128]{2,1,0:T(8,128)(2,1)}) %all-reduce.11.cloned.1.call-update) | async-done | bytes 524304 | tf_op jit(solution)/shard_map/while/body/eval_jaxpr/psum | solution.py:11
  150.2 3.7 gather_fusion
  154.0 3.9 fusion.65
  157.9 5.7 %fusion.67 = f32[16,128,128]{2,0,1:T(8,128)S(1)} fusion(f32[96,128,128]{2,1,0:T(8,128)S(1)} %fusion.65, f32[16,128,128]{2,0,1:T(8,128)S(1)} %get-tuple-element.360, pred[]{:T(512)S(6)} %compare.6, s32[96]{0:T(128)S(1)} %fusion.66, pred[96]{0:T(512)(128)(4,1)S(1)} %iota_compare_fusion.5), kind=kOutput, calls=%fused_computation.14.clone.1 | convolution fusion | flops 302517248 | bytes 8389089 | tf_op jit(solution)/shard_map/while/body/eval_jaxpr/pk,kaf->paf/dot_general | solution.py:45
  167.2 25.6 %reduce-scatter.2.cloned.1.call-done = f32[512,128]{1,0:T(8,128)} async-done(((f32[2048,128]{1,0:T(8,128)}), f32[512,128]{1,0:T(8,128)}) %reduce-scatter.2.cloned.1.call-update) | async-done | bytes 262160 | tf_op jit(solution)/shard_map/reduce_scatter | solution.py:54
  194.3 16.2 %all_gather.7 = bf16[2048,128]{1,0:T(8,128)(2,1)S(1)} all-gather(bf16[512,128]{1,0:T(8,128)(2,1)S(1)} %convolution_convert_fusion), channel_id=1, replica_groups=mesh['section'=8,'rep'=4] {'rep'}, dimensions={0}, use_global_device_ids=true | all-gather | bytes 655360 | tf_op jit(solution)/shard_map/all_gather | solution.py:71
  210.5 8.0 %gather_fusion.2 = bf16[192,128,128]{2,1,0:T(8,128)(2,1)} fusion(bf16[16,128,128]{2,1,0:T(8,128)(2,1)S(1)} %bitcast.60, s32[1024]{0:T(1024)S(1)} %pad_clamp_fusion.1), kind=kCustom, calls=%fused_computation.2 | custom fusion | bytes 12583680 | tf_op jit(solution)/shard_map/jit(_take)/gather | solution.py:74
  218.5 11.6 %fusion.26 = f32[2,96,128,128]{3,2,1,0:T(8,128)} fusion(bf16[2,96,128,128]{3,2,1,0:T(8,128)(2,1)} %bitcast.64, pred[2,96]{1,0:T(4,128)(4,1)S(1)} %compare_and_fusion.2, bf16[1,1,2,96,128,128]{5,4,3,2,1,0:T(8,128)(2,1)} %bitcast.62), kind=kOutput, calls=%fused_computation.34 | convolution fusion | flops 808452096 | bytes 25166016 | tf_op jit(solution)/shard_map/jkab,jkaf->jkbf/dot_general | solution.py:77
  230.1 12.8 %copy.14 = f32[2,96,128,128]{2,1,3,0:T(8,128)} copy(f32[2,96,128,128]{3,2,1,0:T(8,128)} %fusion.26) | data formatting | bytes 25165824 | tf_op jit(solution)/shard_map/jkab,jkaf->jkbf/dot_general | solution.py:77
  242.8 7.2 %fusion.30 = bf16[2,16,128,128]{3,1,2,0:T(8,128)(2,1)S(1)} fusion(f32[2,96,128,128]{2,1,3,0:T(8,128)} %copy.14, s32[2,96]{1,0:T(2,128)S(1)} %copy-done.3, pred[2,96]{1,0:T(4,128)(4,1)S(1)} %iota_compare_fusion.3), kind=kOutput, calls=%fused_computation.38 | convolution fusion | flops 604510208 | bytes 13632448 | tf_op jit(solution)/shard_map/jpk,jkbf->jpbf/dot_general | solution.py:84
  250.1 1.3 copy.12
  252.4 53.3 %all-reduce.7.cloned.1.call-done = bf16[2,2048,128]{2,1,0:T(8,128)(2,1)} async-done(((bf16[2,2048,128]{2,1,0:T(8,128)(2,1)}), bf16[2,2048,128]{2,1,0:T(8,128)(2,1)}) %all-reduce.7.cloned.1.call-update) | async-done | bytes 1048592 | tf_op jit(solution)/shard_map/psum | solution.py:89
  305.7 1.9 fusion.34
  307.7 14.8 %all_gather.6 = bf16[2048,128]{1,0:T(8,128)(2,1)S(1)} all-gather(bf16[512,128]{1,0:T(8,128)(2,1)S(1)} %get-tuple-element.294), channel_id=1, replica_groups=mesh['section'=8,'rep'=4] {'rep'}, dimensions={0}, use_global_device_ids=true | all-gather | bytes 655360 | tf_op jit(solution)/shard_map/all_gather | solution.py:70
  322.5 106.7 %all-reduce.5.cloned.1.call-done = f32[128,128]{1,0:T(8,128)} async-done(((f32[128,128]{1,0:T(8,128)}), f32[128,128]{1,0:T(8,128)}) %all-reduce.5.cloned.1.call-update) | async-done | bytes 65552 | tf_op jit(solution)/shard_map/psum | solution.py:68
  429.2 1.5 broadcast_multiply_fusion
  430.7 41.1 %all-reduce.9.cloned.1.call-done = bf16[2048,128]{1,0:T(8,128)(2,1)} async-done(((bf16[2048,128]{1,0:T(8,128)(2,1)}), bf16[2048,128]{1,0:T(8,128)(2,1)}) %all-reduce.9.cloned.1.call-update) | async-done | bytes 524304 | tf_op jit(solution)/shard_map/psum | solution.py:11
  471.8 6.8 %scatter_custom_fusion = bf16[2048,128]{1,0:T(8,128)(2,1)} fusion(s32[2048]{0:T(1024)S(1)} %get-tuple-element.295, bf16[2048,128]{1,0:T(8,128)(2,1)} %all-reduce.9.cloned.1.call-done, bf16[]{:T(256)} %constant.190.clone.1), kind=kCustom, calls=%fused_computation.44 | custom fusion | bytes 524800 | tf_op jit(solution)/shard_map/scatter | solution.py:94
  (48 shorter events, 18.4 us)
Async XLA Ops:
  8.0 1.5 copy-start
  16.0 176.8 %copy-start.2 = (bf16[128,128]{1,0:T(8,128)(2,1)S(1)}, bf16[128,128]{1,0:T(8,128)(2,1)}, u32[]{:S(2)}) copy-start(bf16[128,128]{1,0:T(8,128)(2,1)} %param.16) | copy-start | bytes 98308
  16.0 62.1 %all-reduce.11.cloned.1.call-start = ((), (), s32[]{:S(2)}) async-start(), calls=%async_computation.5 | async-start | bytes 1048576 | tf_op jit(solution)/shard_map/while/body/eval_jaxpr/psum | solution.py:11
  91.5 58.7 %all-reduce.11.cloned.1.call-start = ((), (), s32[]{:S(2)}) async-start(), calls=%async_computation.5 | async-start | bytes 1048576 | tf_op jit(solution)/shard_map/while/body/eval_jaxpr/psum | solution.py:11
  163.6 29.2 %reduce-scatter.2.cloned.1.call-start = ((), (), s32[]{:S(2)}) async-start(), calls=%async_computation.1 | async-start | bytes 1310720 | tf_op jit(solution)/shard_map/reduce_scatter | solution.py:54
  165.0 140.7 %all-reduce.7.cloned.1.call-start = ((), (), s32[]{:S(2)}) async-start(), calls=%async_computation.3 | async-start | bytes 2097152 | tf_op jit(solution)/shard_map/psum | solution.py:89
  230.1 12.8 %copy-start.3 = (s32[2,96]{1,0:T(2,128)S(1)}, s32[2,96]{1,0:T(2,128)}, u32[]{:S(2)}) copy-start(s32[2,96]{1,0:T(2,128)} %get-tuple-element.411) | copy-start | bytes 2308
  242.8 8.7 %copy-start.1 = (f32[512,128]{1,0:T(8,128)S(1)}, f32[512,128]{1,0:T(8,128)}, u32[]{:S(2)}) copy-start(f32[512,128]{1,0:T(8,128)} %reduce-scatter.2.cloned.1.call-done) | copy-start | bytes 786436
  251.4 177.8 %all-reduce.5.cloned.1.call-start = ((), (), s32[]{:S(2)}) async-start(), calls=%async_computation.2 | async-start | bytes 131072 | tf_op jit(solution)/shard_map/psum | solution.py:68
  252.4 219.4 %all-reduce.9.cloned.1.call-start = ((), (), s32[]{:S(2)}) async-start(), calls=%async_computation.4 | async-start | bytes 1048576 | tf_op jit(solution)/shard_map/psum | solution.py:11
Sparse Core Ops, SparseCore 0:
  20.8 57.2 all-reduce.10
  96.3 53.8 all-reduce.10
Sparse Core Ops, SparseCore 1:
  166.4 26.4 reduce-scatter.1
  251.5 54.2 all-reduce.6
  312.7 116.5 all-reduce.4
  432.3 39.4 all-reduce.8
where the time goes:
time: 488 us; the launch traced here: 487 us
  waiting for transfers between devices  338 us (69%)
  local copies, waits for them, and re-layouts  49.3 us (10%)
  matrix products  40.4 us (8%)
  blocking collectives  31 us (6%)
  between operations  15.8 us (3%)
  other arithmetic  12.4 us (3%)
    psum x3, waiting for transfers between devices, spread(): return lax.psum(kept, axis)  152 us
    psum x1, waiting for transfers between devices, shards(): weight_grad = lax.psum(grad_part, ('section', 'rep')) * grad_scale  107 us
    psum x1, waiting for transfers between devices, shards(): lax.psum(contrib.astype(jnp.bfloat16), 'section').astype(jnp.float32)  53.3 us
    reduce_scatter x1, waiting for transfers between devices, shards(): lax.psum_scatter(partial_sum, 'rep', scatter_dimension=0, tiled=True)  25.6 us
    all_gather x1, blocking collectives, shards(): lax.all_gather(upstream_share, 'rep', axis=0, tiled=True)  16.2 us
    all_gather x1, blocking collectives, shards(): lax.all_gather(hidden_share, 'rep', axis=0, tiled=True)  14.8 us
    dot_general x1, local copies, waits for them, and re-layouts, shards(): jnp.einsum('jkab,jkaf->jkbf', own_tiles, picked_up, preferred_element_typ...  12.8 us
    dot_general x1, matrix products, shards(): jnp.einsum('jkab,jkaf->jkbf', own_tiles, picked_up, preferred_element_typ...  11.6 us
  transfers between devices with their start and end apart: 6, of which 6 were waited for; matrix products, arithmetic and copies ran while one was open for 3% of the time, Pallas kernels for 0%

commit v1 on v0

v1 whole, which is shorter than its diff:
```python
import functools
import math

import jax
import jax.numpy as jnp
from jax import lax
from jax.experimental import pallas as pl
from jax.experimental.pallas import tpu as pltpu
from jax.sharding import PartitionSpec as P

F32 = jnp.float32
BF16 = jnp.bfloat16
MIB = 1 << 20


def params(mib):
    return pltpu.CompilerParams(vmem_limit_bytes=mib * MIB)


def cost(flops, nbytes):
    return pl.CostEstimate(flops=int(flops), bytes_accessed=int(nbytes), transcendentals=0)


def whole_spec(array):
    zeros = (0,) * array.ndim
    return pl.BlockSpec(array.shape, lambda *_: zeros)


def reorder_body(order_ref, feat_ref, out_ref):
    rows, panel = order_ref.shape[0], feat_ref.shape[0]
    hot = lax.broadcasted_iota(jnp.int32, (rows, panel), 1) == order_ref[...]
    hot = jnp.where(hot, 1.0, 0.0).astype(BF16)
    out_ref[...] = jnp.dot(hot, feat_ref[...], preferred_element_type=F32).astype(BF16)


def reorder(order_col, features, part, parts):
    panel, width = features.shape
    rows = panel // parts
    step = min(256, rows)
    first = part * (rows // step)
    return pl.pallas_call(
        reorder_body,
        out_shape=jax.ShapeDtypeStruct((rows, width), BF16),
        grid=(rows // step,),
        in_specs=[
            pl.BlockSpec((step, 1), lambda i: (first + i, 0)),
            whole_spec(features),
        ],
        out_specs=pl.BlockSpec((step, width), lambda i: (i, 0)),
        compiler_params=params(32),
        cost_estimate=cost(2 * rows * panel * width, 4 * rows * width),
        name="reorder",
    )(order_col, features)


def lay_body(rows_ref, cols_ref, live_ref, tile_ref, out_ref):
    j, g = pl.program_id(0), pl.program_id(1)
    group, block = tile_ref.shape[1], tile_ref.shape[2]
    panel = out_ref.shape[1]

    @pl.when(g == 0)
    def _():
        @pl.loop(0, panel // block)
        def _(i):
            at = pl.multiple_of(i * block, block)
            out_ref[0, pl.ds(at, block), :] = jnp.zeros((block, panel), BF16)

    for k in range(group):
        slot = g * group + k

        @pl.when(slot < live_ref[j])
        def _():
            row = pl.multiple_of(rows_ref[j, slot] * block, block)
            col = pl.multiple_of(cols_ref[j, slot] * block, block)
            out_ref[0, pl.ds(row, block), pl.ds(col, block)] = tile_ref[0, k]


def lay_out(tiles, rows, cols, live, panel):
    rounds, slots, block, _ = tiles.shape
    group = math.gcd(slots, 16)
    return pl.pallas_call(
        lay_body,
        out_shape=jax.ShapeDtypeStruct((rounds, panel, panel), BF16),
        grid_spec=pltpu.PrefetchScalarGridSpec(
            num_scalar_prefetch=3,
            grid=(rounds, slots // group),
            in_specs=[pl.BlockSpec((1, group, block, block), lambda j, g, *_: (j, g, 0, 0))],
            out_specs=pl.BlockSpec((1, panel, panel), lambda j, g, *_: (j, 0, 0)),
        ),
        compiler_params=params(40),
        cost_estimate=cost(0, 2 * rounds * panel * panel * 2),
        name="lay_out",
    )(rows, cols, live, tiles)


def forward_body(ids_ref, a_ref, *refs):
    xs, out_ref = refs[:-1], refs[-1]
    halves = len(xs) // a_ref.shape[0]
    acc = None
    for n, x_ref in enumerate(xs):
        slot, half = n // halves, n % halves
        rows = x_ref.shape[0]
        left = a_ref[ids_ref[1 + slot], :, half * rows : (half + 1) * rows]
        term = jnp.dot(left, x_ref[...], preferred_element_type=F32)
        acc = term if acc is None else acc + term
    out_ref[...] = acc.astype(out_ref.dtype)


def forward_share(ids, dense, xs, share_rows, dtype):
    rounds, panel, _ = dense.shape
    width = xs[0].shape[1]
    step = 128
    per = share_rows // step
    return pl.pallas_call(
        forward_body,
        out_shape=jax.ShapeDtypeStruct((share_rows, width), dtype),
        grid_spec=pltpu.PrefetchScalarGridSpec(
            num_scalar_prefetch=1,
            grid=(per,),
            in_specs=[
                pl.BlockSpec((rounds, step, panel), lambda i, ids: (0, ids[0] * per + i, 0))
            ]
            + [whole_spec(x) for x in xs],
            out_specs=pl.BlockSpec((step, width), lambda i, ids: (i, 0)),
        ),
        compiler_params=params(32),
        cost_estimate=cost(
            2 * rounds * share_rows * panel * width, 2 * rounds * share_rows * panel
        ),
        name="forward_share",
    )(ids, dense, *xs)


def middle_body(ids_ref, w_ref, co_ref, *refs):
    count = len(refs) - 5
    shares = refs[:count]
    hidden_ref, up_ref, grad_ref, agg_all, pre_all = refs[count:]
    weight = w_ref[...]
    rows = shares[0].shape[0]
    for n, share in enumerate(shares):
        at = pl.multiple_of(ids_ref[n] * rows, rows)
        agg = share[...]
        agg_all[pl.ds(at, rows), :] = agg
        pre = jnp.dot(agg, weight, preferred_element_type=F32)
        gate = 1.0 / (1.0 + jnp.exp(-pre))
        hidden_ref[pl.ds(at, rows), :] = (pre * gate).astype(BF16)
        co = co_ref[pl.ds(at, rows), :].astype(F32)
        grad_pre = (co * gate * (1.0 + pre * (1.0 - gate))).astype(BF16)
        pre_all[pl.ds(at, rows), :] = grad_pre
        up_ref[:, pl.ds(at, rows)] = lax.dot_general(
            weight, grad_pre, (((1,), (1,)), ((), ())), preferred_element_type=F32
        ).astype(BF16)
    grad_ref[...] = lax.dot_general(
        agg_all[...], pre_all[...], (((0,), (0,)), ((), ())), preferred_element_type=F32
    )


def middle(ids, weight, cotangent, shares):
    panel, width = cotangent.shape
    operands = (weight, cotangent, *shares)
    return pl.pallas_call(
        middle_body,
        out_shape=(
            jax.ShapeDtypeStruct((panel, width), BF16),
            jax.ShapeDtypeStruct((width, panel), BF16),
            jax.ShapeDtypeStruct((width, width), F32),
        ),
        grid_spec=pltpu.PrefetchScalarGridSpec(
            num_scalar_prefetch=1,
            grid=(1,),
            in_specs=[whole_spec(x) for x in operands],
            out_specs=[
                pl.BlockSpec((panel, width), lambda *_: (0, 0)),
                pl.BlockSpec((width, panel), lambda *_: (0, 0)),
                pl.BlockSpec((width, width), lambda *_: (0, 0)),
            ],
            scratch_shapes=[pltpu.VMEM((panel, width), BF16)] * 2,
        ),
        compiler_params=params(32),
        cost_estimate=cost(6 * panel * width * width, 8 * panel * width),
        name="middle",
    )(ids, *operands)


def backward_body(ids_ref, up_ref, a_ref, out_ref):
    out_ref[0, 0] = jnp.dot(up_ref[...], a_ref[0], preferred_element_type=F32).astype(
        out_ref.dtype
    )


def backward(ids, dense, upstream, pairs, chips, dtype):
    panel = dense.shape[1]
    width = upstream.shape[0]
    length = panel // chips
    return pl.pallas_call(
        backward_body,
        out_shape=jax.ShapeDtypeStruct((chips, pairs, width, length), dtype),
        grid_spec=pltpu.PrefetchScalarGridSpec(
            num_scalar_prefetch=1,
            grid=(chips, pairs),
            in_specs=[
                whole_spec(upstream),
                pl.BlockSpec((1, panel, length), lambda d, p, ids: (ids[chips + p], 0, ids[d])),
            ],
            out_specs=pl.BlockSpec((1, 1, width, length), lambda d, p, ids: (d, p, 0, 0)),
        ),
        compiler_params=params(32),
        cost_estimate=cost(2 * pairs * panel * panel * width, 2 * pairs * panel * panel),
        name="backward",
    )(ids, upstream, dense)


def restore_body(ids_ref, order_ref, *refs):
    parts, out_ref = refs[:-1], refs[-1]
    rows = out_ref.shape[0]
    length = parts[0].shape[1]
    base = pl.program_id(0) * rows
    acc = None
    for n, part in enumerate(parts):
        at = pl.multiple_of(ids_ref[n] * length, length)
        target = order_ref[:, pl.ds(at, length)]
        hot = lax.broadcasted_iota(jnp.int32, (rows, length), 0) + base == target
        hot = jnp.where(hot, 1.0, 0.0).astype(BF16)
        term = lax.dot_general(
            hot, part[...], (((1,), (1,)), ((), ())), preferred_element_type=F32
        )
        acc = term if acc is None else acc + term
    out_ref[...] = acc.astype(BF16)


def restore(ids, order_row, parts, panel):
    width = parts[0].shape[0]
    rows = 256
    return pl.pallas_call(
        restore_body,
        out_shape=jax.ShapeDtypeStruct((panel, width), BF16),
        grid_spec=pltpu.PrefetchScalarGridSpec(
            num_scalar_prefetch=1,
            grid=(panel // rows,),
            in_specs=[whole_spec(order_row)] + [whole_spec(p) for p in parts],
            out_specs=pl.BlockSpec((rows, width), lambda i, ids: (i, 0)),
        ),
        compiler_params=params(32),
        cost_estimate=cost(2 * panel * panel * width, 4 * panel * width),
        name="restore",
    )(ids, order_row, *parts)


def tree_sum(terms):
    while len(terms) > 1:
        terms = [terms[i] + terms[i + 1] for i in range(0, len(terms), 2)]
    return terms[0]


def shards(features, order, tiles, tile_rows, tile_cols, live, weight, cotangent):
    reps = lax.axis_size("rep")
    sections = lax.axis_size("section")
    rep = lax.axis_index("rep")
    section = lax.axis_index("section")
    panel, width = features.shape
    rounds = tiles.shape[2]
    chips = sections // 2
    pairs = rounds // 2
    near = reps // 2
    share_rows = panel // reps
    length = panel // chips
    chip, core = section // 2, section % 2

    def over_chips(x, d):
        return lax.ppermute(x, "section", [(s, s ^ (2 * d)) for s in range(sections)])

    def over_cores(x):
        return lax.ppermute(x, "section", [(s, s ^ 1) for s in range(sections)])

    def over_reps(x, d):
        return lax.ppermute(x, "rep", [(r, r ^ d) for r in range(reps)])

    def from_owner(x, d):
        moves = []
        for r in range(reps):
            for j in range(rounds):
                source = j * reps + r
                target = (source ^ (2 * d)) ^ ((d // near) & 1)
                moves.append((source * reps + r, target * reps + r))
        return lax.ppermute(x, ("section", "rep"), moves)

    side = core ^ (rep % 2)
    low = (chip % near) ^ (rep // 2)
    row_of_chip = chip // near
    order_col = order.reshape(panel, 1)
    halves = 2
    mine = [[] for _ in range(pairs)]
    mate = [[] for _ in range(pairs)]
    for h in range(halves):
        own = reorder(order_col, features, h, halves)
        got = [own] + [from_owner(own, d) for d in range(1, chips)]
        for p in range(pairs):
            picked = got[2 * p * near]
            for e in range(2):
                for l in range(near):
                    if e or l:
                        picked = jnp.where(
                            (side == e) & (low == l), got[(2 * p + e) * near + l], picked
                        )
            mine[p].append(picked)
            mate[p].append(over_cores(picked))
    dense = lay_out(tiles[0, 0], tile_rows[0, 0], tile_cols[0, 0], live[0, 0], panel)
    xs, slot_ids = [], []
    for p in range(pairs):
        xs += mine[p] + mate[p]
        slot_ids += [row_of_chip ^ (2 * p + side), row_of_chip ^ (2 * p + 1 - side)]

    def share_of(d, dtype):
        ids = jnp.stack([rep ^ d] + slot_ids).astype(jnp.int32)
        return forward_share(ids, dense, xs, share_rows, dtype)

    sent = {d: over_reps(share_of(d, BF16), d) for d in reversed(range(1, reps))}
    total = share_of(0, F32)
    for d in range(1, reps):
        total = total + sent[d].astype(F32)
    aggregated = total.astype(BF16)
    shares = [aggregated] + [over_reps(aggregated, d) for d in range(1, reps)]
    share_ids = jnp.stack([rep ^ d for d in range(reps)]).astype(jnp.int32)
    hidden, upstream, grad_part = middle(share_ids, weight, cotangent, shares)

    chunk_ids = [chip ^ d for d in range(chips)]
    give = jnp.stack(chunk_ids + [2 * p + 1 - core for p in range(pairs)]).astype(jnp.int32)
    keep = jnp.stack(chunk_ids + [2 * p + core for p in range(pairs)]).astype(jnp.int32)
    given = over_cores(backward(give, dense, upstream, pairs, chips, BF16))
    kept = backward(keep, dense, upstream, pairs, chips, F32)
    chunks = [kept[d] + given[d].astype(F32) for d in range(chips)]
    arrived = [over_chips(chunks[d].astype(BF16), d).astype(F32) for d in range(1, chips)]
    reduced = tree_sum([chunks[0]] + arrived).astype(BF16)

    grad_part = grad_part + over_cores(grad_part)
    weight_grad = tree_sum([grad_part] + [over_chips(grad_part, d) for d in range(1, chips)])
    weight_grad = weight_grad * (1.0 / math.sqrt(panel * sections))

    spread = [reduced] + [over_reps(reduced, d) for d in range(1, reps)]
    stacked = jnp.stack(spread)

    def to_owner(k):
        moves = []
        for s in range(sections):
            u = (s // 2) ^ k
            moves.append((s, (2 * (u // reps) + s % 2) * reps + u % reps))
        u = chip ^ k
        block = stacked[(u % reps) ^ rep, u // reps]
        return lax.ppermute(block, "section", moves)

    parts = [to_owner(k) for k in range(chips)]
    mine_u = (section // reps // 2) * reps + section % reps
    part_ids = jnp.stack([mine_u ^ k for k in range(chips)]).astype(jnp.int32)
    feature_grad = restore(part_ids, order.reshape(1, panel), parts, panel)
    return (hidden, weight_grad, feature_grad)


def solution(mesh):
    placed = (
        P("section", None),
        P("section"),
        P("section", "rep", None, None, None, None),
        P("section", "rep", None, None),
        P("section", "rep", None, None),
        P("section", "rep", None),
        P(),
        P("section", None),
    )
    return jax.shard_map(
        shards,
        mesh=mesh,
        in_specs=placed,
        out_specs=(P("section", None), P(), P("section", None)),
        check_vma=False,
    )
```

time: 488 us -> 139 us (0.28)
  waiting for transfers between devices: 338 us -> 32.2 us
  matrix products: 40.4 us -> 0 us
  starting transfers between devices: 0.26 us -> 40.5 us
  Pallas kernels: 0 us -> 37.3 us
  blocking collectives: 31 us -> 0 us
  local copies, waits for them, and re-layouts: 49.3 us -> 24.4 us
  between operations: 15.8 us -> 1.04 us
  other arithmetic: 12.4 us -> 1.58 us
    psum x5 -> x0, waiting for transfers between devices: 312 us -> none  [the longest x3 152 us: spread(): return lax.psum(kept, axis)]
    ppermute x0 -> x29, starting transfers between devices: none -> 40.5 us  [the longest x9 16.2 us: over_reps(): return lax.ppermute(x, 'rep', [(r, r ^ d) for r in range(reps)])]
    dot_general x9 -> x0, matrix products: 40.4 us -> none  [the longest x1 11.6 us: shards(): jnp.einsum('jkab,jkaf->jkbf', own_tiles, picked_up, preferred_element_typ...]
    pallas_call x0 -> x11, Pallas kernels: none -> 37.3 us  [the longest x4 10.4 us: forward_share(): pl.pallas_call(forward_body, out_shape=jax.ShapeDtypeStruct((share_rows,...]
    ppermute x0 -> x29, waiting for transfers between devices: none -> 32.2 us  [the longest x9 16.3 us: over_reps(): return lax.ppermute(x, 'rep', [(r, r ^ d) for r in range(reps)])]
    all_gather x2 -> x0, blocking collectives: 31 us -> none  [the longest x1 16.2 us: shards(): lax.all_gather(upstream_share, 'rep', axis=0, tiled=True)]
    reduce_scatter x1 -> x0, waiting for transfers between devices: 25.6 us -> none  [shards(): lax.psum_scatter(partial_sum, 'rep', scatter_dimension=0, tiled=True)]
    unnamed x9 -> x22, local copies, waits for them, and re-layouts: 0.82 us -> 23.2 us
  transfers between devices with their start and end apart: 6 -> 29, of which waited for: 6 -> 14; matrix products, arithmetic and copies ran while one was open for 3% -> 1% of each run, Pallas kernels for 0% -> 16%
where the time goes in v1:
time: 139 us; the launch traced here: 137 us
  starting transfers between devices  40.5 us (29%)
  Pallas kernels  37.3 us (27%)
  waiting for transfers between devices  32.2 us (23%)
  local copies, waits for them, and re-layouts  24.4 us (18%)
  other arithmetic  1.58 us (1%)
    unnamed x22, local copies, waits for them, and re-layouts  23.2 us
    ppermute x9, waiting for transfers between devices, over_reps(): return lax.ppermute(x, 'rep', [(r, r ^ d) for r in range(reps)])  16.3 us
    ppermute x9, starting transfers between devices, over_reps(): return lax.ppermute(x, 'rep', [(r, r ^ d) for r in range(reps)])  16.2 us
    ppermute x6, starting transfers between devices, from_owner(): return lax.ppermute(x, ('section', 'rep'), moves)  11.4 us
    pallas_call x4, Pallas kernels, forward_share(): pl.pallas_call(forward_body, out_shape=jax.ShapeDtypeStruct((share_rows,...  10.4 us
    pallas_call x1, Pallas kernels, lay_out(): pl.pallas_call(lay_body, out_shape=jax.ShapeDtypeStruct((rounds, panel, p...  9.56 us
    ppermute x6, waiting for transfers between devices, over_chips(): return lax.ppermute(x, 'section', [(s, s ^ 2 * d) for s in range(sections)])  8.06 us
    ppermute x6, starting transfers between devices, over_chips(): return lax.ppermute(x, 'section', [(s, s ^ 2 * d) for s in range(sections)])  6.65 us
  transfers between devices with their start and end apart: 29, of which 14 were waited for; matrix products, arithmetic and copies ran while one was open for 1% of the time, Pallas kernels for 16%

profile of v1, /device:TPU:0, one launch (start us, length us, event | category | flops | bytes accessed | tf_op | source)
XLA Modules:
  0.0 137.0 jit_solution(16997287163336627327)
XLA Ops:
  4.7 4.9 %collective-permute-start.2 = (bf16[1024,128]{1,0:T(8,128)(2,1)S(1)}, bf16[1024,128]{1,0:T(8,128)(2,1)S(1)}, u32[]{:S(2)}, u32[]{:S(2)}) collective-permute-start(bf16[1024,128]{1,0:T(8,128)(2,1)S(1)} %reorder.2), channel_id=1, source_target_pairs={{0,8},{16,24},{5,13},{21,29},{10,2},{26,18},{15,7},{31,23}} | collective-permute-start | bytes 786440 | tf_op jit(solution)/shard_map/ppermute | solution.py:285
  22.6 2.8 %copy-done.3 = bf16[1,1,2,96,128,128]{5,4,3,2,1,0:T(8,128)(2,1)S(1)} copy-done((bf16[1,1,2,96,128,128]{5,4,3,2,1,0:T(8,128)(2,1)S(1)}, bf16[1,1,2,96,128,128]{5,4,3,2,1,0:T(8,128)(2,1)}, u32[]{:S(2)}) %copy-start.3) | copy-done | bytes 6291480
  27.4 9.6 %lay_out.1.a_ref = bf16[2,2048,2048]{2,1,0:T(8,128)(2,1)} custom-call(s32[2,96]{1,0:T(2,128)S(1)} %bitcast.51, s32[2,96]{1,0:T(2,128)S(1)} %bitcast.52, s32[2]{0:T(128)S(1)} %bitcast.53, bf16[2,96,128,128]{3,2,1,0:T(8,128)(2,1)S(1)} %bitcast.48), custom_call_target="tpu_custom_call" | custom-call | bytes 33554432 | tf_op jit(solution)/shard_map/lay_out/pallas_call | solution.py:81
  37.2 5.8 %copy-done = bf16[2,2048,2048]{2,1,0:T(8,128)(2,1)S(1)} copy-done((bf16[2,2048,2048]{2,1,0:T(8,128)(2,1)S(1)}, bf16[2,2048,2048]{2,1,0:T(8,128)(2,1)}, u32[]{:S(2)}) %copy-start) | copy-done | bytes 16777240
  42.9 2.6 %forward_share.5 = bf16[512,128]{1,0:T(8,128)(2,1)S(1)} custom-call(s32[3]{0:T(128)S(1)} %add_add_fusion.1.ids_ref, bf16[2,2048,2048]{2,1,0:T(8,128)(2,1)S(1)} %copy-done, bf16[1024,128]{1,0:T(8,128)(2,1)S(1)} %select_select_fusion.1.refs_0_, bf16[1024,128]{1,0:T(8,128)(2,1)S(1)} %select_select_fusion.refs_1_, ...), custom_call_target="tpu_custom_call" | custom-call | flops 536870912 | bytes 4194304 | tf_op jit(solution)/shard_map/forward_share/pallas_call | solution.py:114
  46.7 2.6 %forward_share.6 = bf16[512,128]{1,0:T(8,128)(2,1)S(1)} custom-call(s32[3]{0:T(128)S(1)} %add_add_fusion.2.ids_ref, bf16[2,2048,2048]{2,1,0:T(8,128)(2,1)S(1)} %copy-done, bf16[1024,128]{1,0:T(8,128)(2,1)S(1)} %select_select_fusion.1.refs_0_, bf16[1024,128]{1,0:T(8,128)(2,1)S(1)} %select_select_fusion.refs_1_, ...), custom_call_target="tpu_custom_call" | custom-call | flops 536870912 | bytes 4194304 | tf_op jit(solution)/shard_map/forward_share/pallas_call | solution.py:114
  49.3 3.4 %collective-permute-start.9 = (bf16[512,128]{1,0:T(8,128)(2,1)S(1)}, bf16[512,128]{1,0:T(8,128)(2,1)S(1)}, u32[]{:S(2)}, u32[]{:S(2)}) collective-permute-start(bf16[512,128]{1,0:T(8,128)(2,1)S(1)} %forward_share.6), channel_id=1, source_target_pairs={{0,2},{1,3},{2,0},{3,1},{4,6},{5,7},{6,4},{7,5},{8,10},{9,11},{10,... | collective-permute-start | bytes 393224 | tf_op jit(solution)/shard_map/ppermute | solution.py:276
  52.7 2.6 %forward_share.7 = bf16[512,128]{1,0:T(8,128)(2,1)S(1)} custom-call(s32[3]{0:T(128)S(1)} %add_add_fusion.3.ids_ref, bf16[2,2048,2048]{2,1,0:T(8,128)(2,1)S(1)} %copy-done, bf16[1024,128]{1,0:T(8,128)(2,1)S(1)} %select_select_fusion.1.refs_0_, bf16[1024,128]{1,0:T(8,128)(2,1)S(1)} %select_select_fusion.refs_1_, ...), custom_call_target="tpu_custom_call" | custom-call | flops 536870912 | bytes 4194304 | tf_op jit(solution)/shard_map/forward_share/pallas_call | solution.py:114
  56.9 2.6 %forward_share.4 = f32[512,128]{1,0:T(8,128)S(1)} custom-call(s32[3]{0:T(128)S(1)} %add_add_fusion.ids_ref, bf16[2,2048,2048]{2,1,0:T(8,128)(2,1)S(1)} %copy-done, bf16[1024,128]{1,0:T(8,128)(2,1)S(1)} %select_select_fusion.1.refs_0_, bf16[1024,128]{1,0:T(8,128)(2,1)S(1)} %select_select_fusion.refs_1_, bf16[1024,128]{1,0:T(8,128)(2,1)S(1)} %collective-permute-done.6.refs_2_, ...), custom_call_target="tpu_custom_call" | custom-call | flops 536870912 | bytes 4194304 | tf_op jit(solution)/shard_map/forward_share/pallas_call | solution.py:114
  59.6 3.0 %collective-permute-done.10 = bf16[512,128]{1,0:T(8,128)(2,1)S(1)} collective-permute-done((bf16[512,128]{1,0:T(8,128)(2,1)S(1)}, bf16[512,128]{1,0:T(8,128)(2,1)S(1)}, u32[]{:S(2)}, u32[]{:S(2)}) %collective-permute-start.10) | collective-permute-done | bytes 131104 | tf_op jit(solution)/shard_map/ppermute | solution.py:276
  62.7 3.3 %collective-permute-start.13 = (bf16[512,128]{1,0:T(8,128)(2,1)S(1)}, bf16[512,128]{1,0:T(8,128)(2,1)S(1)}, u32[]{:S(2)}, u32[]{:S(2)}) collective-permute-start(bf16[512,128]{1,0:T(8,128)(2,1)S(1)} %add_convert_fusion.refs_0_), channel_id=1, source_target_pairs={{0,3},{1,2},{2,1},{3,0},{4,7},{5,6},{6,5},{7,4},{8,11},{9,10},{10,... | collective-permute-start | bytes 393224 | tf_op jit(solution)/shard_map/ppermute | solution.py:276
  69.7 8.3 %collective-permute-done.12.refs_2_ = bf16[512,128]{1,0:T(8,128)(2,1)S(1)} collective-permute-done((bf16[512,128]{1,0:T(8,128)(2,1)S(1)}, bf16[512,128]{1,0:T(8,128)(2,1)S(1)}, u32[]{:S(2)}, u32[]{:S(2)}) %collective-permute-start.12) | collective-permute-done | bytes 131104 | tf_op jit(solution)/shard_map/ppermute | solution.py:276
  78.0 2.0 %middle.1 = (bf16[2048,128]{1,0:T(8,128)(2,1)}, bf16[128,2048]{1,0:T(8,128)(2,1)S(1)}, f32[128,128]{1,0:T(8,128)S(1)}) custom-call(s32[4]{0:T(128)S(1)} %pad_add_fusion.ids_ref, bf16[128,128]{1,0:T(8,128)(2,1)S(1)} %copy-done.5, bf16[2048,128]{1,0:T(8,128)(2,1)S(1)} %copy-done.4, bf16[512,128]{1,0:T(8,128)(2,1)S(1)} %add_convert_fusion.refs_0_, ...), custom_call_target="tpu_custom_call" | custom-call | flops 201326592 | bytes 2097152 | tf_op jit(solution)/shard_map/middle/pallas_call | solution.py:161
  80.0 5.8 %copy-done.1 = bf16[2,2048,2048]{2,1,0:T(8,128)(2,1)S(1)} copy-done((bf16[2,2048,2048]{2,1,0:T(8,128)(2,1)S(1)}, bf16[2,2048,2048]{2,1,0:T(8,128)(2,1)}, u32[]{:S(2)}) %copy-start.1) | copy-done | bytes 16777240
  85.8 3.1 %backward.3 = bf16[4,1,128,512]{3,2,1,0:T(8,128)(2,1)S(1)} custom-call(s32[5]{0:T(128)S(1)} %stack.124.ids_ref, bf16[128,2048]{1,0:T(8,128)(2,1)S(1)} %get-tuple-element.8.up_ref, bf16[2,2048,2048]{2,1,0:T(8,128)(2,1)S(1)} %copy-done.1), custom_call_target="tpu_custom_call" | custom-call | flops 1073741824 | bytes 8388608 | tf_op jit(solution)/shard_map/backward/pallas_call | solution.py:195
  89.1 5.8 %copy-done.2 = bf16[2,2048,2048]{2,1,0:T(8,128)(2,1)S(1)} copy-done((bf16[2,2048,2048]{2,1,0:T(8,128)(2,1)S(1)}, bf16[2,2048,2048]{2,1,0:T(8,128)(2,1)}, u32[]{:S(2)}) %copy-start.2) | copy-done | bytes 16777240
  94.8 3.1 %backward.2 = f32[4,1,128,512]{3,2,1,0:T(8,128)S(1)} custom-call(s32[5]{0:T(128)S(1)} %stack.122.ids_ref, bf16[128,2048]{1,0:T(8,128)(2,1)S(1)} %get-tuple-element.8.up_ref, bf16[2,2048,2048]{2,1,0:T(8,128)(2,1)S(1)} %copy-done.2), custom_call_target="tpu_custom_call" | custom-call | flops 1073741824 | bytes 8388608 | tf_op jit(solution)/shard_map/backward/pallas_call | solution.py:195
  101.6 2.8 %collective-permute-done.19 = bf16[1,128,512]{2,1,0:T(8,128)(2,1)S(1)} collective-permute-done((bf16[1,128,512]{2,1,0:T(8,128)(2,1)S(1)}, bf16[1,128,512]{2,1,0:T(8,128)(2,1)S(1)}, u32[]{:S(2)}, u32[]{:S(2)}) %collective-permute-start.19) | collective-permute-done | bytes 131104 | tf_op jit(solution)/shard_map/ppermute | solution.py:270
  104.4 3.9 %collective-permute-done.21 = bf16[1,128,512]{2,1,0:T(8,128)(2,1)S(1)} collective-permute-done((bf16[1,128,512]{2,1,0:T(8,128)(2,1)S(1)}, bf16[1,128,512]{2,1,0:T(8,128)(2,1)S(1)}, u32[]{:S(2)}, u32[]{:S(2)}) %collective-permute-start.21) | collective-permute-done | bytes 131104 | tf_op jit(solution)/shard_map/ppermute | solution.py:270
  109.8 2.6 %collective-permute-start.24 = (bf16[1,128,512]{2,1,0:T(8,128)(2,1)S(1)}, bf16[1,128,512]{2,1,0:T(8,128)(2,1)S(1)}, u32[]{:S(2)}, u32[]{:S(2)}) collective-permute-start(bf16[1,128,512]{2,1,0:T(8,128)(2,1)S(1)} %fusion.6), channel_id=1, source_target_pairs={{0,3},{1,2},{2,1},{3,0},{4,7},{5,6},{6,5},{7,4},{8,11},{9,10},{10,... | collective-permute-start | bytes 393224 | tf_op jit(solution)/shard_map/ppermute | solution.py:276
  119.1 3.4 %collective-permute-done.23 = bf16[1,128,512]{2,1,0:T(8,128)(2,1)S(1)} collective-permute-done((bf16[1,128,512]{2,1,0:T(8,128)(2,1)S(1)}, bf16[1,128,512]{2,1,0:T(8,128)(2,1)S(1)}, u32[]{:S(2)}, u32[]{:S(2)}) %collective-permute-start.23) | collective-permute-done | bytes 131104 | tf_op jit(solution)/shard_map/ppermute | solution.py:276
  124.6 3.0 %collective-permute-start.26 = (bf16[128,512]{1,0:T(8,128)(2,1)S(1)}, bf16[128,512]{1,0:T(8,128)(2,1)S(1)}, u32[]{:S(2)}, u32[]{:S(2)}) collective-permute-start(bf16[128,512]{1,0:T(8,128)(2,1)S(1)} %get-tuple-element.14), channel_id=1, source_target_pairs={{0,4},{4,20},{8,0},{12,16},{16,12},{20,28},{24,8},{28,24},{1,5},{5... | collective-permute-start | bytes 393224 | tf_op jit(solution)/shard_map/ppermute | solution.py:349
  128.9 2.8 %collective-permute-done.28.refs_3_ = bf16[128,512]{1,0:T(8,128)(2,1)S(1)} collective-permute-done((bf16[128,512]{1,0:T(8,128)(2,1)S(1)}, bf16[128,512]{1,0:T(8,128)(2,1)S(1)}, u32[]{:S(2)}, u32[]{:S(2)}) %collective-permute-start.28) | collective-permute-done | bytes 131104 | tf_op jit(solution)/shard_map/ppermute | solution.py:349
  131.7 5.2 %restore.1 = bf16[2048,128]{1,0:T(8,128)(2,1)} custom-call(s32[4]{0:T(128)S(1)} %pad_add_fusion.1.ids_ref, s32[1,2048]{1,0:T(1,128)S(1)} %bitcast.50, bf16[128,512]{1,0:T(8,128)(2,1)S(1)} %collective-permute-done.25.refs_0_, bf16[128,512]{1,0:T(8,128)(2,1)S(1)} %collective-permute-done.26.refs_1_, bf16[128,512]{1,0:T(8,128)(2,1)S(1)} %collective-permute-done.27.refs_2_, ...), custom_call_target="tpu_custom_call" | custom-call | flops 1073741824 | bytes 1048576 | tf_op jit(solution)/shard_map/restore/pallas_call | solution.py:234
  (85 shorter events, 41.2 us)
Async XLA Ops:
  4.7 12.1 %collective-permute-start.2 = (bf16[1024,128]{1,0:T(8,128)(2,1)S(1)}, bf16[1024,128]{1,0:T(8,128)(2,1)S(1)}, u32[]{:S(2)}, u32[]{:S(2)}) collective-permute-start(bf16[1024,128]{1,0:T(8,128)(2,1)S(1)} %reorder.2), channel_id=1, source_target_pairs={{0,8},{16,24},{5,13},{21,29},{10,2},{26,18},{15,7},{31,23}} | collective-permute-start | bytes 786440 | tf_op jit(solution)/shard_map/ppermute | solution.py:285
  9.6 8.6 %collective-permute-start.1 = (bf16[1024,128]{1,0:T(8,128)(2,1)S(1)}, bf16[1024,128]{1,0:T(8,128)(2,1)S(1)}, u32[]{:S(2)}, u32[]{:S(2)}) collective-permute-start(bf16[1024,128]{1,0:T(8,128)(2,1)S(1)} %reorder.2), channel_id=1, source_target_pairs={{0,20},{16,4},{5,17},{21,1},{10,30},{26,14},{15,27},{31,11}} | collective-permute-start | bytes 786440 | tf_op jit(solution)/shard_map/ppermute | solution.py:285
  10.9 7.3 %collective-permute-start = (bf16[1024,128]{1,0:T(8,128)(2,1)S(1)}, bf16[1024,128]{1,0:T(8,128)(2,1)S(1)}, u32[]{:S(2)}, u32[]{:S(2)}) collective-permute-start(bf16[1024,128]{1,0:T(8,128)(2,1)S(1)} %reorder.2), channel_id=1, source_target_pairs={{0,28},{16,12},{5,25},{21,9},{10,22},{26,6},{15,19},{31,3}} | collective-permute-start | bytes 786440 | tf_op jit(solution)/shard_map/ppermute | solution.py:285
  18.3 18.9 %collective-permute-start.6 = (bf16[1024,128]{1,0:T(8,128)(2,1)S(1)}, bf16[1024,128]{1,0:T(8,128)(2,1)S(1)}, u32[]{:S(2)}, u32[]{:S(2)}) collective-permute-start(bf16[1024,128]{1,0:T(8,128)(2,1)S(1)} %select_select_fusion.1.refs_0_), channel_id=1, source_target_pairs={{0,4},{4,0},{8,12},{12,8},{16,20},{20,16},{24,28},{28,24},{1,5},{5... | collective-permute-start | bytes 786440 | tf_op jit(solution)/shard_map/ppermute | solution.py:273
  22.2 15.0 %collective-permute-start.7 = (bf16[1024,128]{1,0:T(8,128)(2,1)S(1)}, bf16[1024,128]{1,0:T(8,128)(2,1)S(1)}, u32[]{:S(2)}, u32[]{:S(2)}) collective-permute-start(bf16[1024,128]{1,0:T(8,128)(2,1)S(1)} %select_select_fusion.refs_1_), channel_id=1, source_target_pairs={{0,4},{4,0},{8,12},{12,8},{16,20},{20,16},{24,28},{28,24},{1,5},{5... | collective-permute-start | bytes 786440 | tf_op jit(solution)/shard_map/ppermute | solution.py:273
  45.5 14.0 %collective-permute-start.8 = (bf16[512,128]{1,0:T(8,128)(2,1)S(1)}, bf16[512,128]{1,0:T(8,128)(2,1)S(1)}, u32[]{:S(2)}, u32[]{:S(2)}) collective-permute-start(bf16[512,128]{1,0:T(8,128)(2,1)S(1)} %forward_share.5), channel_id=1, source_target_pairs={{0,1},{1,0},{2,3},{3,2},{4,5},{5,4},{6,7},{7,6},{8,9},{9,8},{10,11... | collective-permute-start | bytes 393224 | tf_op jit(solution)/shard_map/ppermute | solution.py:276
  49.3 10.3 %collective-permute-start.9 = (bf16[512,128]{1,0:T(8,128)(2,1)S(1)}, bf16[512,128]{1,0:T(8,128)(2,1)S(1)}, u32[]{:S(2)}, u32[]{:S(2)}) collective-permute-start(bf16[512,128]{1,0:T(8,128)(2,1)S(1)} %forward_share.6), channel_id=1, source_target_pairs={{0,2},{1,3},{2,0},{3,1},{4,6},{5,7},{6,4},{7,5},{8,10},{9,11},{10,... | collective-permute-start | bytes 393224 | tf_op jit(solution)/shard_map/ppermute | solution.py:276
  55.3 7.2 %collective-permute-start.10 = (bf16[512,128]{1,0:T(8,128)(2,1)S(1)}, bf16[512,128]{1,0:T(8,128)(2,1)S(1)}, u32[]{:S(2)}, u32[]{:S(2)}) collective-permute-start(bf16[512,128]{1,0:T(8,128)(2,1)S(1)} %forward_share.7), channel_id=1, source_target_pairs={{0,3},{1,2},{2,1},{3,0},{4,7},{5,6},{6,5},{7,4},{8,11},{9,10},{10,... | collective-permute-start | bytes 393224 | tf_op jit(solution)/shard_map/ppermute | solution.py:276
  62.7 7.0 %collective-permute-start.13 = (bf16[512,128]{1,0:T(8,128)(2,1)S(1)}, bf16[512,128]{1,0:T(8,128)(2,1)S(1)}, u32[]{:S(2)}, u32[]{:S(2)}) collective-permute-start(bf16[512,128]{1,0:T(8,128)(2,1)S(1)} %add_convert_fusion.refs_0_), channel_id=1, source_target_pairs={{0,3},{1,2},{2,1},{3,0},{4,7},{5,6},{6,5},{7,4},{8,11},{9,10},{10,... | collective-permute-start | bytes 393224 | tf_op jit(solution)/shard_map/ppermute | solution.py:276
  65.9 12.0 %collective-permute-start.12 = (bf16[512,128]{1,0:T(8,128)(2,1)S(1)}, bf16[512,128]{1,0:T(8,128)(2,1)S(1)}, u32[]{:S(2)}, u32[]{:S(2)}) collective-permute-start(bf16[512,128]{1,0:T(8,128)(2,1)S(1)} %add_convert_fusion.refs_0_), channel_id=1, source_target_pairs={{0,2},{1,3},{2,0},{3,1},{4,6},{5,7},{6,4},{7,5},{8,10},{9,11},{10,... | collective-permute-start | bytes 393224 | tf_op jit(solution)/shard_map/ppermute | solution.py:276
  67.8 10.1 %collective-permute-start.11 = (bf16[512,128]{1,0:T(8,128)(2,1)S(1)}, bf16[512,128]{1,0:T(8,128)(2,1)S(1)}, u32[]{:S(2)}, u32[]{:S(2)}) collective-permute-start(bf16[512,128]{1,0:T(8,128)(2,1)S(1)} %add_convert_fusion.refs_0_), channel_id=1, source_target_pairs={{0,1},{1,0},{2,3},{3,2},{4,5},{5,4},{6,7},{7,6},{8,9},{9,8},{10,11... | collective-permute-start | bytes 393224 | tf_op jit(solution)/shard_map/ppermute | solution.py:276
  88.9 9.0 %collective-permute-start.18 = (bf16[4,1,128,512]{3,2,1,0:T(8,128)(2,1)S(1)}, bf16[4,1,128,512]{3,2,1,0:T(8,128)(2,1)S(1)}, u32[]{:S(2)}, u32[]{:S(2)}) collective-permute-start(bf16[4,1,128,512]{3,2,1,0:T(8,128)(2,1)S(1)} %backward.3), channel_id=1, source_target_pairs={{0,4},{4,0},{8,12},{12,8},{16,20},{20,16},{24,28},{28,24},{1,5},{5... | collective-permute-start | bytes 1572872 | tf_op jit(solution)/shard_map/ppermute | solution.py:273
  98.1 6.3 %collective-permute-start.19 = (bf16[1,128,512]{2,1,0:T(8,128)(2,1)S(1)}, bf16[1,128,512]{2,1,0:T(8,128)(2,1)S(1)}, u32[]{:S(2)}, u32[]{:S(2)}) collective-permute-start(bf16[1,128,512]{2,1,0:T(8,128)(2,1)S(1)} %get-tuple-element.9), channel_id=1, source_target_pairs={{0,8},{4,12},{8,0},{12,4},{16,24},{20,28},{24,16},{28,20},{1,9},{5... | collective-permute-start | bytes 393224 | tf_op jit(solution)/shard_map/ppermute | solution.py:270
  100.0 8.3 %collective-permute-start.21 = (bf16[1,128,512]{2,1,0:T(8,128)(2,1)S(1)}, bf16[1,128,512]{2,1,0:T(8,128)(2,1)S(1)}, u32[]{:S(2)}, u32[]{:S(2)}) collective-permute-start(bf16[1,128,512]{2,1,0:T(8,128)(2,1)S(1)} %get-tuple-element.10), channel_id=1, source_target_pairs={{0,24},{4,28},{8,16},{12,20},{16,8},{20,12},{24,0},{28,4},{1,25},{... | collective-permute-start | bytes 393224 | tf_op jit(solution)/shard_map/ppermute | solution.py:270
  101.5 8.1 %collective-permute-start.20 = (bf16[1,128,512]{2,1,0:T(8,128)(2,1)S(1)}, bf16[1,128,512]{2,1,0:T(8,128)(2,1)S(1)}, u32[]{:S(2)}, u32[]{:S(2)}) collective-permute-start(bf16[1,128,512]{2,1,0:T(8,128)(2,1)S(1)} %get-tuple-element.11), channel_id=1, source_target_pairs={{0,16},{4,20},{8,24},{12,28},{16,0},{20,4},{24,8},{28,12},{1,17},{... | collective-permute-start | bytes 393224 | tf_op jit(solution)/shard_map/ppermute | solution.py:270
  109.8 8.3 %collective-permute-start.24 = (bf16[1,128,512]{2,1,0:T(8,128)(2,1)S(1)}, bf16[1,128,512]{2,1,0:T(8,128)(2,1)S(1)}, u32[]{:S(2)}, u32[]{:S(2)}) collective-permute-start(bf16[1,128,512]{2,1,0:T(8,128)(2,1)S(1)} %fusion.6), channel_id=1, source_target_pairs={{0,3},{1,2},{2,1},{3,0},{4,7},{5,6},{6,5},{7,4},{8,11},{9,10},{10,... | collective-permute-start | bytes 393224 | tf_op jit(solution)/shard_map/ppermute | solution.py:276
  112.4 10.0 %collective-permute-start.23 = (bf16[1,128,512]{2,1,0:T(8,128)(2,1)S(1)}, bf16[1,128,512]{2,1,0:T(8,128)(2,1)S(1)}, u32[]{:S(2)}, u32[]{:S(2)}) collective-permute-start(bf16[1,128,512]{2,1,0:T(8,128)(2,1)S(1)} %fusion.6), channel_id=1, source_target_pairs={{0,2},{1,3},{2,0},{3,1},{4,6},{5,7},{6,4},{7,5},{8,10},{9,11},{10,... | collective-permute-start | bytes 393224 | tf_op jit(solution)/shard_map/ppermute | solution.py:276
  112.4 10.0 %collective-permute-start.22 = (bf16[1,128,512]{2,1,0:T(8,128)(2,1)S(1)}, bf16[1,128,512]{2,1,0:T(8,128)(2,1)S(1)}, u32[]{:S(2)}, u32[]{:S(2)}) collective-permute-start(bf16[1,128,512]{2,1,0:T(8,128)(2,1)S(1)} %fusion.6), channel_id=1, source_target_pairs={{0,1},{1,0},{2,3},{3,2},{4,5},{5,4},{6,7},{7,6},{8,9},{9,8},{10,11... | collective-permute-start | bytes 393224 | tf_op jit(solution)/shard_map/ppermute | solution.py:276
  115.5 9.1 %collective-permute-start.17 = (f32[128,128]{1,0:T(8,128)S(1)}, f32[128,128]{1,0:T(8,128)S(1)}, u32[]{:S(2)}, u32[]{:S(2)}) collective-permute-start(f32[128,128]{1,0:T(8,128)S(1)} %add.139), channel_id=1, source_target_pairs={{0,24},{4,28},{8,16},{12,20},{16,8},{20,12},{24,0},{28,4},{1,25},{... | collective-permute-start | bytes 196616 | tf_op jit(solution)/shard_map/ppermute | solution.py:270
  117.0 10.6 %collective-permute-start.16 = (f32[128,128]{1,0:T(8,128)S(1)}, f32[128,128]{1,0:T(8,128)S(1)}, u32[]{:S(2)}, u32[]{:S(2)}) collective-permute-start(f32[128,128]{1,0:T(8,128)S(1)} %add.139), channel_id=1, source_target_pairs={{0,16},{4,20},{8,24},{12,28},{16,0},{20,4},{24,8},{28,12},{1,17},{... | collective-permute-start | bytes 196616 | tf_op jit(solution)/shard_map/ppermute | solution.py:270
  118.1 10.2 %collective-permute-start.15 = (f32[128,128]{1,0:T(8,128)S(1)}, f32[128,128]{1,0:T(8,128)S(1)}, u32[]{:S(2)}, u32[]{:S(2)}) collective-permute-start(f32[128,128]{1,0:T(8,128)S(1)} %add.139), channel_id=1, source_target_pairs={{0,8},{4,12},{8,0},{12,4},{16,24},{20,28},{24,16},{28,20},{1,9},{5... | collective-permute-start | bytes 196616 | tf_op jit(solution)/shard_map/ppermute | solution.py:270
  122.6 9.2 %collective-permute-start.28 = (bf16[128,512]{1,0:T(8,128)(2,1)S(1)}, bf16[128,512]{1,0:T(8,128)(2,1)S(1)}, u32[]{:S(2)}, u32[]{:S(2)}) collective-permute-start(bf16[128,512]{1,0:T(8,128)(2,1)S(1)} %get-tuple-element.12), channel_id=1, source_target_pairs={{0,12},{4,28},{8,8},{12,24},{16,4},{20,20},{24,0},{28,16},{1,13},{... | collective-permute-start | bytes 393224 | tf_op jit(solution)/shard_map/ppermute | solution.py:349
  124.5 7.2 %collective-permute-start.27 = (bf16[128,512]{1,0:T(8,128)(2,1)S(1)}, bf16[128,512]{1,0:T(8,128)(2,1)S(1)}, u32[]{:S(2)}, u32[]{:S(2)}) collective-permute-start(bf16[128,512]{1,0:T(8,128)(2,1)S(1)} %get-tuple-element.13), channel_id=1, source_target_pairs={{0,8},{4,24},{8,12},{12,28},{16,0},{20,16},{24,4},{28,20},{1,9},{5... | collective-permute-start | bytes 393224 | tf_op jit(solution)/shard_map/ppermute | solution.py:349
  124.6 7.2 %collective-permute-start.26 = (bf16[128,512]{1,0:T(8,128)(2,1)S(1)}, bf16[128,512]{1,0:T(8,128)(2,1)S(1)}, u32[]{:S(2)}, u32[]{:S(2)}) collective-permute-start(bf16[128,512]{1,0:T(8,128)(2,1)S(1)} %get-tuple-element.14), channel_id=1, source_target_pairs={{0,4},{4,20},{8,0},{12,16},{16,12},{20,28},{24,8},{28,24},{1,5},{5... | collective-permute-start | bytes 393224 | tf_op jit(solution)/shard_map/ppermute | solution.py:349
  (16 other events, 147.5 us)

commit v2 on v1

v2 whole, which is shorter than its diff:
```python
import functools
import math

import jax
import jax.numpy as jnp
from jax import lax
from jax.experimental import pallas as pl
from jax.experimental.pallas import tpu as pltpu
from jax.sharding import PartitionSpec as P

F32 = jnp.float32
BF16 = jnp.bfloat16
MIB = 1 << 20


def params(mib):
    return pltpu.CompilerParams(vmem_limit_bytes=mib * MIB)


def cost(flops, nbytes):
    return pl.CostEstimate(flops=int(flops), bytes_accessed=int(nbytes), transcendentals=0)


def whole_spec(array):
    zeros = (0,) * array.ndim
    return pl.BlockSpec(array.shape, lambda *_: zeros)


def streamed(array):
    return pltpu.with_memory_space_constraint(array, pltpu.HBM)


def reorder_body(order_ref, feat_ref, out_ref):
    rows, panel = order_ref.shape[0], feat_ref.shape[0]
    hot = lax.broadcasted_iota(jnp.int32, (rows, panel), 1) == order_ref[...]
    hot = jnp.where(hot, 1.0, 0.0).astype(BF16)
    out_ref[...] = jnp.dot(hot, feat_ref[...], preferred_element_type=F32).astype(BF16)


def reorder(order_col, features, part, parts):
    panel, width = features.shape
    rows = panel // parts
    step = min(256, rows)
    first = part * (rows // step)
    return pl.pallas_call(
        reorder_body,
        out_shape=jax.ShapeDtypeStruct((rows, width), BF16),
        grid=(rows // step,),
        in_specs=[
            pl.BlockSpec((step, 1), lambda i: (first + i, 0)),
            whole_spec(features),
        ],
        out_specs=pl.BlockSpec((step, width), lambda i: (i, 0)),
        compiler_params=params(12),
        cost_estimate=cost(2 * rows * panel * width, 4 * rows * width),
        name="reorder",
    )(order_col, features)


def plan_body(rows_ref, cols_ref, live_ref, _, out_ref, *, lists, cap, span, bits):
    rounds, slots = rows_ref.shape

    @pl.loop(0, lists * (cap + 1) // 8)
    def _(n):
        for t in range(8):
            out_ref[n * 8 + t] = 0

    for j in range(rounds):

        @pl.loop(0, live_ref[j])
        def _(k):
            row, col = rows_ref[j, k], cols_ref[j, k]
            name = (row // span) * rounds + j
            count = out_ref[lists * cap + name]
            out_ref[name * cap + count] = (((j * slots + k) << bits | row) << bits) | col
            out_ref[lists * cap + name] = count + 1


def make_plan(rows, cols, live, blocks, reps, after):
    rounds = rows.shape[0]
    lists, span = reps * rounds, blocks // reps
    cap = span * blocks
    body = functools.partial(
        plan_body, lists=lists, cap=cap, span=span, bits=(blocks - 1).bit_length()
    )
    smem = pl.BlockSpec(memory_space=pltpu.SMEM)
    return pl.pallas_call(
        body,
        out_shape=jax.ShapeDtypeStruct((lists * cap + lists,), jnp.int32),
        in_specs=[smem, smem, smem, pl.BlockSpec(memory_space=pl.ANY)],
        out_specs=smem,
        cost_estimate=cost(0, 8 * MIB),
        name="make_plan",
    )(rows, cols, live, after)


UNROLL = 8


def fetch(table_ref, tiles_ref, buf, sems, names, cap, bits):
    for m, name in enumerate(names):

        @pl.loop(0, table_ref[table_ref.shape[0] - lists_in(table_ref, cap) + name])
        def _(i):
            slot = table_ref[name * cap + i] >> (2 * bits)
            pltpu.make_async_copy(
                tiles_ref.at[slot], buf.at[m * cap + i], sems.at[m, i // UNROLL]
            ).start()


def lists_in(table_ref, cap):
    return table_ref.shape[0] // (cap + 1)


def each_group(table_ref, tiles_ref, buf, sems, names, cap, bits, step):
    base = table_ref.shape[0] - lists_in(table_ref, cap)
    for m, name in enumerate(names):
        count = table_ref[base + name]

        @pl.loop(0, (count + UNROLL - 1) // UNROLL)
        def _(g):
            for t in range(UNROLL):

                @pl.when(g * UNROLL + t < count)
                def _():
                    at = m * cap + g * UNROLL + t
                    pltpu.make_async_copy(tiles_ref.at[0], buf.at[at], sems.at[m, g]).wait()

            entries = [table_ref[name * cap + g * UNROLL + t] for t in range(UNROLL)]
            alive = [g * UNROLL + t < count for t in range(UNROLL)]
            step(m, m * cap + g * UNROLL, entries, alive)


def forward_body(ids_ref, table_ref, tiles_ref, *refs, cap, bits, rounds, span):
    xs, (out_ref, x_all, acc, buf, sems) = refs[:-5], refs[-5:]
    halves = len(xs) // rounds
    block = buf.shape[1]
    blocks = 1 << bits
    names = [ids_ref[0] * rounds + j for j in range(rounds)]
    fetch(table_ref, tiles_ref, buf, sems, names, cap, bits)
    for n, x_ref in enumerate(xs):
        slot, half = n // halves, n % halves
        rows = x_ref.shape[0]
        at = pl.multiple_of(ids_ref[1 + slot] * (rows * halves) + half * rows, rows)
        x_all[pl.ds(at, rows), :] = x_ref[...]
    acc[...] = jnp.zeros_like(acc)

    def step(m, first, entries, alive):
        terms = []
        for t in range(UNROLL):
            col = entries[t] & (blocks - 1)
            at = pl.multiple_of((m * blocks + col) * block, block)
            terms.append(
                jnp.dot(buf[first + t], x_all[pl.ds(at, block), :], preferred_element_type=F32)
            )
        for t in range(UNROLL):
            row = (entries[t] >> bits) & (span - 1)
            row = jnp.where(alive[t], row, span)
            acc[row] += terms[t]

    each_group(table_ref, tiles_ref, buf, sems, names, cap, bits, step)
    for i in range(span):
        out_ref[i * block : (i + 1) * block, :] = acc[i].astype(out_ref.dtype)


def forward_share(ids, table, tiles, xs, reps, dtype):
    rounds, slots, block, _ = tiles.shape
    width = xs[0].shape[1]
    panel = sum(x.shape[0] for x in xs) // rounds
    blocks = panel // block
    bits, span = (blocks - 1).bit_length(), blocks // reps
    cap = span * blocks
    return pl.pallas_call(
        functools.partial(forward_body, cap=cap, bits=bits, rounds=rounds, span=span),
        out_shape=jax.ShapeDtypeStruct((span * block, width), dtype),
        grid_spec=pltpu.PrefetchScalarGridSpec(
            num_scalar_prefetch=2,
            grid=(1,),
            in_specs=[pl.BlockSpec(memory_space=pltpu.HBM)] + [whole_spec(x) for x in xs],
            out_specs=pl.BlockSpec((span * block, width), lambda *_: (0, 0)),
            scratch_shapes=[
                pltpu.VMEM((rounds * panel, width), BF16),
                pltpu.VMEM((span + 1, block, width), F32),
                pltpu.VMEM((rounds * cap, block, block), BF16),
                pltpu.SemaphoreType.DMA((rounds, -(-cap // UNROLL))),
            ],
        ),
        compiler_params=params(24),
        cost_estimate=cost(2 * 64 * block * block * width, 6 * MIB),
        name="forward_share",
    )(ids, table, tiles.reshape(rounds * slots, block, block), *xs)


def gradient_of(agg, co, weight):
    pre = jnp.dot(agg, weight, preferred_element_type=F32)
    gate = 1.0 / (1.0 + jnp.exp(-pre))
    grad_pre = (co.astype(F32) * gate * (1.0 + pre * (1.0 - gate))).astype(BF16)
    return pre, gate, grad_pre


def up_body(ids_ref, w_ref, co_ref, *refs):
    shares, out_ref = refs[:-1], refs[-1]
    weight = w_ref[...]
    rows = shares[0].shape[0]
    for n, share in enumerate(shares):
        at = pl.multiple_of(ids_ref[n] * rows, rows)
        _, _, grad_pre = gradient_of(share[...], co_ref[pl.ds(at, rows), :], weight)
        out_ref[n] = lax.dot_general(
            weight, grad_pre, (((1,), (1,)), ((), ())), preferred_element_type=F32
        ).astype(BF16)


def up_shares(ids, weight, cotangent, shares):
    rows, width = shares[0].shape
    shape = (len(shares), width, rows)
    operands = (weight, cotangent, *shares)
    return pl.pallas_call(
        up_body,
        out_shape=jax.ShapeDtypeStruct(shape, BF16),
        grid_spec=pltpu.PrefetchScalarGridSpec(
            num_scalar_prefetch=1,
            grid=(1,),
            in_specs=[whole_spec(x) for x in operands],
            out_specs=pl.BlockSpec(shape, lambda *_: (0, 0, 0)),
        ),
        compiler_params=params(16),
        cost_estimate=cost(4 * len(shares) * rows * width * width, 2 * MIB),
        name="up_shares",
    )(ids, *operands)


def finish_body(ids_ref, w_ref, co_ref, *refs):
    shares, (_, hidden_ref, grad_ref, agg_all, pre_all) = refs[:-5], refs[-5:]
    weight = w_ref[...]
    rows = shares[0].shape[0]
    for n, share in enumerate(shares):
        at = pl.multiple_of(ids_ref[n] * rows, rows)
        agg = share[...]
        pre, gate, grad_pre = gradient_of(agg, co_ref[pl.ds(at, rows), :], weight)
        hidden_ref[pl.ds(at, rows), :] = (pre * gate).astype(BF16)
        agg_all[pl.ds(at, rows), :] = agg
        pre_all[pl.ds(at, rows), :] = grad_pre
    grad_ref[...] = lax.dot_general(
        agg_all[...], pre_all[...], (((0,), (0,)), ((), ())), preferred_element_type=F32
    )


def finish(ids, weight, cotangent, shares, after):
    panel, width = cotangent.shape
    operands = (weight, cotangent, *shares)
    return pl.pallas_call(
        finish_body,
        out_shape=(
            jax.ShapeDtypeStruct((panel, width), BF16),
            jax.ShapeDtypeStruct((width, width), F32),
        ),
        grid_spec=pltpu.PrefetchScalarGridSpec(
            num_scalar_prefetch=1,
            grid=(1,),
            in_specs=[whole_spec(x) for x in operands] + [pl.BlockSpec(memory_space=pl.ANY)],
            out_specs=[
                pl.BlockSpec((panel, width), lambda *_: (0, 0)),
                pl.BlockSpec((width, width), lambda *_: (0, 0)),
            ],
            scratch_shapes=[pltpu.VMEM((panel, width), BF16)] * 2,
        ),
        compiler_params=params(16),
        cost_estimate=cost(6 * panel * width * width, 8 * panel * width),
        name="finish",
    )(ids, *operands, after)


def backward_body(ids_ref, table_ref, tiles_ref, *refs, cap, bits, rounds, span, count, pairs):
    ups, rest = refs[: len(refs) - 4], refs[len(refs) - 4 :]
    out_ref, acc, buf, sems = rest
    start = None
    if len(ups) > 1:
        ups, start = ups[:-1], ups[-1]
    up = ups[0]
    block = buf.shape[1]
    blocks = 1 << bits
    names = [ids_ref[n] * rounds + ids_ref[count + p] for n in range(count) for p in range(pairs)]
    fetch(table_ref, tiles_ref, buf, sems, names, cap, bits)
    dump = pairs * blocks
    if start is None:
        acc[...] = jnp.zeros_like(acc)
    else:
        acc[pl.ds(0, dump)] = start[...]
        acc[dump] = jnp.zeros(acc.shape[1:], F32)

    def step(m, first, entries, alive):
        n, p = m // pairs, m % pairs
        terms = []
        for t in range(UNROLL):
            row = (entries[t] >> bits) & (span - 1)
            at = pl.multiple_of(row * block, block)
            terms.append(
                jnp.dot(up[n, :, pl.ds(at, block)], buf[first + t], preferred_element_type=F32)
            )
        for t in range(UNROLL):
            col = entries[t] & (blocks - 1)
            to = jnp.where(alive[t], p * blocks + col, dump)
            acc[to] += terms[t]

    each_group(table_ref, tiles_ref, buf, sems, names, cap, bits, step)
    if out_ref.shape == start_shape(acc):
        out_ref[...] = acc[pl.ds(0, dump)].astype(out_ref.dtype)
    else:
        chips, _, per = out_ref.shape[:3]
        for d in range(chips):
            for p in range(pairs):
                at = p * blocks + ids_ref[count + pairs + d] * per
                out_ref[d, p] = acc[pl.ds(at, per)].astype(out_ref.dtype)


def start_shape(acc):
    return (acc.shape[0] - 1,) + acc.shape[1:]


def backward(ids, table, tiles, up, start, reps, pairs, chips, dtype):
    rounds, slots, block, _ = tiles.shape
    count, width, rows = up.shape
    span = rows // block
    blocks = span * reps
    bits = (blocks - 1).bit_length()
    cap = span * blocks
    shape = (chips, pairs, blocks // chips, width, block) if chips else (pairs * blocks, width, block)
    zeros = (0,) * len(shape)
    operands = (up,) if start is None else (up, start)
    return pl.pallas_call(
        functools.partial(
            backward_body, cap=cap, bits=bits, rounds=rounds, span=span, count=count, pairs=pairs
        ),
        out_shape=jax.ShapeDtypeStruct(shape, dtype),
        grid_spec=pltpu.PrefetchScalarGridSpec(
            num_scalar_prefetch=2,
            grid=(1,),
            in_specs=[pl.BlockSpec(memory_space=pltpu.HBM)] + [whole_spec(x) for x in operands],
            out_specs=pl.BlockSpec(shape, lambda *_: zeros),
            scratch_shapes=[
                pltpu.VMEM((pairs * blocks + 1, width, block), F32),
                pltpu.VMEM((count * pairs * cap, block, block), BF16),
                pltpu.SemaphoreType.DMA((count * pairs, -(-cap // UNROLL))),
            ],
        ),
        compiler_params=params(40),
        cost_estimate=cost(2 * 64 * block * block * width, 6 * MIB),
        name="backward",
    )(ids, table, tiles.reshape(rounds * slots, block, block), *operands)


def restore_body(ids_ref, order_ref, *refs, count):
    parts, out_ref = refs[:count], refs[-1]
    rows = out_ref.shape[0]
    per, _, block = parts[0].shape
    base = pl.program_id(0) * rows
    acc = refs[count][...] if len(refs) > count + 1 else None
    for n, part in enumerate(parts):
        length = per * block
        at = pl.multiple_of(ids_ref[n] * length, length)
        target = order_ref[:, pl.ds(at, length)]
        hot = lax.broadcasted_iota(jnp.int32, (rows, length), 0) + base == target
        hot = jnp.where(hot, 1.0, 0.0).astype(BF16)
        columns = jnp.concatenate([part[b] for b in range(per)], axis=1)
        term = lax.dot_general(
            hot, columns, (((1,), (1,)), ((), ())), preferred_element_type=F32
        )
        acc = term if acc is None else acc + term
    out_ref[...] = acc.astype(out_ref.dtype)


def restore(ids, order_row, parts, start, dtype):
    panel = order_row.shape[1]
    width = parts[0].shape[1]
    rows = 512
    row_spec = pl.BlockSpec((rows, width), lambda i, ids: (i, 0))
    extra = () if start is None else (start,)
    return pl.pallas_call(
        functools.partial(restore_body, count=len(parts)),
        out_shape=jax.ShapeDtypeStruct((panel, width), dtype),
        grid_spec=pltpu.PrefetchScalarGridSpec(
            num_scalar_prefetch=1,
            grid=(panel // rows,),
            in_specs=[whole_spec(order_row)]
            + [whole_spec(p) for p in parts]
            + [row_spec for _ in extra],
            out_specs=row_spec,
        ),
        compiler_params=params(24),
        cost_estimate=cost(2 * panel * panel * width, 4 * panel * width),
        name="restore",
    )(ids, order_row, *parts, *extra)


def tree_sum(terms):
    while len(terms) > 1:
        terms = [terms[i] + terms[i + 1] for i in range(0, len(terms), 2)]
    return terms[0]


def shards(features, order, tiles, tile_rows, tile_cols, live, weight, cotangent):
    reps = lax.axis_size("rep")
    sections = lax.axis_size("section")
    rep = lax.axis_index("rep")
    section = lax.axis_index("section")
    panel, width = features.shape
    rounds = tiles.shape[2]
    chips = sections // 2
    pairs = rounds // 2
    near = reps // 2
    share_rows = panel // reps
    length = panel // chips
    chip, core = section // 2, section % 2

    def over_chips(x, d):
        return lax.ppermute(x, "section", [(s, s ^ (2 * d)) for s in range(sections)])

    def over_cores(x):
        return lax.ppermute(x, "section", [(s, s ^ 1) for s in range(sections)])

    def over_reps(x, d):
        return lax.ppermute(x, "rep", [(r, r ^ d) for r in range(reps)])

    def from_owner(x, d):
        moves = []
        for r in range(reps):
            for j in range(rounds):
                source = j * reps + r
                target = (source ^ (2 * d)) ^ ((d // near) & 1)
                moves.append((source * reps + r, target * reps + r))
        return lax.ppermute(x, ("section", "rep"), moves)

    side = core ^ (rep % 2)
    low = (chip % near) ^ (rep // 2)
    row_of_chip = chip // near
    order_col = order.reshape(panel, 1)
    halves = 2
    mine = [[] for _ in range(pairs)]
    mate = [[] for _ in range(pairs)]
    owns = [reorder(order_col, features, h, halves) for h in range(halves)]
    gots = [[own] + [from_owner(own, d) for d in range(1, chips)] for own in owns]
    own_tiles = tiles[0, 0]
    blocks = panel // own_tiles.shape[2]
    table = make_plan(tile_rows[0, 0], tile_cols[0, 0], live[0, 0], blocks, reps, owns[-1])
    for h in range(halves):
        got = gots[h]
        for p in range(pairs):
            picked = got[2 * p * near]
            for e in range(2):
                for l in range(near):
                    if e or l:
                        picked = jnp.where(
                            (side == e) & (low == l), got[(2 * p + e) * near + l], picked
                        )
            mine[p].append(picked)
            mate[p].append(over_cores(picked))
    xs, slot_ids = [], []
    for p in range(pairs):
        xs += mine[p] + mate[p]
        slot_ids += [row_of_chip ^ (2 * p + side), row_of_chip ^ (2 * p + 1 - side)]

    def share_of(d, dtype):
        ids = jnp.stack([rep ^ d] + slot_ids).astype(jnp.int32)
        return forward_share(ids, table, own_tiles, xs, reps, dtype)

    sent = {d: over_reps(share_of(d, BF16), d) for d in reversed(range(1, reps))}
    total = share_of(0, F32)
    for d in range(1, reps):
        total = total + sent[d].astype(F32)
    aggregated = total.astype(BF16)
    shares = [aggregated] + [over_reps(aggregated, d) for d in range(1, reps)]

    give = [2 * p + 1 - core for p in range(pairs)]
    keep = [2 * p + core for p in range(pairs)]
    chunk_ids = [chip ^ d for d in range(chips)]
    early, late = list(range(reps // 2)), list(range(reps // 2, reps))

    def id_list(*parts):
        return jnp.stack([x for part in parts for x in part]).astype(jnp.int32)

    early_ids, late_ids = [rep ^ d for d in early], [rep ^ d for d in late]
    up_early = up_shares(id_list(early_ids), weight, cotangent, [shares[d] for d in early])
    up_late = up_shares(id_list(late_ids), weight, cotangent, [shares[d] for d in late])

    def first_half(panels):
        ids = id_list(early_ids, panels)
        return backward(ids, table, own_tiles, up_early, None, reps, pairs, 0, F32)

    def second_half(panels, start, dtype):
        ids = id_list(late_ids, panels, chunk_ids)
        return backward(ids, table, own_tiles, up_late, start, reps, pairs, chips, dtype)

    started_give, started_keep = first_half(give), first_half(keep)
    given = over_cores(second_half(give, started_give, BF16))
    kept = second_half(keep, started_keep, F32)
    hidden, grad_part = finish(
        id_list(early_ids, late_ids), weight, cotangent, shares, kept
    )
    chunks = [kept[d] + given[d].astype(F32) for d in range(chips)]
    arrived = [over_chips(chunks[d].astype(BF16), d).astype(F32) for d in range(1, chips)]
    reduced = tree_sum([chunks[0]] + arrived).astype(BF16)

    grad_part = grad_part + over_cores(grad_part)
    weight_grad = tree_sum([grad_part] + [over_chips(grad_part, d) for d in range(1, chips)])
    weight_grad = weight_grad * (1.0 / math.sqrt(panel * sections))

    spread = [reduced] + [over_reps(reduced, d) for d in range(1, reps)]
    stacked = jnp.stack(spread)

    def to_owner(k):
        moves = []
        for s in range(sections):
            u = (s // 2) ^ k
            moves.append((s, (2 * (u // reps) + s % 2) * reps + u % reps))
        u = chip ^ k
        block = stacked[(u % reps) ^ rep, u // reps]
        return lax.ppermute(block, "section", moves)

    parts = [to_owner(k) for k in range(chips)]
    mine_u = (section // reps // 2) * reps + section % reps
    part_ids = [mine_u ^ k for k in range(chips)]
    order_row = order.reshape(1, panel)
    cut = chips // 2
    started = restore(id_list(part_ids[:cut]), order_row, parts[:cut], None, F32)
    feature_grad = restore(id_list(part_ids[cut:]), order_row, parts[cut:], started, BF16)
    return (hidden, weight_grad, feature_grad)


def solution(mesh):
    placed = (
        P("section", None),
        P("section"),
        P("section", "rep", None, None, None, None),
        P("section", "rep", None, None),
        P("section", "rep", None, None),
        P("section", "rep", None),
        P(),
        P("section", None),
    )
    return jax.shard_map(
        shards,
        mesh=mesh,
        in_specs=placed,
        out_specs=(P("section", None), P(), P("section", None)),
        check_vma=False,
    )
```

time: 139 us -> 130 us (0.935); the launches traced: 137 us -> 130 us
  starting transfers between devices: 40.5 us -> 62.3 us
  Pallas kernels: 37.3 us -> 25.4 us
  local copies, waits for them, and re-layouts: 24.4 us -> 13.2 us
  waiting for transfers between devices: 32.2 us -> 22.9 us
  other arithmetic: 1.58 us -> 4.72 us
    pallas_call x9 -> x14, Pallas kernels: 33.4 us -> 20.7 us  [the longest x2 5.52 us: restore(): pl.pallas_call(functools.partial(restore_body, count=len(parts)), out_sha...]
    unnamed x22 -> x34, local copies, waits for them, and re-layouts: 23.2 us -> 11.9 us
    ppermute x9, waiting for transfers between devices: 16.3 us -> 6.36 us  [over_reps(): return lax.ppermute(x, 'rep', [(r, r ^ d) for r in range(reps)])]
    ppermute x6, starting transfers between devices: 6.65 us -> 15.6 us  [over_chips(): return lax.ppermute(x, 'section', [(s, s ^ 2 * d) for s in range(sections)])]
    ppermute x9, starting transfers between devices: 16.2 us -> 25.1 us  [over_reps(): return lax.ppermute(x, 'rep', [(r, r ^ d) for r in range(reps)])]
    ppermute x6, starting transfers between devices: 11.4 us -> 14.2 us  [from_owner(): return lax.ppermute(x, ('section', 'rep'), moves)]
    ppermute x4, waiting for transfers between devices: 2.82 us -> 5.42 us  [to_owner(): return lax.ppermute(block, 'section', moves)]
    ppermute x4, starting transfers between devices: 0.55 us -> 2.5 us  [over_cores(): return lax.ppermute(x, 'section', [(s, s ^ 1) for s in range(sections)])]
  transfers between devices with their start and end apart: 29 -> 29, of which waited for: 14 -> 13; matrix products, arithmetic and copies ran while one was open for 1% -> 2% of each run, Pallas kernels for 16% -> 13%
where the time goes in v2:
time: 130 us
  starting transfers between devices  62.3 us (48%)
  Pallas kernels  25.4 us (20%)
  waiting for transfers between devices  22.9 us (18%)
  local copies, waits for them, and re-layouts  13.2 us (10%)
  other arithmetic  4.72 us (4%)
    ppermute x9, starting transfers between devices, over_reps(): return lax.ppermute(x, 'rep', [(r, r ^ d) for r in range(reps)])  25.1 us
    ppermute x6, starting transfers between devices, over_chips(): return lax.ppermute(x, 'section', [(s, s ^ 2 * d) for s in range(sections)])  15.6 us
    ppermute x6, starting transfers between devices, from_owner(): return lax.ppermute(x, ('section', 'rep'), moves)  14.2 us
    unnamed x34, local copies, waits for them, and re-layouts  11.9 us
    ppermute x6, waiting for transfers between devices, over_chips(): return lax.ppermute(x, 'section', [(s, s ^ 2 * d) for s in range(sections)])  6.58 us
    ppermute x9, waiting for transfers between devices, over_reps(): return lax.ppermute(x, 'rep', [(r, r ^ d) for r in range(reps)])  6.36 us
    pallas_call x2, Pallas kernels, restore(): pl.pallas_call(functools.partial(restore_body, count=len(parts)), out_sha...  5.52 us
    ppermute x4, waiting for transfers between devices, to_owner(): return lax.ppermute(block, 'section', moves)  5.42 us
  transfers between devices with their start and end apart: 29, of which 13 were waited for; matrix products, arithmetic and copies ran while one was open for 2% of the time, Pallas kernels for 13%

profile of v2, /device:TPU:0, one launch (start us, length us, event | category | flops | bytes accessed | tf_op | source)
XLA Modules:
  0.0 129.7 jit_solution(5052798621179894805)
XLA Ops:
  4.7 5.6 %collective-permute-start.2 = (bf16[1024,128]{1,0:T(8,128)(2,1)S(1)}, bf16[1024,128]{1,0:T(8,128)(2,1)}, u32[]{:S(2)}, u32[]{:S(2)}) collective-permute-start(bf16[1024,128]{1,0:T(8,128)(2,1)S(1)} %reorder.3), channel_id=1, source_target_pairs={{0,8},{16,24},{5,13},{21,29},{10,2},{26,18},{15,7},{31,23}} | collective-permute-start | bytes 786440 | tf_op jit(solution)/shard_map/ppermute | solution.py:431
  10.3 2.0 %collective-permute-start.1 = (bf16[1024,128]{1,0:T(8,128)(2,1)S(1)}, bf16[1024,128]{1,0:T(8,128)(2,1)}, u32[]{:S(2)}, u32[]{:S(2)}) collective-permute-start(bf16[1024,128]{1,0:T(8,128)(2,1)S(1)} %reorder.3), channel_id=1, source_target_pairs={{0,20},{16,4},{5,17},{21,1},{10,30},{26,14},{15,27},{31,11}} | collective-permute-start | bytes 786440 | tf_op jit(solution)/shard_map/ppermute | solution.py:431
  14.2 2.7 %reorder.2._ = bf16[1024,128]{1,0:T(8,128)(2,1)} custom-call(s32[2048,1]{1,0:T(8,128)S(1)} %copy.11.order_ref, bf16[2048,128]{1,0:T(8,128)(2,1)S(1)} %copy-done.14), custom_call_target="tpu_custom_call" | custom-call | flops 536870912 | bytes 524288 | tf_op jit(solution)/shard_map/reorder/pallas_call | solution.py:45
  19.6 2.0 %collective-permute-start.3 = (bf16[1024,128]{1,0:T(8,128)(2,1)}, bf16[1024,128]{1,0:T(8,128)(2,1)}, u32[]{:S(2)}, u32[]{:S(2)}) collective-permute-start(bf16[1024,128]{1,0:T(8,128)(2,1)} %reorder.2._), channel_id=1, source_target_pairs={{0,28},{16,12},{5,25},{21,9},{10,22},{26,6},{15,19},{31,3}} | collective-permute-start | bytes 786440 | tf_op jit(solution)/shard_map/ppermute | solution.py:431
  28.7 2.9 %copy-done = bf16[1,1,2,96,128,128]{5,4,3,2,1,0:T(8,128)(2,1)S(1)} copy-done((bf16[1,1,2,96,128,128]{5,4,3,2,1,0:T(8,128)(2,1)S(1)}, bf16[1,1,2,96,128,128]{5,4,3,2,1,0:T(8,128)(2,1)}, u32[]{:S(2)}) %copy-start) | copy-done | bytes 6291480
  33.2 4.9 %collective-permute-start.8 = (bf16[512,128]{1,0:T(8,128)(2,1)S(1)}, bf16[512,128]{1,0:T(8,128)(2,1)S(1)}, u32[]{:S(2)}, u32[]{:S(2)}) collective-permute-start(bf16[512,128]{1,0:T(8,128)(2,1)S(1)} %forward_share.5), channel_id=1, source_target_pairs={{0,1},{1,0},{2,3},{3,2},{4,5},{5,4},{6,7},{7,6},{8,9},{9,8},{10,11... | collective-permute-start | bytes 393224 | tf_op jit(solution)/shard_map/ppermute | solution.py:422
  39.3 6.2 %collective-permute-start.9 = (bf16[512,128]{1,0:T(8,128)(2,1)S(1)}, bf16[512,128]{1,0:T(8,128)(2,1)S(1)}, u32[]{:S(2)}, u32[]{:S(2)}) collective-permute-start(bf16[512,128]{1,0:T(8,128)(2,1)S(1)} %forward_share.6), channel_id=1, source_target_pairs={{0,2},{1,3},{2,0},{3,1},{4,6},{5,7},{6,4},{7,5},{8,10},{9,11},{10,... | collective-permute-start | bytes 393224 | tf_op jit(solution)/shard_map/ppermute | solution.py:422
  47.4 4.3 %collective-permute-start.10 = (bf16[512,128]{1,0:T(8,128)(2,1)S(1)}, bf16[512,128]{1,0:T(8,128)(2,1)S(1)}, u32[]{:S(2)}, u32[]{:S(2)}) collective-permute-start(bf16[512,128]{1,0:T(8,128)(2,1)S(1)} %forward_share.7), channel_id=1, source_target_pairs={{0,3},{1,2},{2,1},{3,0},{4,7},{5,6},{6,5},{7,4},{8,11},{9,10},{10,... | collective-permute-start | bytes 393224 | tf_op jit(solution)/shard_map/ppermute | solution.py:422
  54.9 2.4 %collective-permute-start.11 = (bf16[512,128]{1,0:T(8,128)(2,1)S(1)}, bf16[512,128]{1,0:T(8,128)(2,1)S(1)}, u32[]{:S(2)}, u32[]{:S(2)}) collective-permute-start(bf16[512,128]{1,0:T(8,128)(2,1)S(1)} %add_convert_fusion.refs_0_), channel_id=1, source_target_pairs={{0,1},{1,0},{2,3},{3,2},{4,5},{5,4},{6,7},{7,6},{8,9},{9,8},{10,11... | collective-permute-start | bytes 393224 | tf_op jit(solution)/shard_map/ppermute | solution.py:422
  57.4 2.8 %collective-permute-start.13 = (bf16[512,128]{1,0:T(8,128)(2,1)S(1)}, bf16[512,128]{1,0:T(8,128)(2,1)S(1)}, u32[]{:S(2)}, u32[]{:S(2)}) collective-permute-start(bf16[512,128]{1,0:T(8,128)(2,1)S(1)} %add_convert_fusion.refs_0_), channel_id=1, source_target_pairs={{0,3},{1,2},{2,1},{3,0},{4,7},{5,6},{6,5},{7,4},{8,11},{9,10},{10,... | collective-permute-start | bytes 393224 | tf_op jit(solution)/shard_map/ppermute | solution.py:422
  63.0 2.8 %copy-done.1 = bf16[1,1,2,96,128,128]{5,4,3,2,1,0:T(8,128)(2,1)S(1)} copy-done((bf16[1,1,2,96,128,128]{5,4,3,2,1,0:T(8,128)(2,1)S(1)}, bf16[1,1,2,96,128,128]{5,4,3,2,1,0:T(8,128)(2,1)}, u32[]{:S(2)}) %copy-start.1) | copy-done | bytes 6291480
  67.0 3.3 %collective-permute-done.12.refs_0_.refs_2_ = bf16[512,128]{1,0:T(8,128)(2,1)S(1)} collective-permute-done((bf16[512,128]{1,0:T(8,128)(2,1)S(1)}, bf16[512,128]{1,0:T(8,128)(2,1)S(1)}, u32[]{:S(2)}, u32[]{:S(2)}) %collective-permute-start.12) | collective-permute-done | bytes 131104 | tf_op jit(solution)/shard_map/ppermute | solution.py:422
  73.1 2.2 %collective-permute-start.18 = (bf16[4,1,4,128,128]{4,3,2,1,0:T(8,128)(2,1)}, bf16[4,1,4,128,128]{4,3,2,1,0:T(8,128)(2,1)}, u32[]{:S(2)}, u32[]{:S(2)}) collective-permute-start(bf16[4,1,4,128,128]{4,3,2,1,0:T(8,128)(2,1)} %backward.7), channel_id=1, source_target_pairs={{0,4},{4,0},{8,12},{12,8},{16,20},{20,16},{24,28},{28,24},{1,5},{5... | collective-permute-start | bytes 1572872 | tf_op jit(solution)/shard_map/ppermute | solution.py:419
  75.4 2.8 %copy-done.2 = bf16[1,1,2,96,128,128]{5,4,3,2,1,0:T(8,128)(2,1)S(1)} copy-done((bf16[1,1,2,96,128,128]{5,4,3,2,1,0:T(8,128)(2,1)S(1)}, bf16[1,1,2,96,128,128]{5,4,3,2,1,0:T(8,128)(2,1)}, u32[]{:S(2)}) %copy-start.2) | copy-done | bytes 6291480
  81.4 7.1 %collective-permute-start.19 = (bf16[1,4,128,128]{3,2,1,0:T(8,128)(2,1)S(1)}, bf16[1,4,128,128]{3,2,1,0:T(8,128)(2,1)S(1)}, u32[]{:S(2)}, u32[]{:S(2)}) collective-permute-start(bf16[1,4,128,128]{3,2,1,0:T(8,128)(2,1)S(1)} %get-tuple-element.7), channel_id=1, source_target_pairs={{0,8},{4,12},{8,0},{12,4},{16,24},{20,28},{24,16},{28,20},{1,9},{5... | collective-permute-start | bytes 393224 | tf_op jit(solution)/shard_map/ppermute | solution.py:416
  88.5 4.9 %collective-permute-start.21 = (bf16[1,4,128,128]{3,2,1,0:T(8,128)(2,1)S(1)}, bf16[1,4,128,128]{3,2,1,0:T(8,128)(2,1)S(1)}, u32[]{:S(2)}, u32[]{:S(2)}) collective-permute-start(bf16[1,4,128,128]{3,2,1,0:T(8,128)(2,1)S(1)} %get-tuple-element.8), channel_id=1, source_target_pairs={{0,24},{4,28},{8,16},{12,20},{16,8},{20,12},{24,0},{28,4},{1,25},{... | collective-permute-start | bytes 393224 | tf_op jit(solution)/shard_map/ppermute | solution.py:416
  93.7 4.2 %collective-permute-done.21 = bf16[1,4,128,128]{3,2,1,0:T(8,128)(2,1)S(1)} collective-permute-done((bf16[1,4,128,128]{3,2,1,0:T(8,128)(2,1)S(1)}, bf16[1,4,128,128]{3,2,1,0:T(8,128)(2,1)S(1)}, u32[]{:S(2)}, u32[]{:S(2)}) %collective-permute-start.21) | collective-permute-done | bytes 131104 | tf_op jit(solution)/shard_map/ppermute | solution.py:416
  101.4 3.2 %collective-permute-start.22 = (bf16[1,4,128,128]{3,2,1,0:T(8,128)(2,1)S(1)}, bf16[1,4,128,128]{3,2,1,0:T(8,128)(2,1)S(1)}, u32[]{:S(2)}, u32[]{:S(2)}) collective-permute-start(bf16[1,4,128,128]{3,2,1,0:T(8,128)(2,1)S(1)} %fusion.6), channel_id=1, source_target_pairs={{0,1},{1,0},{2,3},{3,2},{4,5},{5,4},{6,7},{7,6},{8,9},{9,8},{10,11... | collective-permute-start | bytes 393224 | tf_op jit(solution)/shard_map/ppermute | solution.py:422
  104.6 2.0 %finish.1 = (bf16[2048,128]{1,0:T(8,128)(2,1)}, f32[128,128]{1,0:T(8,128)S(1)}) custom-call(s32[4]{0:T(128)S(1)} %pad_add_fusion.ids_ref, bf16[128,128]{1,0:T(8,128)(2,1)S(1)} %copy-done.12, bf16[2048,128]{1,0:T(8,128)(2,1)S(1)} %copy-done.3, bf16[512,128]{1,0:T(8,128)(2,1)S(1)} %add_convert_fusion.refs_0_, ...), custom_call_target="tpu_custom_call" | custom-call | flops 201326592 | bytes 2097152 | tf_op jit(solution)/shard_map/finish/pallas_call | solution.py:251
  109.5 2.0 %collective-permute-start.15 = (f32[128,128]{1,0:T(8,128)S(1)}, f32[128,128]{1,0:T(8,128)S(1)}, u32[]{:S(2)}, u32[]{:S(2)}) collective-permute-start(f32[128,128]{1,0:T(8,128)S(1)} %add.139), channel_id=1, source_target_pairs={{0,8},{4,12},{8,0},{12,4},{16,24},{20,28},{24,16},{28,20},{1,9},{5... | collective-permute-start | bytes 196616 | tf_op jit(solution)/shard_map/ppermute | solution.py:416
  113.8 4.2 %collective-permute-start.26 = (bf16[4,128,128]{2,1,0:T(8,128)(2,1)S(1)}, bf16[4,128,128]{2,1,0:T(8,128)(2,1)S(1)}, u32[]{:S(2)}, u32[]{:S(2)}) collective-permute-start(bf16[4,128,128]{2,1,0:T(8,128)(2,1)S(1)} %get-tuple-element.12), channel_id=1, source_target_pairs={{0,12},{4,28},{8,8},{12,24},{16,4},{20,20},{24,0},{28,16},{1,13},{... | collective-permute-start | bytes 393224 | tf_op jit(solution)/shard_map/ppermute | solution.py:517
  118.7 2.3 %restore.2.refs_2_ = f32[2048,128]{1,0:T(8,128)S(1)} custom-call(s32[2]{0:T(128)S(1)} %pad_add_fusion.7.ids_ref, s32[1,2048]{1,0:T(1,128)S(1)} %bitcast.59, bf16[4,128,128]{2,1,0:T(8,128)(2,1)S(1)} %collective-permute-done.27.refs_0_, bf16[4,128,128]{2,1,0:T(8,128)(2,1)S(1)} %collective-permute-done.28.refs_1_), custom_call_target="tpu_custom_call" | custom-call | flops 1073741824 | bytes 1048576 | tf_op jit(solution)/shard_map/restore/pallas_call | solution.py:378
  123.0 3.4 %collective-permute-done.25.refs_0_ = bf16[4,128,128]{2,1,0:T(8,128)(2,1)S(1)} collective-permute-done((bf16[4,128,128]{2,1,0:T(8,128)(2,1)S(1)}, bf16[4,128,128]{2,1,0:T(8,128)(2,1)S(1)}, u32[]{:S(2)}, u32[]{:S(2)}) %collective-permute-start.25) | collective-permute-done | bytes 131104 | tf_op jit(solution)/shard_map/ppermute | solution.py:517
  126.5 3.2 %restore.3 = bf16[2048,128]{1,0:T(8,128)(2,1)} custom-call(s32[2]{0:T(128)S(1)} %pad_add_fusion.5.ids_ref, s32[1,2048]{1,0:T(1,128)S(1)} %bitcast.60, bf16[4,128,128]{2,1,0:T(8,128)(2,1)S(1)} %collective-permute-done.25.refs_0_, bf16[4,128,128]{2,1,0:T(8,128)(2,1)S(1)} %collective-permute-done.26.refs_1_, f32[2048,128]{1,0:T(8,128)S(1)} %restore.2.refs_2_), custom_call_target="tpu_custom_call" | custom-call | flops 1073741824 | bytes 1048576 | tf_op jit(solution)/shard_map/restore/pallas_call | solution.py:378
  (107 shorter events, 45.0 us)
Async XLA Ops:
  4.7 14.9 %collective-permute-start.2 = (bf16[1024,128]{1,0:T(8,128)(2,1)S(1)}, bf16[1024,128]{1,0:T(8,128)(2,1)}, u32[]{:S(2)}, u32[]{:S(2)}) collective-permute-start(bf16[1024,128]{1,0:T(8,128)(2,1)S(1)} %reorder.3), channel_id=1, source_target_pairs={{0,8},{16,24},{5,13},{21,29},{10,2},{26,18},{15,7},{31,23}} | collective-permute-start | bytes 786440 | tf_op jit(solution)/shard_map/ppermute | solution.py:431
  10.3 11.5 %collective-permute-start.1 = (bf16[1024,128]{1,0:T(8,128)(2,1)S(1)}, bf16[1024,128]{1,0:T(8,128)(2,1)}, u32[]{:S(2)}, u32[]{:S(2)}) collective-permute-start(bf16[1024,128]{1,0:T(8,128)(2,1)S(1)} %reorder.3), channel_id=1, source_target_pairs={{0,20},{16,4},{5,17},{21,1},{10,30},{26,14},{15,27},{31,11}} | collective-permute-start | bytes 786440 | tf_op jit(solution)/shard_map/ppermute | solution.py:431
  12.3 9.5 %collective-permute-start = (bf16[1024,128]{1,0:T(8,128)(2,1)S(1)}, bf16[1024,128]{1,0:T(8,128)(2,1)}, u32[]{:S(2)}, u32[]{:S(2)}) collective-permute-start(bf16[1024,128]{1,0:T(8,128)(2,1)S(1)} %reorder.3), channel_id=1, source_target_pairs={{0,28},{16,12},{5,25},{21,9},{10,22},{26,6},{15,19},{31,3}} | collective-permute-start | bytes 786440 | tf_op jit(solution)/shard_map/ppermute | solution.py:431
  21.8 6.9 %collective-permute-start.6 = (bf16[1024,128]{1,0:T(8,128)(2,1)S(1)}, bf16[1024,128]{1,0:T(8,128)(2,1)S(1)}, u32[]{:S(2)}, u32[]{:S(2)}) collective-permute-start(bf16[1024,128]{1,0:T(8,128)(2,1)S(1)} %select_select_fusion.1.refs_0_), channel_id=1, source_target_pairs={{0,4},{4,0},{8,12},{12,8},{16,20},{20,16},{24,28},{28,24},{1,5},{5... | collective-permute-start | bytes 786440 | tf_op jit(solution)/shard_map/ppermute | solution.py:419
  33.2 19.9 %collective-permute-start.8 = (bf16[512,128]{1,0:T(8,128)(2,1)S(1)}, bf16[512,128]{1,0:T(8,128)(2,1)S(1)}, u32[]{:S(2)}, u32[]{:S(2)}) collective-permute-start(bf16[512,128]{1,0:T(8,128)(2,1)S(1)} %forward_share.5), channel_id=1, source_target_pairs={{0,1},{1,0},{2,3},{3,2},{4,5},{5,4},{6,7},{7,6},{8,9},{9,8},{10,11... | collective-permute-start | bytes 393224 | tf_op jit(solution)/shard_map/ppermute | solution.py:422
  39.3 13.7 %collective-permute-start.9 = (bf16[512,128]{1,0:T(8,128)(2,1)S(1)}, bf16[512,128]{1,0:T(8,128)(2,1)S(1)}, u32[]{:S(2)}, u32[]{:S(2)}) collective-permute-start(bf16[512,128]{1,0:T(8,128)(2,1)S(1)} %forward_share.6), channel_id=1, source_target_pairs={{0,2},{1,3},{2,0},{3,1},{4,6},{5,7},{6,4},{7,5},{8,10},{9,11},{10,... | collective-permute-start | bytes 393224 | tf_op jit(solution)/shard_map/ppermute | solution.py:422
  47.4 7.4 %collective-permute-start.10 = (bf16[512,128]{1,0:T(8,128)(2,1)S(1)}, bf16[512,128]{1,0:T(8,128)(2,1)S(1)}, u32[]{:S(2)}, u32[]{:S(2)}) collective-permute-start(bf16[512,128]{1,0:T(8,128)(2,1)S(1)} %forward_share.7), channel_id=1, source_target_pairs={{0,3},{1,2},{2,1},{3,0},{4,7},{5,6},{6,5},{7,4},{8,11},{9,10},{10,... | collective-permute-start | bytes 393224 | tf_op jit(solution)/shard_map/ppermute | solution.py:422
  54.9 6.3 %collective-permute-start.11 = (bf16[512,128]{1,0:T(8,128)(2,1)S(1)}, bf16[512,128]{1,0:T(8,128)(2,1)S(1)}, u32[]{:S(2)}, u32[]{:S(2)}) collective-permute-start(bf16[512,128]{1,0:T(8,128)(2,1)S(1)} %add_convert_fusion.refs_0_), channel_id=1, source_target_pairs={{0,1},{1,0},{2,3},{3,2},{4,5},{5,4},{6,7},{7,6},{8,9},{9,8},{10,11... | collective-permute-start | bytes 393224 | tf_op jit(solution)/shard_map/ppermute | solution.py:422
  57.4 9.6 %collective-permute-start.13 = (bf16[512,128]{1,0:T(8,128)(2,1)S(1)}, bf16[512,128]{1,0:T(8,128)(2,1)S(1)}, u32[]{:S(2)}, u32[]{:S(2)}) collective-permute-start(bf16[512,128]{1,0:T(8,128)(2,1)S(1)} %add_convert_fusion.refs_0_), channel_id=1, source_target_pairs={{0,3},{1,2},{2,1},{3,0},{4,7},{5,6},{6,5},{7,4},{8,11},{9,10},{10,... | collective-permute-start | bytes 393224 | tf_op jit(solution)/shard_map/ppermute | solution.py:422
  60.2 10.2 %collective-permute-start.12 = (bf16[512,128]{1,0:T(8,128)(2,1)S(1)}, bf16[512,128]{1,0:T(8,128)(2,1)S(1)}, u32[]{:S(2)}, u32[]{:S(2)}) collective-permute-start(bf16[512,128]{1,0:T(8,128)(2,1)S(1)} %add_convert_fusion.refs_0_), channel_id=1, source_target_pairs={{0,2},{1,3},{2,0},{3,1},{4,6},{5,7},{6,4},{7,5},{8,10},{9,11},{10,... | collective-permute-start | bytes 393224 | tf_op jit(solution)/shard_map/ppermute | solution.py:422
  73.1 7.2 %collective-permute-start.18 = (bf16[4,1,4,128,128]{4,3,2,1,0:T(8,128)(2,1)}, bf16[4,1,4,128,128]{4,3,2,1,0:T(8,128)(2,1)}, u32[]{:S(2)}, u32[]{:S(2)}) collective-permute-start(bf16[4,1,4,128,128]{4,3,2,1,0:T(8,128)(2,1)} %backward.7), channel_id=1, source_target_pairs={{0,4},{4,0},{8,12},{12,8},{16,20},{20,16},{24,28},{28,24},{1,5},{5... | collective-permute-start | bytes 1572872 | tf_op jit(solution)/shard_map/ppermute | solution.py:419
  81.4 12.2 %collective-permute-start.19 = (bf16[1,4,128,128]{3,2,1,0:T(8,128)(2,1)S(1)}, bf16[1,4,128,128]{3,2,1,0:T(8,128)(2,1)S(1)}, u32[]{:S(2)}, u32[]{:S(2)}) collective-permute-start(bf16[1,4,128,128]{3,2,1,0:T(8,128)(2,1)S(1)} %get-tuple-element.7), channel_id=1, source_target_pairs={{0,8},{4,12},{8,0},{12,4},{16,24},{20,28},{24,16},{28,20},{1,9},{5... | collective-permute-start | bytes 393224 | tf_op jit(solution)/shard_map/ppermute | solution.py:416
  88.5 9.3 %collective-permute-start.21 = (bf16[1,4,128,128]{3,2,1,0:T(8,128)(2,1)S(1)}, bf16[1,4,128,128]{3,2,1,0:T(8,128)(2,1)S(1)}, u32[]{:S(2)}, u32[]{:S(2)}) collective-permute-start(bf16[1,4,128,128]{3,2,1,0:T(8,128)(2,1)S(1)} %get-tuple-element.8), channel_id=1, source_target_pairs={{0,24},{4,28},{8,16},{12,20},{16,8},{20,12},{24,0},{28,4},{1,25},{... | collective-permute-start | bytes 393224 | tf_op jit(solution)/shard_map/ppermute | solution.py:416
  93.4 5.8 %collective-permute-start.20 = (bf16[1,4,128,128]{3,2,1,0:T(8,128)(2,1)S(1)}, bf16[1,4,128,128]{3,2,1,0:T(8,128)(2,1)S(1)}, u32[]{:S(2)}, u32[]{:S(2)}) collective-permute-start(bf16[1,4,128,128]{3,2,1,0:T(8,128)(2,1)S(1)} %get-tuple-element.9), channel_id=1, source_target_pairs={{0,16},{4,20},{8,24},{12,28},{16,0},{20,4},{24,8},{28,12},{1,17},{... | collective-permute-start | bytes 393224 | tf_op jit(solution)/shard_map/ppermute | solution.py:416
  100.2 9.3 %collective-permute-start.24 = (bf16[1,4,128,128]{3,2,1,0:T(8,128)(2,1)S(1)}, bf16[1,4,128,128]{3,2,1,0:T(8,128)(2,1)S(1)}, u32[]{:S(2)}, u32[]{:S(2)}) collective-permute-start(bf16[1,4,128,128]{3,2,1,0:T(8,128)(2,1)S(1)} %fusion.6), channel_id=1, source_target_pairs={{0,3},{1,2},{2,1},{3,0},{4,7},{5,6},{6,5},{7,4},{8,11},{9,10},{10,... | collective-permute-start | bytes 393224 | tf_op jit(solution)/shard_map/ppermute | solution.py:422
  101.2 10.6 %collective-permute-start.23 = (bf16[1,4,128,128]{3,2,1,0:T(8,128)(2,1)S(1)}, bf16[1,4,128,128]{3,2,1,0:T(8,128)(2,1)S(1)}, u32[]{:S(2)}, u32[]{:S(2)}) collective-permute-start(bf16[1,4,128,128]{3,2,1,0:T(8,128)(2,1)S(1)} %fusion.6), channel_id=1, source_target_pairs={{0,2},{1,3},{2,0},{3,1},{4,6},{5,7},{6,4},{7,5},{8,10},{9,11},{10,... | collective-permute-start | bytes 393224 | tf_op jit(solution)/shard_map/ppermute | solution.py:422
  101.4 10.4 %collective-permute-start.22 = (bf16[1,4,128,128]{3,2,1,0:T(8,128)(2,1)S(1)}, bf16[1,4,128,128]{3,2,1,0:T(8,128)(2,1)S(1)}, u32[]{:S(2)}, u32[]{:S(2)}) collective-permute-start(bf16[1,4,128,128]{3,2,1,0:T(8,128)(2,1)S(1)} %fusion.6), channel_id=1, source_target_pairs={{0,1},{1,0},{2,3},{3,2},{4,5},{5,4},{6,7},{7,6},{8,9},{9,8},{10,11... | collective-permute-start | bytes 393224 | tf_op jit(solution)/shard_map/ppermute | solution.py:422
  107.9 5.8 %collective-permute-start.17 = (f32[128,128]{1,0:T(8,128)S(1)}, f32[128,128]{1,0:T(8,128)S(1)}, u32[]{:S(2)}, u32[]{:S(2)}) collective-permute-start(f32[128,128]{1,0:T(8,128)S(1)} %add.139), channel_id=1, source_target_pairs={{0,24},{4,28},{8,16},{12,20},{16,8},{20,12},{24,0},{28,4},{1,25},{... | collective-permute-start | bytes 196616 | tf_op jit(solution)/shard_map/ppermute | solution.py:416
  108.6 9.4 %collective-permute-start.16 = (f32[128,128]{1,0:T(8,128)S(1)}, f32[128,128]{1,0:T(8,128)S(1)}, u32[]{:S(2)}, u32[]{:S(2)}) collective-permute-start(f32[128,128]{1,0:T(8,128)S(1)} %add.139), channel_id=1, source_target_pairs={{0,16},{4,20},{8,24},{12,28},{16,0},{20,4},{24,8},{28,12},{1,17},{... | collective-permute-start | bytes 196616 | tf_op jit(solution)/shard_map/ppermute | solution.py:416
  109.5 8.6 %collective-permute-start.15 = (f32[128,128]{1,0:T(8,128)S(1)}, f32[128,128]{1,0:T(8,128)S(1)}, u32[]{:S(2)}, u32[]{:S(2)}) collective-permute-start(f32[128,128]{1,0:T(8,128)S(1)} %add.139), channel_id=1, source_target_pairs={{0,8},{4,12},{8,0},{12,4},{16,24},{20,28},{24,16},{28,20},{1,9},{5... | collective-permute-start | bytes 196616 | tf_op jit(solution)/shard_map/ppermute | solution.py:416
  112.0 6.8 %collective-permute-start.28 = (bf16[4,128,128]{2,1,0:T(8,128)(2,1)S(1)}, bf16[4,128,128]{2,1,0:T(8,128)(2,1)S(1)}, u32[]{:S(2)}, u32[]{:S(2)}) collective-permute-start(bf16[4,128,128]{2,1,0:T(8,128)(2,1)S(1)} %get-tuple-element.10), channel_id=1, source_target_pairs={{0,4},{4,20},{8,0},{12,16},{16,12},{20,28},{24,8},{28,24},{1,5},{5... | collective-permute-start | bytes 393224 | tf_op jit(solution)/shard_map/ppermute | solution.py:517
  112.0 6.7 %collective-permute-start.27 = (bf16[4,128,128]{2,1,0:T(8,128)(2,1)S(1)}, bf16[4,128,128]{2,1,0:T(8,128)(2,1)S(1)}, u32[]{:S(2)}, u32[]{:S(2)}) collective-permute-start(bf16[4,128,128]{2,1,0:T(8,128)(2,1)S(1)} %get-tuple-element.11), channel_id=1, source_target_pairs={{0,0},{4,16},{8,4},{12,20},{16,8},{20,24},{24,12},{28,28},{1,1},{5... | collective-permute-start | bytes 393224 | tf_op jit(solution)/shard_map/ppermute | solution.py:517
  113.8 9.3 %collective-permute-start.26 = (bf16[4,128,128]{2,1,0:T(8,128)(2,1)S(1)}, bf16[4,128,128]{2,1,0:T(8,128)(2,1)S(1)}, u32[]{:S(2)}, u32[]{:S(2)}) collective-permute-start(bf16[4,128,128]{2,1,0:T(8,128)(2,1)S(1)} %get-tuple-element.12), channel_id=1, source_target_pairs={{0,12},{4,28},{8,8},{12,24},{16,4},{20,20},{24,0},{28,16},{1,13},{... | collective-permute-start | bytes 393224 | tf_op jit(solution)/shard_map/ppermute | solution.py:517
  118.0 8.5 %collective-permute-start.25 = (bf16[4,128,128]{2,1,0:T(8,128)(2,1)S(1)}, bf16[4,128,128]{2,1,0:T(8,128)(2,1)S(1)}, u32[]{:S(2)}, u32[]{:S(2)}) collective-permute-start(bf16[4,128,128]{2,1,0:T(8,128)(2,1)S(1)} %get-tuple-element.13), channel_id=1, source_target_pairs={{0,8},{4,24},{8,12},{12,28},{16,0},{20,16},{24,4},{28,20},{1,9},{5... | collective-permute-start | bytes 393224 | tf_op jit(solution)/shard_map/ppermute | solution.py:517
  (22 other events, 234.5 us)

commit v3 on v0

v3 whole, which is shorter than its diff:
```python
import functools
import math

import jax
import jax.numpy as jnp
from jax import lax
from jax.experimental import pallas as pl
from jax.experimental.pallas import tpu as pltpu
from jax.sharding import PartitionSpec as P

F32 = jnp.float32
BF16 = jnp.bfloat16
MIB = 1 << 20


def params(mib):
    return pltpu.CompilerParams(vmem_limit_bytes=mib * MIB)


def cost(flops, nbytes):
    return pl.CostEstimate(flops=int(flops), bytes_accessed=int(nbytes), transcendentals=0)


def whole_spec(array):
    zeros = (0,) * array.ndim
    return pl.BlockSpec(array.shape, lambda *_: zeros)


def reorder_body(order_ref, feat_ref, out_ref):
    rows, panel = order_ref.shape[0], feat_ref.shape[0]
    hot = lax.broadcasted_iota(jnp.int32, (rows, panel), 1) == order_ref[...]
    hot = jnp.where(hot, 1.0, 0.0).astype(BF16)
    out_ref[...] = jnp.dot(hot, feat_ref[...], preferred_element_type=F32).astype(BF16)


def reorder(order_col, features, part, parts):
    panel, width = features.shape
    rows = panel // parts
    step = min(256, rows)
    first = part * (rows // step)
    return pl.pallas_call(
        reorder_body,
        out_shape=jax.ShapeDtypeStruct((rows, width), BF16),
        grid=(rows // step,),
        in_specs=[
            pl.BlockSpec((step, 1), lambda i: (first + i, 0)),
            whole_spec(features),
        ],
        out_specs=pl.BlockSpec((step, width), lambda i: (i, 0)),
        compiler_params=params(12),
        cost_estimate=cost(2 * rows * panel * width, 4 * rows * width),
        name="reorder",
    )(order_col, features)


REP, CHIP, CORE, SIDE, ROW, LOW, LIVE = range(7)
HALVES = 2
GROUP = 16


def in_vmem(array):
    return pltpu.with_memory_space_constraint(array, pltpu.VMEM)


def call(body, meta, operands, outs, scratch=(), vmem=(), mib=12, estimate=None, name=None):
    specs = [
        pl.BlockSpec(memory_space=pltpu.VMEM) if n in vmem else whole_spec(x)
        for n, x in enumerate(operands)
    ]
    operands = [in_vmem(x) if n in vmem else x for n, x in enumerate(operands)]
    return pl.pallas_call(
        body,
        out_shape=outs,
        grid_spec=pltpu.PrefetchScalarGridSpec(
            num_scalar_prefetch=1,
            grid=(1,),
            in_specs=specs,
            out_specs=jax.tree.map(whole_spec, outs),
            scratch_shapes=list(scratch),
        ),
        compiler_params=params(mib),
        cost_estimate=estimate or cost(0, MIB),
        name=name,
    )(meta, *operands)


def pick_body(meta_ref, *refs, near):
    options, out_ref = refs[:-1], refs[-1]
    for n, option in enumerate(options):

        @pl.when((meta_ref[SIDE] == n // near) & (meta_ref[LOW] == n % near))
        def _():
            out_ref[...] = option[...]


def pick(meta, options, near):
    out = jax.ShapeDtypeStruct(options[0].shape, options[0].dtype)
    return call(functools.partial(pick_body, near=near), meta, options, out, name="pick")


def walk(meta_ref, j, rounds, slots, step):
    count = meta_ref[LIVE + j]

    @pl.loop(0, (count + GROUP - 1) // GROUP)
    def _(g):
        first = j * slots + g * GROUP
        entries = [meta_ref[LIVE + rounds + first + t] for t in range(GROUP)]
        step(first, entries, [g * GROUP + t < count for t in range(GROUP)])


def forward_body(meta_ref, tiles_ref, *refs, rounds, slots, pairs, last):
    xs, rest = refs[: pairs * HALVES], refs[pairs * HALVES :]
    panel_ref, acc = rest[-2:]
    blocks, block, width = panel_ref.shape
    bits = (blocks - 1).bit_length()
    if last:
        start, outs = rest[0], rest[1:-2]
        acc[pl.ds(0, blocks)] = start[...]
        acc[blocks] = jnp.zeros((block, width), F32)
    else:
        outs = rest[:-2]
        acc[...] = jnp.zeros_like(acc)
    per = blocks // HALVES
    for p in range(pairs):
        for h in range(HALVES):
            panel_ref[h * per : (h + 1) * per] = xs[p * HALVES + h][...].reshape(per, block, width)

        def step(first, entries, alive):
            terms = []
            for t in range(GROUP):
                x = panel_ref[entries[t] & (blocks - 1)]
                terms.append(jnp.dot(tiles_ref[first + t], x, preferred_element_type=F32))
            for t in range(GROUP):
                acc[jnp.where(alive[t], entries[t] >> bits, blocks)] += terms[t]

        side = meta_ref[SIDE]
        j = meta_ref[ROW] ^ (2 * p + (1 - side if last else side))
        walk(meta_ref, j, rounds, slots, step)
    if last:
        span = blocks // len(outs)
        for d, out in enumerate(outs):
            at = (meta_ref[REP] ^ d) * span
            out[...] = acc[pl.ds(at, span)].reshape(out.shape).astype(out.dtype)
    else:
        outs[0][...] = acc[pl.ds(0, blocks)]


def forward(meta, tiles, rounds, xs, start, reps):
    block = tiles.shape[1]
    width = xs[0].shape[1]
    pairs = len(xs) // HALVES
    blocks = xs[0].shape[0] * HALVES // block
    last = start is not None
    if last:
        rows = blocks * block // reps
        outs = [jax.ShapeDtypeStruct((rows, width), BF16 if d else F32) for d in range(reps)]
    else:
        outs = [jax.ShapeDtypeStruct((blocks, block, width), F32)]
    body = functools.partial(
        forward_body, rounds=rounds, slots=tiles.shape[0] // rounds, pairs=pairs, last=last
    )
    got = call(
        body,
        meta,
        [tiles, *xs] + ([start] if last else []),
        outs,
        scratch=[pltpu.VMEM((blocks, block, width), BF16), pltpu.VMEM((blocks + 1, block, width), F32)],
        vmem=(0,),
        estimate=cost(2 * 64 * block * block * width, 12 * MIB),
        name="forward",
    )
    return got if last else got[0]


def total_body(_, own_ref, *refs):
    total = own_ref[...]
    for ref in refs[:-1]:
        total = total + ref[...].astype(F32)
    refs[-1][...] = total.astype(BF16)


def total_of(meta, own, others):
    out = jax.ShapeDtypeStruct(own.shape, BF16)
    return call(total_body, meta, [own, *others], out, name="total_of")


def gradient_of(agg, co, weight):
    pre = jnp.dot(agg, weight, preferred_element_type=F32)
    gate = 1.0 / (1.0 + jnp.exp(-pre))
    grad_pre = (co.astype(F32) * gate * (1.0 + pre * (1.0 - gate))).astype(BF16)
    return pre, gate, grad_pre


def up_body(meta_ref, w_ref, co_ref, *refs, first):
    shares, out_ref = refs[:-1], refs[-1]
    weight = w_ref[...]
    rows = shares[0].shape[0]
    for n, share in enumerate(shares):
        at = pl.multiple_of((meta_ref[REP] ^ (first + n)) * rows, rows)
        _, _, grad_pre = gradient_of(share[...], co_ref[pl.ds(at, rows), :], weight)
        out_ref[n] = lax.dot_general(
            weight, grad_pre, (((1,), (1,)), ((), ())), preferred_element_type=F32
        ).astype(BF16)


def up_shares(meta, weight, cotangent, shares, first):
    rows, width = shares[0].shape
    out = jax.ShapeDtypeStruct((len(shares), width, rows), BF16)
    return call(
        functools.partial(up_body, first=first),
        meta,
        [weight, cotangent, *shares],
        out,
        estimate=cost(4 * len(shares) * rows * width * width, 2 * MIB),
        name="up_shares",
    )


def finish_body(meta_ref, w_ref, co_ref, *refs):
    shares, (hidden_ref, grad_ref, agg_all, pre_all) = refs[:-5], refs[-4:]
    weight = w_ref[...]
    rows = shares[0].shape[0]
    for n, share in enumerate(shares):
        at = pl.multiple_of((meta_ref[REP] ^ n) * rows, rows)
        agg = share[...]
        pre, gate, grad_pre = gradient_of(agg, co_ref[pl.ds(at, rows), :], weight)
        hidden_ref[pl.ds(at, rows), :] = (pre * gate).astype(BF16)
        agg_all[pl.ds(at, rows), :] = agg
        pre_all[pl.ds(at, rows), :] = grad_pre
    grad_ref[...] = lax.dot_general(
        agg_all[...], pre_all[...], (((0,), (0,)), ((), ())), preferred_element_type=F32
    )


def finish(meta, weight, cotangent, shares, after):
    panel, width = cotangent.shape
    outs = (
        jax.ShapeDtypeStruct((panel, width), BF16),
        jax.ShapeDtypeStruct((width, width), F32),
    )
    after = after.reshape(-1, after.shape[-1])[:8]
    return call(
        finish_body,
        meta,
        [weight, cotangent, *shares, after],
        outs,
        scratch=[pltpu.VMEM((panel, width), BF16)] * 2,
        estimate=cost(6 * panel * width * width, 8 * panel * width),
        name="finish",
    )


def backward_body(meta_ref, tiles_ref, *refs, rounds, slots, pairs, keep):
    ups, (out_ref, up_all, acc) = refs[:-3], refs[-3:]
    chips, _, per, width, block = out_ref.shape
    blocks = chips * per
    bits = (blocks - 1).bit_length()
    count, _, rows = ups[0].shape
    for m, up in enumerate(ups):
        for n in range(count):
            at = pl.multiple_of((meta_ref[REP] ^ (m * count + n)) * rows, rows)
            up_all[:, pl.ds(at, rows)] = up[n]
    core = meta_ref[CORE]
    for p in range(pairs):
        acc[...] = jnp.zeros_like(acc)

        def step(first, entries, alive):
            terms = []
            for t in range(GROUP):
                at = pl.multiple_of((entries[t] >> bits) * block, block)
                terms.append(
                    jnp.dot(
                        up_all[:, pl.ds(at, block)],
                        tiles_ref[first + t],
                        preferred_element_type=F32,
                    )
                )
            for t in range(GROUP):
                acc[jnp.where(alive[t], entries[t] & (blocks - 1), blocks)] += terms[t]

        walk(meta_ref, 2 * p + (core if keep else 1 - core), rounds, slots, step)
        for d in range(chips):
            at = (meta_ref[CHIP] ^ d) * per
            out_ref[d, p] = acc[pl.ds(at, per)].astype(out_ref.dtype)


def backward(meta, tiles, rounds, ups, pairs, chips, keep):
    block = tiles.shape[1]
    count, width, rows = ups[0].shape
    panel = len(ups) * count * rows
    blocks = panel // block
    out = jax.ShapeDtypeStruct((chips, pairs, blocks // chips, width, block), F32 if keep else BF16)
    body = functools.partial(
        backward_body, rounds=rounds, slots=tiles.shape[0] // rounds, pairs=pairs, keep=keep
    )
    return call(
        body,
        meta,
        [tiles, *ups],
        out,
        scratch=[pltpu.VMEM((width, panel), BF16), pltpu.VMEM((blocks + 1, width, block), F32)],
        vmem=(0,),
        estimate=cost(2 * 64 * block * block * width, 12 * MIB),
        name="backward",
    )


def route_body(meta_ref, *refs, reps, chips):
    spread, outs = refs[:reps], refs[reps:]
    for k in range(chips):
        u = meta_ref[CHIP] ^ k
        p = u // reps
        for d in range(reps):

            @pl.when(((u % reps) ^ meta_ref[REP]) == d)
            def _():
                outs[k][...] = spread[d][p]


def route(meta, spread, chips):
    outs = [jax.ShapeDtypeStruct(spread[0].shape[1:], BF16)] * chips
    body = functools.partial(route_body, reps=len(spread), chips=chips)
    return call(body, meta, spread, outs, name="route")


def restore_body(ids_ref, order_ref, *refs, count):
    parts, out_ref = refs[:count], refs[-1]
    rows = out_ref.shape[0]
    per, _, block = parts[0].shape
    base = pl.program_id(0) * rows
    acc = refs[count][...] if len(refs) > count + 1 else None
    for n, part in enumerate(parts):
        length = per * block
        at = pl.multiple_of(ids_ref[n] * length, length)
        target = order_ref[:, pl.ds(at, length)]
        hot = lax.broadcasted_iota(jnp.int32, (rows, length), 0) + base == target
        hot = jnp.where(hot, 1.0, 0.0).astype(BF16)
        columns = jnp.concatenate([part[b] for b in range(per)], axis=1)
        term = lax.dot_general(
            hot, columns, (((1,), (1,)), ((), ())), preferred_element_type=F32
        )
        acc = term if acc is None else acc + term
    out_ref[...] = acc.astype(out_ref.dtype)


def restore(ids, order_row, parts, start, dtype):
    panel = order_row.shape[1]
    width = parts[0].shape[1]
    rows = 512
    row_spec = pl.BlockSpec((rows, width), lambda i, ids: (i, 0))
    extra = () if start is None else (start,)
    return pl.pallas_call(
        functools.partial(restore_body, count=len(parts)),
        out_shape=jax.ShapeDtypeStruct((panel, width), dtype),
        grid_spec=pltpu.PrefetchScalarGridSpec(
            num_scalar_prefetch=1,
            grid=(panel // rows,),
            in_specs=[whole_spec(order_row)]
            + [whole_spec(p) for p in parts]
            + [row_spec for _ in extra],
            out_specs=row_spec,
        ),
        compiler_params=params(24),
        cost_estimate=cost(2 * panel * panel * width, 4 * panel * width),
        name="restore",
    )(ids, order_row, *parts, *extra)


def tree_sum(terms):
    while len(terms) > 1:
        terms = [terms[i] + terms[i + 1] for i in range(0, len(terms), 2)]
    return terms[0]


def shards(features, order, tiles, tile_rows, tile_cols, live, weight, cotangent):
    reps = lax.axis_size("rep")
    sections = lax.axis_size("section")
    rep = lax.axis_index("rep")
    section = lax.axis_index("section")
    panel, width = features.shape
    rounds, slots, block, _ = tiles.shape[2:]
    blocks = panel // block
    chips = sections // 2
    pairs = rounds // 2
    near = reps // 2
    chip, core = section // 2, section % 2

    def over_chips(x, d):
        return lax.ppermute(x, "section", [(s, s ^ (2 * d)) for s in range(sections)])

    def over_cores(x):
        return lax.ppermute(x, "section", [(s, s ^ 1) for s in range(sections)])

    def over_reps(x, d):
        return lax.ppermute(x, "rep", [(r, r ^ d) for r in range(reps)])

    def from_owner(x, d):
        moves = []
        for r in range(reps):
            for j in range(rounds):
                source = j * reps + r
                target = (source ^ (2 * d)) ^ ((d // near) & 1)
                moves.append((source * reps + r, target * reps + r))
        return lax.ppermute(x, ("section", "rep"), moves)

    order_col = order.reshape(panel, 1)
    owns = [reorder(order_col, features, h, HALVES) for h in range(HALVES)]
    gots = [[own] + [from_owner(own, d) for d in range(1, chips)] for own in owns]
    side = core ^ (rep % 2)
    low = (chip % near) ^ (rep // 2)
    rows_in, cols_in, live_in, _ = lax.optimization_barrier(
        (tile_rows, tile_cols, live, owns[-1])
    )
    place = jnp.stack([rep, chip, core, side, chip // near, low])
    entries = (rows_in << (blocks - 1).bit_length()) | cols_in
    meta = jnp.concatenate([place, live_in.reshape(-1), entries.reshape(-1)]).astype(jnp.int32)
    own_tiles = tiles.reshape(rounds * slots, block, block)

    mine, mate = [], []
    for p in range(pairs):
        for h in range(HALVES):
            picked = pick(meta, gots[h][2 * p * near : 2 * (p + 1) * near], near)
            mine.append(picked)
            mate.append(over_cores(picked))

    started = forward(meta, own_tiles, rounds, mine, None, reps)
    own, *others = forward(meta, own_tiles, rounds, mate, started, reps)
    sent = {d: over_reps(others[d - 1], d) for d in reversed(range(1, reps))}
    aggregated = total_of(meta, own, [sent[d] for d in range(1, reps)])
    shares = [aggregated] + [over_reps(aggregated, d) for d in range(1, reps)]

    cut = reps // 2
    ups = [
        up_shares(meta, weight, cotangent, shares[:cut], 0),
        up_shares(meta, weight, cotangent, shares[cut:], cut),
    ]
    given = over_cores(backward(meta, own_tiles, rounds, ups, pairs, chips, False))
    kept = backward(meta, own_tiles, rounds, ups, pairs, chips, True)
    hidden, grad_part = finish(meta, weight, cotangent, shares, kept)
    chunks = [kept[d] + given[d].astype(F32) for d in range(chips)]
    arrived = [over_chips(chunks[d].astype(BF16), d).astype(F32) for d in range(1, chips)]
    reduced = tree_sum([chunks[0]] + arrived).astype(BF16)

    grad_part = grad_part + over_cores(grad_part)
    weight_grad = tree_sum([grad_part] + [over_chips(grad_part, d) for d in range(1, chips)])
    weight_grad = weight_grad * (1.0 / math.sqrt(panel * sections))

    spread = [reduced] + [over_reps(reduced, d) for d in range(1, reps)]
    routed = route(meta, spread, chips)

    def to_owner(k):
        moves = []
        for s in range(sections):
            u = (s // 2) ^ k
            moves.append((s, (2 * (u // reps) + s % 2) * reps + u % reps))
        return lax.ppermute(routed[k], "section", moves)

    parts = [to_owner(k) for k in range(chips)]
    mine_u = (section // reps // 2) * reps + section % reps
    part_ids = jnp.stack([mine_u ^ k for k in range(chips)]).astype(jnp.int32)
    order_row = order.reshape(1, panel)
    cut = chips // 2
    begun = restore(part_ids[:cut], order_row, parts[:cut], None, F32)
    feature_grad = restore(part_ids[cut:], order_row, parts[cut:], begun, BF16)
    return (hidden, weight_grad, feature_grad)


def solution(mesh):
    placed = (
        P("section", None),
        P("section"),
        P("section", "rep", None, None, None, None),
        P("section", "rep", None, None),
        P("section", "rep", None, None),
        P("section", "rep", None),
        P(),
        P("section", None),
    )
    return jax.shard_map(
        shards,
        mesh=mesh,
        in_specs=placed,
        out_specs=(P("section", None), P(), P("section", None)),
        check_vma=False,
    )
```

time: 488 us -> 120 us (0.25)
  waiting for transfers between devices: 338 us -> 35.8 us
  starting transfers between devices: 0.26 us -> 42.8 us
  matrix products: 40.4 us -> 0 us
  local copies, waits for them, and re-layouts: 49.3 us -> 9.87 us
  blocking collectives: 31 us -> 0 us
  Pallas kernels: 0 us -> 25.3 us
  between operations: 15.8 us -> 0.96 us
  other arithmetic: 12.4 us -> 3.91 us
    psum x5 -> x0, waiting for transfers between devices: 312 us -> none  [the longest x3 152 us: spread(): return lax.psum(kept, axis)]
    ppermute x0 -> x29, starting transfers between devices: none -> 42.8 us  [the longest x9 14.3 us: over_reps(): return lax.ppermute(x, 'rep', [(r, r ^ d) for r in range(reps)])]
    dot_general x9 -> x0, matrix products: 40.4 us -> none  [the longest x1 11.6 us: shards(): jnp.einsum('jkab,jkaf->jkbf', own_tiles, picked_up, preferred_element_typ...]
    ppermute x0 -> x29, waiting for transfers between devices: none -> 35.8 us  [the longest x9 22 us: over_reps(): return lax.ppermute(x, 'rep', [(r, r ^ d) for r in range(reps)])]
    all_gather x2 -> x0, blocking collectives: 31 us -> none  [the longest x1 16.2 us: shards(): lax.all_gather(upstream_share, 'rep', axis=0, tiled=True)]
    reduce_scatter x1 -> x0, waiting for transfers between devices: 25.6 us -> none  [shards(): lax.psum_scatter(partial_sum, 'rep', scatter_dimension=0, tiled=True)]
    pallas_call x0 -> x15, Pallas kernels: none -> 25.3 us  [the longest x11 15.1 us: call(): pl.pallas_call(body, out_shape=outs, grid_spec=pltpu.PrefetchScalarGridSp...]
    gather x4 -> x0, local copies, waits for them, and re-layouts: 21.6 us -> none  [the longest x1 7.97 us: shards(): jnp.take(up_blocks, row_table.reshape(-1), axis=0)]
  transfers between devices with their start and end apart: 6 -> 29, of which waited for: 6 -> 11; matrix products, arithmetic and copies ran while one was open for 3% -> 3% of each run, Pallas kernels for 0% -> 13%
where the time goes in v3:
time: 120 us; the launch traced here: 119 us
  starting transfers between devices  42.8 us (36%)
  waiting for transfers between devices  35.8 us (30%)
  Pallas kernels  25.3 us (21%)
  local copies, waits for them, and re-layouts  9.87 us (8%)
  other arithmetic  3.91 us (3%)
    ppermute x9, waiting for transfers between devices, over_reps(): return lax.ppermute(x, 'rep', [(r, r ^ d) for r in range(reps)])  22 us
    pallas_call x11, Pallas kernels, call(): pl.pallas_call(body, out_shape=outs, grid_spec=pltpu.PrefetchScalarGridSp...  15.1 us
    ppermute x9, starting transfers between devices, over_reps(): return lax.ppermute(x, 'rep', [(r, r ^ d) for r in range(reps)])  14.3 us
    ppermute x6, starting transfers between devices, from_owner(): return lax.ppermute(x, ('section', 'rep'), moves)  14 us
    ppermute x6, waiting for transfers between devices, over_chips(): return lax.ppermute(x, 'section', [(s, s ^ 2 * d) for s in range(sections)])  7.84 us
    unnamed x20, local copies, waits for them, and re-layouts  7.31 us
    ppermute x6, starting transfers between devices, over_chips(): return lax.ppermute(x, 'section', [(s, s ^ 2 * d) for s in range(sections)])  7.17 us
    ppermute x4, starting transfers between devices, to_owner(): return lax.ppermute(routed[k], 'section', moves)  6.65 us
  transfers between devices with their start and end apart: 29, of which 11 were waited for; matrix products, arithmetic and copies ran while one was open for 3% of the time, Pallas kernels for 13%

profile of v3, /device:TPU:0, one launch (start us, length us, event | category | flops | bytes accessed | tf_op | source)
XLA Modules:
  0.0 118.6 jit_solution(5371695601758765308)
XLA Ops:
  2.7 2.7 %reorder.3.refs_0_ = bf16[1024,128]{1,0:T(8,128)(2,1)} custom-call(s32[2048,1]{1,0:T(8,128)S(1)} %copy.11.order_ref, bf16[2048,128]{1,0:T(8,128)(2,1)S(1)} %copy-done.6), custom_call_target="tpu_custom_call" | custom-call | flops 536870912 | bytes 524288 | tf_op jit(solution)/shard_map/reorder/pallas_call | solution.py:41
  5.5 5.4 %collective-permute-start.2 = (bf16[1024,128]{1,0:T(8,128)(2,1)}, bf16[1024,128]{1,0:T(8,128)(2,1)S(1)}, u32[]{:S(2)}, u32[]{:S(2)}) collective-permute-start(bf16[1024,128]{1,0:T(8,128)(2,1)} %reorder.3.refs_0_), channel_id=1, source_target_pairs={{0,28},{16,12},{5,25},{21,9},{10,22},{26,6},{15,19},{31,3}} | collective-permute-start | bytes 786440 | tf_op jit(solution)/shard_map/ppermute | solution.py:404
  10.8 2.0 %collective-permute-start.1 = (bf16[1024,128]{1,0:T(8,128)(2,1)}, bf16[1024,128]{1,0:T(8,128)(2,1)}, u32[]{:S(2)}, u32[]{:S(2)}) collective-permute-start(bf16[1024,128]{1,0:T(8,128)(2,1)} %reorder.3.refs_0_), channel_id=1, source_target_pairs={{0,20},{16,4},{5,17},{21,1},{10,30},{26,14},{15,27},{31,11}} | collective-permute-start | bytes 786440 | tf_op jit(solution)/shard_map/ppermute | solution.py:404
  12.8 2.0 %collective-permute-start = (bf16[1024,128]{1,0:T(8,128)(2,1)}, bf16[1024,128]{1,0:T(8,128)(2,1)}, u32[]{:S(2)}, u32[]{:S(2)}) collective-permute-start(bf16[1024,128]{1,0:T(8,128)(2,1)} %reorder.3.refs_0_), channel_id=1, source_target_pairs={{0,8},{16,24},{5,13},{21,29},{10,2},{26,18},{15,7},{31,23}} | collective-permute-start | bytes 786440 | tf_op jit(solution)/shard_map/ppermute | solution.py:404
  21.2 2.0 %collective-permute-start.4 = (bf16[1024,128]{1,0:T(8,128)(2,1)S(1)}, bf16[1024,128]{1,0:T(8,128)(2,1)}, u32[]{:S(2)}, u32[]{:S(2)}) collective-permute-start(bf16[1024,128]{1,0:T(8,128)(2,1)S(1)} %reorder.2.refs_0_), channel_id=1, source_target_pairs={{0,8},{16,24},{5,13},{21,29},{10,2},{26,18},{15,7},{31,23}} | collective-permute-start | bytes 786440 | tf_op jit(solution)/shard_map/ppermute | solution.py:404
  29.5 2.8 %copy-done = bf16[1,1,2,96,128,128]{5,4,3,2,1,0:T(8,128)(2,1)S(1)} copy-done((bf16[1,1,2,96,128,128]{5,4,3,2,1,0:T(8,128)(2,1)S(1)}, bf16[1,1,2,96,128,128]{5,4,3,2,1,0:T(8,128)(2,1)}, u32[]{:S(2)}) %copy-start) | copy-done | bytes 6291480
  35.9 3.1 %collective-permute-start.8 = (bf16[512,128]{1,0:T(8,128)(2,1)S(1)}, bf16[512,128]{1,0:T(8,128)(2,1)S(1)}, u32[]{:S(2)}, u32[]{:S(2)}) collective-permute-start(bf16[512,128]{1,0:T(8,128)(2,1)S(1)} %get-tuple-element.20), channel_id=1, source_target_pairs={{0,1},{1,0},{2,3},{3,2},{4,5},{5,4},{6,7},{7,6},{8,9},{9,8},{10,11... | collective-permute-start | bytes 393224 | tf_op jit(solution)/shard_map/ppermute | solution.py:395
  43.3 7.7 %collective-permute-done.9.refs_1_ = bf16[512,128]{1,0:T(8,128)(2,1)S(1)} collective-permute-done((bf16[512,128]{1,0:T(8,128)(2,1)S(1)}, bf16[512,128]{1,0:T(8,128)(2,1)S(1)}, u32[]{:S(2)}, u32[]{:S(2)}) %collective-permute-start.9) | collective-permute-done | bytes 131104 | tf_op jit(solution)/shard_map/ppermute | solution.py:395
  51.6 2.0 %collective-permute-start.11 = (bf16[512,128]{1,0:T(8,128)(2,1)S(1)}, bf16[512,128]{1,0:T(8,128)(2,1)S(1)}, u32[]{:S(2)}, u32[]{:S(2)}) collective-permute-start(bf16[512,128]{1,0:T(8,128)(2,1)S(1)} %total_of.1.refs_0_), channel_id=1, source_target_pairs={{0,1},{1,0},{2,3},{3,2},{4,5},{5,4},{6,7},{7,6},{8,9},{9,8},{10,11... | collective-permute-start | bytes 393224 | tf_op jit(solution)/shard_map/ppermute | solution.py:395
  53.6 2.3 %collective-permute-start.13 = (bf16[512,128]{1,0:T(8,128)(2,1)S(1)}, bf16[512,128]{1,0:T(8,128)(2,1)S(1)}, u32[]{:S(2)}, u32[]{:S(2)}) collective-permute-start(bf16[512,128]{1,0:T(8,128)(2,1)S(1)} %total_of.1.refs_0_), channel_id=1, source_target_pairs={{0,3},{1,2},{2,1},{3,0},{4,7},{5,6},{6,5},{7,4},{8,11},{9,10},{10,... | collective-permute-start | bytes 393224 | tf_op jit(solution)/shard_map/ppermute | solution.py:395
  57.7 5.5 %collective-permute-done.13.refs_1_.refs_3_ = bf16[512,128]{1,0:T(8,128)(2,1)S(1)} collective-permute-done((bf16[512,128]{1,0:T(8,128)(2,1)S(1)}, bf16[512,128]{1,0:T(8,128)(2,1)S(1)}, u32[]{:S(2)}, u32[]{:S(2)}) %collective-permute-start.13) | collective-permute-done | bytes 131104 | tf_op jit(solution)/shard_map/ppermute | solution.py:395
  63.2 3.4 %collective-permute-done.12.refs_0_.refs_2_ = bf16[512,128]{1,0:T(8,128)(2,1)S(1)} collective-permute-done((bf16[512,128]{1,0:T(8,128)(2,1)S(1)}, bf16[512,128]{1,0:T(8,128)(2,1)S(1)}, u32[]{:S(2)}, u32[]{:S(2)}) %collective-permute-start.12) | collective-permute-done | bytes 131104 | tf_op jit(solution)/shard_map/ppermute | solution.py:395
  69.2 2.4 %backward.2 = f32[4,1,4,128,128]{4,3,2,1,0:T(8,128)} custom-call(s32[200]{0:T(256)S(1)} %concatenate.5.meta_ref._, bf16[192,128,128]{2,1,0:T(8,128)(2,1)S(1)} %bitcast.34, bf16[2,128,512]{2,1,0:T(8,128)(2,1)S(1)} %up_shares.2.refs_0_, bf16[2,128,512]{2,1,0:T(8,128)(2,1)S(1)} %up_shares.3.refs_1_), custom_call_target="tpu_custom_call" | custom-call | flops 268435456 | bytes 12582912 | tf_op jit(solution)/shard_map/backward/pallas_call | solution.py:71
  72.9 2.1 %collective-permute-start.19 = (bf16[1,4,128,128]{3,2,1,0:T(8,128)(2,1)S(1)}, bf16[1,4,128,128]{3,2,1,0:T(8,128)(2,1)S(1)}, u32[]{:S(2)}, u32[]{:S(2)}) collective-permute-start(bf16[1,4,128,128]{3,2,1,0:T(8,128)(2,1)S(1)} %get-tuple-element.29), channel_id=1, source_target_pairs={{0,8},{4,12},{8,0},{12,4},{16,24},{20,28},{24,16},{28,20},{1,9},{5... | collective-permute-start | bytes 393224 | tf_op jit(solution)/shard_map/ppermute | solution.py:389
  77.2 2.0 %collective-permute-done.19 = bf16[1,4,128,128]{3,2,1,0:T(8,128)(2,1)S(1)} collective-permute-done((bf16[1,4,128,128]{3,2,1,0:T(8,128)(2,1)S(1)}, bf16[1,4,128,128]{3,2,1,0:T(8,128)(2,1)S(1)}, u32[]{:S(2)}, u32[]{:S(2)}) %collective-permute-start.19) | collective-permute-done | bytes 131104 | tf_op jit(solution)/shard_map/ppermute | solution.py:389
  79.1 4.2 %collective-permute-done.21 = bf16[1,4,128,128]{3,2,1,0:T(8,128)(2,1)S(1)} collective-permute-done((bf16[1,4,128,128]{3,2,1,0:T(8,128)(2,1)S(1)}, bf16[1,4,128,128]{3,2,1,0:T(8,128)(2,1)S(1)}, u32[]{:S(2)}, u32[]{:S(2)}) %collective-permute-start.21) | collective-permute-done | bytes 131104 | tf_op jit(solution)/shard_map/ppermute | solution.py:389
  87.2 2.0 %finish.1 = (bf16[2048,128]{1,0:T(8,128)(2,1)}, f32[128,128]{1,0:T(8,128)S(1)}) custom-call(s32[200]{0:T(256)S(1)} %concatenate.5.meta_ref._, bf16[128,128]{1,0:T(8,128)(2,1)S(1)} %copy-done.2, bf16[2048,128]{1,0:T(8,128)(2,1)S(1)} %copy-done.1, bf16[512,128]{1,0:T(8,128)(2,1)S(1)} %total_of.1.refs_0_, bf16[512,128]{1,0:T(8,128)(2,1)S(1)} %collective-permute-done.11.refs_1_, ...), custom_call_target="tpu_custom_call" | custom-call | flops 201326592 | bytes 2097152 | tf_op jit(solution)/shard_map/finish/pallas_call | solution.py:71
  89.2 3.4 %collective-permute-start.22 = (bf16[1,4,128,128]{3,2,1,0:T(8,128)(2,1)S(1)}, bf16[1,4,128,128]{3,2,1,0:T(8,128)(2,1)S(1)}, u32[]{:S(2)}, u32[]{:S(2)}) collective-permute-start(bf16[1,4,128,128]{3,2,1,0:T(8,128)(2,1)S(1)} %fusion.6.refs_0_), channel_id=1, source_target_pairs={{0,1},{1,0},{2,3},{3,2},{4,5},{5,4},{6,7},{7,6},{8,9},{9,8},{10,11... | collective-permute-start | bytes 393224 | tf_op jit(solution)/shard_map/ppermute | solution.py:395
  96.3 2.6 %collective-permute-done.23.refs_2_ = bf16[1,4,128,128]{3,2,1,0:T(8,128)(2,1)S(1)} collective-permute-done((bf16[1,4,128,128]{3,2,1,0:T(8,128)(2,1)S(1)}, bf16[1,4,128,128]{3,2,1,0:T(8,128)(2,1)S(1)}, u32[]{:S(2)}, u32[]{:S(2)}) %collective-permute-start.23) | collective-permute-done | bytes 131104 | tf_op jit(solution)/shard_map/ppermute | solution.py:395
  100.4 2.0 %collective-permute-start.26 = (bf16[4,128,128]{2,1,0:T(8,128)(2,1)S(1)}, bf16[4,128,128]{2,1,0:T(8,128)(2,1)S(1)}, u32[]{:S(2)}, u32[]{:S(2)}) collective-permute-start(bf16[4,128,128]{2,1,0:T(8,128)(2,1)S(1)} %get-tuple-element.26), channel_id=1, source_target_pairs={{0,12},{4,28},{8,8},{12,24},{16,4},{20,20},{24,0},{28,16},{1,13},{... | collective-permute-start | bytes 393224 | tf_op jit(solution)/shard_map/ppermute | solution.py:456
  103.2 3.3 %collective-permute-start.28 = (bf16[4,128,128]{2,1,0:T(8,128)(2,1)S(1)}, bf16[4,128,128]{2,1,0:T(8,128)(2,1)S(1)}, u32[]{:S(2)}, u32[]{:S(2)}) collective-permute-start(bf16[4,128,128]{2,1,0:T(8,128)(2,1)S(1)} %get-tuple-element.28), channel_id=1, source_target_pairs={{0,4},{4,20},{8,0},{12,16},{16,12},{20,28},{24,8},{28,24},{1,5},{5... | collective-permute-start | bytes 393224 | tf_op jit(solution)/shard_map/ppermute | solution.py:456
  107.1 5.9 %collective-permute-done.28.refs_1_ = bf16[4,128,128]{2,1,0:T(8,128)(2,1)S(1)} collective-permute-done((bf16[4,128,128]{2,1,0:T(8,128)(2,1)S(1)}, bf16[4,128,128]{2,1,0:T(8,128)(2,1)S(1)}, u32[]{:S(2)}, u32[]{:S(2)}) %collective-permute-start.28) | collective-permute-done | bytes 131104 | tf_op jit(solution)/shard_map/ppermute | solution.py:456
  113.0 2.3 %restore.2.refs_2_ = f32[2048,128]{1,0:T(8,128)S(1)} custom-call(s32[2]{0:T(128)S(1)} %pad_add_fusion.1.ids_ref, s32[1,2048]{1,0:T(1,128)S(1)} %bitcast.36, bf16[4,128,128]{2,1,0:T(8,128)(2,1)S(1)} %collective-permute-done.27.refs_0_, bf16[4,128,128]{2,1,0:T(8,128)(2,1)S(1)} %collective-permute-done.28.refs_1_), custom_call_target="tpu_custom_call" | custom-call | flops 1073741824 | bytes 1048576 | tf_op jit(solution)/shard_map/restore/pallas_call | solution.py:352
  115.4 3.2 %restore.3 = bf16[2048,128]{1,0:T(8,128)(2,1)} custom-call(s32[2]{0:T(128)S(1)} %pad_add_fusion.ids_ref, s32[1,2048]{1,0:T(1,128)S(1)} %bitcast.37, bf16[4,128,128]{2,1,0:T(8,128)(2,1)S(1)} %collective-permute-done.25.refs_0_, bf16[4,128,128]{2,1,0:T(8,128)(2,1)S(1)} %collective-permute-done.26.refs_1_, f32[2048,128]{1,0:T(8,128)S(1)} %restore.2.refs_2_), custom_call_target="tpu_custom_call" | custom-call | flops 1073741824 | bytes 1048576 | tf_op jit(solution)/shard_map/restore/pallas_call | solution.py:352
  (81 shorter events, 41.3 us)
Async XLA Ops:
  5.5 15.0 %collective-permute-start.2 = (bf16[1024,128]{1,0:T(8,128)(2,1)}, bf16[1024,128]{1,0:T(8,128)(2,1)S(1)}, u32[]{:S(2)}, u32[]{:S(2)}) collective-permute-start(bf16[1024,128]{1,0:T(8,128)(2,1)} %reorder.3.refs_0_), channel_id=1, source_target_pairs={{0,28},{16,12},{5,25},{21,9},{10,22},{26,6},{15,19},{31,3}} | collective-permute-start | bytes 786440 | tf_op jit(solution)/shard_map/ppermute | solution.py:404
  10.8 13.9 %collective-permute-start.1 = (bf16[1024,128]{1,0:T(8,128)(2,1)}, bf16[1024,128]{1,0:T(8,128)(2,1)}, u32[]{:S(2)}, u32[]{:S(2)}) collective-permute-start(bf16[1024,128]{1,0:T(8,128)(2,1)} %reorder.3.refs_0_), channel_id=1, source_target_pairs={{0,20},{16,4},{5,17},{21,1},{10,30},{26,14},{15,27},{31,11}} | collective-permute-start | bytes 786440 | tf_op jit(solution)/shard_map/ppermute | solution.py:404
  12.8 11.8 %collective-permute-start = (bf16[1024,128]{1,0:T(8,128)(2,1)}, bf16[1024,128]{1,0:T(8,128)(2,1)}, u32[]{:S(2)}, u32[]{:S(2)}) collective-permute-start(bf16[1024,128]{1,0:T(8,128)(2,1)} %reorder.3.refs_0_), channel_id=1, source_target_pairs={{0,8},{16,24},{5,13},{21,29},{10,2},{26,18},{15,7},{31,23}} | collective-permute-start | bytes 786440 | tf_op jit(solution)/shard_map/ppermute | solution.py:404
  17.8 9.6 %collective-permute-start.6 = (bf16[1024,128]{1,0:T(8,128)(2,1)S(1)}, bf16[1024,128]{1,0:T(8,128)(2,1)S(1)}, u32[]{:S(2)}, u32[]{:S(2)}) collective-permute-start(bf16[1024,128]{1,0:T(8,128)(2,1)S(1)} %reorder.2.refs_0_), channel_id=1, source_target_pairs={{0,28},{16,12},{5,25},{21,9},{10,22},{26,6},{15,19},{31,3}} | collective-permute-start | bytes 786440 | tf_op jit(solution)/shard_map/ppermute | solution.py:404
  19.1 8.3 %collective-permute-start.5 = (bf16[1024,128]{1,0:T(8,128)(2,1)S(1)}, bf16[1024,128]{1,0:T(8,128)(2,1)S(1)}, u32[]{:S(2)}, u32[]{:S(2)}) collective-permute-start(bf16[1024,128]{1,0:T(8,128)(2,1)S(1)} %reorder.2.refs_0_), channel_id=1, source_target_pairs={{0,20},{16,4},{5,17},{21,1},{10,30},{26,14},{15,27},{31,11}} | collective-permute-start | bytes 786440 | tf_op jit(solution)/shard_map/ppermute | solution.py:404
  21.2 6.3 %collective-permute-start.4 = (bf16[1024,128]{1,0:T(8,128)(2,1)S(1)}, bf16[1024,128]{1,0:T(8,128)(2,1)}, u32[]{:S(2)}, u32[]{:S(2)}) collective-permute-start(bf16[1024,128]{1,0:T(8,128)(2,1)S(1)} %reorder.2.refs_0_), channel_id=1, source_target_pairs={{0,8},{16,24},{5,13},{21,29},{10,2},{26,18},{15,7},{31,23}} | collective-permute-start | bytes 786440 | tf_op jit(solution)/shard_map/ppermute | solution.py:404
  27.4 6.4 %collective-permute-start.3 = (bf16[1024,128]{1,0:T(8,128)(2,1)S(1)}, bf16[1024,128]{1,0:T(8,128)(2,1)S(1)}, u32[]{:S(2)}, u32[]{:S(2)}) collective-permute-start(bf16[1024,128]{1,0:T(8,128)(2,1)S(1)} %pick.2.refs_0_), channel_id=1, source_target_pairs={{0,4},{4,0},{8,12},{12,8},{16,20},{20,16},{24,28},{28,24},{1,5},{5... | collective-permute-start | bytes 786440 | tf_op jit(solution)/shard_map/ppermute | solution.py:392
  35.9 7.4 %collective-permute-start.8 = (bf16[512,128]{1,0:T(8,128)(2,1)S(1)}, bf16[512,128]{1,0:T(8,128)(2,1)S(1)}, u32[]{:S(2)}, u32[]{:S(2)}) collective-permute-start(bf16[512,128]{1,0:T(8,128)(2,1)S(1)} %get-tuple-element.20), channel_id=1, source_target_pairs={{0,1},{1,0},{2,3},{3,2},{4,5},{5,4},{6,7},{7,6},{8,9},{9,8},{10,11... | collective-permute-start | bytes 393224 | tf_op jit(solution)/shard_map/ppermute | solution.py:395
  38.9 12.0 %collective-permute-start.9 = (bf16[512,128]{1,0:T(8,128)(2,1)S(1)}, bf16[512,128]{1,0:T(8,128)(2,1)S(1)}, u32[]{:S(2)}, u32[]{:S(2)}) collective-permute-start(bf16[512,128]{1,0:T(8,128)(2,1)S(1)} %get-tuple-element.21), channel_id=1, source_target_pairs={{0,2},{1,3},{2,0},{3,1},{4,6},{5,7},{6,4},{7,5},{8,10},{9,11},{10,... | collective-permute-start | bytes 393224 | tf_op jit(solution)/shard_map/ppermute | solution.py:395
  40.0 11.0 %collective-permute-start.10 = (bf16[512,128]{1,0:T(8,128)(2,1)S(1)}, bf16[512,128]{1,0:T(8,128)(2,1)S(1)}, u32[]{:S(2)}, u32[]{:S(2)}) collective-permute-start(bf16[512,128]{1,0:T(8,128)(2,1)S(1)} %get-tuple-element.22), channel_id=1, source_target_pairs={{0,3},{1,2},{2,1},{3,0},{4,7},{5,6},{6,5},{7,4},{8,11},{9,10},{10,... | collective-permute-start | bytes 393224 | tf_op jit(solution)/shard_map/ppermute | solution.py:395
  53.6 9.6 %collective-permute-start.13 = (bf16[512,128]{1,0:T(8,128)(2,1)S(1)}, bf16[512,128]{1,0:T(8,128)(2,1)S(1)}, u32[]{:S(2)}, u32[]{:S(2)}) collective-permute-start(bf16[512,128]{1,0:T(8,128)(2,1)S(1)} %total_of.1.refs_0_), channel_id=1, source_target_pairs={{0,3},{1,2},{2,1},{3,0},{4,7},{5,6},{6,5},{7,4},{8,11},{9,10},{10,... | collective-permute-start | bytes 393224 | tf_op jit(solution)/shard_map/ppermute | solution.py:395
  56.0 10.7 %collective-permute-start.12 = (bf16[512,128]{1,0:T(8,128)(2,1)S(1)}, bf16[512,128]{1,0:T(8,128)(2,1)S(1)}, u32[]{:S(2)}, u32[]{:S(2)}) collective-permute-start(bf16[512,128]{1,0:T(8,128)(2,1)S(1)} %total_of.1.refs_0_), channel_id=1, source_target_pairs={{0,2},{1,3},{2,0},{3,1},{4,6},{5,7},{6,4},{7,5},{8,10},{9,11},{10,... | collective-permute-start | bytes 393224 | tf_op jit(solution)/shard_map/ppermute | solution.py:395
  72.9 6.3 %collective-permute-start.19 = (bf16[1,4,128,128]{3,2,1,0:T(8,128)(2,1)S(1)}, bf16[1,4,128,128]{3,2,1,0:T(8,128)(2,1)S(1)}, u32[]{:S(2)}, u32[]{:S(2)}) collective-permute-start(bf16[1,4,128,128]{3,2,1,0:T(8,128)(2,1)S(1)} %get-tuple-element.29), channel_id=1, source_target_pairs={{0,8},{4,12},{8,0},{12,4},{16,24},{20,28},{24,16},{28,20},{1,9},{5... | collective-permute-start | bytes 393224 | tf_op jit(solution)/shard_map/ppermute | solution.py:389
  74.9 8.4 %collective-permute-start.21 = (bf16[1,4,128,128]{3,2,1,0:T(8,128)(2,1)S(1)}, bf16[1,4,128,128]{3,2,1,0:T(8,128)(2,1)S(1)}, u32[]{:S(2)}, u32[]{:S(2)}) collective-permute-start(bf16[1,4,128,128]{3,2,1,0:T(8,128)(2,1)S(1)} %get-tuple-element.30), channel_id=1, source_target_pairs={{0,24},{4,28},{8,16},{12,20},{16,8},{20,12},{24,0},{28,4},{1,25},{... | collective-permute-start | bytes 393224 | tf_op jit(solution)/shard_map/ppermute | solution.py:389
  76.2 8.8 %collective-permute-start.20 = (bf16[1,4,128,128]{3,2,1,0:T(8,128)(2,1)S(1)}, bf16[1,4,128,128]{3,2,1,0:T(8,128)(2,1)S(1)}, u32[]{:S(2)}, u32[]{:S(2)}) collective-permute-start(bf16[1,4,128,128]{3,2,1,0:T(8,128)(2,1)S(1)} %get-tuple-element.31), channel_id=1, source_target_pairs={{0,16},{4,20},{8,24},{12,28},{16,0},{20,4},{24,8},{28,12},{1,17},{... | collective-permute-start | bytes 393224 | tf_op jit(solution)/shard_map/ppermute | solution.py:389
  86.1 8.5 %collective-permute-start.24 = (bf16[1,4,128,128]{3,2,1,0:T(8,128)(2,1)S(1)}, bf16[1,4,128,128]{3,2,1,0:T(8,128)(2,1)S(1)}, u32[]{:S(2)}, u32[]{:S(2)}) collective-permute-start(bf16[1,4,128,128]{3,2,1,0:T(8,128)(2,1)S(1)} %fusion.6.refs_0_), channel_id=1, source_target_pairs={{0,3},{1,2},{2,1},{3,0},{4,7},{5,6},{6,5},{7,4},{8,11},{9,10},{10,... | collective-permute-start | bytes 393224 | tf_op jit(solution)/shard_map/ppermute | solution.py:395
  89.2 9.7 %collective-permute-start.23 = (bf16[1,4,128,128]{3,2,1,0:T(8,128)(2,1)S(1)}, bf16[1,4,128,128]{3,2,1,0:T(8,128)(2,1)S(1)}, u32[]{:S(2)}, u32[]{:S(2)}) collective-permute-start(bf16[1,4,128,128]{3,2,1,0:T(8,128)(2,1)S(1)} %fusion.6.refs_0_), channel_id=1, source_target_pairs={{0,2},{1,3},{2,0},{3,1},{4,6},{5,7},{6,4},{7,5},{8,10},{9,11},{10,... | collective-permute-start | bytes 393224 | tf_op jit(solution)/shard_map/ppermute | solution.py:395
  89.2 9.8 %collective-permute-start.22 = (bf16[1,4,128,128]{3,2,1,0:T(8,128)(2,1)S(1)}, bf16[1,4,128,128]{3,2,1,0:T(8,128)(2,1)S(1)}, u32[]{:S(2)}, u32[]{:S(2)}) collective-permute-start(bf16[1,4,128,128]{3,2,1,0:T(8,128)(2,1)S(1)} %fusion.6.refs_0_), channel_id=1, source_target_pairs={{0,1},{1,0},{2,3},{3,2},{4,5},{5,4},{6,7},{7,6},{8,9},{9,8},{10,11... | collective-permute-start | bytes 393224 | tf_op jit(solution)/shard_map/ppermute | solution.py:395
  92.7 9.8 %collective-permute-start.17 = (f32[128,128]{1,0:T(8,128)S(1)}, f32[128,128]{1,0:T(8,128)S(1)}, u32[]{:S(2)}, u32[]{:S(2)}) collective-permute-start(f32[128,128]{1,0:T(8,128)S(1)} %add.95), channel_id=1, source_target_pairs={{0,24},{4,28},{8,16},{12,20},{16,8},{20,12},{24,0},{28,4},{1,25},{... | collective-permute-start | bytes 196616 | tf_op jit(solution)/shard_map/ppermute | solution.py:389
  93.4 9.7 %collective-permute-start.16 = (f32[128,128]{1,0:T(8,128)S(1)}, f32[128,128]{1,0:T(8,128)S(1)}, u32[]{:S(2)}, u32[]{:S(2)}) collective-permute-start(f32[128,128]{1,0:T(8,128)S(1)} %add.95), channel_id=1, source_target_pairs={{0,16},{4,20},{8,24},{12,28},{16,0},{20,4},{24,8},{28,12},{1,17},{... | collective-permute-start | bytes 196616 | tf_op jit(solution)/shard_map/ppermute | solution.py:389
  94.6 11.9 %collective-permute-start.15 = (f32[128,128]{1,0:T(8,128)S(1)}, f32[128,128]{1,0:T(8,128)S(1)}, u32[]{:S(2)}, u32[]{:S(2)}) collective-permute-start(f32[128,128]{1,0:T(8,128)S(1)} %add.95), channel_id=1, source_target_pairs={{0,8},{4,12},{8,0},{12,4},{16,24},{20,28},{24,16},{28,20},{1,9},{5... | collective-permute-start | bytes 196616 | tf_op jit(solution)/shard_map/ppermute | solution.py:389
  99.8 15.6 %collective-permute-start.25 = (bf16[4,128,128]{2,1,0:T(8,128)(2,1)S(1)}, bf16[4,128,128]{2,1,0:T(8,128)(2,1)S(1)}, u32[]{:S(2)}, u32[]{:S(2)}) collective-permute-start(bf16[4,128,128]{2,1,0:T(8,128)(2,1)S(1)} %get-tuple-element.25), channel_id=1, source_target_pairs={{0,8},{4,24},{8,12},{12,28},{16,0},{20,16},{24,4},{28,20},{1,9},{5... | collective-permute-start | bytes 393224 | tf_op jit(solution)/shard_map/ppermute | solution.py:456
  100.4 14.9 %collective-permute-start.26 = (bf16[4,128,128]{2,1,0:T(8,128)(2,1)S(1)}, bf16[4,128,128]{2,1,0:T(8,128)(2,1)S(1)}, u32[]{:S(2)}, u32[]{:S(2)}) collective-permute-start(bf16[4,128,128]{2,1,0:T(8,128)(2,1)S(1)} %get-tuple-element.26), channel_id=1, source_target_pairs={{0,12},{4,28},{8,8},{12,24},{16,4},{20,20},{24,0},{28,16},{1,13},{... | collective-permute-start | bytes 393224 | tf_op jit(solution)/shard_map/ppermute | solution.py:456
  103.2 9.9 %collective-permute-start.28 = (bf16[4,128,128]{2,1,0:T(8,128)(2,1)S(1)}, bf16[4,128,128]{2,1,0:T(8,128)(2,1)S(1)}, u32[]{:S(2)}, u32[]{:S(2)}) collective-permute-start(bf16[4,128,128]{2,1,0:T(8,128)(2,1)S(1)} %get-tuple-element.28), channel_id=1, source_target_pairs={{0,4},{4,20},{8,0},{12,16},{16,12},{20,28},{24,8},{28,24},{1,5},{5... | collective-permute-start | bytes 393224 | tf_op jit(solution)/shard_map/ppermute | solution.py:456
  (15 other events, 147.2 us)

commit v4 on v3

v4 whole, which is shorter than its diff:
```python
import functools
import math

import jax
import jax.numpy as jnp
from jax import lax
from jax.experimental import pallas as pl
from jax.experimental.pallas import tpu as pltpu
from jax.sharding import PartitionSpec as P

F32 = jnp.float32
BF16 = jnp.bfloat16
MIB = 1 << 20


def params(mib):
    return pltpu.CompilerParams(vmem_limit_bytes=mib * MIB)


def cost(flops, nbytes):
    return pl.CostEstimate(flops=int(flops), bytes_accessed=int(nbytes), transcendentals=0)


def whole_spec(array):
    zeros = (0,) * array.ndim
    return pl.BlockSpec(array.shape, lambda *_: zeros)


HALVES = 2
GROUP = 16


class Place:
    def __init__(self):
        reps = lax.axis_size("rep")
        section = lax.axis_index("section")
        self.rep = lax.axis_index("rep")
        self.chip = section // 2
        self.core = section % 2
        self.side = (section + self.rep) % 2
        self.row = section // reps
        self.low = ((section % reps) // 2) ^ (self.rep // 2)


def in_vmem(array):
    return pltpu.with_memory_space_constraint(array, pltpu.VMEM)


def call(body, operands, outs, scalars=(), scratch=(), vmem=(), mib=12, estimate=None, name=None):
    specs = [
        pl.BlockSpec(memory_space=pltpu.VMEM) if n in vmem else whole_spec(x)
        for n, x in enumerate(operands)
    ]
    operands = [in_vmem(x) if n in vmem else x for n, x in enumerate(operands)]
    return pl.pallas_call(
        body,
        out_shape=outs,
        grid_spec=pltpu.PrefetchScalarGridSpec(
            num_scalar_prefetch=len(scalars),
            grid=(1,),
            in_specs=specs,
            out_specs=jax.tree.map(whole_spec, outs),
            scratch_shapes=list(scratch),
        ),
        compiler_params=params(mib),
        cost_estimate=estimate or cost(0, MIB),
        name=name,
    )(*scalars, *operands)


def like(array, dtype=None):
    return jax.ShapeDtypeStruct(array.shape, dtype or array.dtype)


def reorder_body(order_ref, feat_ref, *outs):
    panel = feat_ref.shape[0]
    rows = outs[0].shape[0]
    step = min(256, rows)
    for i in range(panel // step):
        hot = lax.broadcasted_iota(jnp.int32, (step, panel), 1) == order_ref[pl.ds(i * step, step), :]
        hot = jnp.where(hot, 1.0, 0.0).astype(BF16)
        at = i * step % rows
        outs[i * step // rows][at : at + step, :] = jnp.dot(
            hot, feat_ref[...], preferred_element_type=F32
        ).astype(BF16)


def reorder(order_col, features):
    panel, width = features.shape
    outs = [jax.ShapeDtypeStruct((panel // HALVES, width), BF16)] * HALVES
    return call(
        reorder_body,
        [order_col, features],
        outs,
        estimate=cost(2 * panel * panel * width, 4 * panel * width),
        name="reorder",
    )


def entry_body(rows_ref, cols_ref, _, out_ref, *, bits):
    out_ref[...] = (rows_ref[0, 0] << bits) | cols_ref[0, 0]


def entries_of(rows, cols, bits, after):
    out = jax.ShapeDtypeStruct(rows.shape[2:], jnp.int32)
    return call(
        functools.partial(entry_body, bits=bits), [rows, cols, after], out, name="entries_of"
    )


def pick_body(*refs, near):
    options, out_ref = refs[:-1], refs[-1]
    place = Place()
    for n, option in enumerate(options):

        @pl.when((place.side == n // near) & (place.low == n % near))
        def _():
            out_ref[...] = option[...]


def pick(options, near):
    return call(functools.partial(pick_body, near=near), options, like(options[0]), name="pick")


def walk(live_ref, entry_ref, j, slots, step):
    count = live_ref[j]

    @pl.loop(0, (count + GROUP - 1) // GROUP)
    def _(g):
        entries = [entry_ref[j, g * GROUP + t] for t in range(GROUP)]
        alive = [g * GROUP + t < count for t in range(GROUP)]
        step(j * slots + g * GROUP, entries, alive)


def forward_body(live_ref, entry_ref, tiles_ref, *refs, slots, pairs, last):
    place = Place()
    xs, rest = refs[: pairs * HALVES], refs[pairs * HALVES :]
    panel_ref, acc = rest[-2:]
    blocks, block, width = panel_ref.shape
    bits = (blocks - 1).bit_length()
    if last:
        start, outs = rest[0], rest[1:-2]
        acc[pl.ds(0, blocks)] = start[...]
        acc[blocks] = jnp.zeros((block, width), F32)
    else:
        outs = rest[:-2]
        acc[...] = jnp.zeros_like(acc)
    per = blocks // HALVES
    for p in range(pairs):
        for h in range(HALVES):
            panel_ref[h * per : (h + 1) * per] = xs[p * HALVES + h][...].reshape(per, block, width)

        def step(first, entries, alive):
            terms = []
            for t in range(GROUP):
                x = panel_ref[entries[t] & (blocks - 1)]
                terms.append(jnp.dot(tiles_ref[first + t], x, preferred_element_type=F32))
            for t in range(GROUP):
                acc[jnp.where(alive[t], entries[t] >> bits, blocks)] += terms[t]

        j = place.row ^ (2 * p + (1 - place.side if last else place.side))
        walk(live_ref, entry_ref, j, slots, step)
    if last:
        span = blocks // len(outs)
        for d, out in enumerate(outs):
            at = (place.rep ^ d) * span
            out[...] = acc[pl.ds(at, span)].reshape(out.shape).astype(out.dtype)
    else:
        outs[0][...] = acc[pl.ds(0, blocks)]


def forward(plan, tiles, xs, start, reps):
    block = tiles.shape[1]
    width = xs[0].shape[1]
    pairs = len(xs) // HALVES
    blocks = xs[0].shape[0] * HALVES // block
    last = start is not None
    if last:
        rows = blocks * block // reps
        outs = [jax.ShapeDtypeStruct((rows, width), BF16 if d else F32) for d in range(reps)]
    else:
        outs = [jax.ShapeDtypeStruct((blocks, block, width), F32)]
    body = functools.partial(
        forward_body, slots=plan[1].shape[1], pairs=pairs, last=last
    )
    got = call(
        body,
        [tiles, *xs] + ([start] if last else []),
        outs,
        scalars=plan,
        scratch=[pltpu.VMEM((blocks, block, width), BF16), pltpu.VMEM((blocks + 1, block, width), F32)],
        vmem=(0,),
        estimate=cost(2 * 64 * block * block * width, 12 * MIB),
        name="forward",
    )
    return got if last else got[0]


def total_body(own_ref, *refs):
    total = own_ref[...]
    for ref in refs[:-1]:
        total = total + ref[...].astype(F32)
    refs[-1][...] = total.astype(BF16)


def total_of(own, others):
    return call(total_body, [own, *others], like(own, BF16), name="total_of")


def gradient_of(agg, co, weight):
    pre = jnp.dot(agg, weight, preferred_element_type=F32)
    gate = 1.0 / (1.0 + jnp.exp(-pre))
    grad_pre = (co.astype(F32) * gate * (1.0 + pre * (1.0 - gate))).astype(BF16)
    return pre, gate, grad_pre


def up_body(w_ref, co_ref, *refs, first):
    place = Place()
    shares, out_ref = refs[:-1], refs[-1]
    weight = w_ref[...]
    rows = shares[0].shape[0]
    for n, share in enumerate(shares):
        at = pl.multiple_of((place.rep ^ (first + n)) * rows, rows)
        _, _, grad_pre = gradient_of(share[...], co_ref[pl.ds(at, rows), :], weight)
        out_ref[n] = lax.dot_general(
            weight, grad_pre, (((1,), (1,)), ((), ())), preferred_element_type=F32
        ).astype(BF16)


def up_shares(weight, cotangent, shares, first):
    rows, width = shares[0].shape
    out = jax.ShapeDtypeStruct((len(shares), width, rows), BF16)
    return call(
        functools.partial(up_body, first=first),
        [weight, cotangent, *shares],
        out,
        estimate=cost(4 * len(shares) * rows * width * width, 2 * MIB),
        name="up_shares",
    )


def finish_body(w_ref, co_ref, *refs):
    place = Place()
    shares, (hidden_ref, grad_ref, agg_all, pre_all) = refs[:-4], refs[-4:]
    weight = w_ref[...]
    rows = shares[0].shape[0]
    for n, share in enumerate(shares):
        at = pl.multiple_of((place.rep ^ n) * rows, rows)
        agg = share[...]
        pre, gate, grad_pre = gradient_of(agg, co_ref[pl.ds(at, rows), :], weight)
        hidden_ref[pl.ds(at, rows), :] = (pre * gate).astype(BF16)
        agg_all[pl.ds(at, rows), :] = agg
        pre_all[pl.ds(at, rows), :] = grad_pre
    grad_ref[...] = lax.dot_general(
        agg_all[...], pre_all[...], (((0,), (0,)), ((), ())), preferred_element_type=F32
    )


def finish(weight, cotangent, shares):
    panel, width = cotangent.shape
    outs = (like(cotangent), jax.ShapeDtypeStruct((width, width), F32))
    return call(
        finish_body,
        [weight, cotangent, *shares],
        outs,
        scratch=[pltpu.VMEM((panel, width), BF16)] * 2,
        estimate=cost(6 * panel * width * width, 8 * panel * width),
        name="finish",
    )


def backward_body(live_ref, entry_ref, tiles_ref, *refs, slots, keep):
    ups, (out_ref, up_all, acc) = refs[:-3], refs[-3:]
    place = Place()
    cuts, chips, pairs, per, width, block = out_ref.shape
    blocks = cuts * chips * per
    bits = (blocks - 1).bit_length()
    count, _, rows = ups[0].shape
    for m, up in enumerate(ups):
        for n in range(count):
            at = pl.multiple_of((place.rep ^ (m * count + n)) * rows, rows)
            up_all[:, pl.ds(at, rows)] = up[n]
    for p in range(pairs):
        acc[...] = jnp.zeros_like(acc)

        def step(first, entries, alive):
            terms = []
            for t in range(GROUP):
                at = pl.multiple_of((entries[t] >> bits) * block, block)
                terms.append(
                    jnp.dot(
                        up_all[:, pl.ds(at, block)],
                        tiles_ref[first + t],
                        preferred_element_type=F32,
                    )
                )
            for t in range(GROUP):
                acc[jnp.where(alive[t], entries[t] & (blocks - 1), blocks)] += terms[t]

        core = place.core
        walk(live_ref, entry_ref, 2 * p + (core if keep else 1 - core), slots, step)
        for h in range(cuts):
            for d in range(chips):
                at = ((place.chip ^ d) * cuts + h) * per
                out_ref[h, d, p] = acc[pl.ds(at, per)].astype(out_ref.dtype)


def backward(plan, tiles, ups, pairs, chips, cuts, keep):
    block = tiles.shape[1]
    count, width, rows = ups[0].shape
    panel = len(ups) * count * rows
    blocks = panel // block
    shape = (cuts, chips, pairs, blocks // chips // cuts, width, block)
    return call(
        functools.partial(backward_body, slots=plan[1].shape[1], keep=keep),
        [tiles, *ups],
        jax.ShapeDtypeStruct(shape, F32 if keep else BF16),
        scalars=plan,
        scratch=[pltpu.VMEM((width, panel), BF16), pltpu.VMEM((blocks + 1, width, block), F32)],
        vmem=(0,),
        estimate=cost(2 * 64 * block * block * width, 12 * MIB),
        name="backward",
    )


def join_body(kept_ref, given_ref, *outs):
    cuts, chips = kept_ref.shape[:2]
    for h in range(cuts):
        for d in range(chips):
            out = outs[h * chips + d]
            out[...] = (kept_ref[h, d] + given_ref[h, d].astype(F32)).astype(out.dtype)


def join(kept, given):
    cuts, chips = kept.shape[:2]
    outs = [
        jax.ShapeDtypeStruct(kept.shape[2:], BF16 if d else F32)
        for _ in range(cuts)
        for d in range(chips)
    ]
    got = call(join_body, [kept, given], outs, name="join")
    return [got[h * chips : (h + 1) * chips] for h in range(cuts)]


def gather_body(*refs, count):
    terms = [ref[...].astype(F32) for ref in refs[:count]]
    refs[-1][...] = tree_sum(terms).astype(BF16)


def gather_sum(terms, after):
    return call(
        functools.partial(gather_body, count=len(terms)),
        [*terms, *after],
        like(terms[0], BF16),
        name="gather_sum",
    )


def route_body(*refs, reps, chips):
    spread, outs = refs[:reps], refs[reps:]
    place = Place()
    for k in range(chips):
        u = place.chip ^ k
        for d in range(reps):

            @pl.when(((u % reps) ^ place.rep) == d)
            def _():
                outs[k][...] = spread[d][u // reps]


def route(spread, chips):
    outs = [jax.ShapeDtypeStruct(spread[0].shape[1:], BF16)] * chips
    body = functools.partial(route_body, reps=len(spread), chips=chips)
    return call(body, spread, outs, name="route")


def restore_body(ids_ref, order_ref, *refs, count):
    parts, out_ref = refs[:count], refs[-1]
    rows = out_ref.shape[0]
    per, _, block = parts[0].shape
    base = pl.program_id(0) * rows
    acc = refs[count][...] if len(refs) > count + 1 else None
    for n, part in enumerate(parts):
        length = per * block
        at = pl.multiple_of(ids_ref[n] * length, length)
        target = order_ref[:, pl.ds(at, length)]
        hot = lax.broadcasted_iota(jnp.int32, (rows, length), 0) + base == target
        hot = jnp.where(hot, 1.0, 0.0).astype(BF16)
        columns = jnp.concatenate([part[b] for b in range(per)], axis=1)
        term = lax.dot_general(
            hot, columns, (((1,), (1,)), ((), ())), preferred_element_type=F32
        )
        acc = term if acc is None else acc + term
    out_ref[...] = acc.astype(out_ref.dtype)


def restore(ids, order_row, parts, start, dtype):
    panel = order_row.shape[1]
    width = parts[0].shape[1]
    rows = 512
    row_spec = pl.BlockSpec((rows, width), lambda i, ids: (i, 0))
    extra = () if start is None else (start,)
    return pl.pallas_call(
        functools.partial(restore_body, count=len(parts)),
        out_shape=jax.ShapeDtypeStruct((panel, width), dtype),
        grid_spec=pltpu.PrefetchScalarGridSpec(
            num_scalar_prefetch=1,
            grid=(panel // rows,),
            in_specs=[whole_spec(order_row)]
            + [whole_spec(p) for p in parts]
            + [row_spec for _ in extra],
            out_specs=row_spec,
        ),
        compiler_params=params(24),
        cost_estimate=cost(2 * panel * panel * width, 4 * panel * width),
        name="restore",
    )(ids, order_row, *parts, *extra)


def tree_sum(terms):
    while len(terms) > 1:
        terms = [terms[i] + terms[i + 1] for i in range(0, len(terms), 2)]
    return terms[0]


def shards(features, order, tiles, tile_rows, tile_cols, live, weight, cotangent):
    reps = lax.axis_size("rep")
    sections = lax.axis_size("section")
    section = lax.axis_index("section")
    panel, width = features.shape
    rounds, slots, block, _ = tiles.shape[2:]
    blocks = panel // block
    chips = sections // 2
    pairs = rounds // 2
    near = reps // 2

    def over_chips(x, d):
        return lax.ppermute(x, "section", [(s, s ^ (2 * d)) for s in range(sections)])

    def over_cores(x):
        return lax.ppermute(x, "section", [(s, s ^ 1) for s in range(sections)])

    def over_reps(x, d):
        return lax.ppermute(x, "rep", [(r, r ^ d) for r in range(reps)])

    def from_owner(x, d):
        moves = []
        for r in range(reps):
            for j in range(rounds):
                source = j * reps + r
                target = (source ^ (2 * d)) ^ ((d // near) & 1)
                moves.append((source * reps + r, target * reps + r))
        return lax.ppermute(x, ("section", "rep"), moves)

    order_col = order.reshape(panel, 1)
    owns = reorder(order_col, features)
    gots = [[own] + [from_owner(own, d) for d in range(1, chips)] for own in owns]
    bits = (blocks - 1).bit_length()
    plan = (live.reshape(rounds), entries_of(tile_rows, tile_cols, bits, owns[-1][:16]))
    own_tiles = tiles.reshape(rounds * slots, block, block)

    mine, mate = [], []
    for p in range(pairs):
        for h in range(HALVES):
            picked = pick(gots[h][2 * p * near : 2 * (p + 1) * near], near)
            mine.append(picked)
            mate.append(over_cores(picked))

    started = forward(plan, own_tiles, mine, None, reps)
    own, *others = forward(plan, own_tiles, mate, started, reps)
    sent = {d: over_reps(others[d - 1], d) for d in reversed(range(1, reps))}
    aggregated = total_of(own, [sent[d] for d in range(1, reps)])
    shares = [aggregated] + [over_reps(aggregated, d) for d in range(1, reps)]

    ups = [
        up_shares(weight, cotangent, shares[:near], 0),
        up_shares(weight, cotangent, shares[near:], near),
    ]
    cuts = math.gcd(2, blocks // chips)
    given = over_cores(backward(plan, own_tiles, ups, pairs, chips, cuts, False))
    kept = backward(plan, own_tiles, ups, pairs, chips, cuts, True)
    chunks = join(kept, given)
    arrived = [[over_chips(c[d], d) for d in range(1, chips)] for c in chunks]
    late_shares = lax.optimization_barrier((shares, chunks[-1][-1]))[0]
    hidden, grad_part = finish(weight, cotangent, late_shares)
    reduced = [
        gather_sum([c[0], *a], [grad_part] if h == 0 else [])
        for h, (c, a) in enumerate(zip(chunks, arrived, strict=True))
    ]

    def to_owner(block, k):
        moves = []
        for s in range(sections):
            u = (s // 2) ^ k
            moves.append((s, (2 * (u // reps) + s % 2) * reps + u % reps))
        return lax.ppermute(block, "section", moves)

    mine_u = (section // reps // 2) * reps + section % reps
    order_row = order.reshape(1, panel)
    feature_grad = None
    for h in range(cuts):
        spread = [reduced[h]] + [over_reps(reduced[h], d) for d in range(1, reps)]
        parts = [to_owner(block, k) for k, block in enumerate(route(spread, chips))]
        ids = jnp.stack([(mine_u ^ k) * cuts + h for k in range(chips)]).astype(jnp.int32)
        kind = BF16 if h == cuts - 1 else F32
        feature_grad = restore(ids, order_row, parts, feature_grad, kind)

    grad_part = grad_part + over_cores(grad_part)
    weight_grad = tree_sum([grad_part] + [over_chips(grad_part, d) for d in range(1, chips)])
    weight_grad = weight_grad * (1.0 / math.sqrt(panel * sections))
    return (hidden, weight_grad, feature_grad)


def solution(mesh):
    placed = (
        P("section", None),
        P("section"),
        P("section", "rep", None, None, None, None),
        P("section", "rep", None, None),
        P("section", "rep", None, None),
        P("section", "rep", None),
        P(),
        P("section", None),
    )
    return jax.shard_map(
        shards,
        mesh=mesh,
        in_specs=placed,
        out_specs=(P("section", None), P(), P("section", None)),
        check_vma=False,
    )
```

time: 120 us -> 106 us (0.88); the launches traced: 119 us -> 107 us
  starting transfers between devices: 42.8 us -> 56 us
  Pallas kernels: 25.3 us -> 16.4 us
  local copies, waits for them, and re-layouts: 9.87 us -> 2.15 us
  waiting for transfers between devices: 35.8 us -> 30.3 us
  other arithmetic: 3.91 us -> 0.81 us
    ppermute x6 -> x9, waiting for transfers between devices: 7.84 us -> 0.02 us  [over_chips(): return lax.ppermute(x, 'section', [(s, s ^ 2 * d) for s in range(sections)])]
    ppermute x4 -> x8, starting transfers between devices: 6.65 us -> 14.2 us  [to_owner(): return lax.ppermute(block, 'section', moves)]
    unnamed x20 -> x16, local copies, waits for them, and re-layouts: 7.31 us -> 1.07 us
    ppermute x9 -> x12, starting transfers between devices: 14.3 us -> 20.3 us  [over_reps(): return lax.ppermute(x, 'rep', [(r, r ^ d) for r in range(reps)])]
    ppermute x6, waiting for transfers between devices: 0.02 us -> 5.3 us  [from_owner(): return lax.ppermute(x, ('section', 'rep'), moves)]
    pallas_call x2 -> x0, Pallas kernels: 4.65 us -> none  [reorder(): pl.pallas_call(reorder_body, out_shape=jax.ShapeDtypeStruct((rows, width)...]
    ppermute x4 -> x8, waiting for transfers between devices: 5.93 us -> 1.65 us  [to_owner(): return lax.ppermute(block, 'section', moves)]
    pallas_call x11 -> x17, Pallas kernels: 15.1 us -> 10.8 us  [call(): pl.pallas_call(body, out_shape=outs, grid_spec=pltpu.PrefetchScalarGridSp...]
  transfers between devices with their start and end apart: 29 -> 39, of which waited for: 11 -> 13; matrix products, arithmetic and copies ran while one was open for 3% -> 1% of each run, Pallas kernels for 13% -> 7%
where the time goes in v4:
time: 106 us; the launch traced here: 107 us
  starting transfers between devices  56 us (53%)
  waiting for transfers between devices  30.3 us (29%)
  Pallas kernels  16.4 us (15%)
  local copies, waits for them, and re-layouts  2.15 us (2%)
  between operations  1.09 us (1%)
    ppermute x12, waiting for transfers between devices, over_reps(): return lax.ppermute(x, 'rep', [(r, r ^ d) for r in range(reps)])  22.8 us
    ppermute x12, starting transfers between devices, over_reps(): return lax.ppermute(x, 'rep', [(r, r ^ d) for r in range(reps)])  20.3 us
    ppermute x8, starting transfers between devices, to_owner(): return lax.ppermute(block, 'section', moves)  14.2 us
    ppermute x6, starting transfers between devices, from_owner(): return lax.ppermute(x, ('section', 'rep'), moves)  11.4 us
    pallas_call x17, Pallas kernels, call(): pl.pallas_call(body, out_shape=outs, grid_spec=pltpu.PrefetchScalarGridSp...  10.8 us
    ppermute x9, starting transfers between devices, over_chips(): return lax.ppermute(x, 'section', [(s, s ^ 2 * d) for s in range(sections)])  9.64 us
    pallas_call x2, Pallas kernels, restore(): pl.pallas_call(functools.partial(restore_body, count=len(parts)), out_sha...  5.53 us
    ppermute x6, waiting for transfers between devices, from_owner(): return lax.ppermute(x, ('section', 'rep'), moves)  5.3 us
  transfers between devices with their start and end apart: 39, of which 13 were waited for; matrix products, arithmetic and copies ran while one was open for 1% of the time, Pallas kernels for 7%

profile of v4, /device:TPU:0, one launch (start us, length us, event | category | flops | bytes accessed | tf_op | source)
XLA Modules:
  0.0 106.8 jit_solution(15951945911583769354)
XLA Ops:
  2.8 2.4 %reorder.1 = (bf16[1024,128]{1,0:T(8,128)(2,1)S(1)}, bf16[1024,128]{1,0:T(8,128)(2,1)S(1)}) custom-call(s32[2048,1]{1,0:T(8,128)S(1)} %copy.11.order_ref, bf16[2048,128]{1,0:T(8,128)(2,1)S(1)} %copy-done.7), custom_call_target="tpu_custom_call" | custom-call | flops 1073741824 | bytes 1048576 | tf_op jit(solution)/shard_map/reorder/pallas_call | solution.py:55
  5.2 4.9 %collective-permute-start.4 = (bf16[1024,128]{1,0:T(8,128)(2,1)S(1)}, bf16[1024,128]{1,0:T(8,128)(2,1)S(1)}, u32[]{:S(2)}, u32[]{:S(2)}) collective-permute-start(bf16[1024,128]{1,0:T(8,128)(2,1)S(1)} %get-tuple-element.31.refs_0_), channel_id=1, source_target_pairs={{0,8},{16,24},{5,13},{21,29},{10,2},{26,18},{15,7},{31,23}} | collective-permute-start | bytes 786440 | tf_op jit(solution)/shard_map/ppermute | solution.py:453
  17.1 2.4 %collective-permute-done.refs_1_ = bf16[1024,128]{1,0:T(8,128)(2,1)S(1)} collective-permute-done((bf16[1024,128]{1,0:T(8,128)(2,1)S(1)}, bf16[1024,128]{1,0:T(8,128)(2,1)S(1)}, u32[]{:S(2)}, u32[]{:S(2)}) %collective-permute-start) | collective-permute-done | bytes 262176 | tf_op jit(solution)/shard_map/ppermute | solution.py:453
  19.5 2.8 %collective-permute-done.2.refs_3_ = bf16[1024,128]{1,0:T(8,128)(2,1)S(1)} collective-permute-done((bf16[1024,128]{1,0:T(8,128)(2,1)S(1)}, bf16[1024,128]{1,0:T(8,128)(2,1)S(1)}, u32[]{:S(2)}, u32[]{:S(2)}) %collective-permute-start.2) | collective-permute-done | bytes 262176 | tf_op jit(solution)/shard_map/ppermute | solution.py:453
  25.3 5.1 %collective-permute-start.10 = (bf16[512,128]{1,0:T(8,128)(2,1)S(1)}, bf16[512,128]{1,0:T(8,128)(2,1)S(1)}, u32[]{:S(2)}, u32[]{:S(2)}) collective-permute-start(bf16[512,128]{1,0:T(8,128)(2,1)S(1)} %get-tuple-element.36), channel_id=1, source_target_pairs={{0,3},{1,2},{2,1},{3,0},{4,7},{5,6},{6,5},{7,4},{8,11},{9,10},{10,... | collective-permute-start | bytes 393224 | tf_op jit(solution)/shard_map/ppermute | solution.py:444
  31.1 3.6 %collective-permute-done.10.refs_2_ = bf16[512,128]{1,0:T(8,128)(2,1)S(1)} collective-permute-done((bf16[512,128]{1,0:T(8,128)(2,1)S(1)}, bf16[512,128]{1,0:T(8,128)(2,1)S(1)}, u32[]{:S(2)}, u32[]{:S(2)}) %collective-permute-start.10) | collective-permute-done | bytes 131104 | tf_op jit(solution)/shard_map/ppermute | solution.py:444
  34.7 3.9 %collective-permute-done.8.refs_0_ = bf16[512,128]{1,0:T(8,128)(2,1)S(1)} collective-permute-done((bf16[512,128]{1,0:T(8,128)(2,1)S(1)}, bf16[512,128]{1,0:T(8,128)(2,1)S(1)}, u32[]{:S(2)}, u32[]{:S(2)}) %collective-permute-start.8) | collective-permute-done | bytes 131104 | tf_op jit(solution)/shard_map/ppermute | solution.py:444
  38.6 3.8 %collective-permute-done.9.refs_1_ = bf16[512,128]{1,0:T(8,128)(2,1)S(1)} collective-permute-done((bf16[512,128]{1,0:T(8,128)(2,1)S(1)}, bf16[512,128]{1,0:T(8,128)(2,1)S(1)}, u32[]{:S(2)}, u32[]{:S(2)}) %collective-permute-start.9) | collective-permute-done | bytes 131104 | tf_op jit(solution)/shard_map/ppermute | solution.py:444
  42.5 3.2 %collective-permute-start.12 = (bf16[512,128]{1,0:T(8,128)(2,1)S(1)}, bf16[512,128]{1,0:T(8,128)(2,1)S(1)}, u32[]{:S(2)}, u32[]{:S(2)}) collective-permute-start(bf16[512,128]{1,0:T(8,128)(2,1)S(1)} %total_of.1.refs_0_), channel_id=1, source_target_pairs={{0,2},{1,3},{2,0},{3,1},{4,6},{5,7},{6,4},{7,5},{8,10},{9,11},{10,... | collective-permute-start | bytes 393224 | tf_op jit(solution)/shard_map/ppermute | solution.py:444
  46.9 2.1 %collective-permute-done.11.refs_1_ = bf16[512,128]{1,0:T(8,128)(2,1)S(1)} collective-permute-done((bf16[512,128]{1,0:T(8,128)(2,1)S(1)}, bf16[512,128]{1,0:T(8,128)(2,1)S(1)}, u32[]{:S(2)}, u32[]{:S(2)}) %collective-permute-start.11) | collective-permute-done | bytes 131104 | tf_op jit(solution)/shard_map/ppermute | solution.py:444
  49.5 6.0 %collective-permute-done.12.refs_0_.refs_2_ = bf16[512,128]{1,0:T(8,128)(2,1)S(1)} collective-permute-done((bf16[512,128]{1,0:T(8,128)(2,1)S(1)}, bf16[512,128]{1,0:T(8,128)(2,1)S(1)}, u32[]{:S(2)}, u32[]{:S(2)}) %collective-permute-start.12) | collective-permute-done | bytes 131104 | tf_op jit(solution)/shard_map/ppermute | solution.py:444
  61.0 2.0 %collective-permute-start.31 = (bf16[1,2,128,128]{3,2,1,0:T(8,128)(2,1)S(1)}, bf16[1,2,128,128]{3,2,1,0:T(8,128)(2,1)S(1)}, u32[]{:S(2)}, u32[]{:S(2)}) collective-permute-start(bf16[1,2,128,128]{3,2,1,0:T(8,128)(2,1)S(1)} %get-tuple-element.54), channel_id=1, source_target_pairs={{0,24},{4,28},{8,16},{12,20},{16,8},{20,12},{24,0},{28,4},{1,25},{... | collective-permute-start | bytes 196616 | tf_op jit(solution)/shard_map/ppermute | solution.py:438
  64.5 2.0 %collective-permute-start.21 = (bf16[1,2,128,128]{3,2,1,0:T(8,128)(2,1)S(1)}, bf16[1,2,128,128]{3,2,1,0:T(8,128)(2,1)S(1)}, u32[]{:S(2)}, u32[]{:S(2)}) collective-permute-start(bf16[1,2,128,128]{3,2,1,0:T(8,128)(2,1)S(1)} %get-tuple-element.37), channel_id=1, source_target_pairs={{0,24},{4,28},{8,16},{12,20},{16,8},{20,12},{24,0},{28,4},{1,25},{... | collective-permute-start | bytes 196616 | tf_op jit(solution)/shard_map/ppermute | solution.py:438
  68.1 1.7 %collective-permute-start.32 = (bf16[1,2,128,128]{3,2,1,0:T(8,128)(2,1)S(1)}, bf16[1,2,128,128]{3,2,1,0:T(8,128)(2,1)S(1)}, u32[]{:S(2)}, u32[]{:S(2)}) collective-permute-start(bf16[1,2,128,128]{3,2,1,0:T(8,128)(2,1)S(1)} %gather_sum.3.refs_0_), channel_id=1, source_target_pairs={{0,1},{1,0},{2,3},{3,2},{4,5},{5,4},{6,7},{7,6},{8,9},{9,8},{10,11... | collective-permute-start | bytes 196616 | tf_op jit(solution)/shard_map/ppermute | solution.py:444
  69.8 2.4 %collective-permute-start.33 = (bf16[1,2,128,128]{3,2,1,0:T(8,128)(2,1)S(1)}, bf16[1,2,128,128]{3,2,1,0:T(8,128)(2,1)S(1)}, u32[]{:S(2)}, u32[]{:S(2)}) collective-permute-start(bf16[1,2,128,128]{3,2,1,0:T(8,128)(2,1)S(1)} %gather_sum.3.refs_0_), channel_id=1, source_target_pairs={{0,2},{1,3},{2,0},{3,1},{4,6},{5,7},{6,4},{7,5},{8,10},{9,11},{10,... | collective-permute-start | bytes 196616 | tf_op jit(solution)/shard_map/ppermute | solution.py:444
  74.3 2.4 %collective-permute-start.23 = (bf16[1,2,128,128]{3,2,1,0:T(8,128)(2,1)S(1)}, bf16[1,2,128,128]{3,2,1,0:T(8,128)(2,1)S(1)}, u32[]{:S(2)}, u32[]{:S(2)}) collective-permute-start(bf16[1,2,128,128]{3,2,1,0:T(8,128)(2,1)S(1)} %gather_sum.2.refs_0_), channel_id=1, source_target_pairs={{0,2},{1,3},{2,0},{3,1},{4,6},{5,7},{6,4},{7,5},{8,10},{9,11},{10,... | collective-permute-start | bytes 196616 | tf_op jit(solution)/shard_map/ppermute | solution.py:444
  79.3 1.6 %collective-permute-start.17 = (f32[128,128]{1,0:T(8,128)S(1)}, f32[128,128]{1,0:T(8,128)S(1)}, u32[]{:S(2)}, u32[]{:S(2)}) collective-permute-start(f32[128,128]{1,0:T(8,128)S(1)} %add.33), channel_id=1, source_target_pairs={{0,16},{4,20},{8,24},{12,28},{16,0},{20,4},{24,8},{28,12},{1,17},{... | collective-permute-start | bytes 196616 | tf_op jit(solution)/shard_map/ppermute | solution.py:438
  82.0 2.6 %collective-permute-done.23.refs_2_ = bf16[1,2,128,128]{3,2,1,0:T(8,128)(2,1)S(1)} collective-permute-done((bf16[1,2,128,128]{3,2,1,0:T(8,128)(2,1)S(1)}, bf16[1,2,128,128]{3,2,1,0:T(8,128)(2,1)S(1)}, u32[]{:S(2)}, u32[]{:S(2)}) %collective-permute-start.23) | collective-permute-done | bytes 65568 | tf_op jit(solution)/shard_map/ppermute | solution.py:444
  88.0 3.4 %collective-permute-start.38 = (bf16[2,128,128]{2,1,0:T(8,128)(2,1)S(1)}, bf16[2,128,128]{2,1,0:T(8,128)(2,1)S(1)}, u32[]{:S(2)}, u32[]{:S(2)}) collective-permute-start(bf16[2,128,128]{2,1,0:T(8,128)(2,1)S(1)} %get-tuple-element.58), channel_id=1, source_target_pairs={{0,12},{4,28},{8,8},{12,24},{16,4},{20,20},{24,0},{28,16},{1,13},{... | collective-permute-start | bytes 196616 | tf_op jit(solution)/shard_map/ppermute | solution.py:496
  92.7 3.0 %collective-permute-start.26 = (bf16[2,128,128]{2,1,0:T(8,128)(2,1)S(1)}, bf16[2,128,128]{2,1,0:T(8,128)(2,1)S(1)}, u32[]{:S(2)}, u32[]{:S(2)}) collective-permute-start(bf16[2,128,128]{2,1,0:T(8,128)(2,1)S(1)} %get-tuple-element.48), channel_id=1, source_target_pairs={{0,4},{4,20},{8,0},{12,16},{16,12},{20,28},{24,8},{28,24},{1,5},{5... | collective-permute-start | bytes 196616 | tf_op jit(solution)/shard_map/ppermute | solution.py:496
  95.9 3.6 %collective-permute-start.28 = (bf16[2,128,128]{2,1,0:T(8,128)(2,1)S(1)}, bf16[2,128,128]{2,1,0:T(8,128)(2,1)S(1)}, u32[]{:S(2)}, u32[]{:S(2)}) collective-permute-start(bf16[2,128,128]{2,1,0:T(8,128)(2,1)S(1)} %get-tuple-element.50), channel_id=1, source_target_pairs={{0,12},{4,28},{8,8},{12,24},{16,4},{20,20},{24,0},{28,16},{1,13},{... | collective-permute-start | bytes 196616 | tf_op jit(solution)/shard_map/ppermute | solution.py:496
  99.6 2.3 %restore.2.refs_4_ = f32[2048,128]{1,0:T(8,128)S(1)} custom-call(s32[4]{0:T(128)S(1)} %pad_add_fusion.1.ids_ref, s32[1,2048]{1,0:T(1,128)S(1)} %bitcast.17, bf16[2,128,128]{2,1,0:T(8,128)(2,1)S(1)} %collective-permute-done.35.refs_0_, bf16[2,128,128]{2,1,0:T(8,128)(2,1)S(1)} %collective-permute-done.36.refs_1_, ...), custom_call_target="tpu_custom_call" | custom-call | flops 1073741824 | bytes 1048576 | tf_op jit(solution)/shard_map/restore/pallas_call | solution.py:403
  101.9 1.6 %collective-permute-done.28.refs_3_ = bf16[2,128,128]{2,1,0:T(8,128)(2,1)S(1)} collective-permute-done((bf16[2,128,128]{2,1,0:T(8,128)(2,1)S(1)}, bf16[2,128,128]{2,1,0:T(8,128)(2,1)S(1)}, u32[]{:S(2)}, u32[]{:S(2)}) %collective-permute-start.28) | collective-permute-done | bytes 65568 | tf_op jit(solution)/shard_map/ppermute | solution.py:496
  103.6 3.2 %restore.3 = bf16[2048,128]{1,0:T(8,128)(2,1)} custom-call(s32[4]{0:T(128)S(1)} %pad_add_fusion.ids_ref, s32[1,2048]{1,0:T(1,128)S(1)} %bitcast.18, bf16[2,128,128]{2,1,0:T(8,128)(2,1)S(1)} %collective-permute-done.25.refs_0_, bf16[2,128,128]{2,1,0:T(8,128)(2,1)S(1)} %collective-permute-done.26.refs_1_, ...), custom_call_target="tpu_custom_call" | custom-call | flops 1073741824 | bytes 1048576 | tf_op jit(solution)/shard_map/restore/pallas_call | solution.py:403
  (95 shorter events, 33.7 us)
Async XLA Ops:
  5.2 10.1 %collective-permute-start.4 = (bf16[1024,128]{1,0:T(8,128)(2,1)S(1)}, bf16[1024,128]{1,0:T(8,128)(2,1)S(1)}, u32[]{:S(2)}, u32[]{:S(2)}) collective-permute-start(bf16[1024,128]{1,0:T(8,128)(2,1)S(1)} %get-tuple-element.31.refs_0_), channel_id=1, source_target_pairs={{0,8},{16,24},{5,13},{21,29},{10,2},{26,18},{15,7},{31,23}} | collective-permute-start | bytes 786440 | tf_op jit(solution)/shard_map/ppermute | solution.py:453
  25.3 9.4 %collective-permute-start.10 = (bf16[512,128]{1,0:T(8,128)(2,1)S(1)}, bf16[512,128]{1,0:T(8,128)(2,1)S(1)}, u32[]{:S(2)}, u32[]{:S(2)}) collective-permute-start(bf16[512,128]{1,0:T(8,128)(2,1)S(1)} %get-tuple-element.36), channel_id=1, source_target_pairs={{0,3},{1,2},{2,1},{3,0},{4,7},{5,6},{6,5},{7,4},{8,11},{9,10},{10,... | collective-permute-start | bytes 393224 | tf_op jit(solution)/shard_map/ppermute | solution.py:444
  30.4 8.2 %collective-permute-start.8 = (bf16[512,128]{1,0:T(8,128)(2,1)S(1)}, bf16[512,128]{1,0:T(8,128)(2,1)S(1)}, u32[]{:S(2)}, u32[]{:S(2)}) collective-permute-start(bf16[512,128]{1,0:T(8,128)(2,1)S(1)} %get-tuple-element.34), channel_id=1, source_target_pairs={{0,1},{1,0},{2,3},{3,2},{4,5},{5,4},{6,7},{7,6},{8,9},{9,8},{10,11... | collective-permute-start | bytes 393224 | tf_op jit(solution)/shard_map/ppermute | solution.py:444
  31.1 11.3 %collective-permute-start.9 = (bf16[512,128]{1,0:T(8,128)(2,1)S(1)}, bf16[512,128]{1,0:T(8,128)(2,1)S(1)}, u32[]{:S(2)}, u32[]{:S(2)}) collective-permute-start(bf16[512,128]{1,0:T(8,128)(2,1)S(1)} %get-tuple-element.35), channel_id=1, source_target_pairs={{0,2},{1,3},{2,0},{3,1},{4,6},{5,7},{6,4},{7,5},{8,10},{9,11},{10,... | collective-permute-start | bytes 393224 | tf_op jit(solution)/shard_map/ppermute | solution.py:444
  42.5 13.0 %collective-permute-start.12 = (bf16[512,128]{1,0:T(8,128)(2,1)S(1)}, bf16[512,128]{1,0:T(8,128)(2,1)S(1)}, u32[]{:S(2)}, u32[]{:S(2)}) collective-permute-start(bf16[512,128]{1,0:T(8,128)(2,1)S(1)} %total_of.1.refs_0_), channel_id=1, source_target_pairs={{0,2},{1,3},{2,0},{3,1},{4,6},{5,7},{6,4},{7,5},{8,10},{9,11},{10,... | collective-permute-start | bytes 393224 | tf_op jit(solution)/shard_map/ppermute | solution.py:444
  45.7 9.8 %collective-permute-start.13 = (bf16[512,128]{1,0:T(8,128)(2,1)S(1)}, bf16[512,128]{1,0:T(8,128)(2,1)S(1)}, u32[]{:S(2)}, u32[]{:S(2)}) collective-permute-start(bf16[512,128]{1,0:T(8,128)(2,1)S(1)} %total_of.1.refs_0_), channel_id=1, source_target_pairs={{0,3},{1,2},{2,1},{3,0},{4,7},{5,6},{6,5},{7,4},{8,11},{9,10},{10,... | collective-permute-start | bytes 393224 | tf_op jit(solution)/shard_map/ppermute | solution.py:444
  59.6 8.5 %collective-permute-start.30 = (bf16[1,2,128,128]{3,2,1,0:T(8,128)(2,1)S(1)}, bf16[1,2,128,128]{3,2,1,0:T(8,128)(2,1)S(1)}, u32[]{:S(2)}, u32[]{:S(2)}) collective-permute-start(bf16[1,2,128,128]{3,2,1,0:T(8,128)(2,1)S(1)} %get-tuple-element.53), channel_id=1, source_target_pairs={{0,16},{4,20},{8,24},{12,28},{16,0},{20,4},{24,8},{28,12},{1,17},{... | collective-permute-start | bytes 196616 | tf_op jit(solution)/shard_map/ppermute | solution.py:438
  63.1 9.1 %collective-permute-start.20 = (bf16[1,2,128,128]{3,2,1,0:T(8,128)(2,1)S(1)}, bf16[1,2,128,128]{3,2,1,0:T(8,128)(2,1)S(1)}, u32[]{:S(2)}, u32[]{:S(2)}) collective-permute-start(bf16[1,2,128,128]{3,2,1,0:T(8,128)(2,1)S(1)} %get-tuple-element.46), channel_id=1, source_target_pairs={{0,16},{4,20},{8,24},{12,28},{16,0},{20,4},{24,8},{28,12},{1,17},{... | collective-permute-start | bytes 196616 | tf_op jit(solution)/shard_map/ppermute | solution.py:438
  64.5 9.2 %collective-permute-start.21 = (bf16[1,2,128,128]{3,2,1,0:T(8,128)(2,1)S(1)}, bf16[1,2,128,128]{3,2,1,0:T(8,128)(2,1)S(1)}, u32[]{:S(2)}, u32[]{:S(2)}) collective-permute-start(bf16[1,2,128,128]{3,2,1,0:T(8,128)(2,1)S(1)} %get-tuple-element.37), channel_id=1, source_target_pairs={{0,24},{4,28},{8,16},{12,20},{16,8},{20,12},{24,0},{28,4},{1,25},{... | collective-permute-start | bytes 196616 | tf_op jit(solution)/shard_map/ppermute | solution.py:438
  68.1 8.7 %collective-permute-start.32 = (bf16[1,2,128,128]{3,2,1,0:T(8,128)(2,1)S(1)}, bf16[1,2,128,128]{3,2,1,0:T(8,128)(2,1)S(1)}, u32[]{:S(2)}, u32[]{:S(2)}) collective-permute-start(bf16[1,2,128,128]{3,2,1,0:T(8,128)(2,1)S(1)} %gather_sum.3.refs_0_), channel_id=1, source_target_pairs={{0,1},{1,0},{2,3},{3,2},{4,5},{5,4},{6,7},{7,6},{8,9},{9,8},{10,11... | collective-permute-start | bytes 196616 | tf_op jit(solution)/shard_map/ppermute | solution.py:444
  69.8 8.5 %collective-permute-start.33 = (bf16[1,2,128,128]{3,2,1,0:T(8,128)(2,1)S(1)}, bf16[1,2,128,128]{3,2,1,0:T(8,128)(2,1)S(1)}, u32[]{:S(2)}, u32[]{:S(2)}) collective-permute-start(bf16[1,2,128,128]{3,2,1,0:T(8,128)(2,1)S(1)} %gather_sum.3.refs_0_), channel_id=1, source_target_pairs={{0,2},{1,3},{2,0},{3,1},{4,6},{5,7},{6,4},{7,5},{8,10},{9,11},{10,... | collective-permute-start | bytes 196616 | tf_op jit(solution)/shard_map/ppermute | solution.py:444
  73.7 7.2 %collective-permute-start.22 = (bf16[1,2,128,128]{3,2,1,0:T(8,128)(2,1)S(1)}, bf16[1,2,128,128]{3,2,1,0:T(8,128)(2,1)S(1)}, u32[]{:S(2)}, u32[]{:S(2)}) collective-permute-start(bf16[1,2,128,128]{3,2,1,0:T(8,128)(2,1)S(1)} %gather_sum.2.refs_0_), channel_id=1, source_target_pairs={{0,1},{1,0},{2,3},{3,2},{4,5},{5,4},{6,7},{7,6},{8,9},{9,8},{10,11... | collective-permute-start | bytes 196616 | tf_op jit(solution)/shard_map/ppermute | solution.py:444
  74.3 10.2 %collective-permute-start.23 = (bf16[1,2,128,128]{3,2,1,0:T(8,128)(2,1)S(1)}, bf16[1,2,128,128]{3,2,1,0:T(8,128)(2,1)S(1)}, u32[]{:S(2)}, u32[]{:S(2)}) collective-permute-start(bf16[1,2,128,128]{3,2,1,0:T(8,128)(2,1)S(1)} %gather_sum.2.refs_0_), channel_id=1, source_target_pairs={{0,2},{1,3},{2,0},{3,1},{4,6},{5,7},{6,4},{7,5},{8,10},{9,11},{10,... | collective-permute-start | bytes 196616 | tf_op jit(solution)/shard_map/ppermute | solution.py:444
  76.8 8.4 %collective-permute-start.24 = (bf16[1,2,128,128]{3,2,1,0:T(8,128)(2,1)S(1)}, bf16[1,2,128,128]{3,2,1,0:T(8,128)(2,1)S(1)}, u32[]{:S(2)}, u32[]{:S(2)}) collective-permute-start(bf16[1,2,128,128]{3,2,1,0:T(8,128)(2,1)S(1)} %gather_sum.2.refs_0_), channel_id=1, source_target_pairs={{0,3},{1,2},{2,1},{3,0},{4,7},{5,6},{6,5},{7,4},{8,11},{9,10},{10,... | collective-permute-start | bytes 196616 | tf_op jit(solution)/shard_map/ppermute | solution.py:444
  78.3 8.4 %collective-permute-start.16 = (f32[128,128]{1,0:T(8,128)S(1)}, f32[128,128]{1,0:T(8,128)S(1)}, u32[]{:S(2)}, u32[]{:S(2)}) collective-permute-start(f32[128,128]{1,0:T(8,128)S(1)} %add.33), channel_id=1, source_target_pairs={{0,8},{4,12},{8,0},{12,4},{16,24},{20,28},{24,16},{28,20},{1,9},{5... | collective-permute-start | bytes 196616 | tf_op jit(solution)/shard_map/ppermute | solution.py:438
  79.3 8.7 %collective-permute-start.17 = (f32[128,128]{1,0:T(8,128)S(1)}, f32[128,128]{1,0:T(8,128)S(1)}, u32[]{:S(2)}, u32[]{:S(2)}) collective-permute-start(f32[128,128]{1,0:T(8,128)S(1)} %add.33), channel_id=1, source_target_pairs={{0,16},{4,20},{8,24},{12,28},{16,0},{20,4},{24,8},{28,12},{1,17},{... | collective-permute-start | bytes 196616 | tf_op jit(solution)/shard_map/ppermute | solution.py:438
  80.9 10.5 %collective-permute-start.18 = (f32[128,128]{1,0:T(8,128)S(1)}, f32[128,128]{1,0:T(8,128)S(1)}, u32[]{:S(2)}, u32[]{:S(2)}) collective-permute-start(f32[128,128]{1,0:T(8,128)S(1)} %add.33), channel_id=1, source_target_pairs={{0,24},{4,28},{8,16},{12,20},{16,8},{20,12},{24,0},{28,4},{1,25},{... | collective-permute-start | bytes 196616 | tf_op jit(solution)/shard_map/ppermute | solution.py:438
  84.6 8.1 %collective-permute-start.35 = (bf16[2,128,128]{2,1,0:T(8,128)(2,1)S(1)}, bf16[2,128,128]{2,1,0:T(8,128)(2,1)S(1)}, u32[]{:S(2)}, u32[]{:S(2)}) collective-permute-start(bf16[2,128,128]{2,1,0:T(8,128)(2,1)S(1)} %get-tuple-element.55), channel_id=1, source_target_pairs={{0,0},{4,16},{8,4},{12,20},{16,8},{20,24},{24,12},{28,28},{1,1},{5... | collective-permute-start | bytes 196616 | tf_op jit(solution)/shard_map/ppermute | solution.py:496
  85.2 10.5 %collective-permute-start.36 = (bf16[2,128,128]{2,1,0:T(8,128)(2,1)S(1)}, bf16[2,128,128]{2,1,0:T(8,128)(2,1)S(1)}, u32[]{:S(2)}, u32[]{:S(2)}) collective-permute-start(bf16[2,128,128]{2,1,0:T(8,128)(2,1)S(1)} %get-tuple-element.56), channel_id=1, source_target_pairs={{0,4},{4,20},{8,0},{12,16},{16,12},{20,28},{24,8},{28,24},{1,5},{5... | collective-permute-start | bytes 196616 | tf_op jit(solution)/shard_map/ppermute | solution.py:496
  86.7 9.2 %collective-permute-start.37 = (bf16[2,128,128]{2,1,0:T(8,128)(2,1)S(1)}, bf16[2,128,128]{2,1,0:T(8,128)(2,1)S(1)}, u32[]{:S(2)}, u32[]{:S(2)}) collective-permute-start(bf16[2,128,128]{2,1,0:T(8,128)(2,1)S(1)} %get-tuple-element.57), channel_id=1, source_target_pairs={{0,8},{4,24},{8,12},{12,28},{16,0},{20,16},{24,4},{28,20},{1,9},{5... | collective-permute-start | bytes 196616 | tf_op jit(solution)/shard_map/ppermute | solution.py:496
  88.0 11.6 %collective-permute-start.38 = (bf16[2,128,128]{2,1,0:T(8,128)(2,1)S(1)}, bf16[2,128,128]{2,1,0:T(8,128)(2,1)S(1)}, u32[]{:S(2)}, u32[]{:S(2)}) collective-permute-start(bf16[2,128,128]{2,1,0:T(8,128)(2,1)S(1)} %get-tuple-element.58), channel_id=1, source_target_pairs={{0,12},{4,28},{8,8},{12,24},{16,4},{20,20},{24,0},{28,16},{1,13},{... | collective-permute-start | bytes 196616 | tf_op jit(solution)/shard_map/ppermute | solution.py:496
  91.4 10.5 %collective-permute-start.25 = (bf16[2,128,128]{2,1,0:T(8,128)(2,1)S(1)}, bf16[2,128,128]{2,1,0:T(8,128)(2,1)S(1)}, u32[]{:S(2)}, u32[]{:S(2)}) collective-permute-start(bf16[2,128,128]{2,1,0:T(8,128)(2,1)S(1)} %get-tuple-element.47), channel_id=1, source_target_pairs={{0,0},{4,16},{8,4},{12,20},{16,8},{20,24},{24,12},{28,28},{1,1},{5... | collective-permute-start | bytes 196616 | tf_op jit(solution)/shard_map/ppermute | solution.py:496
  92.7 9.2 %collective-permute-start.26 = (bf16[2,128,128]{2,1,0:T(8,128)(2,1)S(1)}, bf16[2,128,128]{2,1,0:T(8,128)(2,1)S(1)}, u32[]{:S(2)}, u32[]{:S(2)}) collective-permute-start(bf16[2,128,128]{2,1,0:T(8,128)(2,1)S(1)} %get-tuple-element.48), channel_id=1, source_target_pairs={{0,4},{4,20},{8,0},{12,16},{16,12},{20,28},{24,8},{28,24},{1,5},{5... | collective-permute-start | bytes 196616 | tf_op jit(solution)/shard_map/ppermute | solution.py:496
  95.9 7.6 %collective-permute-start.28 = (bf16[2,128,128]{2,1,0:T(8,128)(2,1)S(1)}, bf16[2,128,128]{2,1,0:T(8,128)(2,1)S(1)}, u32[]{:S(2)}, u32[]{:S(2)}) collective-permute-start(bf16[2,128,128]{2,1,0:T(8,128)(2,1)S(1)} %get-tuple-element.50), channel_id=1, source_target_pairs={{0,12},{4,28},{8,8},{12,24},{16,4},{20,20},{24,0},{28,16},{1,13},{... | collective-permute-start | bytes 196616 | tf_op jit(solution)/shard_map/ppermute | solution.py:496
  (23 other events, 265.8 us)

commit v5 on v4

--- a/solution.py
+++ b/solution.py
@@ -74,10 +74,11 @@
 
 def reorder_body(order_ref, feat_ref, *outs):
     panel = feat_ref.shape[0]
+    order = jnp.broadcast_to(order_ref[...], (8, panel)).T
     rows = outs[0].shape[0]
     step = min(256, rows)
     for i in range(panel // step):
-        hot = lax.broadcasted_iota(jnp.int32, (step, panel), 1) == order_ref[pl.ds(i * step, step), :]
+        hot = lax.broadcasted_iota(jnp.int32, (step, panel), 1) == order[i * step : (i + 1) * step, :1]
         hot = jnp.where(hot, 1.0, 0.0).astype(BF16)
         at = i * step % rows
         outs[i * step // rows][at : at + step, :] = jnp.dot(
@@ -85,12 +86,12 @@
         ).astype(BF16)
 
 
-def reorder(order_col, features):
+def reorder(order_row, features):
     panel, width = features.shape
     outs = [jax.ShapeDtypeStruct((panel // HALVES, width), BF16)] * HALVES
     return call(
         reorder_body,
-        [order_col, features],
+        [order_row, features],
         outs,
         estimate=cost(2 * panel * panel * width, 4 * panel * width),
         name="reorder",
@@ -214,14 +215,29 @@
     return pre, gate, grad_pre
 
 
-def up_body(w_ref, co_ref, *refs, first):
+def two_parts(value):
+    high = value.astype(BF16)
+    return high, (value - high.astype(F32)).astype(BF16)
+
+
+def sum_of_parts(ref, at, rows):
+    return ref[at : at + rows, :].astype(F32) + ref[at + rows : at + 2 * rows, :].astype(F32)
+
+
+def up_body(w_ref, co_ref, *refs, first, count):
     place = Place()
-    shares, out_ref = refs[:-1], refs[-1]
+    shares, out_ref = refs[:count], refs[count]
     weight = w_ref[...]
     rows = shares[0].shape[0]
     for n, share in enumerate(shares):
         at = pl.multiple_of((place.rep ^ (first + n)) * rows, rows)
         _, _, grad_pre = gradient_of(share[...], co_ref[pl.ds(at, rows), :], weight)
+        if first + n == 0:
+            grad = lax.dot_general(
+                share[...], grad_pre, (((0,), (0,)), ((), ())), preferred_element_type=F32
+            )
+            width = grad.shape[0]
+            refs[count + 1][:width, :], refs[count + 1][width:, :] = two_parts(grad)
         out_ref[n] = lax.dot_general(
             weight, grad_pre, (((1,), (1,)), ((), ())), preferred_element_type=F32
         ).astype(BF16)
@@ -229,50 +245,43 @@
 
 def up_shares(weight, cotangent, shares, first):
     rows, width = shares[0].shape
-    out = jax.ShapeDtypeStruct((len(shares), width, rows), BF16)
+    outs = [jax.ShapeDtypeStruct((len(shares), width, rows), BF16)]
+    if first == 0:
+        outs.append(jax.ShapeDtypeStruct((2 * width, width), BF16))
     return call(
-        functools.partial(up_body, first=first),
+        functools.partial(up_body, first=first, count=len(shares)),
         [weight, cotangent, *shares],
-        out,
+        outs,
         estimate=cost(4 * len(shares) * rows * width * width, 2 * MIB),
         name="up_shares",
     )
 
 
-def finish_body(w_ref, co_ref, *refs):
+def finish_body(w_ref, *refs):
     place = Place()
-    shares, (hidden_ref, grad_ref, agg_all, pre_all) = refs[:-4], refs[-4:]
-    weight = w_ref[...]
+    shares, (hidden_ref, token_ref) = refs[:-2], refs[-2:]
     rows = shares[0].shape[0]
     for n, share in enumerate(shares):
         at = pl.multiple_of((place.rep ^ n) * rows, rows)
-        agg = share[...]
-        pre, gate, grad_pre = gradient_of(agg, co_ref[pl.ds(at, rows), :], weight)
-        hidden_ref[pl.ds(at, rows), :] = (pre * gate).astype(BF16)
-        agg_all[pl.ds(at, rows), :] = agg
-        pre_all[pl.ds(at, rows), :] = grad_pre
-    grad_ref[...] = lax.dot_general(
-        agg_all[...], pre_all[...], (((0,), (0,)), ((), ())), preferred_element_type=F32
-    )
-
-
-def finish(weight, cotangent, shares):
-    panel, width = cotangent.shape
-    outs = (like(cotangent), jax.ShapeDtypeStruct((width, width), F32))
-    return call(
-        finish_body,
-        [weight, cotangent, *shares],
-        outs,
-        scratch=[pltpu.VMEM((panel, width), BF16)] * 2,
-        estimate=cost(6 * panel * width * width, 8 * panel * width),
-        name="finish",
-    )
-
-
-def backward_body(live_ref, entry_ref, tiles_ref, *refs, slots, keep):
-    ups, (out_ref, up_all, acc) = refs[:-3], refs[-3:]
+        pre = jnp.dot(share[...], w_ref[...], preferred_element_type=F32)
+        hidden_ref[pl.ds(at, rows), :] = (pre * (1.0 / (1.0 + jnp.exp(-pre)))).astype(BF16)
+    token_ref[...] = jnp.zeros_like(token_ref)
+
+
+def finish(weight, shares):
+    rows, width = shares[0].shape
+    outs = (
+        jax.ShapeDtypeStruct((rows * len(shares), width), BF16),
+        jax.ShapeDtypeStruct((8, 128), jnp.int32),
+    )
+    return call(finish_body, [weight, *shares], outs, estimate=cost(0, 4 * MIB), name="finish")
+
+
+def backward_body(live_ref, entry_ref, tiles_ref, *refs, slots, keep, shape):
+    refs, (out_ref, up_all, acc) = refs[:-3], refs[-3:]
+    ups = refs if keep else refs[:-1]
     place = Place()
-    cuts, chips, pairs, per, width, block = out_ref.shape
+    cuts, chips, pairs, per, width, block = shape
     blocks = cuts * chips * per
     bits = (blocks - 1).bit_length()
     count, _, rows = ups[0].shape
@@ -302,19 +311,25 @@
         for h in range(cuts):
             for d in range(chips):
                 at = ((place.chip ^ d) * cuts + h) * per
-                out_ref[h, d, p] = acc[pl.ds(at, per)].astype(out_ref.dtype)
-
-
-def backward(plan, tiles, ups, pairs, chips, cuts, keep):
+                to = ((h * chips + d) * pairs + p) * per
+                out_ref[to : to + per] = acc[pl.ds(at, per)].astype(out_ref.dtype)
+    if not keep:
+        for n in range(2):
+            out_ref[pairs * blocks + n] = refs[-1][n * width : (n + 1) * width, :]
+
+
+def backward(plan, tiles, ups, pairs, chips, cuts, term=None):
     block = tiles.shape[1]
     count, width, rows = ups[0].shape
     panel = len(ups) * count * rows
     blocks = panel // block
     shape = (cuts, chips, pairs, blocks // chips // cuts, width, block)
+    keep = term is None
+    out_shape = (pairs * blocks + (0 if keep else 2), width, block)
     return call(
-        functools.partial(backward_body, slots=plan[1].shape[1], keep=keep),
-        [tiles, *ups],
-        jax.ShapeDtypeStruct(shape, F32 if keep else BF16),
+        functools.partial(backward_body, slots=plan[1].shape[1], keep=keep, shape=shape),
+        [tiles, *ups] + ([] if keep else [term]),
+        jax.ShapeDtypeStruct(out_shape, F32 if keep else BF16),
         scalars=plan,
         scratch=[pltpu.VMEM((width, panel), BF16), pltpu.VMEM((blocks + 1, width, block), F32)],
         vmem=(0,),
@@ -323,61 +338,122 @@
     )
 
 
-def join_body(kept_ref, given_ref, *outs):
-    cuts, chips = kept_ref.shape[:2]
+def join_body(kept_ref, given_ref, term_ref, *refs, cuts, chips):
+    outs, grad = refs[:-1], refs[-1]
+    place = Place()
+    width = grad.shape[0]
+    blocks = kept_ref.shape[0]
+    mate = given_ref[blocks].astype(F32) + given_ref[blocks + 1].astype(F32)
+    grad[...] = sum_of_parts(term_ref, 0, width) + mate
+    per = blocks // (cuts * chips)
     for h in range(cuts):
         for d in range(chips):
             out = outs[h * chips + d]
-            out[...] = (kept_ref[h, d] + given_ref[h, d].astype(F32)).astype(out.dtype)
-
-
-def join(kept, given):
-    cuts, chips = kept.shape[:2]
+            for b in range(per):
+                n = (h * chips + d) * per + b
+                out[b * width : (b + 1) * width, :] = (
+                    kept_ref[n] + given_ref[n].astype(F32)
+                ).astype(out.dtype)
+            if h == 0:
+                rows, end = width // chips, per * width
+                high, low = two_parts(grad[pl.ds((place.chip ^ d) * rows, rows), :])
+                if d == 0:
+                    out[end : end + rows, :] = high.astype(F32) + low.astype(F32)
+                else:
+                    out[end : end + rows, :] = high
+                    out[end + rows : end + 2 * rows, :] = low
+
+
+def join(kept, given, term, cuts, chips):
+    blocks, width, block = kept.shape
+    rows = blocks // (cuts * chips) * width
+    extra = width // chips
     outs = [
-        jax.ShapeDtypeStruct(kept.shape[2:], BF16 if d else F32)
-        for _ in range(cuts)
+        jax.ShapeDtypeStruct(
+            (rows + (0 if h else 2 * extra if d else extra), block), BF16 if d else F32
+        )
+        for h in range(cuts)
         for d in range(chips)
     ]
-    got = call(join_body, [kept, given], outs, name="join")
+    got = call(
+        functools.partial(join_body, cuts=cuts, chips=chips),
+        [kept, given, term],
+        outs,
+        scratch=[pltpu.VMEM((width, width), F32)],
+        name="join",
+    )
     return [got[h * chips : (h + 1) * chips] for h in range(cuts)]
 
 
-def gather_body(*refs, count):
-    terms = [ref[...].astype(F32) for ref in refs[:count]]
-    refs[-1][...] = tree_sum(terms).astype(BF16)
-
-
-def gather_sum(terms, after):
+def gather_body(*refs, count, rows):
+    out_ref = refs[-1]
+    terms = [ref[:rows, :].astype(F32) for ref in refs[:count]]
+    out_ref[:rows, :] = tree_sum(terms).astype(BF16)
+    extra = (out_ref.shape[0] - rows) // 2
+    if extra:
+        terms = [refs[0][rows : rows + extra, :]]
+        terms += [sum_of_parts(ref, rows, extra) for ref in refs[1:count]]
+        high, low = two_parts(tree_sum(terms))
+        out_ref[rows : rows + extra, :] = high
+        out_ref[rows + extra : rows + 2 * extra, :] = low
+
+
+def gather_sum(terms, after, rows):
     return call(
-        functools.partial(gather_body, count=len(terms)),
+        functools.partial(gather_body, count=len(terms), rows=rows),
         [*terms, *after],
-        like(terms[0], BF16),
+        like(terms[-1]),
         name="gather_sum",
     )
 
 
-def route_body(*refs, reps, chips):
+def route_body(*refs, reps, chips, rows, pairs):
     spread, outs = refs[:reps], refs[reps:]
     place = Place()
+    each = rows // pairs
+    extra = (spread[0].shape[0] - rows) // 2
+    if extra:
+        high, low = two_parts(tree_sum([sum_of_parts(ref, rows, extra) for ref in spread]))
     for k in range(chips):
         u = place.chip ^ k
         for d in range(reps):
 
             @pl.when(((u % reps) ^ place.rep) == d)
             def _():
-                outs[k][...] = spread[d][u // reps]
-
-
-def route(spread, chips):
-    outs = [jax.ShapeDtypeStruct(spread[0].shape[1:], BF16)] * chips
-    body = functools.partial(route_body, reps=len(spread), chips=chips)
+                at = pl.multiple_of(u // reps * each, each)
+                outs[k][:each, :] = spread[d][pl.ds(at, each), :]
+
+        if extra:
+            outs[k][each : each + extra, :] = high
+            outs[k][each + extra : each + 2 * extra, :] = low
+
+
+def route(spread, chips, rows, pairs):
+    height, width = spread[0].shape
+    outs = [jax.ShapeDtypeStruct((height - rows + rows // pairs, width), BF16)] * chips
+    body = functools.partial(route_body, reps=len(spread), chips=chips, rows=rows, pairs=pairs)
     return call(body, spread, outs, name="route")
 
 
-def restore_body(ids_ref, order_ref, *refs, count):
+def grad_body(*refs, reps, pairs, rows, scale):
+    parts, out_ref = refs[:-1], refs[-1]
+    section = lax.axis_index("section")
+    extra = out_ref.shape[0] // len(parts)
+    for k, part in enumerate(parts):
+        chip = ((section // reps // 2) * reps + section % reps) ^ k
+        out_ref[pl.ds(chip * extra, extra), :] = sum_of_parts(part, rows, extra) * scale
+
+
+def grad_of(parts, reps, pairs, rows, scale):
+    width = parts[0].shape[1]
+    body = functools.partial(grad_body, reps=reps, pairs=pairs, rows=rows, scale=scale)
+    return call(body, parts, jax.ShapeDtypeStruct((width, width), F32), name="grad_of")
+
+
+def restore_body(ids_ref, order_ref, *refs, count, per):
     parts, out_ref = refs[:count], refs[-1]
     rows = out_ref.shape[0]
-    per, _, block = parts[0].shape
+    block = parts[0].shape[1]
     base = pl.program_id(0) * rows
     acc = refs[count][...] if len(refs) > count + 1 else None
     for n, part in enumerate(parts):
@@ -386,7 +462,9 @@
         target = order_ref[:, pl.ds(at, length)]
         hot = lax.broadcasted_iota(jnp.int32, (rows, length), 0) + base == target
         hot = jnp.where(hot, 1.0, 0.0).astype(BF16)
-        columns = jnp.concatenate([part[b] for b in range(per)], axis=1)
+        columns = jnp.concatenate(
+            [part[b * block : (b + 1) * block, :] for b in range(per)], axis=1
+        )
         term = lax.dot_general(
             hot, columns, (((1,), (1,)), ((), ())), preferred_element_type=F32
         )
@@ -394,14 +472,14 @@
     out_ref[...] = acc.astype(out_ref.dtype)
 
 
-def restore(ids, order_row, parts, start, dtype):
+def restore(ids, order_row, parts, start, per, dtype):
     panel = order_row.shape[1]
     width = parts[0].shape[1]
     rows = 512
     row_spec = pl.BlockSpec((rows, width), lambda i, ids: (i, 0))
     extra = () if start is None else (start,)
     return pl.pallas_call(
-        functools.partial(restore_body, count=len(parts)),
+        functools.partial(restore_body, count=len(parts), per=per),
         out_shape=jax.ShapeDtypeStruct((panel, width), dtype),
         grid_spec=pltpu.PrefetchScalarGridSpec(
             num_scalar_prefetch=1,
@@ -452,8 +530,8 @@
                 moves.append((source * reps + r, target * reps + r))
         return lax.ppermute(x, ("section", "rep"), moves)
 
-    order_col = order.reshape(panel, 1)
-    owns = reorder(order_col, features)
+    order_row = order.reshape(1, panel)
+    owns = reorder(order_row, features)
     gots = [[own] + [from_owner(own, d) for d in range(1, chips)] for own in owns]
     bits = (blocks - 1).bit_length()
     plan = (live.reshape(rounds), entries_of(tile_rows, tile_cols, bits, owns[-1][:16]))
@@ -472,19 +550,19 @@
     aggregated = total_of(own, [sent[d] for d in range(1, reps)])
     shares = [aggregated] + [over_reps(aggregated, d) for d in range(1, reps)]
 
-    ups = [
-        up_shares(weight, cotangent, shares[:near], 0),
-        up_shares(weight, cotangent, shares[near:], near),
-    ]
+    up_early, term = up_shares(weight, cotangent, shares[:near], 0)
+    ups = [up_early, *up_shares(weight, cotangent, shares[near:], near)]
     cuts = math.gcd(2, blocks // chips)
-    given = over_cores(backward(plan, own_tiles, ups, pairs, chips, cuts, False))
-    kept = backward(plan, own_tiles, ups, pairs, chips, cuts, True)
-    chunks = join(kept, given)
+    given = over_cores(backward(plan, own_tiles, ups, pairs, chips, cuts, term))
+    kept = backward(plan, own_tiles, ups, pairs, chips, cuts)
+    chunks = join(kept, given, term, cuts, chips)
     arrived = [[over_chips(c[d], d) for d in range(1, chips)] for c in chunks]
     late_shares = lax.optimization_barrier((shares, chunks[-1][-1]))[0]
-    hidden, grad_part = finish(weight, cotangent, late_shares)
+    hidden, token = finish(weight, late_shares)
+    per = blocks // chips // cuts
+    height = pairs * per * width
     reduced = [
-        gather_sum([c[0], *a], [grad_part] if h == 0 else [])
+        gather_sum([c[0], *a], [token] if h == cuts - 1 else [], height)
         for h, (c, a) in enumerate(zip(chunks, arrived, strict=True))
     ]
 
@@ -496,18 +574,17 @@
         return lax.ppermute(block, "section", moves)
 
     mine_u = (section // reps // 2) * reps + section % reps
-    order_row = order.reshape(1, panel)
     feature_grad = None
     for h in range(cuts):
         spread = [reduced[h]] + [over_reps(reduced[h], d) for d in range(1, reps)]
-        parts = [to_owner(block, k) for k, block in enumerate(route(spread, chips))]
+        routed = route(spread, chips, height, pairs)
+        parts = [to_owner(block, k) for k, block in enumerate(routed)]
+        if h == 0:
+            scale = 1.0 / math.sqrt(panel * sections)
+            weight_grad = grad_of(parts, reps, pairs, per * width, scale)
         ids = jnp.stack([(mine_u ^ k) * cuts + h for k in range(chips)]).astype(jnp.int32)
         kind = BF16 if h == cuts - 1 else F32
-        feature_grad = restore(ids, order_row, parts, feature_grad, kind)
-
-    grad_part = grad_part + over_cores(grad_part)
-    weight_grad = tree_sum([grad_part] + [over_chips(grad_part, d) for d in range(1, chips)])
-    weight_grad = weight_grad * (1.0 / math.sqrt(panel * sections))
+        feature_grad = restore(ids, order_row, parts, feature_grad, per, kind)
     return (hidden, weight_grad, feature_grad)
 
 

time: 106 us -> 110 us (1.038)
  waiting for transfers between devices: 30.3 us -> 35.7 us
  starting transfers between devices: 56 us -> 53.1 us
    ppermute x12, waiting for transfers between devices: 22.8 us -> 25.9 us  [over_reps(): return lax.ppermute(x, 'rep', [(r, r ^ d) for r in range(reps)])]
    ppermute x9 -> x6, waiting for transfers between devices: 0.02 us -> 2.92 us  [over_chips(): return lax.ppermute(x, 'section', [(s, s ^ 2 * d) for s in range(sections)])]
    ppermute x9 -> x6, starting transfers between devices: 9.64 us -> 7.43 us  [over_chips(): return lax.ppermute(x, 'section', [(s, s ^ 2 * d) for s in range(sections)])]
    unnamed x16 -> x18, local copies, waits for them, and re-layouts: 1.07 us -> 2.61 us
    pallas_call x17 -> x18, Pallas kernels: 10.8 us -> 11.8 us  [call(): pl.pallas_call(body, out_shape=outs, grid_spec=pltpu.PrefetchScalarGridSp...]
  transfers between devices with their start and end apart: 39 -> 35, of which waited for: 13 -> 14; matrix products, arithmetic and copies ran while one was open for 1% -> 0% of each run, Pallas kernels for 7% -> 7%
where the time goes in v5:
time: 110 us
  starting transfers between devices  53.1 us (48%)
  waiting for transfers between devices  35.7 us (32%)
  Pallas kernels  17.3 us (16%)
  local copies, waits for them, and re-layouts  2.61 us (2%)
    ppermute x12, waiting for transfers between devices, over_reps(): return lax.ppermute(x, 'rep', [(r, r ^ d) for r in range(reps)])  25.9 us
    ppermute x12, starting transfers between devices, over_reps(): return lax.ppermute(x, 'rep', [(r, r ^ d) for r in range(reps)])  19.7 us
    ppermute x8, starting transfers between devices, to_owner(): return lax.ppermute(block, 'section', moves)  14.2 us
    pallas_call x18, Pallas kernels, call(): pl.pallas_call(body, out_shape=outs, grid_spec=pltpu.PrefetchScalarGridSp...  11.8 us
    ppermute x6, starting transfers between devices, from_owner(): return lax.ppermute(x, ('section', 'rep'), moves)  11.4 us
    ppermute x6, starting transfers between devices, over_chips(): return lax.ppermute(x, 'section', [(s, s ^ 2 * d) for s in range(sections)])  7.43 us
    pallas_call x2, Pallas kernels, restore(): pl.pallas_call(functools.partial(restore_body, count=len(parts), per=per)...  5.53 us
    ppermute x6, waiting for transfers between devices, from_owner(): return lax.ppermute(x, ('section', 'rep'), moves)  5.32 us
  transfers between devices with their start and end apart: 35, of which 14 were waited for; matrix products, arithmetic and copies ran while one was open for 0% of the time, Pallas kernels for 7%

profile of v5, /device:TPU:0, one launch (start us, length us, event | category | flops | bytes accessed | tf_op | source)
XLA Modules:
  0.0 109.9 jit_solution(10096231929315428253)
XLA Ops:
  3.3 3.4 %reorder.1 = (bf16[1024,128]{1,0:T(8,128)(2,1)S(1)}, bf16[1024,128]{1,0:T(8,128)(2,1)S(1)}) custom-call(s32[1,2048]{1,0:T(1,128)S(1)} %bitcast.19, bf16[2048,128]{1,0:T(8,128)(2,1)S(1)} %copy-done.6), custom_call_target="tpu_custom_call" | custom-call | flops 1073741824 | bytes 1048576 | tf_op jit(solution)/shard_map/reorder/pallas_call | solution.py:55
  6.6 4.9 %collective-permute-start.4 = (bf16[1024,128]{1,0:T(8,128)(2,1)S(1)}, bf16[1024,128]{1,0:T(8,128)(2,1)S(1)}, u32[]{:S(2)}, u32[]{:S(2)}) collective-permute-start(bf16[1024,128]{1,0:T(8,128)(2,1)S(1)} %get-tuple-element.33.refs_0_), channel_id=1, source_target_pairs={{0,8},{16,24},{5,13},{21,29},{10,2},{26,18},{15,7},{31,23}} | collective-permute-start | bytes 786440 | tf_op jit(solution)/shard_map/ppermute | solution.py:531
  18.6 2.4 %collective-permute-done.refs_1_ = bf16[1024,128]{1,0:T(8,128)(2,1)S(1)} collective-permute-done((bf16[1024,128]{1,0:T(8,128)(2,1)S(1)}, bf16[1024,128]{1,0:T(8,128)(2,1)S(1)}, u32[]{:S(2)}, u32[]{:S(2)}) %collective-permute-start) | collective-permute-done | bytes 262176 | tf_op jit(solution)/shard_map/ppermute | solution.py:531
  21.0 2.8 %collective-permute-done.2.refs_3_ = bf16[1024,128]{1,0:T(8,128)(2,1)S(1)} collective-permute-done((bf16[1024,128]{1,0:T(8,128)(2,1)S(1)}, bf16[1024,128]{1,0:T(8,128)(2,1)S(1)}, u32[]{:S(2)}, u32[]{:S(2)}) %collective-permute-start.2) | collective-permute-done | bytes 262176 | tf_op jit(solution)/shard_map/ppermute | solution.py:531
  26.5 4.4 %collective-permute-start.10 = (bf16[512,128]{1,0:T(8,128)(2,1)S(1)}, bf16[512,128]{1,0:T(8,128)(2,1)S(1)}, u32[]{:S(2)}, u32[]{:S(2)}) collective-permute-start(bf16[512,128]{1,0:T(8,128)(2,1)S(1)} %get-tuple-element.38), channel_id=1, source_target_pairs={{0,3},{1,2},{2,1},{3,0},{4,7},{5,6},{6,5},{7,4},{8,11},{9,10},{10,... | collective-permute-start | bytes 393224 | tf_op jit(solution)/shard_map/ppermute | solution.py:522
  31.9 3.4 %collective-permute-done.10.refs_2_ = bf16[512,128]{1,0:T(8,128)(2,1)S(1)} collective-permute-done((bf16[512,128]{1,0:T(8,128)(2,1)S(1)}, bf16[512,128]{1,0:T(8,128)(2,1)S(1)}, u32[]{:S(2)}, u32[]{:S(2)}) %collective-permute-start.10) | collective-permute-done | bytes 131104 | tf_op jit(solution)/shard_map/ppermute | solution.py:522
  35.4 2.8 %collective-permute-done.8.refs_0_ = bf16[512,128]{1,0:T(8,128)(2,1)S(1)} collective-permute-done((bf16[512,128]{1,0:T(8,128)(2,1)S(1)}, bf16[512,128]{1,0:T(8,128)(2,1)S(1)}, u32[]{:S(2)}, u32[]{:S(2)}) %collective-permute-start.8) | collective-permute-done | bytes 131104 | tf_op jit(solution)/shard_map/ppermute | solution.py:522
  38.2 5.4 %collective-permute-done.9.refs_1_ = bf16[512,128]{1,0:T(8,128)(2,1)S(1)} collective-permute-done((bf16[512,128]{1,0:T(8,128)(2,1)S(1)}, bf16[512,128]{1,0:T(8,128)(2,1)S(1)}, u32[]{:S(2)}, u32[]{:S(2)}) %collective-permute-start.9) | collective-permute-done | bytes 131104 | tf_op jit(solution)/shard_map/ppermute | solution.py:522
  44.4 3.4 %collective-permute-start.12 = (bf16[512,128]{1,0:T(8,128)(2,1)S(1)}, bf16[512,128]{1,0:T(8,128)(2,1)S(1)}, u32[]{:S(2)}, u32[]{:S(2)}) collective-permute-start(bf16[512,128]{1,0:T(8,128)(2,1)S(1)} %total_of.1.refs_0_), channel_id=1, source_target_pairs={{0,2},{1,3},{2,0},{3,1},{4,6},{5,7},{6,4},{7,5},{8,10},{9,11},{10,... | collective-permute-start | bytes 393224 | tf_op jit(solution)/shard_map/ppermute | solution.py:522
  48.2 3.4 %collective-permute-done.11.refs_1_ = bf16[512,128]{1,0:T(8,128)(2,1)S(1)} collective-permute-done((bf16[512,128]{1,0:T(8,128)(2,1)S(1)}, bf16[512,128]{1,0:T(8,128)(2,1)S(1)}, u32[]{:S(2)}, u32[]{:S(2)}) %collective-permute-start.11) | collective-permute-done | bytes 131104 | tf_op jit(solution)/shard_map/ppermute | solution.py:522
  52.2 5.5 %collective-permute-done.12.refs_0_.refs_2_ = bf16[512,128]{1,0:T(8,128)(2,1)S(1)} collective-permute-done((bf16[512,128]{1,0:T(8,128)(2,1)S(1)}, bf16[512,128]{1,0:T(8,128)(2,1)S(1)}, u32[]{:S(2)}, u32[]{:S(2)}) %collective-permute-start.12) | collective-permute-done | bytes 131104 | tf_op jit(solution)/shard_map/ppermute | solution.py:522
  63.6 2.4 %collective-permute-start.16 = (bf16[320,128]{1,0:T(8,128)(2,1)S(1)}, bf16[320,128]{1,0:T(8,128)(2,1)S(1)}, u32[]{:S(2)}, u32[]{:S(2)}) collective-permute-start(bf16[320,128]{1,0:T(8,128)(2,1)S(1)} %get-tuple-element.49), channel_id=1, source_target_pairs={{0,16},{4,20},{8,24},{12,28},{16,0},{20,4},{24,8},{28,12},{1,17},{... | collective-permute-start | bytes 245768 | tf_op jit(solution)/shard_map/ppermute | solution.py:516
  70.2 2.9 %collective-permute-done.26.refs_2_ = bf16[256,128]{1,0:T(8,128)(2,1)S(1)} collective-permute-done((bf16[256,128]{1,0:T(8,128)(2,1)S(1)}, bf16[256,128]{1,0:T(8,128)(2,1)S(1)}, u32[]{:S(2)}, u32[]{:S(2)}) %collective-permute-start.26) | collective-permute-done | bytes 65568 | tf_op jit(solution)/shard_map/ppermute | solution.py:516
  73.1 2.0 %collective-permute-start.28 = (bf16[256,128]{1,0:T(8,128)(2,1)S(1)}, bf16[256,128]{1,0:T(8,128)(2,1)S(1)}, u32[]{:S(2)}, u32[]{:S(2)}) collective-permute-start(bf16[256,128]{1,0:T(8,128)(2,1)S(1)} %gather_sum.3.refs_0_), channel_id=1, source_target_pairs={{0,1},{1,0},{2,3},{3,2},{4,5},{5,4},{6,7},{7,6},{8,9},{9,8},{10,11... | collective-permute-start | bytes 196616 | tf_op jit(solution)/shard_map/ppermute | solution.py:522
  76.6 2.0 %collective-permute-start.18 = (bf16[320,128]{1,0:T(8,128)(2,1)S(1)}, bf16[320,128]{1,0:T(8,128)(2,1)S(1)}, u32[]{:S(2)}, u32[]{:S(2)}) collective-permute-start(bf16[320,128]{1,0:T(8,128)(2,1)S(1)} %gather_sum.2.refs_0_), channel_id=1, source_target_pairs={{0,1},{1,0},{2,3},{3,2},{4,5},{5,4},{6,7},{7,6},{8,9},{9,8},{10,11... | collective-permute-start | bytes 245768 | tf_op jit(solution)/shard_map/ppermute | solution.py:522
  78.6 2.4 %collective-permute-start.20 = (bf16[320,128]{1,0:T(8,128)(2,1)S(1)}, bf16[320,128]{1,0:T(8,128)(2,1)S(1)}, u32[]{:S(2)}, u32[]{:S(2)}) collective-permute-start(bf16[320,128]{1,0:T(8,128)(2,1)S(1)} %gather_sum.2.refs_0_), channel_id=1, source_target_pairs={{0,3},{1,2},{2,1},{3,0},{4,7},{5,6},{6,5},{7,4},{8,11},{9,10},{10,... | collective-permute-start | bytes 245768 | tf_op jit(solution)/shard_map/ppermute | solution.py:522
  81.8 1.9 %collective-permute-start.30 = (bf16[256,128]{1,0:T(8,128)(2,1)S(1)}, bf16[256,128]{1,0:T(8,128)(2,1)S(1)}, u32[]{:S(2)}, u32[]{:S(2)}) collective-permute-start(bf16[256,128]{1,0:T(8,128)(2,1)S(1)} %gather_sum.3.refs_0_), channel_id=1, source_target_pairs={{0,3},{1,2},{2,1},{3,0},{4,7},{5,6},{6,5},{7,4},{8,11},{9,10},{10,... | collective-permute-start | bytes 196616 | tf_op jit(solution)/shard_map/ppermute | solution.py:522
  83.6 4.6 %collective-permute-done.19.refs_2_ = bf16[320,128]{1,0:T(8,128)(2,1)S(1)} collective-permute-done((bf16[320,128]{1,0:T(8,128)(2,1)S(1)}, bf16[320,128]{1,0:T(8,128)(2,1)S(1)}, u32[]{:S(2)}, u32[]{:S(2)}) %collective-permute-start.19) | collective-permute-done | bytes 81952 | tf_op jit(solution)/shard_map/ppermute | solution.py:522
  89.1 2.8 %collective-permute-start.22 = (bf16[320,128]{1,0:T(8,128)(2,1)S(1)}, bf16[320,128]{1,0:T(8,128)(2,1)S(1)}, u32[]{:S(2)}, u32[]{:S(2)}) collective-permute-start(bf16[320,128]{1,0:T(8,128)(2,1)S(1)} %get-tuple-element.52), channel_id=1, source_target_pairs={{0,4},{4,20},{8,0},{12,16},{16,12},{20,28},{24,8},{28,24},{1,5},{5... | collective-permute-start | bytes 245768 | tf_op jit(solution)/shard_map/ppermute | solution.py:574
  91.9 4.1 %collective-permute-start.24 = (bf16[320,128]{1,0:T(8,128)(2,1)S(1)}, bf16[320,128]{1,0:T(8,128)(2,1)S(1)}, u32[]{:S(2)}, u32[]{:S(2)}) collective-permute-start(bf16[320,128]{1,0:T(8,128)(2,1)S(1)} %get-tuple-element.54), channel_id=1, source_target_pairs={{0,12},{4,28},{8,8},{12,24},{16,4},{20,20},{24,0},{28,16},{1,13},{... | collective-permute-start | bytes 245768 | tf_op jit(solution)/shard_map/ppermute | solution.py:574
  96.9 2.0 %collective-permute-start.32 = (bf16[256,128]{1,0:T(8,128)(2,1)S(1)}, bf16[256,128]{1,0:T(8,128)(2,1)S(1)}, u32[]{:S(2)}, u32[]{:S(2)}) collective-permute-start(bf16[256,128]{1,0:T(8,128)(2,1)S(1)} %get-tuple-element.60), channel_id=1, source_target_pairs={{0,4},{4,20},{8,0},{12,16},{16,12},{20,28},{24,8},{28,24},{1,5},{5... | collective-permute-start | bytes 196616 | tf_op jit(solution)/shard_map/ppermute | solution.py:574
  99.2 3.6 %collective-permute-start.34 = (bf16[256,128]{1,0:T(8,128)(2,1)S(1)}, bf16[256,128]{1,0:T(8,128)(2,1)S(1)}, u32[]{:S(2)}, u32[]{:S(2)}) collective-permute-start(bf16[256,128]{1,0:T(8,128)(2,1)S(1)} %get-tuple-element.62), channel_id=1, source_target_pairs={{0,12},{4,28},{8,8},{12,24},{16,4},{20,20},{24,0},{28,16},{1,13},{... | collective-permute-start | bytes 196616 | tf_op jit(solution)/shard_map/ppermute | solution.py:574
  103.5 2.3 %restore.2.refs_4_ = f32[2048,128]{1,0:T(8,128)S(1)} custom-call(s32[4]{0:T(128)S(1)} %pad_add_fusion.1.ids_ref, s32[1,2048]{1,0:T(1,128)S(1)} %bitcast.20, bf16[320,128]{1,0:T(8,128)(2,1)S(1)} %collective-permute-done.21.refs_0_, bf16[320,128]{1,0:T(8,128)(2,1)S(1)} %collective-permute-done.22.refs_1_, ...), custom_call_target="tpu_custom_call" | custom-call | flops 1073741824 | bytes 1048576 | tf_op jit(solution)/shard_map/restore/pallas_call | solution.py:481
  106.7 3.2 %restore.3 = bf16[2048,128]{1,0:T(8,128)(2,1)} custom-call(s32[4]{0:T(128)S(1)} %pad_add_fusion.ids_ref, s32[1,2048]{1,0:T(1,128)S(1)} %bitcast.21, bf16[256,128]{1,0:T(8,128)(2,1)S(1)} %collective-permute-done.31.refs_0_, bf16[256,128]{1,0:T(8,128)(2,1)S(1)} %collective-permute-done.32.refs_1_, bf16[256,128]{1,0:T(8,128)(2,1)S(1)} %collective-permute-done.33.refs_2_, ...), custom_call_target="tpu_custom_call" | custom-call | flops 1073741824 | bytes 1048576 | tf_op jit(solution)/shard_map/restore/pallas_call | solution.py:481
  (87 shorter events, 30.7 us)
Async XLA Ops:
  6.6 10.1 %collective-permute-start.4 = (bf16[1024,128]{1,0:T(8,128)(2,1)S(1)}, bf16[1024,128]{1,0:T(8,128)(2,1)S(1)}, u32[]{:S(2)}, u32[]{:S(2)}) collective-permute-start(bf16[1024,128]{1,0:T(8,128)(2,1)S(1)} %get-tuple-element.33.refs_0_), channel_id=1, source_target_pairs={{0,8},{16,24},{5,13},{21,29},{10,2},{26,18},{15,7},{31,23}} | collective-permute-start | bytes 786440 | tf_op jit(solution)/shard_map/ppermute | solution.py:531
  18.2 7.1 %collective-permute-start.7 = (bf16[1024,128]{1,0:T(8,128)(2,1)S(1)}, bf16[1024,128]{1,0:T(8,128)(2,1)S(1)}, u32[]{:S(2)}, u32[]{:S(2)}) collective-permute-start(bf16[1024,128]{1,0:T(8,128)(2,1)S(1)} %pick.3.refs_1_), channel_id=1, source_target_pairs={{0,4},{4,0},{8,12},{12,8},{16,20},{20,16},{24,28},{28,24},{1,5},{5... | collective-permute-start | bytes 786440 | tf_op jit(solution)/shard_map/ppermute | solution.py:519
  26.5 8.9 %collective-permute-start.10 = (bf16[512,128]{1,0:T(8,128)(2,1)S(1)}, bf16[512,128]{1,0:T(8,128)(2,1)S(1)}, u32[]{:S(2)}, u32[]{:S(2)}) collective-permute-start(bf16[512,128]{1,0:T(8,128)(2,1)S(1)} %get-tuple-element.38), channel_id=1, source_target_pairs={{0,3},{1,2},{2,1},{3,0},{4,7},{5,6},{6,5},{7,4},{8,11},{9,10},{10,... | collective-permute-start | bytes 393224 | tf_op jit(solution)/shard_map/ppermute | solution.py:522
  30.9 7.3 %collective-permute-start.8 = (bf16[512,128]{1,0:T(8,128)(2,1)S(1)}, bf16[512,128]{1,0:T(8,128)(2,1)S(1)}, u32[]{:S(2)}, u32[]{:S(2)}) collective-permute-start(bf16[512,128]{1,0:T(8,128)(2,1)S(1)} %get-tuple-element.36), channel_id=1, source_target_pairs={{0,1},{1,0},{2,3},{3,2},{4,5},{5,4},{6,7},{7,6},{8,9},{9,8},{10,11... | collective-permute-start | bytes 393224 | tf_op jit(solution)/shard_map/ppermute | solution.py:522
  31.9 11.7 %collective-permute-start.9 = (bf16[512,128]{1,0:T(8,128)(2,1)S(1)}, bf16[512,128]{1,0:T(8,128)(2,1)S(1)}, u32[]{:S(2)}, u32[]{:S(2)}) collective-permute-start(bf16[512,128]{1,0:T(8,128)(2,1)S(1)} %get-tuple-element.37), channel_id=1, source_target_pairs={{0,2},{1,3},{2,0},{3,1},{4,6},{5,7},{6,4},{7,5},{8,10},{9,11},{10,... | collective-permute-start | bytes 393224 | tf_op jit(solution)/shard_map/ppermute | solution.py:522
  43.7 7.9 %collective-permute-start.11 = (bf16[512,128]{1,0:T(8,128)(2,1)S(1)}, bf16[512,128]{1,0:T(8,128)(2,1)S(1)}, u32[]{:S(2)}, u32[]{:S(2)}) collective-permute-start(bf16[512,128]{1,0:T(8,128)(2,1)S(1)} %total_of.1.refs_0_), channel_id=1, source_target_pairs={{0,1},{1,0},{2,3},{3,2},{4,5},{5,4},{6,7},{7,6},{8,9},{9,8},{10,11... | collective-permute-start | bytes 393224 | tf_op jit(solution)/shard_map/ppermute | solution.py:522
  44.4 13.4 %collective-permute-start.12 = (bf16[512,128]{1,0:T(8,128)(2,1)S(1)}, bf16[512,128]{1,0:T(8,128)(2,1)S(1)}, u32[]{:S(2)}, u32[]{:S(2)}) collective-permute-start(bf16[512,128]{1,0:T(8,128)(2,1)S(1)} %total_of.1.refs_0_), channel_id=1, source_target_pairs={{0,2},{1,3},{2,0},{3,1},{4,6},{5,7},{6,4},{7,5},{8,10},{9,11},{10,... | collective-permute-start | bytes 393224 | tf_op jit(solution)/shard_map/ppermute | solution.py:522
  47.8 10.0 %collective-permute-start.13 = (bf16[512,128]{1,0:T(8,128)(2,1)S(1)}, bf16[512,128]{1,0:T(8,128)(2,1)S(1)}, u32[]{:S(2)}, u32[]{:S(2)}) collective-permute-start(bf16[512,128]{1,0:T(8,128)(2,1)S(1)} %total_of.1.refs_0_), channel_id=1, source_target_pairs={{0,3},{1,2},{2,1},{3,0},{4,7},{5,6},{6,5},{7,4},{8,11},{9,10},{10,... | collective-permute-start | bytes 393224 | tf_op jit(solution)/shard_map/ppermute | solution.py:522
  62.1 14.4 %collective-permute-start.15 = (bf16[320,128]{1,0:T(8,128)(2,1)S(1)}, bf16[320,128]{1,0:T(8,128)(2,1)S(1)}, u32[]{:S(2)}, u32[]{:S(2)}) collective-permute-start(bf16[320,128]{1,0:T(8,128)(2,1)S(1)} %get-tuple-element.48), channel_id=1, source_target_pairs={{0,8},{4,12},{8,0},{12,4},{16,24},{20,28},{24,16},{28,20},{1,9},{5... | collective-permute-start | bytes 245768 | tf_op jit(solution)/shard_map/ppermute | solution.py:516
  63.6 13.0 %collective-permute-start.16 = (bf16[320,128]{1,0:T(8,128)(2,1)S(1)}, bf16[320,128]{1,0:T(8,128)(2,1)S(1)}, u32[]{:S(2)}, u32[]{:S(2)}) collective-permute-start(bf16[320,128]{1,0:T(8,128)(2,1)S(1)} %get-tuple-element.49), channel_id=1, source_target_pairs={{0,16},{4,20},{8,24},{12,28},{16,0},{20,4},{24,8},{28,12},{1,17},{... | collective-permute-start | bytes 245768 | tf_op jit(solution)/shard_map/ppermute | solution.py:516
  66.0 10.5 %collective-permute-start.17 = (bf16[320,128]{1,0:T(8,128)(2,1)S(1)}, bf16[320,128]{1,0:T(8,128)(2,1)S(1)}, u32[]{:S(2)}, u32[]{:S(2)}) collective-permute-start(bf16[320,128]{1,0:T(8,128)(2,1)S(1)} %get-tuple-element.50), channel_id=1, source_target_pairs={{0,24},{4,28},{8,16},{12,20},{16,8},{20,12},{24,0},{28,4},{1,25},{... | collective-permute-start | bytes 245768 | tf_op jit(solution)/shard_map/ppermute | solution.py:516
  66.0 7.1 %collective-permute-start.26 = (bf16[256,128]{1,0:T(8,128)(2,1)S(1)}, bf16[256,128]{1,0:T(8,128)(2,1)S(1)}, u32[]{:S(2)}, u32[]{:S(2)}) collective-permute-start(bf16[256,128]{1,0:T(8,128)(2,1)S(1)} %get-tuple-element.57), channel_id=1, source_target_pairs={{0,16},{4,20},{8,24},{12,28},{16,0},{20,4},{24,8},{28,12},{1,17},{... | collective-permute-start | bytes 196616 | tf_op jit(solution)/shard_map/ppermute | solution.py:516
  73.1 18.7 %collective-permute-start.28 = (bf16[256,128]{1,0:T(8,128)(2,1)S(1)}, bf16[256,128]{1,0:T(8,128)(2,1)S(1)}, u32[]{:S(2)}, u32[]{:S(2)}) collective-permute-start(bf16[256,128]{1,0:T(8,128)(2,1)S(1)} %gather_sum.3.refs_0_), channel_id=1, source_target_pairs={{0,1},{1,0},{2,3},{3,2},{4,5},{5,4},{6,7},{7,6},{8,9},{9,8},{10,11... | collective-permute-start | bytes 196616 | tf_op jit(solution)/shard_map/ppermute | solution.py:522
  75.1 16.8 %collective-permute-start.29 = (bf16[256,128]{1,0:T(8,128)(2,1)S(1)}, bf16[256,128]{1,0:T(8,128)(2,1)S(1)}, u32[]{:S(2)}, u32[]{:S(2)}) collective-permute-start(bf16[256,128]{1,0:T(8,128)(2,1)S(1)} %gather_sum.3.refs_0_), channel_id=1, source_target_pairs={{0,2},{1,3},{2,0},{3,1},{4,6},{5,7},{6,4},{7,5},{8,10},{9,11},{10,... | collective-permute-start | bytes 196616 | tf_op jit(solution)/shard_map/ppermute | solution.py:522
  78.6 9.6 %collective-permute-start.19 = (bf16[320,128]{1,0:T(8,128)(2,1)S(1)}, bf16[320,128]{1,0:T(8,128)(2,1)S(1)}, u32[]{:S(2)}, u32[]{:S(2)}) collective-permute-start(bf16[320,128]{1,0:T(8,128)(2,1)S(1)} %gather_sum.2.refs_0_), channel_id=1, source_target_pairs={{0,2},{1,3},{2,0},{3,1},{4,6},{5,7},{6,4},{7,5},{8,10},{9,11},{10,... | collective-permute-start | bytes 245768 | tf_op jit(solution)/shard_map/ppermute | solution.py:522
  78.6 9.6 %collective-permute-start.20 = (bf16[320,128]{1,0:T(8,128)(2,1)S(1)}, bf16[320,128]{1,0:T(8,128)(2,1)S(1)}, u32[]{:S(2)}, u32[]{:S(2)}) collective-permute-start(bf16[320,128]{1,0:T(8,128)(2,1)S(1)} %gather_sum.2.refs_0_), channel_id=1, source_target_pairs={{0,3},{1,2},{2,1},{3,0},{4,7},{5,6},{6,5},{7,4},{8,11},{9,10},{10,... | collective-permute-start | bytes 245768 | tf_op jit(solution)/shard_map/ppermute | solution.py:522
  81.8 14.3 %collective-permute-start.30 = (bf16[256,128]{1,0:T(8,128)(2,1)S(1)}, bf16[256,128]{1,0:T(8,128)(2,1)S(1)}, u32[]{:S(2)}, u32[]{:S(2)}) collective-permute-start(bf16[256,128]{1,0:T(8,128)(2,1)S(1)} %gather_sum.3.refs_0_), channel_id=1, source_target_pairs={{0,3},{1,2},{2,1},{3,0},{4,7},{5,6},{6,5},{7,4},{8,11},{9,10},{10,... | collective-permute-start | bytes 196616 | tf_op jit(solution)/shard_map/ppermute | solution.py:522
  88.4 8.5 %collective-permute-start.21 = (bf16[320,128]{1,0:T(8,128)(2,1)S(1)}, bf16[320,128]{1,0:T(8,128)(2,1)S(1)}, u32[]{:S(2)}, u32[]{:S(2)}) collective-permute-start(bf16[320,128]{1,0:T(8,128)(2,1)S(1)} %get-tuple-element.51), channel_id=1, source_target_pairs={{0,0},{4,16},{8,4},{12,20},{16,8},{20,24},{24,12},{28,28},{1,1},{5... | collective-permute-start | bytes 245768 | tf_op jit(solution)/shard_map/ppermute | solution.py:574
  89.1 9.8 %collective-permute-start.22 = (bf16[320,128]{1,0:T(8,128)(2,1)S(1)}, bf16[320,128]{1,0:T(8,128)(2,1)S(1)}, u32[]{:S(2)}, u32[]{:S(2)}) collective-permute-start(bf16[320,128]{1,0:T(8,128)(2,1)S(1)} %get-tuple-element.52), channel_id=1, source_target_pairs={{0,4},{4,20},{8,0},{12,16},{16,12},{20,28},{24,8},{28,24},{1,5},{5... | collective-permute-start | bytes 245768 | tf_op jit(solution)/shard_map/ppermute | solution.py:574
  91.9 7.4 %collective-permute-start.23 = (bf16[320,128]{1,0:T(8,128)(2,1)S(1)}, bf16[320,128]{1,0:T(8,128)(2,1)S(1)}, u32[]{:S(2)}, u32[]{:S(2)}) collective-permute-start(bf16[320,128]{1,0:T(8,128)(2,1)S(1)} %get-tuple-element.53), channel_id=1, source_target_pairs={{0,8},{4,24},{8,12},{12,28},{16,0},{20,16},{24,4},{28,20},{1,9},{5... | collective-permute-start | bytes 245768 | tf_op jit(solution)/shard_map/ppermute | solution.py:574
  91.9 11.0 %collective-permute-start.24 = (bf16[320,128]{1,0:T(8,128)(2,1)S(1)}, bf16[320,128]{1,0:T(8,128)(2,1)S(1)}, u32[]{:S(2)}, u32[]{:S(2)}) collective-permute-start(bf16[320,128]{1,0:T(8,128)(2,1)S(1)} %get-tuple-element.54), channel_id=1, source_target_pairs={{0,12},{4,28},{8,8},{12,24},{16,4},{20,20},{24,0},{28,16},{1,13},{... | collective-permute-start | bytes 245768 | tf_op jit(solution)/shard_map/ppermute | solution.py:574
  96.2 9.6 %collective-permute-start.31 = (bf16[256,128]{1,0:T(8,128)(2,1)S(1)}, bf16[256,128]{1,0:T(8,128)(2,1)S(1)}, u32[]{:S(2)}, u32[]{:S(2)}) collective-permute-start(bf16[256,128]{1,0:T(8,128)(2,1)S(1)} %get-tuple-element.59), channel_id=1, source_target_pairs={{0,0},{4,16},{8,4},{12,20},{16,8},{20,24},{24,12},{28,28},{1,1},{5... | collective-permute-start | bytes 196616 | tf_op jit(solution)/shard_map/ppermute | solution.py:574
  96.9 9.0 %collective-permute-start.32 = (bf16[256,128]{1,0:T(8,128)(2,1)S(1)}, bf16[256,128]{1,0:T(8,128)(2,1)S(1)}, u32[]{:S(2)}, u32[]{:S(2)}) collective-permute-start(bf16[256,128]{1,0:T(8,128)(2,1)S(1)} %get-tuple-element.60), channel_id=1, source_target_pairs={{0,4},{4,20},{8,0},{12,16},{16,12},{20,28},{24,8},{28,24},{1,5},{5... | collective-permute-start | bytes 196616 | tf_op jit(solution)/shard_map/ppermute | solution.py:574
  99.2 7.5 %collective-permute-start.34 = (bf16[256,128]{1,0:T(8,128)(2,1)S(1)}, bf16[256,128]{1,0:T(8,128)(2,1)S(1)}, u32[]{:S(2)}, u32[]{:S(2)}) collective-permute-start(bf16[256,128]{1,0:T(8,128)(2,1)S(1)} %get-tuple-element.62), channel_id=1, source_target_pairs={{0,12},{4,28},{8,8},{12,24},{16,4},{20,20},{24,0},{28,16},{1,13},{... | collective-permute-start | bytes 196616 | tf_op jit(solution)/shard_map/ppermute | solution.py:574
  (20 other events, 251.2 us)

commit v6 on v5

--- a/solution.py
+++ b/solution.py
@@ -74,11 +74,10 @@
 
 def reorder_body(order_ref, feat_ref, *outs):
     panel = feat_ref.shape[0]
-    order = jnp.broadcast_to(order_ref[...], (8, panel)).T
     rows = outs[0].shape[0]
     step = min(256, rows)
     for i in range(panel // step):
-        hot = lax.broadcasted_iota(jnp.int32, (step, panel), 1) == order[i * step : (i + 1) * step, :1]
+        hot = lax.broadcasted_iota(jnp.int32, (step, panel), 1) == order_ref[pl.ds(i * step, step), :]
         hot = jnp.where(hot, 1.0, 0.0).astype(BF16)
         at = i * step % rows
         outs[i * step // rows][at : at + step, :] = jnp.dot(
@@ -86,12 +85,12 @@
         ).astype(BF16)
 
 
-def reorder(order_row, features):
+def reorder(order_col, features):
     panel, width = features.shape
     outs = [jax.ShapeDtypeStruct((panel // HALVES, width), BF16)] * HALVES
     return call(
         reorder_body,
-        [order_row, features],
+        [order_col, features],
         outs,
         estimate=cost(2 * panel * panel * width, 4 * panel * width),
         name="reorder",
@@ -435,32 +434,29 @@
     return call(body, spread, outs, name="route")
 
 
-def grad_body(*refs, reps, pairs, rows, scale):
-    parts, out_ref = refs[:-1], refs[-1]
+def restore_body(order_ref, *refs, first, count, per, scale, reps):
+    parts, refs = refs[:count], refs[count:]
+    start, (out_ref, grad_ref) = refs[:-2], refs[-2:]
     section = lax.axis_index("section")
-    extra = out_ref.shape[0] // len(parts)
-    for k, part in enumerate(parts):
-        chip = ((section // reps // 2) * reps + section % reps) ^ k
-        out_ref[pl.ds(chip * extra, extra), :] = sum_of_parts(part, rows, extra) * scale
-
-
-def grad_of(parts, reps, pairs, rows, scale):
-    width = parts[0].shape[1]
-    body = functools.partial(grad_body, reps=reps, pairs=pairs, rows=rows, scale=scale)
-    return call(body, parts, jax.ShapeDtypeStruct((width, width), F32), name="grad_of")
-
-
-def restore_body(ids_ref, order_ref, *refs, count, per):
-    parts, out_ref = refs[:count], refs[-1]
+    base_u = (section // reps // 2) * reps + section % reps
     rows = out_ref.shape[0]
     block = parts[0].shape[1]
-    base = pl.program_id(0) * rows
-    acc = refs[count][...] if len(refs) > count + 1 else None
+    step = pl.program_id(0)
+    acc = start[0][...] if start else None
+
+    @pl.when(step == 0)
+    def _():
+        grad_ref[...] = start[1][...] if start else jnp.zeros_like(grad_ref)
+        extra = (parts[0].shape[0] - per * block) // 2
+        for n, part in enumerate(parts):
+            at = pl.multiple_of((base_u ^ (first + n)) * extra, extra)
+            grad_ref[pl.ds(at, extra), :] = sum_of_parts(part, per * block, extra) * scale
+
     for n, part in enumerate(parts):
         length = per * block
-        at = pl.multiple_of(ids_ref[n] * length, length)
+        at = pl.multiple_of((base_u ^ (first + n)) * length, length)
         target = order_ref[:, pl.ds(at, length)]
-        hot = lax.broadcasted_iota(jnp.int32, (rows, length), 0) + base == target
+        hot = lax.broadcasted_iota(jnp.int32, (rows, length), 0) + step * rows == target
         hot = jnp.where(hot, 1.0, 0.0).astype(BF16)
         columns = jnp.concatenate(
             [part[b * block : (b + 1) * block, :] for b in range(per)], axis=1
@@ -472,27 +468,29 @@
     out_ref[...] = acc.astype(out_ref.dtype)
 
 
-def restore(ids, order_row, parts, start, per, dtype):
+def restore(order_row, parts, first, start, per, scale, reps):
     panel = order_row.shape[1]
     width = parts[0].shape[1]
     rows = 512
-    row_spec = pl.BlockSpec((rows, width), lambda i, ids: (i, 0))
-    extra = () if start is None else (start,)
+    row_spec = pl.BlockSpec((rows, width), lambda i: (i, 0))
+    grad_spec = pl.BlockSpec((width, width), lambda i: (0, 0))
+    body = functools.partial(
+        restore_body, first=first, count=len(parts), per=per, scale=scale, reps=reps
+    )
     return pl.pallas_call(
-        functools.partial(restore_body, count=len(parts), per=per),
-        out_shape=jax.ShapeDtypeStruct((panel, width), dtype),
-        grid_spec=pltpu.PrefetchScalarGridSpec(
-            num_scalar_prefetch=1,
-            grid=(panel // rows,),
-            in_specs=[whole_spec(order_row)]
-            + [whole_spec(p) for p in parts]
-            + [row_spec for _ in extra],
-            out_specs=row_spec,
+        body,
+        out_shape=(
+            jax.ShapeDtypeStruct((panel, width), BF16 if start else F32),
+            jax.ShapeDtypeStruct((width, width), F32),
         ),
+        grid=(panel // rows,),
+        in_specs=[whole_spec(x) for x in (order_row, *parts)]
+        + ([row_spec, grad_spec] if start else []),
+        out_specs=(row_spec, grad_spec),
         compiler_params=params(24),
         cost_estimate=cost(2 * panel * panel * width, 4 * panel * width),
         name="restore",
-    )(ids, order_row, *parts, *extra)
+    )(order_row, *parts, *start)
 
 
 def tree_sum(terms):
@@ -504,7 +502,6 @@
 def shards(features, order, tiles, tile_rows, tile_cols, live, weight, cotangent):
     reps = lax.axis_size("rep")
     sections = lax.axis_size("section")
-    section = lax.axis_index("section")
     panel, width = features.shape
     rounds, slots, block, _ = tiles.shape[2:]
     blocks = panel // block
@@ -531,7 +528,7 @@
         return lax.ppermute(x, ("section", "rep"), moves)
 
     order_row = order.reshape(1, panel)
-    owns = reorder(order_row, features)
+    owns = reorder(order.reshape(panel, 1), features)
     gots = [[own] + [from_owner(own, d) for d in range(1, chips)] for own in owns]
     bits = (blocks - 1).bit_length()
     plan = (live.reshape(rounds), entries_of(tile_rows, tile_cols, bits, owns[-1][:16]))
@@ -552,7 +549,7 @@
 
     up_early, term = up_shares(weight, cotangent, shares[:near], 0)
     ups = [up_early, *up_shares(weight, cotangent, shares[near:], near)]
-    cuts = math.gcd(2, blocks // chips)
+    cuts = 1
     given = over_cores(backward(plan, own_tiles, ups, pairs, chips, cuts, term))
     kept = backward(plan, own_tiles, ups, pairs, chips, cuts)
     chunks = join(kept, given, term, cuts, chips)
@@ -561,10 +558,7 @@
     hidden, token = finish(weight, late_shares)
     per = blocks // chips // cuts
     height = pairs * per * width
-    reduced = [
-        gather_sum([c[0], *a], [token] if h == cuts - 1 else [], height)
-        for h, (c, a) in enumerate(zip(chunks, arrived, strict=True))
-    ]
+    reduced = gather_sum([chunks[0][0], *arrived[0]], [token], height)
 
     def to_owner(block, k):
         moves = []
@@ -573,18 +567,12 @@
             moves.append((s, (2 * (u // reps) + s % 2) * reps + u % reps))
         return lax.ppermute(block, "section", moves)
 
-    mine_u = (section // reps // 2) * reps + section % reps
-    feature_grad = None
-    for h in range(cuts):
-        spread = [reduced[h]] + [over_reps(reduced[h], d) for d in range(1, reps)]
-        routed = route(spread, chips, height, pairs)
-        parts = [to_owner(block, k) for k, block in enumerate(routed)]
-        if h == 0:
-            scale = 1.0 / math.sqrt(panel * sections)
-            weight_grad = grad_of(parts, reps, pairs, per * width, scale)
-        ids = jnp.stack([(mine_u ^ k) * cuts + h for k in range(chips)]).astype(jnp.int32)
-        kind = BF16 if h == cuts - 1 else F32
-        feature_grad = restore(ids, order_row, parts, feature_grad, per, kind)
+    spread = [reduced] + [over_reps(reduced, d) for d in range(1, reps)]
+    parts = [to_owner(block, k) for k, block in enumerate(route(spread, chips, height, pairs))]
+    scale = 1.0 / math.sqrt(panel * sections)
+    half = chips // 2
+    begun = restore(order_row, parts[:half], 0, (), per, scale, reps)
+    feature_grad, weight_grad = restore(order_row, parts[half:], half, begun, per, scale, reps)
     return (hidden, weight_grad, feature_grad)
 
 

time: 110 us -> 102 us (0.927)
  starting transfers between devices: 53.1 us -> 38.6 us
  waiting for transfers between devices: 35.7 us -> 41.8 us
  Pallas kernels: 17.3 us -> 18.5 us
    ppermute x8 -> x4, starting transfers between devices: 14.2 us -> 8.18 us  [to_owner(): return lax.ppermute(block, 'section', moves)]
    ppermute x12 -> x9, starting transfers between devices: 19.7 us -> 14.9 us  [over_reps(): return lax.ppermute(x, 'rep', [(r, r ^ d) for r in range(reps)])]
    ppermute x6 -> x3, starting transfers between devices: 7.43 us -> 3.55 us  [over_chips(): return lax.ppermute(x, 'section', [(s, s ^ 2 * d) for s in range(sections)])]
    ppermute x12 -> x9, waiting for transfers between devices: 25.9 us -> 28.7 us  [over_reps(): return lax.ppermute(x, 'rep', [(r, r ^ d) for r in range(reps)])]
    ppermute x8 -> x4, waiting for transfers between devices: 0.86 us -> 3 us  [to_owner(): return lax.ppermute(block, 'section', moves)]
    pallas_call x18 -> x15, Pallas kernels: 11.8 us -> 13.9 us  [call(): pl.pallas_call(body, out_shape=outs, grid_spec=pltpu.PrefetchScalarGridSp...]
    ppermute x6 -> x3, waiting for transfers between devices: 2.92 us -> 4.52 us  [over_chips(): return lax.ppermute(x, 'section', [(s, s ^ 2 * d) for s in range(sections)])]
    unnamed x18 -> x16, local copies, waits for them, and re-layouts: 2.61 us -> 1.07 us
  transfers between devices with their start and end apart: 35 -> 25, of which waited for: 14 -> 14; matrix products, arithmetic and copies ran while one was open for 0% -> 0% of each run, Pallas kernels for 7% -> 8%
where the time goes in v6:
time: 102 us
  waiting for transfers between devices  41.8 us (41%)
  starting transfers between devices  38.6 us (38%)
  Pallas kernels  18.5 us (18%)
  local copies, waits for them, and re-layouts  2.15 us (2%)
    ppermute x9, waiting for transfers between devices, over_reps(): return lax.ppermute(x, 'rep', [(r, r ^ d) for r in range(reps)])  28.7 us
    ppermute x9, starting transfers between devices, over_reps(): return lax.ppermute(x, 'rep', [(r, r ^ d) for r in range(reps)])  14.9 us
    pallas_call x15, Pallas kernels, call(): pl.pallas_call(body, out_shape=outs, grid_spec=pltpu.PrefetchScalarGridSp...  13.9 us
    ppermute x6, starting transfers between devices, from_owner(): return lax.ppermute(x, ('section', 'rep'), moves)  11.8 us
    ppermute x4, starting transfers between devices, to_owner(): return lax.ppermute(block, 'section', moves)  8.18 us
    ppermute x6, waiting for transfers between devices, from_owner(): return lax.ppermute(x, ('section', 'rep'), moves)  5.58 us
    pallas_call x2, Pallas kernels, restore(): pl.pallas_call(body, out_shape=(jax.ShapeDtypeStruct((panel, width), BF16...  4.57 us
    ppermute x3, waiting for transfers between devices, over_chips(): return lax.ppermute(x, 'section', [(s, s ^ 2 * d) for s in range(sections)])  4.52 us
  transfers between devices with their start and end apart: 25, of which 14 were waited for; matrix products, arithmetic and copies ran while one was open for 0% of the time, Pallas kernels for 8%

profile of v6, /device:TPU:0, one launch (start us, length us, event | category | flops | bytes accessed | tf_op | source)
XLA Modules:
  0.0 102.1 jit_solution(5011111436576580274)
XLA Ops:
  2.8 2.4 %reorder.1 = (bf16[1024,128]{1,0:T(8,128)(2,1)S(1)}, bf16[1024,128]{1,0:T(8,128)(2,1)S(1)}) custom-call(s32[2048,1]{1,0:T(8,128)S(1)} %copy.11.order_ref, bf16[2048,128]{1,0:T(8,128)(2,1)S(1)} %copy-done.7), custom_call_target="tpu_custom_call" | custom-call | flops 1073741824 | bytes 1048576 | tf_op jit(solution)/shard_map/reorder/pallas_call | solution.py:55
  5.2 5.3 %collective-permute-start.2 = (bf16[1024,128]{1,0:T(8,128)(2,1)S(1)}, bf16[1024,128]{1,0:T(8,128)(2,1)S(1)}, u32[]{:S(2)}, u32[]{:S(2)}) collective-permute-start(bf16[1024,128]{1,0:T(8,128)(2,1)S(1)} %get-tuple-element.30.refs_0_), channel_id=1, source_target_pairs={{0,28},{16,12},{5,25},{21,9},{10,22},{26,6},{15,19},{31,3}} | collective-permute-start | bytes 786440 | tf_op jit(solution)/shard_map/ppermute | solution.py:528
  17.2 2.7 %collective-permute-done.6.refs_3_ = bf16[1024,128]{1,0:T(8,128)(2,1)S(1)} collective-permute-done((bf16[1024,128]{1,0:T(8,128)(2,1)S(1)}, bf16[1024,128]{1,0:T(8,128)(2,1)S(1)}, u32[]{:S(2)}, u32[]{:S(2)}) %collective-permute-start.6) | collective-permute-done | bytes 262176 | tf_op jit(solution)/shard_map/ppermute | solution.py:528
  19.9 2.8 %collective-permute-done.4.refs_1_ = bf16[1024,128]{1,0:T(8,128)(2,1)S(1)} collective-permute-done((bf16[1024,128]{1,0:T(8,128)(2,1)S(1)}, bf16[1024,128]{1,0:T(8,128)(2,1)S(1)}, u32[]{:S(2)}, u32[]{:S(2)}) %collective-permute-start.4) | collective-permute-done | bytes 262176 | tf_op jit(solution)/shard_map/ppermute | solution.py:528
  22.9 2.0 %forward.2.refs_2_ = f32[16,128,128]{2,1,0:T(8,128)S(1)} custom-call(s32[2]{0:T(128)S(1)} %bitcast.11, s32[2,96]{1,0:T(2,128)S(1)} %entries_of.1.entry_ref, bf16[192,128,128]{2,1,0:T(8,128)(2,1)S(1)} %bitcast.4, bf16[1024,128]{1,0:T(8,128)(2,1)S(1)} %pick.2.refs_0_, bf16[1024,128]{1,0:T(8,128)(2,1)S(1)} %pick.3.refs_1_), custom_call_target="tpu_custom_call" | custom-call | flops 268435456 | bytes 12582912 | tf_op jit(solution)/shard_map/forward/pallas_call | solution.py:55
  25.0 2.3 %forward.3 = (f32[512,128]{1,0:T(8,128)S(1)}, bf16[512,128]{1,0:T(8,128)(2,1)S(1)}, bf16[512,128]{1,0:T(8,128)(2,1)S(1)}, bf16[512,128]{1,0:T(8,128)(2,1)S(1)}) custom-call(s32[2]{0:T(128)S(1)} %bitcast.12, s32[2,96]{1,0:T(2,128)S(1)} %entries_of.1.entry_ref, bf16[192,128,128]{2,1,0:T(8,128)(2,1)S(1)} %bitcast.5, ...), custom_call_target="tpu_custom_call" | custom-call | flops 268435456 | bytes 12582912 | tf_op jit(solution)/shard_map/forward/pallas_call | solution.py:55
  28.6 3.0 %collective-permute-start.9 = (bf16[512,128]{1,0:T(8,128)(2,1)S(1)}, bf16[512,128]{1,0:T(8,128)(2,1)S(1)}, u32[]{:S(2)}, u32[]{:S(2)}) collective-permute-start(bf16[512,128]{1,0:T(8,128)(2,1)S(1)} %get-tuple-element.33), channel_id=1, source_target_pairs={{0,2},{1,3},{2,0},{3,1},{4,6},{5,7},{6,4},{7,5},{8,10},{9,11},{10,... | collective-permute-start | bytes 393224 | tf_op jit(solution)/shard_map/ppermute | solution.py:519
  31.7 3.2 %collective-permute-done.8.refs_0_ = bf16[512,128]{1,0:T(8,128)(2,1)S(1)} collective-permute-done((bf16[512,128]{1,0:T(8,128)(2,1)S(1)}, bf16[512,128]{1,0:T(8,128)(2,1)S(1)}, u32[]{:S(2)}, u32[]{:S(2)}) %collective-permute-start.8) | collective-permute-done | bytes 131104 | tf_op jit(solution)/shard_map/ppermute | solution.py:519
  35.6 5.4 %collective-permute-done.10.refs_2_ = bf16[512,128]{1,0:T(8,128)(2,1)S(1)} collective-permute-done((bf16[512,128]{1,0:T(8,128)(2,1)S(1)}, bf16[512,128]{1,0:T(8,128)(2,1)S(1)}, u32[]{:S(2)}, u32[]{:S(2)}) %collective-permute-start.10) | collective-permute-done | bytes 131104 | tf_op jit(solution)/shard_map/ppermute | solution.py:519
  41.1 2.6 %collective-permute-start.11 = (bf16[512,128]{1,0:T(8,128)(2,1)S(1)}, bf16[512,128]{1,0:T(8,128)(2,1)S(1)}, u32[]{:S(2)}, u32[]{:S(2)}) collective-permute-start(bf16[512,128]{1,0:T(8,128)(2,1)S(1)} %total_of.1.refs_0_), channel_id=1, source_target_pairs={{0,1},{1,0},{2,3},{3,2},{4,5},{5,4},{6,7},{7,6},{8,9},{9,8},{10,11... | collective-permute-start | bytes 393224 | tf_op jit(solution)/shard_map/ppermute | solution.py:519
  43.7 3.4 %collective-permute-start.13 = (bf16[512,128]{1,0:T(8,128)(2,1)S(1)}, bf16[512,128]{1,0:T(8,128)(2,1)S(1)}, u32[]{:S(2)}, u32[]{:S(2)}) collective-permute-start(bf16[512,128]{1,0:T(8,128)(2,1)S(1)} %total_of.1.refs_0_), channel_id=1, source_target_pairs={{0,3},{1,2},{2,1},{3,0},{4,7},{5,6},{6,5},{7,4},{8,11},{9,10},{10,... | collective-permute-start | bytes 393224 | tf_op jit(solution)/shard_map/ppermute | solution.py:519
  47.7 6.6 %collective-permute-done.13.refs_1_.refs_3_ = bf16[512,128]{1,0:T(8,128)(2,1)S(1)} collective-permute-done((bf16[512,128]{1,0:T(8,128)(2,1)S(1)}, bf16[512,128]{1,0:T(8,128)(2,1)S(1)}, u32[]{:S(2)}, u32[]{:S(2)}) %collective-permute-start.13) | collective-permute-done | bytes 131104 | tf_op jit(solution)/shard_map/ppermute | solution.py:519
  54.3 3.3 %collective-permute-done.12.refs_0_.refs_2_ = bf16[512,128]{1,0:T(8,128)(2,1)S(1)} collective-permute-done((bf16[512,128]{1,0:T(8,128)(2,1)S(1)}, bf16[512,128]{1,0:T(8,128)(2,1)S(1)}, u32[]{:S(2)}, u32[]{:S(2)}) %collective-permute-start.12) | collective-permute-done | bytes 131104 | tf_op jit(solution)/shard_map/ppermute | solution.py:519
  58.1 2.3 %backward.3 = bf16[18,128,128]{2,1,0:T(8,128)(2,1)S(1)} custom-call(s32[2]{0:T(128)S(1)} %bitcast.13, s32[2,96]{1,0:T(2,128)S(1)} %entries_of.1.entry_ref, bf16[192,128,128]{2,1,0:T(8,128)(2,1)S(1)} %bitcast.6, bf16[2,128,512]{2,1,0:T(8,128)(2,1)S(1)} %get-tuple-element.35.refs_0_, bf16[2,128,512]{2,1,0:T(8,128)(2,1)S(1)} %up_shares.3.refs_1_, ...), custom_call_target="tpu_custom_call" | custom-call | flops 268435456 | bytes 12582912 | tf_op jit(solution)/shard_map/backward/pallas_call | solution.py:55
  60.6 2.0 %backward.2.kept_ref = f32[16,128,128]{2,1,0:T(8,128)S(1)} custom-call(s32[2]{0:T(128)S(1)} %bitcast.14, s32[2,96]{1,0:T(2,128)S(1)} %entries_of.1.entry_ref, bf16[192,128,128]{2,1,0:T(8,128)(2,1)S(1)} %bitcast.7, bf16[2,128,512]{2,1,0:T(8,128)(2,1)S(1)} %get-tuple-element.35.refs_0_, bf16[2,128,512]{2,1,0:T(8,128)(2,1)S(1)} %up_shares.3.refs_1_), custom_call_target="tpu_custom_call" | custom-call | flops 268435456 | bytes 12582912 | tf_op jit(solution)/shard_map/backward/pallas_call | solution.py:55
  63.0 3.2 %collective-permute-start.17 = (bf16[576,128]{1,0:T(8,128)(2,1)S(1)}, bf16[576,128]{1,0:T(8,128)(2,1)S(1)}, u32[]{:S(2)}, u32[]{:S(2)}) collective-permute-start(bf16[576,128]{1,0:T(8,128)(2,1)S(1)} %get-tuple-element.37), channel_id=1, source_target_pairs={{0,24},{4,28},{8,16},{12,20},{16,8},{20,12},{24,0},{28,4},{1,25},{... | collective-permute-start | bytes 442376 | tf_op jit(solution)/shard_map/ppermute | solution.py:513
  69.5 2.6 %collective-permute-done.16.refs_2_ = bf16[576,128]{1,0:T(8,128)(2,1)S(1)} collective-permute-done((bf16[576,128]{1,0:T(8,128)(2,1)S(1)}, bf16[576,128]{1,0:T(8,128)(2,1)S(1)}, u32[]{:S(2)}, u32[]{:S(2)}) %collective-permute-start.16) | collective-permute-done | bytes 147488 | tf_op jit(solution)/shard_map/ppermute | solution.py:513
  73.9 2.7 %collective-permute-start.18 = (bf16[576,128]{1,0:T(8,128)(2,1)S(1)}, bf16[576,128]{1,0:T(8,128)(2,1)S(1)}, u32[]{:S(2)}, u32[]{:S(2)}) collective-permute-start(bf16[576,128]{1,0:T(8,128)(2,1)S(1)} %gather_sum.1.refs_0_), channel_id=1, source_target_pairs={{0,1},{1,0},{2,3},{3,2},{4,5},{5,4},{6,7},{7,6},{8,9},{9,8},{10,11... | collective-permute-start | bytes 442376 | tf_op jit(solution)/shard_map/ppermute | solution.py:519
  76.6 4.2 %collective-permute-done.20.refs_3_ = bf16[576,128]{1,0:T(8,128)(2,1)S(1)} collective-permute-done((bf16[576,128]{1,0:T(8,128)(2,1)S(1)}, bf16[576,128]{1,0:T(8,128)(2,1)S(1)}, u32[]{:S(2)}, u32[]{:S(2)}) %collective-permute-start.20) | collective-permute-done | bytes 147488 | tf_op jit(solution)/shard_map/ppermute | solution.py:519
  80.8 5.3 %collective-permute-done.19.refs_2_ = bf16[576,128]{1,0:T(8,128)(2,1)S(1)} collective-permute-done((bf16[576,128]{1,0:T(8,128)(2,1)S(1)}, bf16[576,128]{1,0:T(8,128)(2,1)S(1)}, u32[]{:S(2)}, u32[]{:S(2)}) %collective-permute-start.19) | collective-permute-done | bytes 147488 | tf_op jit(solution)/shard_map/ppermute | solution.py:519
  86.9 2.8 %collective-permute-start.24 = (bf16[576,128]{1,0:T(8,128)(2,1)S(1)}, bf16[576,128]{1,0:T(8,128)(2,1)S(1)}, u32[]{:S(2)}, u32[]{:S(2)}) collective-permute-start(bf16[576,128]{1,0:T(8,128)(2,1)S(1)} %get-tuple-element.50), channel_id=1, source_target_pairs={{0,4},{4,20},{8,0},{12,16},{16,12},{20,28},{24,8},{28,24},{1,5},{5... | collective-permute-start | bytes 442376 | tf_op jit(solution)/shard_map/ppermute | solution.py:568
  90.0 4.5 %collective-permute-start.22 = (bf16[576,128]{1,0:T(8,128)(2,1)S(1)}, bf16[576,128]{1,0:T(8,128)(2,1)S(1)}, u32[]{:S(2)}, u32[]{:S(2)}) collective-permute-start(bf16[576,128]{1,0:T(8,128)(2,1)S(1)} %get-tuple-element.48), channel_id=1, source_target_pairs={{0,12},{4,28},{8,8},{12,24},{16,4},{20,20},{24,0},{28,16},{1,13},{... | collective-permute-start | bytes 442376 | tf_op jit(solution)/shard_map/ppermute | solution.py:568
  94.5 2.6 %collective-permute-done.24.refs_1_ = bf16[576,128]{1,0:T(8,128)(2,1)S(1)} collective-permute-done((bf16[576,128]{1,0:T(8,128)(2,1)S(1)}, bf16[576,128]{1,0:T(8,128)(2,1)S(1)}, u32[]{:S(2)}, u32[]{:S(2)}) %collective-permute-start.24) | collective-permute-done | bytes 147488 | tf_op jit(solution)/shard_map/ppermute | solution.py:568
  99.3 2.7 %restore.3 = (bf16[2048,128]{1,0:T(8,128)(2,1)}, f32[128,128]{1,0:T(8,128)}) custom-call(s32[1,2048]{1,0:T(1,128)S(1)} %bitcast.10, bf16[576,128]{1,0:T(8,128)(2,1)S(1)} %collective-permute-done.21.refs_0_, bf16[576,128]{1,0:T(8,128)(2,1)S(1)} %collective-permute-done.22.refs_1_, f32[2048,128]{1,0:T(8,128)S(1)} %get-tuple-element.51.refs_2_, ...), custom_call_target="tpu_custom_call" | custom-call | flops 1073741824 | bytes 1048576 | tf_op jit(solution)/shard_map/restore/pallas_call | solution.py:480
  (61 shorter events, 21.2 us)
Async XLA Ops:
  5.2 10.5 %collective-permute-start.2 = (bf16[1024,128]{1,0:T(8,128)(2,1)S(1)}, bf16[1024,128]{1,0:T(8,128)(2,1)S(1)}, u32[]{:S(2)}, u32[]{:S(2)}) collective-permute-start(bf16[1024,128]{1,0:T(8,128)(2,1)S(1)} %get-tuple-element.30.refs_0_), channel_id=1, source_target_pairs={{0,28},{16,12},{5,25},{21,9},{10,22},{26,6},{15,19},{31,3}} | collective-permute-start | bytes 786440 | tf_op jit(solution)/shard_map/ppermute | solution.py:528
  10.5 6.6 %collective-permute-start.1 = (bf16[1024,128]{1,0:T(8,128)(2,1)S(1)}, bf16[1024,128]{1,0:T(8,128)(2,1)S(1)}, u32[]{:S(2)}, u32[]{:S(2)}) collective-permute-start(bf16[1024,128]{1,0:T(8,128)(2,1)S(1)} %get-tuple-element.30.refs_0_), channel_id=1, source_target_pairs={{0,20},{16,4},{5,17},{21,1},{10,30},{26,14},{15,27},{31,11}} | collective-permute-start | bytes 786440 | tf_op jit(solution)/shard_map/ppermute | solution.py:528
  11.8 5.4 %collective-permute-start = (bf16[1024,128]{1,0:T(8,128)(2,1)S(1)}, bf16[1024,128]{1,0:T(8,128)(2,1)S(1)}, u32[]{:S(2)}, u32[]{:S(2)}) collective-permute-start(bf16[1024,128]{1,0:T(8,128)(2,1)S(1)} %get-tuple-element.30.refs_0_), channel_id=1, source_target_pairs={{0,8},{16,24},{5,13},{21,29},{10,2},{26,18},{15,7},{31,23}} | collective-permute-start | bytes 786440 | tf_op jit(solution)/shard_map/ppermute | solution.py:528
  13.1 6.8 %collective-permute-start.6 = (bf16[1024,128]{1,0:T(8,128)(2,1)S(1)}, bf16[1024,128]{1,0:T(8,128)(2,1)S(1)}, u32[]{:S(2)}, u32[]{:S(2)}) collective-permute-start(bf16[1024,128]{1,0:T(8,128)(2,1)S(1)} %get-tuple-element.29.refs_0_), channel_id=1, source_target_pairs={{0,28},{16,12},{5,25},{21,9},{10,22},{26,6},{15,19},{31,3}} | collective-permute-start | bytes 786440 | tf_op jit(solution)/shard_map/ppermute | solution.py:528
  14.4 5.5 %collective-permute-start.5 = (bf16[1024,128]{1,0:T(8,128)(2,1)S(1)}, bf16[1024,128]{1,0:T(8,128)(2,1)S(1)}, u32[]{:S(2)}, u32[]{:S(2)}) collective-permute-start(bf16[1024,128]{1,0:T(8,128)(2,1)S(1)} %get-tuple-element.29.refs_0_), channel_id=1, source_target_pairs={{0,20},{16,4},{5,17},{21,1},{10,30},{26,14},{15,27},{31,11}} | collective-permute-start | bytes 786440 | tf_op jit(solution)/shard_map/ppermute | solution.py:528
  15.7 7.0 %collective-permute-start.4 = (bf16[1024,128]{1,0:T(8,128)(2,1)S(1)}, bf16[1024,128]{1,0:T(8,128)(2,1)S(1)}, u32[]{:S(2)}, u32[]{:S(2)}) collective-permute-start(bf16[1024,128]{1,0:T(8,128)(2,1)S(1)} %get-tuple-element.29.refs_0_), channel_id=1, source_target_pairs={{0,8},{16,24},{5,13},{21,29},{10,2},{26,18},{15,7},{31,23}} | collective-permute-start | bytes 786440 | tf_op jit(solution)/shard_map/ppermute | solution.py:528
  17.2 7.8 %collective-permute-start.3 = (bf16[1024,128]{1,0:T(8,128)(2,1)S(1)}, bf16[1024,128]{1,0:T(8,128)(2,1)S(1)}, u32[]{:S(2)}, u32[]{:S(2)}) collective-permute-start(bf16[1024,128]{1,0:T(8,128)(2,1)S(1)} %pick.2.refs_0_), channel_id=1, source_target_pairs={{0,4},{4,0},{8,12},{12,8},{16,20},{20,16},{24,28},{28,24},{1,5},{5... | collective-permute-start | bytes 786440 | tf_op jit(solution)/shard_map/ppermute | solution.py:516
  22.8 2.2 %collective-permute-start.7 = (bf16[1024,128]{1,0:T(8,128)(2,1)S(1)}, bf16[1024,128]{1,0:T(8,128)(2,1)S(1)}, u32[]{:S(2)}, u32[]{:S(2)}) collective-permute-start(bf16[1024,128]{1,0:T(8,128)(2,1)S(1)} %pick.3.refs_1_), channel_id=1, source_target_pairs={{0,4},{4,0},{8,12},{12,8},{16,20},{20,16},{24,28},{28,24},{1,5},{5... | collective-permute-start | bytes 786440 | tf_op jit(solution)/shard_map/ppermute | solution.py:516
  27.2 7.7 %collective-permute-start.8 = (bf16[512,128]{1,0:T(8,128)(2,1)S(1)}, bf16[512,128]{1,0:T(8,128)(2,1)S(1)}, u32[]{:S(2)}, u32[]{:S(2)}) collective-permute-start(bf16[512,128]{1,0:T(8,128)(2,1)S(1)} %get-tuple-element.32), channel_id=1, source_target_pairs={{0,1},{1,0},{2,3},{3,2},{4,5},{5,4},{6,7},{7,6},{8,9},{9,8},{10,11... | collective-permute-start | bytes 393224 | tf_op jit(solution)/shard_map/ppermute | solution.py:519
  28.6 6.9 %collective-permute-start.9 = (bf16[512,128]{1,0:T(8,128)(2,1)S(1)}, bf16[512,128]{1,0:T(8,128)(2,1)S(1)}, u32[]{:S(2)}, u32[]{:S(2)}) collective-permute-start(bf16[512,128]{1,0:T(8,128)(2,1)S(1)} %get-tuple-element.33), channel_id=1, source_target_pairs={{0,2},{1,3},{2,0},{3,1},{4,6},{5,7},{6,4},{7,5},{8,10},{9,11},{10,... | collective-permute-start | bytes 393224 | tf_op jit(solution)/shard_map/ppermute | solution.py:519
  31.6 9.4 %collective-permute-start.10 = (bf16[512,128]{1,0:T(8,128)(2,1)S(1)}, bf16[512,128]{1,0:T(8,128)(2,1)S(1)}, u32[]{:S(2)}, u32[]{:S(2)}) collective-permute-start(bf16[512,128]{1,0:T(8,128)(2,1)S(1)} %get-tuple-element.34), channel_id=1, source_target_pairs={{0,3},{1,2},{2,1},{3,0},{4,7},{5,6},{6,5},{7,4},{8,11},{9,10},{10,... | collective-permute-start | bytes 393224 | tf_op jit(solution)/shard_map/ppermute | solution.py:519
  41.1 6.0 %collective-permute-start.11 = (bf16[512,128]{1,0:T(8,128)(2,1)S(1)}, bf16[512,128]{1,0:T(8,128)(2,1)S(1)}, u32[]{:S(2)}, u32[]{:S(2)}) collective-permute-start(bf16[512,128]{1,0:T(8,128)(2,1)S(1)} %total_of.1.refs_0_), channel_id=1, source_target_pairs={{0,1},{1,0},{2,3},{3,2},{4,5},{5,4},{6,7},{7,6},{8,9},{9,8},{10,11... | collective-permute-start | bytes 393224 | tf_op jit(solution)/shard_map/ppermute | solution.py:519
  43.7 10.7 %collective-permute-start.13 = (bf16[512,128]{1,0:T(8,128)(2,1)S(1)}, bf16[512,128]{1,0:T(8,128)(2,1)S(1)}, u32[]{:S(2)}, u32[]{:S(2)}) collective-permute-start(bf16[512,128]{1,0:T(8,128)(2,1)S(1)} %total_of.1.refs_0_), channel_id=1, source_target_pairs={{0,3},{1,2},{2,1},{3,0},{4,7},{5,6},{6,5},{7,4},{8,11},{9,10},{10,... | collective-permute-start | bytes 393224 | tf_op jit(solution)/shard_map/ppermute | solution.py:519
  47.0 10.6 %collective-permute-start.12 = (bf16[512,128]{1,0:T(8,128)(2,1)S(1)}, bf16[512,128]{1,0:T(8,128)(2,1)S(1)}, u32[]{:S(2)}, u32[]{:S(2)}) collective-permute-start(bf16[512,128]{1,0:T(8,128)(2,1)S(1)} %total_of.1.refs_0_), channel_id=1, source_target_pairs={{0,2},{1,3},{2,0},{3,1},{4,6},{5,7},{6,4},{7,5},{8,10},{9,11},{10,... | collective-permute-start | bytes 393224 | tf_op jit(solution)/shard_map/ppermute | solution.py:519
  62.7 6.8 %collective-permute-start.15 = (bf16[576,128]{1,0:T(8,128)(2,1)S(1)}, bf16[576,128]{1,0:T(8,128)(2,1)S(1)}, u32[]{:S(2)}, u32[]{:S(2)}) collective-permute-start(bf16[576,128]{1,0:T(8,128)(2,1)S(1)} %get-tuple-element.44), channel_id=1, source_target_pairs={{0,8},{4,12},{8,0},{12,4},{16,24},{20,28},{24,16},{28,20},{1,9},{5... | collective-permute-start | bytes 442376 | tf_op jit(solution)/shard_map/ppermute | solution.py:513
  63.0 9.0 %collective-permute-start.16 = (bf16[576,128]{1,0:T(8,128)(2,1)S(1)}, bf16[576,128]{1,0:T(8,128)(2,1)S(1)}, u32[]{:S(2)}, u32[]{:S(2)}) collective-permute-start(bf16[576,128]{1,0:T(8,128)(2,1)S(1)} %get-tuple-element.45), channel_id=1, source_target_pairs={{0,16},{4,20},{8,24},{12,28},{16,0},{20,4},{24,8},{28,12},{1,17},{... | collective-permute-start | bytes 442376 | tf_op jit(solution)/shard_map/ppermute | solution.py:513
  63.0 9.0 %collective-permute-start.17 = (bf16[576,128]{1,0:T(8,128)(2,1)S(1)}, bf16[576,128]{1,0:T(8,128)(2,1)S(1)}, u32[]{:S(2)}, u32[]{:S(2)}) collective-permute-start(bf16[576,128]{1,0:T(8,128)(2,1)S(1)} %get-tuple-element.37), channel_id=1, source_target_pairs={{0,24},{4,28},{8,16},{12,20},{16,8},{20,12},{24,0},{28,4},{1,25},{... | collective-permute-start | bytes 442376 | tf_op jit(solution)/shard_map/ppermute | solution.py:513
  72.1 8.7 %collective-permute-start.20 = (bf16[576,128]{1,0:T(8,128)(2,1)S(1)}, bf16[576,128]{1,0:T(8,128)(2,1)S(1)}, u32[]{:S(2)}, u32[]{:S(2)}) collective-permute-start(bf16[576,128]{1,0:T(8,128)(2,1)S(1)} %gather_sum.1.refs_0_), channel_id=1, source_target_pairs={{0,3},{1,2},{2,1},{3,0},{4,7},{5,6},{6,5},{7,4},{8,11},{9,10},{10,... | collective-permute-start | bytes 442376 | tf_op jit(solution)/shard_map/ppermute | solution.py:519
  73.9 12.2 %collective-permute-start.19 = (bf16[576,128]{1,0:T(8,128)(2,1)S(1)}, bf16[576,128]{1,0:T(8,128)(2,1)S(1)}, u32[]{:S(2)}, u32[]{:S(2)}) collective-permute-start(bf16[576,128]{1,0:T(8,128)(2,1)S(1)} %gather_sum.1.refs_0_), channel_id=1, source_target_pairs={{0,2},{1,3},{2,0},{3,1},{4,6},{5,7},{6,4},{7,5},{8,10},{9,11},{10,... | collective-permute-start | bytes 442376 | tf_op jit(solution)/shard_map/ppermute | solution.py:519
  73.9 12.2 %collective-permute-start.18 = (bf16[576,128]{1,0:T(8,128)(2,1)S(1)}, bf16[576,128]{1,0:T(8,128)(2,1)S(1)}, u32[]{:S(2)}, u32[]{:S(2)}) collective-permute-start(bf16[576,128]{1,0:T(8,128)(2,1)S(1)} %gather_sum.1.refs_0_), channel_id=1, source_target_pairs={{0,1},{1,0},{2,3},{3,2},{4,5},{5,4},{6,7},{7,6},{8,9},{9,8},{10,11... | collective-permute-start | bytes 442376 | tf_op jit(solution)/shard_map/ppermute | solution.py:519
  86.3 8.2 %collective-permute-start.23 = (bf16[576,128]{1,0:T(8,128)(2,1)S(1)}, bf16[576,128]{1,0:T(8,128)(2,1)S(1)}, u32[]{:S(2)}, u32[]{:S(2)}) collective-permute-start(bf16[576,128]{1,0:T(8,128)(2,1)S(1)} %get-tuple-element.49), channel_id=1, source_target_pairs={{0,0},{4,16},{8,4},{12,20},{16,8},{20,24},{24,12},{28,28},{1,1},{5... | collective-permute-start | bytes 442376 | tf_op jit(solution)/shard_map/ppermute | solution.py:568
  86.9 10.2 %collective-permute-start.24 = (bf16[576,128]{1,0:T(8,128)(2,1)S(1)}, bf16[576,128]{1,0:T(8,128)(2,1)S(1)}, u32[]{:S(2)}, u32[]{:S(2)}) collective-permute-start(bf16[576,128]{1,0:T(8,128)(2,1)S(1)} %get-tuple-element.50), channel_id=1, source_target_pairs={{0,4},{4,20},{8,0},{12,16},{16,12},{20,28},{24,8},{28,24},{1,5},{5... | collective-permute-start | bytes 442376 | tf_op jit(solution)/shard_map/ppermute | solution.py:568
  89.7 9.2 %collective-permute-start.21 = (bf16[576,128]{1,0:T(8,128)(2,1)S(1)}, bf16[576,128]{1,0:T(8,128)(2,1)S(1)}, u32[]{:S(2)}, u32[]{:S(2)}) collective-permute-start(bf16[576,128]{1,0:T(8,128)(2,1)S(1)} %get-tuple-element.47), channel_id=1, source_target_pairs={{0,8},{4,24},{8,12},{12,28},{16,0},{20,16},{24,4},{28,20},{1,9},{5... | collective-permute-start | bytes 442376 | tf_op jit(solution)/shard_map/ppermute | solution.py:568
  90.0 9.3 %collective-permute-start.22 = (bf16[576,128]{1,0:T(8,128)(2,1)S(1)}, bf16[576,128]{1,0:T(8,128)(2,1)S(1)}, u32[]{:S(2)}, u32[]{:S(2)}) collective-permute-start(bf16[576,128]{1,0:T(8,128)(2,1)S(1)} %get-tuple-element.48), channel_id=1, source_target_pairs={{0,12},{4,28},{8,8},{12,24},{16,4},{20,20},{24,0},{28,16},{1,13},{... | collective-permute-start | bytes 442376 | tf_op jit(solution)/shard_map/ppermute | solution.py:568
  (9 other events, 170.9 us)

commit v7 on v6

--- a/solution.py
+++ b/solution.py
@@ -44,6 +44,10 @@
 
 def in_vmem(array):
     return pltpu.with_memory_space_constraint(array, pltpu.VMEM)
+
+
+def in_hbm(array):
+    return pltpu.with_memory_space_constraint(array, pltpu.HBM)
 
 
 def call(body, operands, outs, scalars=(), scratch=(), vmem=(), mib=12, estimate=None, name=None):
@@ -72,44 +76,60 @@
     return jax.ShapeDtypeStruct(array.shape, dtype or array.dtype)
 
 
-def reorder_body(order_ref, feat_ref, *outs):
+def reorder_body(order_ref, feat_ref, out_ref, *, first):
     panel = feat_ref.shape[0]
-    rows = outs[0].shape[0]
+    rows = out_ref.shape[0]
     step = min(256, rows)
-    for i in range(panel // step):
+    for i in range(first // step, (first + rows) // step):
         hot = lax.broadcasted_iota(jnp.int32, (step, panel), 1) == order_ref[pl.ds(i * step, step), :]
         hot = jnp.where(hot, 1.0, 0.0).astype(BF16)
-        at = i * step % rows
-        outs[i * step // rows][at : at + step, :] = jnp.dot(
+        at = i * step - first
+        out_ref[at : at + step, :] = jnp.dot(
             hot, feat_ref[...], preferred_element_type=F32
         ).astype(BF16)
 
 
-def reorder(order_col, features):
+def reorder(order_col, features, half):
     panel, width = features.shape
-    outs = [jax.ShapeDtypeStruct((panel // HALVES, width), BF16)] * HALVES
+    rows = panel // HALVES
     return call(
-        reorder_body,
+        functools.partial(reorder_body, first=half * rows),
         [order_col, features],
-        outs,
-        estimate=cost(2 * panel * panel * width, 4 * panel * width),
+        jax.ShapeDtypeStruct((rows, width), BF16),
+        estimate=cost(2 * rows * panel * width, 4 * rows * width),
         name="reorder",
     )
 
 
-def entry_body(rows_ref, cols_ref, _, out_ref, *, bits):
-    out_ref[...] = (rows_ref[0, 0] << bits) | cols_ref[0, 0]
-
-
-def entries_of(rows, cols, bits, after):
-    out = jax.ShapeDtypeStruct(rows.shape[2:], jnp.int32)
-    return call(
-        functools.partial(entry_body, bits=bits), [rows, cols, after], out, name="entries_of"
-    )
-
-
-def pick_body(*refs, near):
-    options, out_ref = refs[:-1], refs[-1]
+def entry_body(rows_ref, cols_ref, live_ref, _, out_ref, *, bits):
+    rounds, slots = rows_ref.shape[2:]
+    out_ref[:, :slots] = (rows_ref[0, 0] << bits) | cols_ref[0, 0]
+    for j in range(rounds):
+        out_ref[j : j + 1, slots:] = jnp.full((1, 1), live_ref[0, 0, j], jnp.int32)
+
+
+def entries_of(rows, cols, live, bits, after):
+    rounds, slots = rows.shape[2:]
+    shape = (rounds, slots + 1)
+    return pl.pallas_call(
+        functools.partial(entry_body, bits=bits),
+        out_shape=jax.ShapeDtypeStruct(shape, jnp.int32),
+        grid=(1,),
+        in_specs=[
+            whole_spec(rows),
+            whole_spec(cols),
+            pl.BlockSpec(memory_space=pltpu.SMEM),
+            whole_spec(after),
+        ],
+        out_specs=pl.BlockSpec(shape, lambda i: (0, 0)),
+        compiler_params=params(12),
+        cost_estimate=cost(0, MIB),
+        name="entries_of",
+    )(*map(in_hbm, (rows, cols, live)), after)
+
+
+def pick_body(*refs, near, count):
+    options, out_ref = refs[:count], refs[-1]
     place = Place()
     for n, option in enumerate(options):
 
@@ -118,12 +138,13 @@
             out_ref[...] = option[...]
 
 
-def pick(options, near):
-    return call(functools.partial(pick_body, near=near), options, like(options[0]), name="pick")
-
-
-def walk(live_ref, entry_ref, j, slots, step):
-    count = live_ref[j]
+def pick(options, near, after):
+    body = functools.partial(pick_body, near=near, count=len(options))
+    return call(body, [*options, *after], like(options[0]), name="pick")
+
+
+def walk(entry_ref, j, slots, step):
+    count = entry_ref[j, slots]
 
     @pl.loop(0, (count + GROUP - 1) // GROUP)
     def _(g):
@@ -132,7 +153,7 @@
         step(j * slots + g * GROUP, entries, alive)
 
 
-def forward_body(live_ref, entry_ref, tiles_ref, *refs, slots, pairs, last):
+def forward_body(entry_ref, tiles_ref, *refs, slots, pairs, last):
     place = Place()
     xs, rest = refs[: pairs * HALVES], refs[pairs * HALVES :]
     panel_ref, acc = rest[-2:]
@@ -159,7 +180,7 @@
                 acc[jnp.where(alive[t], entries[t] >> bits, blocks)] += terms[t]
 
         j = place.row ^ (2 * p + (1 - place.side if last else place.side))
-        walk(live_ref, entry_ref, j, slots, step)
+        walk(entry_ref, j, slots, step)
     if last:
         span = blocks // len(outs)
         for d, out in enumerate(outs):
@@ -181,13 +202,13 @@
     else:
         outs = [jax.ShapeDtypeStruct((blocks, block, width), F32)]
     body = functools.partial(
-        forward_body, slots=plan[1].shape[1], pairs=pairs, last=last
+        forward_body, slots=plan.shape[1] - 1, pairs=pairs, last=last
     )
     got = call(
         body,
         [tiles, *xs] + ([start] if last else []),
         outs,
-        scalars=plan,
+        scalars=(plan,),
         scratch=[pltpu.VMEM((blocks, block, width), BF16), pltpu.VMEM((blocks + 1, block, width), F32)],
         vmem=(0,),
         estimate=cost(2 * 64 * block * block * width, 12 * MIB),
@@ -276,7 +297,7 @@
     return call(finish_body, [weight, *shares], outs, estimate=cost(0, 4 * MIB), name="finish")
 
 
-def backward_body(live_ref, entry_ref, tiles_ref, *refs, slots, keep, shape):
+def backward_body(entry_ref, tiles_ref, *refs, slots, keep, shape):
     refs, (out_ref, up_all, acc) = refs[:-3], refs[-3:]
     ups = refs if keep else refs[:-1]
     place = Place()
@@ -306,7 +327,7 @@
                 acc[jnp.where(alive[t], entries[t] & (blocks - 1), blocks)] += terms[t]
 
         core = place.core
-        walk(live_ref, entry_ref, 2 * p + (core if keep else 1 - core), slots, step)
+        walk(entry_ref, 2 * p + (core if keep else 1 - core), slots, step)
         for h in range(cuts):
             for d in range(chips):
                 at = ((place.chip ^ d) * cuts + h) * per
@@ -326,10 +347,10 @@
     keep = term is None
     out_shape = (pairs * blocks + (0 if keep else 2), width, block)
     return call(
-        functools.partial(backward_body, slots=plan[1].shape[1], keep=keep, shape=shape),
+        functools.partial(backward_body, slots=plan.shape[1] - 1, keep=keep, shape=shape),
         [tiles, *ups] + ([] if keep else [term]),
         jax.ShapeDtypeStruct(out_shape, F32 if keep else BF16),
-        scalars=plan,
+        scalars=(plan,),
         scratch=[pltpu.VMEM((width, panel), BF16), pltpu.VMEM((blocks + 1, width, block), F32)],
         vmem=(0,),
         estimate=cost(2 * 64 * block * block * width, 12 * MIB),
@@ -407,7 +428,7 @@
 
 
 def route_body(*refs, reps, chips, rows, pairs):
-    spread, outs = refs[:reps], refs[reps:]
+    spread, outs = refs[:reps], refs[reps + 1 :]
     place = Place()
     each = rows // pairs
     extra = (spread[0].shape[0] - rows) // 2
@@ -427,70 +448,97 @@
             outs[k][each + extra : each + 2 * extra, :] = low
 
 
-def route(spread, chips, rows, pairs):
+def route(spread, after, chips, rows, pairs):
     height, width = spread[0].shape
     outs = [jax.ShapeDtypeStruct((height - rows + rows // pairs, width), BF16)] * chips
     body = functools.partial(route_body, reps=len(spread), chips=chips, rows=rows, pairs=pairs)
-    return call(body, spread, outs, name="route")
-
-
-def restore_body(order_ref, *refs, first, count, per, scale, reps):
+    return call(body, [*spread, after], outs, name="route")
+
+
+def hot_body(order_ref, _, out_ref, token_ref):
+    panel = out_ref.shape[0]
+    rows = 256
+    target = order_ref[...]
+    token_ref[...] = jnp.zeros_like(token_ref)
+
+    @pl.loop(0, panel // rows)
+    def _(i):
+        at = pl.multiple_of(i * rows, rows)
+        hot = lax.broadcasted_iota(jnp.int32, (rows, panel), 0) + at == target
+        out_ref[pl.ds(at, rows), :] = jnp.where(hot, 1.0, 0.0).astype(BF16)
+
+
+def inverse_hot(order_row, after):
+    panel = order_row.shape[1]
+    return pl.pallas_call(
+        hot_body,
+        out_shape=(
+            pltpu.VMEM((panel, panel), BF16),
+            jax.ShapeDtypeStruct((8, 128), jnp.int32),
+        ),
+        grid=(1,),
+        in_specs=[whole_spec(order_row), pl.BlockSpec(memory_space=pl.ANY)],
+        out_specs=(
+            pl.BlockSpec(memory_space=pltpu.VMEM),
+            pl.BlockSpec((8, 128), lambda i: (0, 0)),
+        ),
+        compiler_params=params(8),
+        cost_estimate=cost(0, 6 * MIB),
+        name="inverse_hot",
+    )(order_row, after)
+
+
+def restore_body(hot_ref, *refs, first, count, per, scale, reps):
     parts, refs = refs[:count], refs[count:]
     start, (out_ref, grad_ref) = refs[:-2], refs[-2:]
     section = lax.axis_index("section")
     base_u = (section // reps // 2) * reps + section % reps
-    rows = out_ref.shape[0]
     block = parts[0].shape[1]
-    step = pl.program_id(0)
-    acc = start[0][...] if start else None
-
-    @pl.when(step == 0)
-    def _():
-        grad_ref[...] = start[1][...] if start else jnp.zeros_like(grad_ref)
-        extra = (parts[0].shape[0] - per * block) // 2
-        for n, part in enumerate(parts):
-            at = pl.multiple_of((base_u ^ (first + n)) * extra, extra)
-            grad_ref[pl.ds(at, extra), :] = sum_of_parts(part, per * block, extra) * scale
-
+    extra = (parts[0].shape[0] - per * block) // 2
+    length = per * block
+    grad_ref[...] = start[1][...] if start else jnp.zeros_like(grad_ref)
+    columns, places = [], []
     for n, part in enumerate(parts):
-        length = per * block
-        at = pl.multiple_of((base_u ^ (first + n)) * length, length)
-        target = order_ref[:, pl.ds(at, length)]
-        hot = lax.broadcasted_iota(jnp.int32, (rows, length), 0) + step * rows == target
-        hot = jnp.where(hot, 1.0, 0.0).astype(BF16)
-        columns = jnp.concatenate(
-            [part[b * block : (b + 1) * block, :] for b in range(per)], axis=1
+        u = base_u ^ (first + n)
+        at = pl.multiple_of(u * extra, extra)
+        grad_ref[pl.ds(at, extra), :] = sum_of_parts(part, length, extra) * scale
+        columns.append(
+            jnp.concatenate([part[b * block : (b + 1) * block, :] for b in range(per)], axis=1)
         )
-        term = lax.dot_general(
-            hot, columns, (((1,), (1,)), ((), ())), preferred_element_type=F32
-        )
-        acc = term if acc is None else acc + term
-    out_ref[...] = acc.astype(out_ref.dtype)
-
-
-def restore(order_row, parts, first, start, per, scale, reps):
-    panel = order_row.shape[1]
+        places.append(pl.multiple_of(u * length, length))
+    rows = 512
+    for i in range(out_ref.shape[0] // rows):
+        span = slice(i * rows, (i + 1) * rows)
+        acc = start[0][span, :] if start else None
+        for n, at in enumerate(places):
+            term = lax.dot_general(
+                hot_ref[span, pl.ds(at, length)],
+                columns[n],
+                (((1,), (1,)), ((), ())),
+                preferred_element_type=F32,
+            )
+            acc = term if acc is None else acc + term
+        out_ref[span, :] = acc.astype(out_ref.dtype)
+
+
+def restore(hot, parts, first, start, per, scale, reps):
+    panel = hot.shape[0]
     width = parts[0].shape[1]
-    rows = 512
-    row_spec = pl.BlockSpec((rows, width), lambda i: (i, 0))
-    grad_spec = pl.BlockSpec((width, width), lambda i: (0, 0))
     body = functools.partial(
         restore_body, first=first, count=len(parts), per=per, scale=scale, reps=reps
     )
-    return pl.pallas_call(
+    outs = (
+        jax.ShapeDtypeStruct((panel, width), BF16 if start else F32),
+        jax.ShapeDtypeStruct((width, width), F32),
+    )
+    return call(
         body,
-        out_shape=(
-            jax.ShapeDtypeStruct((panel, width), BF16 if start else F32),
-            jax.ShapeDtypeStruct((width, width), F32),
-        ),
-        grid=(panel // rows,),
-        in_specs=[whole_spec(x) for x in (order_row, *parts)]
-        + ([row_spec, grad_spec] if start else []),
-        out_specs=(row_spec, grad_spec),
-        compiler_params=params(24),
-        cost_estimate=cost(2 * panel * panel * width, 4 * panel * width),
+        [hot, *parts, *start],
+        outs,
+        vmem=(0,),
+        estimate=cost(2 * panel * panel * width, 4 * panel * width),
         name="restore",
-    )(order_row, *parts, *start)
+    )
 
 
 def tree_sum(terms):
@@ -527,17 +575,18 @@
                 moves.append((source * reps + r, target * reps + r))
         return lax.ppermute(x, ("section", "rep"), moves)
 
-    order_row = order.reshape(1, panel)
-    owns = reorder(order.reshape(panel, 1), features)
+    order_col, order_row = order.reshape(panel, 1), order.reshape(1, panel)
+    owns = [reorder(order_col, features, h) for h in range(HALVES)]
     gots = [[own] + [from_owner(own, d) for d in range(1, chips)] for own in owns]
     bits = (blocks - 1).bit_length()
-    plan = (live.reshape(rounds), entries_of(tile_rows, tile_cols, bits, owns[-1][:16]))
+    plan = entries_of(tile_rows, tile_cols, live, bits, owns[-1][:16])
     own_tiles = tiles.reshape(rounds * slots, block, block)
 
     mine, mate = [], []
     for p in range(pairs):
         for h in range(HALVES):
-            picked = pick(gots[h][2 * p * near : 2 * (p + 1) * near], near)
+            first = 2 * p * near
+            picked = pick(gots[h][first : first + 2 * near], near, [] if h else [plan])
             mine.append(picked)
             mate.append(over_cores(picked))
 
@@ -568,11 +617,13 @@
         return lax.ppermute(block, "section", moves)
 
     spread = [reduced] + [over_reps(reduced, d) for d in range(1, reps)]
-    parts = [to_owner(block, k) for k, block in enumerate(route(spread, chips, height, pairs))]
+    hot, ready = inverse_hot(order_row, reduced)
+    routed = route(spread, ready, chips, height, pairs)
+    parts = [to_owner(block, k) for k, block in enumerate(routed)]
     scale = 1.0 / math.sqrt(panel * sections)
     half = chips // 2
-    begun = restore(order_row, parts[:half], 0, (), per, scale, reps)
-    feature_grad, weight_grad = restore(order_row, parts[half:], half, begun, per, scale, reps)
+    begun = restore(hot, parts[:half], 0, (), per, scale, reps)
+    feature_grad, weight_grad = restore(hot, parts[half:], half, begun, per, scale, reps)
     return (hidden, weight_grad, feature_grad)
 
 

time: 102 us -> 99.7 us (0.977)
  Pallas kernels: 18.5 us -> 16.5 us
    pallas_call x2, Pallas kernels: 4.57 us -> 2.26 us  [the longest x1 1.46 us: inverse_hot(): pl.pallas_call(hot_body, out_shape=(pltpu.VMEM((panel, panel), BF16), jax...]
    ppermute x6, waiting for transfers between devices: 5.58 us -> 3.41 us  [from_owner(): return lax.ppermute(x, ('section', 'rep'), moves)]
    ppermute x3, waiting for transfers between devices: 4.52 us -> 6.07 us  [over_chips(): return lax.ppermute(x, 'section', [(s, s ^ 2 * d) for s in range(sections)])]
    ppermute x3, waiting for transfers between devices: 0.01 us -> 1.4 us  [over_cores(): return lax.ppermute(x, 'section', [(s, s ^ 1) for s in range(sections)])]
    ppermute x9, waiting for transfers between devices: 28.7 us -> 27.5 us  [over_reps(): return lax.ppermute(x, 'rep', [(r, r ^ d) for r in range(reps)])]
    pallas_call x15 -> x17, Pallas kernels: 13.9 us -> 14.2 us  [call(): pl.pallas_call(body, out_shape=outs, grid_spec=pltpu.PrefetchScalarGridSp...]
  transfers between devices with their start and end apart: 25 -> 25, of which waited for: 14 -> 16; matrix products, arithmetic and copies ran while one was open for 0% -> 0% of each run, Pallas kernels for 8% -> 9%
where the time goes in v7:
time: 99.7 us; the launch traced here: 99.9 us
  waiting for transfers between devices  42.1 us (42%)
  starting transfers between devices  38.2 us (38%)
  Pallas kernels  16.5 us (17%)
  local copies, waits for them, and re-layouts  2.12 us (2%)
    ppermute x9, waiting for transfers between devices, over_reps(): return lax.ppermute(x, 'rep', [(r, r ^ d) for r in range(reps)])  27.5 us
    ppermute x9, starting transfers between devices, over_reps(): return lax.ppermute(x, 'rep', [(r, r ^ d) for r in range(reps)])  15.1 us
    pallas_call x17, Pallas kernels, call(): pl.pallas_call(body, out_shape=outs, grid_spec=pltpu.PrefetchScalarGridSp...  14.2 us
    ppermute x6, starting transfers between devices, from_owner(): return lax.ppermute(x, ('section', 'rep'), moves)  11.9 us
    ppermute x4, starting transfers between devices, to_owner(): return lax.ppermute(block, 'section', moves)  7.29 us
    ppermute x3, waiting for transfers between devices, over_chips(): return lax.ppermute(x, 'section', [(s, s ^ 2 * d) for s in range(sections)])  6.07 us
    ppermute x4, waiting for transfers between devices, to_owner(): return lax.ppermute(block, 'section', moves)  3.74 us
    ppermute x3, starting transfers between devices, over_chips(): return lax.ppermute(x, 'section', [(s, s ^ 2 * d) for s in range(sections)])  3.68 us
  transfers between devices with their start and end apart: 25, of which 16 were waited for; matrix products, arithmetic and copies ran while one was open for 0% of the time, Pallas kernels for 9%

profile of v7, /device:TPU:0, one launch (start us, length us, event | category | flops | bytes accessed | tf_op | source)
XLA Modules:
  0.0 99.9 jit_solution(6697424732443012085)
XLA Ops:
  4.1 5.4 %collective-permute-start.2 = (bf16[1024,128]{1,0:T(8,128)(2,1)S(1)}, bf16[1024,128]{1,0:T(8,128)(2,1)S(1)}, u32[]{:S(2)}, u32[]{:S(2)}) collective-permute-start(bf16[1024,128]{1,0:T(8,128)(2,1)S(1)} %reorder.3.refs_0_), channel_id=1, source_target_pairs={{0,28},{16,12},{5,25},{21,9},{10,22},{26,6},{15,19},{31,3}} | collective-permute-start | bytes 786440 | tf_op jit(solution)/shard_map/ppermute | solution.py:576
  19.9 1.9 %collective-permute-done.4.refs_1_ = bf16[1024,128]{1,0:T(8,128)(2,1)S(1)} collective-permute-done((bf16[1024,128]{1,0:T(8,128)(2,1)S(1)}, bf16[1024,128]{1,0:T(8,128)(2,1)S(1)}, u32[]{:S(2)}, u32[]{:S(2)}) %collective-permute-start.4) | collective-permute-done | bytes 262176 | tf_op jit(solution)/shard_map/ppermute | solution.py:576
  23.4 1.6 %forward.3 = (f32[512,128]{1,0:T(8,128)S(1)}, bf16[512,128]{1,0:T(8,128)(2,1)S(1)}, bf16[512,128]{1,0:T(8,128)(2,1)S(1)}, bf16[512,128]{1,0:T(8,128)(2,1)S(1)}) custom-call(s32[2,97]{1,0:T(2,128)S(1)} %entries_of.1.refs_4_.entry_ref, bf16[192,128,128]{2,1,0:T(8,128)(2,1)S(1)} %bitcast.4, bf16[1024,128]{1,0:T(8,128)(2,1)S(1)} %collective-permute-done.3.refs_0_, ...), custom_call_target="tpu_custom_call" | custom-call | flops 268435456 | bytes 12582912 | tf_op jit(solution)/shard_map/forward/pallas_call | solution.py:59
  25.0 2.2 %collective-permute-start.8 = (bf16[512,128]{1,0:T(8,128)(2,1)S(1)}, bf16[512,128]{1,0:T(8,128)(2,1)S(1)}, u32[]{:S(2)}, u32[]{:S(2)}) collective-permute-start(bf16[512,128]{1,0:T(8,128)(2,1)S(1)} %get-tuple-element.30), channel_id=1, source_target_pairs={{0,1},{1,0},{2,3},{3,2},{4,5},{5,4},{6,7},{7,6},{8,9},{9,8},{10,11... | collective-permute-start | bytes 393224 | tf_op jit(solution)/shard_map/ppermute | solution.py:567
  27.3 2.7 %collective-permute-start.9 = (bf16[512,128]{1,0:T(8,128)(2,1)S(1)}, bf16[512,128]{1,0:T(8,128)(2,1)S(1)}, u32[]{:S(2)}, u32[]{:S(2)}) collective-permute-start(bf16[512,128]{1,0:T(8,128)(2,1)S(1)} %get-tuple-element.31), channel_id=1, source_target_pairs={{0,2},{1,3},{2,0},{3,1},{4,6},{5,7},{6,4},{7,5},{8,10},{9,11},{10,... | collective-permute-start | bytes 393224 | tf_op jit(solution)/shard_map/ppermute | solution.py:567
  30.0 4.2 %collective-permute-done.8.refs_0_ = bf16[512,128]{1,0:T(8,128)(2,1)S(1)} collective-permute-done((bf16[512,128]{1,0:T(8,128)(2,1)S(1)}, bf16[512,128]{1,0:T(8,128)(2,1)S(1)}, u32[]{:S(2)}, u32[]{:S(2)}) %collective-permute-start.8) | collective-permute-done | bytes 131104 | tf_op jit(solution)/shard_map/ppermute | solution.py:567
  34.2 5.7 %collective-permute-done.9.refs_1_ = bf16[512,128]{1,0:T(8,128)(2,1)S(1)} collective-permute-done((bf16[512,128]{1,0:T(8,128)(2,1)S(1)}, bf16[512,128]{1,0:T(8,128)(2,1)S(1)}, u32[]{:S(2)}, u32[]{:S(2)}) %collective-permute-start.9) | collective-permute-done | bytes 131104 | tf_op jit(solution)/shard_map/ppermute | solution.py:567
  39.9 2.6 %collective-permute-start.11 = (bf16[512,128]{1,0:T(8,128)(2,1)S(1)}, bf16[512,128]{1,0:T(8,128)(2,1)S(1)}, u32[]{:S(2)}, u32[]{:S(2)}) collective-permute-start(bf16[512,128]{1,0:T(8,128)(2,1)S(1)} %total_of.1.refs_0_), channel_id=1, source_target_pairs={{0,1},{1,0},{2,3},{3,2},{4,5},{5,4},{6,7},{7,6},{8,9},{9,8},{10,11... | collective-permute-start | bytes 393224 | tf_op jit(solution)/shard_map/ppermute | solution.py:567
  42.5 3.2 %collective-permute-start.13 = (bf16[512,128]{1,0:T(8,128)(2,1)S(1)}, bf16[512,128]{1,0:T(8,128)(2,1)S(1)}, u32[]{:S(2)}, u32[]{:S(2)}) collective-permute-start(bf16[512,128]{1,0:T(8,128)(2,1)S(1)} %total_of.1.refs_0_), channel_id=1, source_target_pairs={{0,3},{1,2},{2,1},{3,0},{4,7},{5,6},{6,5},{7,4},{8,11},{9,10},{10,... | collective-permute-start | bytes 393224 | tf_op jit(solution)/shard_map/ppermute | solution.py:567
  46.4 6.5 %collective-permute-done.13.refs_1_.refs_3_ = bf16[512,128]{1,0:T(8,128)(2,1)S(1)} collective-permute-done((bf16[512,128]{1,0:T(8,128)(2,1)S(1)}, bf16[512,128]{1,0:T(8,128)(2,1)S(1)}, u32[]{:S(2)}, u32[]{:S(2)}) %collective-permute-start.13) | collective-permute-done | bytes 131104 | tf_op jit(solution)/shard_map/ppermute | solution.py:567
  52.9 3.6 %collective-permute-done.12.refs_0_.refs_2_ = bf16[512,128]{1,0:T(8,128)(2,1)S(1)} collective-permute-done((bf16[512,128]{1,0:T(8,128)(2,1)S(1)}, bf16[512,128]{1,0:T(8,128)(2,1)S(1)}, u32[]{:S(2)}, u32[]{:S(2)}) %collective-permute-start.12) | collective-permute-done | bytes 131104 | tf_op jit(solution)/shard_map/ppermute | solution.py:567
  57.0 1.7 %backward.3 = bf16[18,128,128]{2,1,0:T(8,128)(2,1)S(1)} custom-call(s32[2,97]{1,0:T(2,128)S(1)} %entries_of.1.refs_4_.entry_ref, bf16[192,128,128]{2,1,0:T(8,128)(2,1)S(1)} %bitcast.5, bf16[2,128,512]{2,1,0:T(8,128)(2,1)S(1)} %get-tuple-element.33.refs_0_, bf16[2,128,512]{2,1,0:T(8,128)(2,1)S(1)} %up_shares.3.refs_1_, ...), custom_call_target="tpu_custom_call" | custom-call | flops 268435456 | bytes 12582912 | tf_op jit(solution)/shard_map/backward/pallas_call | solution.py:59
  60.9 2.1 %collective-permute-start.15 = (bf16[576,128]{1,0:T(8,128)(2,1)S(1)}, bf16[576,128]{1,0:T(8,128)(2,1)S(1)}, u32[]{:S(2)}, u32[]{:S(2)}) collective-permute-start(bf16[576,128]{1,0:T(8,128)(2,1)S(1)} %get-tuple-element.42), channel_id=1, source_target_pairs={{0,8},{4,12},{8,0},{12,4},{16,24},{20,28},{24,16},{28,20},{1,9},{5... | collective-permute-start | bytes 442376 | tf_op jit(solution)/shard_map/ppermute | solution.py:561
  63.2 1.4 %collective-permute-start.17 = (bf16[576,128]{1,0:T(8,128)(2,1)S(1)}, bf16[576,128]{1,0:T(8,128)(2,1)S(1)}, u32[]{:S(2)}, u32[]{:S(2)}) collective-permute-start(bf16[576,128]{1,0:T(8,128)(2,1)S(1)} %get-tuple-element.35), channel_id=1, source_target_pairs={{0,24},{4,28},{8,16},{12,20},{16,8},{20,12},{24,0},{28,4},{1,25},{... | collective-permute-start | bytes 442376 | tf_op jit(solution)/shard_map/ppermute | solution.py:561
  65.8 1.8 %collective-permute-done.15.refs_1_ = bf16[576,128]{1,0:T(8,128)(2,1)S(1)} collective-permute-done((bf16[576,128]{1,0:T(8,128)(2,1)S(1)}, bf16[576,128]{1,0:T(8,128)(2,1)S(1)}, u32[]{:S(2)}, u32[]{:S(2)}) %collective-permute-start.15) | collective-permute-done | bytes 147488 | tf_op jit(solution)/shard_map/ppermute | solution.py:561
  67.6 4.3 %collective-permute-done.16.refs_2_ = bf16[576,128]{1,0:T(8,128)(2,1)S(1)} collective-permute-done((bf16[576,128]{1,0:T(8,128)(2,1)S(1)}, bf16[576,128]{1,0:T(8,128)(2,1)S(1)}, u32[]{:S(2)}, u32[]{:S(2)}) %collective-permute-start.16) | collective-permute-done | bytes 147488 | tf_op jit(solution)/shard_map/ppermute | solution.py:561
  73.1 3.3 %collective-permute-start.18 = (bf16[576,128]{1,0:T(8,128)(2,1)S(1)}, bf16[576,128]{1,0:T(8,128)(2,1)S(1)}, u32[]{:S(2)}, u32[]{:S(2)}) collective-permute-start(bf16[576,128]{1,0:T(8,128)(2,1)S(1)} %gather_sum.1._.refs_0_), channel_id=1, source_target_pairs={{0,1},{1,0},{2,3},{3,2},{4,5},{5,4},{6,7},{7,6},{8,9},{9,8},{10,11... | collective-permute-start | bytes 442376 | tf_op jit(solution)/shard_map/ppermute | solution.py:567
  76.4 1.5 %inverse_hot.1 = (bf16[2048,2048]{1,0:T(8,128)(2,1)S(1)}, s32[8,128]{1,0:T(8,128)S(1)}) custom-call(s32[1,2048]{1,0:T(1,128)S(1)} %bitcast.8, bf16[576,128]{1,0:T(8,128)(2,1)S(1)} %gather_sum.1._.refs_0_), custom_call_target="tpu_custom_call" | custom-call | bytes 6291456 | tf_op jit(solution)/shard_map/inverse_hot/pallas_call | solution.py:473
  77.9 2.7 %collective-permute-done.20.refs_3_ = bf16[576,128]{1,0:T(8,128)(2,1)S(1)} collective-permute-done((bf16[576,128]{1,0:T(8,128)(2,1)S(1)}, bf16[576,128]{1,0:T(8,128)(2,1)S(1)}, u32[]{:S(2)}, u32[]{:S(2)}) %collective-permute-start.20) | collective-permute-done | bytes 147488 | tf_op jit(solution)/shard_map/ppermute | solution.py:567
  80.6 4.8 %collective-permute-done.19.refs_2_ = bf16[576,128]{1,0:T(8,128)(2,1)S(1)} collective-permute-done((bf16[576,128]{1,0:T(8,128)(2,1)S(1)}, bf16[576,128]{1,0:T(8,128)(2,1)S(1)}, u32[]{:S(2)}, u32[]{:S(2)}) %collective-permute-start.19) | collective-permute-done | bytes 147488 | tf_op jit(solution)/shard_map/ppermute | solution.py:567
  86.2 1.9 %collective-permute-start.24 = (bf16[576,128]{1,0:T(8,128)(2,1)S(1)}, bf16[576,128]{1,0:T(8,128)(2,1)S(1)}, u32[]{:S(2)}, u32[]{:S(2)}) collective-permute-start(bf16[576,128]{1,0:T(8,128)(2,1)S(1)} %get-tuple-element.50), channel_id=1, source_target_pairs={{0,4},{4,20},{8,0},{12,16},{16,12},{20,28},{24,8},{28,24},{1,5},{5... | collective-permute-start | bytes 442376 | tf_op jit(solution)/shard_map/ppermute | solution.py:617
  88.5 4.3 %collective-permute-start.22 = (bf16[576,128]{1,0:T(8,128)(2,1)S(1)}, bf16[576,128]{1,0:T(8,128)(2,1)S(1)}, u32[]{:S(2)}, u32[]{:S(2)}) collective-permute-start(bf16[576,128]{1,0:T(8,128)(2,1)S(1)} %get-tuple-element.48), channel_id=1, source_target_pairs={{0,12},{4,28},{8,8},{12,24},{16,4},{20,20},{24,0},{28,16},{1,13},{... | collective-permute-start | bytes 442376 | tf_op jit(solution)/shard_map/ppermute | solution.py:617
  92.9 3.0 %collective-permute-done.24.refs_1_ = bf16[576,128]{1,0:T(8,128)(2,1)S(1)} collective-permute-done((bf16[576,128]{1,0:T(8,128)(2,1)S(1)}, bf16[576,128]{1,0:T(8,128)(2,1)S(1)}, u32[]{:S(2)}, u32[]{:S(2)}) %collective-permute-start.24) | collective-permute-done | bytes 147488 | tf_op jit(solution)/shard_map/ppermute | solution.py:617
  97.9 2.0 %restore.3 = (bf16[2048,128]{1,0:T(8,128)(2,1)}, f32[128,128]{1,0:T(8,128)}) custom-call(bf16[2048,2048]{1,0:T(8,128)(2,1)S(1)} %get-tuple-element.45.hot_ref, bf16[576,128]{1,0:T(8,128)(2,1)S(1)} %collective-permute-done.21.refs_0_, bf16[576,128]{1,0:T(8,128)(2,1)S(1)} %collective-permute-done.22.refs_1_, f32[2048,128]{1,0:T(8,128)S(1)} %get-tuple-element.51.refs_2_, ...), custom_call_target="tpu_custom_call" | custom-call | flops 1073741824 | bytes 1048576 | tf_op jit(solution)/shard_map/restore/pallas_call | solution.py:59
  (57 shorter events, 24.7 us)
Async XLA Ops:
  4.1 12.0 %collective-permute-start.2 = (bf16[1024,128]{1,0:T(8,128)(2,1)S(1)}, bf16[1024,128]{1,0:T(8,128)(2,1)S(1)}, u32[]{:S(2)}, u32[]{:S(2)}) collective-permute-start(bf16[1024,128]{1,0:T(8,128)(2,1)S(1)} %reorder.3.refs_0_), channel_id=1, source_target_pairs={{0,28},{16,12},{5,25},{21,9},{10,22},{26,6},{15,19},{31,3}} | collective-permute-start | bytes 786440 | tf_op jit(solution)/shard_map/ppermute | solution.py:576
  9.4 8.7 %collective-permute-start.1 = (bf16[1024,128]{1,0:T(8,128)(2,1)S(1)}, bf16[1024,128]{1,0:T(8,128)(2,1)S(1)}, u32[]{:S(2)}, u32[]{:S(2)}) collective-permute-start(bf16[1024,128]{1,0:T(8,128)(2,1)S(1)} %reorder.3.refs_0_), channel_id=1, source_target_pairs={{0,20},{16,4},{5,17},{21,1},{10,30},{26,14},{15,27},{31,11}} | collective-permute-start | bytes 786440 | tf_op jit(solution)/shard_map/ppermute | solution.py:576
  10.8 7.4 %collective-permute-start = (bf16[1024,128]{1,0:T(8,128)(2,1)S(1)}, bf16[1024,128]{1,0:T(8,128)(2,1)S(1)}, u32[]{:S(2)}, u32[]{:S(2)}) collective-permute-start(bf16[1024,128]{1,0:T(8,128)(2,1)S(1)} %reorder.3.refs_0_), channel_id=1, source_target_pairs={{0,8},{16,24},{5,13},{21,29},{10,2},{26,18},{15,7},{31,23}} | collective-permute-start | bytes 786440 | tf_op jit(solution)/shard_map/ppermute | solution.py:576
  13.4 5.5 %collective-permute-start.6 = (bf16[1024,128]{1,0:T(8,128)(2,1)S(1)}, bf16[1024,128]{1,0:T(8,128)(2,1)S(1)}, u32[]{:S(2)}, u32[]{:S(2)}) collective-permute-start(bf16[1024,128]{1,0:T(8,128)(2,1)S(1)} %reorder.2.refs_0_), channel_id=1, source_target_pairs={{0,28},{16,12},{5,25},{21,9},{10,22},{26,6},{15,19},{31,3}} | collective-permute-start | bytes 786440 | tf_op jit(solution)/shard_map/ppermute | solution.py:576
  14.7 5.2 %collective-permute-start.5 = (bf16[1024,128]{1,0:T(8,128)(2,1)S(1)}, bf16[1024,128]{1,0:T(8,128)(2,1)S(1)}, u32[]{:S(2)}, u32[]{:S(2)}) collective-permute-start(bf16[1024,128]{1,0:T(8,128)(2,1)S(1)} %reorder.2.refs_0_), channel_id=1, source_target_pairs={{0,20},{16,4},{5,17},{21,1},{10,30},{26,14},{15,27},{31,11}} | collective-permute-start | bytes 786440 | tf_op jit(solution)/shard_map/ppermute | solution.py:576
  16.0 5.7 %collective-permute-start.4 = (bf16[1024,128]{1,0:T(8,128)(2,1)S(1)}, bf16[1024,128]{1,0:T(8,128)(2,1)S(1)}, u32[]{:S(2)}, u32[]{:S(2)}) collective-permute-start(bf16[1024,128]{1,0:T(8,128)(2,1)S(1)} %reorder.2.refs_0_), channel_id=1, source_target_pairs={{0,8},{16,24},{5,13},{21,29},{10,2},{26,18},{15,7},{31,23}} | collective-permute-start | bytes 786440 | tf_op jit(solution)/shard_map/ppermute | solution.py:576
  18.2 4.7 %collective-permute-start.3 = (bf16[1024,128]{1,0:T(8,128)(2,1)S(1)}, bf16[1024,128]{1,0:T(8,128)(2,1)S(1)}, u32[]{:S(2)}, u32[]{:S(2)}) collective-permute-start(bf16[1024,128]{1,0:T(8,128)(2,1)S(1)} %pick.2.refs_0_), channel_id=1, source_target_pairs={{0,4},{4,0},{8,12},{12,8},{16,20},{20,16},{24,28},{28,24},{1,5},{5... | collective-permute-start | bytes 786440 | tf_op jit(solution)/shard_map/ppermute | solution.py:564
  25.0 9.1 %collective-permute-start.8 = (bf16[512,128]{1,0:T(8,128)(2,1)S(1)}, bf16[512,128]{1,0:T(8,128)(2,1)S(1)}, u32[]{:S(2)}, u32[]{:S(2)}) collective-permute-start(bf16[512,128]{1,0:T(8,128)(2,1)S(1)} %get-tuple-element.30), channel_id=1, source_target_pairs={{0,1},{1,0},{2,3},{3,2},{4,5},{5,4},{6,7},{7,6},{8,9},{9,8},{10,11... | collective-permute-start | bytes 393224 | tf_op jit(solution)/shard_map/ppermute | solution.py:567
  27.3 12.6 %collective-permute-start.9 = (bf16[512,128]{1,0:T(8,128)(2,1)S(1)}, bf16[512,128]{1,0:T(8,128)(2,1)S(1)}, u32[]{:S(2)}, u32[]{:S(2)}) collective-permute-start(bf16[512,128]{1,0:T(8,128)(2,1)S(1)} %get-tuple-element.31), channel_id=1, source_target_pairs={{0,2},{1,3},{2,0},{3,1},{4,6},{5,7},{6,4},{7,5},{8,10},{9,11},{10,... | collective-permute-start | bytes 393224 | tf_op jit(solution)/shard_map/ppermute | solution.py:567
  30.0 9.8 %collective-permute-start.10 = (bf16[512,128]{1,0:T(8,128)(2,1)S(1)}, bf16[512,128]{1,0:T(8,128)(2,1)S(1)}, u32[]{:S(2)}, u32[]{:S(2)}) collective-permute-start(bf16[512,128]{1,0:T(8,128)(2,1)S(1)} %get-tuple-element.32), channel_id=1, source_target_pairs={{0,3},{1,2},{2,1},{3,0},{4,7},{5,6},{6,5},{7,4},{8,11},{9,10},{10,... | collective-permute-start | bytes 393224 | tf_op jit(solution)/shard_map/ppermute | solution.py:567
  39.9 5.9 %collective-permute-start.11 = (bf16[512,128]{1,0:T(8,128)(2,1)S(1)}, bf16[512,128]{1,0:T(8,128)(2,1)S(1)}, u32[]{:S(2)}, u32[]{:S(2)}) collective-permute-start(bf16[512,128]{1,0:T(8,128)(2,1)S(1)} %total_of.1.refs_0_), channel_id=1, source_target_pairs={{0,1},{1,0},{2,3},{3,2},{4,5},{5,4},{6,7},{7,6},{8,9},{9,8},{10,11... | collective-permute-start | bytes 393224 | tf_op jit(solution)/shard_map/ppermute | solution.py:567
  42.5 10.4 %collective-permute-start.13 = (bf16[512,128]{1,0:T(8,128)(2,1)S(1)}, bf16[512,128]{1,0:T(8,128)(2,1)S(1)}, u32[]{:S(2)}, u32[]{:S(2)}) collective-permute-start(bf16[512,128]{1,0:T(8,128)(2,1)S(1)} %total_of.1.refs_0_), channel_id=1, source_target_pairs={{0,3},{1,2},{2,1},{3,0},{4,7},{5,6},{6,5},{7,4},{8,11},{9,10},{10,... | collective-permute-start | bytes 393224 | tf_op jit(solution)/shard_map/ppermute | solution.py:567
  45.7 10.8 %collective-permute-start.12 = (bf16[512,128]{1,0:T(8,128)(2,1)S(1)}, bf16[512,128]{1,0:T(8,128)(2,1)S(1)}, u32[]{:S(2)}, u32[]{:S(2)}) collective-permute-start(bf16[512,128]{1,0:T(8,128)(2,1)S(1)} %total_of.1.refs_0_), channel_id=1, source_target_pairs={{0,2},{1,3},{2,0},{3,1},{4,6},{5,7},{6,4},{7,5},{8,10},{9,11},{10,... | collective-permute-start | bytes 393224 | tf_op jit(solution)/shard_map/ppermute | solution.py:567
  58.7 2.1 %collective-permute-start.14 = (bf16[18,128,128]{2,1,0:T(8,128)(2,1)S(1)}, bf16[18,128,128]{2,1,0:T(8,128)(2,1)S(1)}, u32[]{:S(2)}, u32[]{:S(2)}) collective-permute-start(bf16[18,128,128]{2,1,0:T(8,128)(2,1)S(1)} %backward.3), channel_id=1, source_target_pairs={{0,4},{4,0},{8,12},{12,8},{16,20},{20,16},{24,28},{28,24},{1,5},{5... | collective-permute-start | bytes 1769480 | tf_op jit(solution)/shard_map/ppermute | solution.py:564
  60.9 6.7 %collective-permute-start.15 = (bf16[576,128]{1,0:T(8,128)(2,1)S(1)}, bf16[576,128]{1,0:T(8,128)(2,1)S(1)}, u32[]{:S(2)}, u32[]{:S(2)}) collective-permute-start(bf16[576,128]{1,0:T(8,128)(2,1)S(1)} %get-tuple-element.42), channel_id=1, source_target_pairs={{0,8},{4,12},{8,0},{12,4},{16,24},{20,28},{24,16},{28,20},{1,9},{5... | collective-permute-start | bytes 442376 | tf_op jit(solution)/shard_map/ppermute | solution.py:561
  63.0 8.8 %collective-permute-start.16 = (bf16[576,128]{1,0:T(8,128)(2,1)S(1)}, bf16[576,128]{1,0:T(8,128)(2,1)S(1)}, u32[]{:S(2)}, u32[]{:S(2)}) collective-permute-start(bf16[576,128]{1,0:T(8,128)(2,1)S(1)} %get-tuple-element.43), channel_id=1, source_target_pairs={{0,16},{4,20},{8,24},{12,28},{16,0},{20,4},{24,8},{28,12},{1,17},{... | collective-permute-start | bytes 442376 | tf_op jit(solution)/shard_map/ppermute | solution.py:561
  63.2 8.7 %collective-permute-start.17 = (bf16[576,128]{1,0:T(8,128)(2,1)S(1)}, bf16[576,128]{1,0:T(8,128)(2,1)S(1)}, u32[]{:S(2)}, u32[]{:S(2)}) collective-permute-start(bf16[576,128]{1,0:T(8,128)(2,1)S(1)} %get-tuple-element.35), channel_id=1, source_target_pairs={{0,24},{4,28},{8,16},{12,20},{16,8},{20,12},{24,0},{28,4},{1,25},{... | collective-permute-start | bytes 442376 | tf_op jit(solution)/shard_map/ppermute | solution.py:561
  72.0 8.7 %collective-permute-start.20 = (bf16[576,128]{1,0:T(8,128)(2,1)S(1)}, bf16[576,128]{1,0:T(8,128)(2,1)S(1)}, u32[]{:S(2)}, u32[]{:S(2)}) collective-permute-start(bf16[576,128]{1,0:T(8,128)(2,1)S(1)} %gather_sum.1._.refs_0_), channel_id=1, source_target_pairs={{0,3},{1,2},{2,1},{3,0},{4,7},{5,6},{6,5},{7,4},{8,11},{9,10},{10,... | collective-permute-start | bytes 442376 | tf_op jit(solution)/shard_map/ppermute | solution.py:567
  73.1 12.3 %collective-permute-start.19 = (bf16[576,128]{1,0:T(8,128)(2,1)S(1)}, bf16[576,128]{1,0:T(8,128)(2,1)S(1)}, u32[]{:S(2)}, u32[]{:S(2)}) collective-permute-start(bf16[576,128]{1,0:T(8,128)(2,1)S(1)} %gather_sum.1._.refs_0_), channel_id=1, source_target_pairs={{0,2},{1,3},{2,0},{3,1},{4,6},{5,7},{6,4},{7,5},{8,10},{9,11},{10,... | collective-permute-start | bytes 442376 | tf_op jit(solution)/shard_map/ppermute | solution.py:567
  73.1 12.3 %collective-permute-start.18 = (bf16[576,128]{1,0:T(8,128)(2,1)S(1)}, bf16[576,128]{1,0:T(8,128)(2,1)S(1)}, u32[]{:S(2)}, u32[]{:S(2)}) collective-permute-start(bf16[576,128]{1,0:T(8,128)(2,1)S(1)} %gather_sum.1._.refs_0_), channel_id=1, source_target_pairs={{0,1},{1,0},{2,3},{3,2},{4,5},{5,4},{6,7},{7,6},{8,9},{9,8},{10,11... | collective-permute-start | bytes 442376 | tf_op jit(solution)/shard_map/ppermute | solution.py:567
  85.6 7.3 %collective-permute-start.23 = (bf16[576,128]{1,0:T(8,128)(2,1)S(1)}, bf16[576,128]{1,0:T(8,128)(2,1)S(1)}, u32[]{:S(2)}, u32[]{:S(2)}) collective-permute-start(bf16[576,128]{1,0:T(8,128)(2,1)S(1)} %get-tuple-element.49), channel_id=1, source_target_pairs={{0,0},{4,16},{8,4},{12,20},{16,8},{20,24},{24,12},{28,28},{1,1},{5... | collective-permute-start | bytes 442376 | tf_op jit(solution)/shard_map/ppermute | solution.py:617
  86.2 9.6 %collective-permute-start.24 = (bf16[576,128]{1,0:T(8,128)(2,1)S(1)}, bf16[576,128]{1,0:T(8,128)(2,1)S(1)}, u32[]{:S(2)}, u32[]{:S(2)}) collective-permute-start(bf16[576,128]{1,0:T(8,128)(2,1)S(1)} %get-tuple-element.50), channel_id=1, source_target_pairs={{0,4},{4,20},{8,0},{12,16},{16,12},{20,28},{24,8},{28,24},{1,5},{5... | collective-permute-start | bytes 442376 | tf_op jit(solution)/shard_map/ppermute | solution.py:617
  88.1 9.0 %collective-permute-start.21 = (bf16[576,128]{1,0:T(8,128)(2,1)S(1)}, bf16[576,128]{1,0:T(8,128)(2,1)S(1)}, u32[]{:S(2)}, u32[]{:S(2)}) collective-permute-start(bf16[576,128]{1,0:T(8,128)(2,1)S(1)} %get-tuple-element.47), channel_id=1, source_target_pairs={{0,8},{4,24},{8,12},{12,28},{16,0},{20,16},{24,4},{28,20},{1,9},{5... | collective-permute-start | bytes 442376 | tf_op jit(solution)/shard_map/ppermute | solution.py:617
  88.5 9.4 %collective-permute-start.22 = (bf16[576,128]{1,0:T(8,128)(2,1)S(1)}, bf16[576,128]{1,0:T(8,128)(2,1)S(1)}, u32[]{:S(2)}, u32[]{:S(2)}) collective-permute-start(bf16[576,128]{1,0:T(8,128)(2,1)S(1)} %get-tuple-element.48), channel_id=1, source_target_pairs={{0,12},{4,28},{8,8},{12,24},{16,4},{20,20},{24,0},{28,16},{1,13},{... | collective-permute-start | bytes 442376 | tf_op jit(solution)/shard_map/ppermute | solution.py:617
  (6 other events, 89.2 us)

commit v8 on v7

--- a/solution.py
+++ b/solution.py
@@ -79,9 +79,10 @@
 def reorder_body(order_ref, feat_ref, out_ref, *, first):
     panel = feat_ref.shape[0]
     rows = out_ref.shape[0]
-    step = min(256, rows)
+    step = order_ref.shape[1]
+    order = order_ref[...].T
     for i in range(first // step, (first + rows) // step):
-        hot = lax.broadcasted_iota(jnp.int32, (step, panel), 1) == order_ref[pl.ds(i * step, step), :]
+        hot = lax.broadcasted_iota(jnp.int32, (step, panel), 1) == order[:, i : i + 1]
         hot = jnp.where(hot, 1.0, 0.0).astype(BF16)
         at = i * step - first
         out_ref[at : at + step, :] = jnp.dot(
@@ -89,12 +90,12 @@
         ).astype(BF16)
 
 
-def reorder(order_col, features, half):
+def reorder(order_rows, features, half):
     panel, width = features.shape
     rows = panel // HALVES
     return call(
         functools.partial(reorder_body, first=half * rows),
-        [order_col, features],
+        [in_hbm(order_rows), in_hbm(features)],
         jax.ShapeDtypeStruct((rows, width), BF16),
         estimate=cost(2 * rows * panel * width, 4 * rows * width),
         name="reorder",
@@ -326,8 +327,7 @@
             for t in range(GROUP):
                 acc[jnp.where(alive[t], entries[t] & (blocks - 1), blocks)] += terms[t]
 
-        core = place.core
-        walk(entry_ref, 2 * p + (core if keep else 1 - core), slots, step)
+        walk(entry_ref, 2 * p + (place.side if keep else 1 - place.side), slots, step)
         for h in range(cuts):
             for d in range(chips):
                 at = ((place.chip ^ d) * cuts + h) * per
@@ -427,6 +427,11 @@
     )
 
 
+def owner_of(chip, core, k, reps):
+    to = chip ^ k
+    return 2 * to + (core ^ (to // (reps // 2) % 2))
+
+
 def route_body(*refs, reps, chips, rows, pairs):
     spread, outs = refs[:reps], refs[reps + 1 :]
     place = Place()
@@ -435,12 +440,12 @@
     if extra:
         high, low = two_parts(tree_sum([sum_of_parts(ref, rows, extra) for ref in spread]))
     for k in range(chips):
-        u = place.chip ^ k
+        target = owner_of(place.chip, place.core, k, reps)
         for d in range(reps):
 
-            @pl.when(((u % reps) ^ place.rep) == d)
+            @pl.when(((target % reps) ^ place.rep) == d)
             def _():
-                at = pl.multiple_of(u // reps * each, each)
+                at = pl.multiple_of(target // reps // 2 * each, each)
                 outs[k][:each, :] = spread[d][pl.ds(at, each), :]
 
         if extra:
@@ -488,18 +493,17 @@
     )(order_row, after)
 
 
-def restore_body(hot_ref, *refs, first, count, per, scale, reps):
+def restore_body(hot_ref, *refs, first, count, per, scale):
     parts, refs = refs[:count], refs[count:]
     start, (out_ref, grad_ref) = refs[:-2], refs[-2:]
-    section = lax.axis_index("section")
-    base_u = (section // reps // 2) * reps + section % reps
+    chip = lax.axis_index("section") // 2
     block = parts[0].shape[1]
     extra = (parts[0].shape[0] - per * block) // 2
     length = per * block
     grad_ref[...] = start[1][...] if start else jnp.zeros_like(grad_ref)
     columns, places = [], []
     for n, part in enumerate(parts):
-        u = base_u ^ (first + n)
+        u = chip ^ (first + n)
         at = pl.multiple_of(u * extra, extra)
         grad_ref[pl.ds(at, extra), :] = sum_of_parts(part, length, extra) * scale
         columns.append(
@@ -521,11 +525,11 @@
         out_ref[span, :] = acc.astype(out_ref.dtype)
 
 
-def restore(hot, parts, first, start, per, scale, reps):
+def restore(hot, parts, first, start, per, scale):
     panel = hot.shape[0]
     width = parts[0].shape[1]
     body = functools.partial(
-        restore_body, first=first, count=len(parts), per=per, scale=scale, reps=reps
+        restore_body, first=first, count=len(parts), per=per, scale=scale
     )
     outs = (
         jax.ShapeDtypeStruct((panel, width), BF16 if start else F32),
@@ -575,8 +579,8 @@
                 moves.append((source * reps + r, target * reps + r))
         return lax.ppermute(x, ("section", "rep"), moves)
 
-    order_col, order_row = order.reshape(panel, 1), order.reshape(1, panel)
-    owns = [reorder(order_col, features, h) for h in range(HALVES)]
+    order_rows, order_row = order.reshape(panel // block, block), order.reshape(1, panel)
+    owns = [reorder(order_rows, features, h) for h in range(HALVES)]
     gots = [[own] + [from_owner(own, d) for d in range(1, chips)] for own in owns]
     bits = (blocks - 1).bit_length()
     plan = entries_of(tile_rows, tile_cols, live, bits, owns[-1][:16])
@@ -610,10 +614,7 @@
     reduced = gather_sum([chunks[0][0], *arrived[0]], [token], height)
 
     def to_owner(block, k):
-        moves = []
-        for s in range(sections):
-            u = (s // 2) ^ k
-            moves.append((s, (2 * (u // reps) + s % 2) * reps + u % reps))
+        moves = [(s, owner_of(s // 2, s % 2, k, reps)) for s in range(sections)]
         return lax.ppermute(block, "section", moves)
 
     spread = [reduced] + [over_reps(reduced, d) for d in range(1, reps)]
@@ -622,8 +623,8 @@
     parts = [to_owner(block, k) for k, block in enumerate(routed)]
     scale = 1.0 / math.sqrt(panel * sections)
     half = chips // 2
-    begun = restore(hot, parts[:half], 0, (), per, scale, reps)
-    feature_grad, weight_grad = restore(hot, parts[half:], half, begun, per, scale, reps)
+    begun = restore(hot, parts[:half], 0, (), per, scale)
+    feature_grad, weight_grad = restore(hot, parts[half:], half, begun, per, scale)
     return (hidden, weight_grad, feature_grad)
 
 

time: 99.7 us -> 99 us (level)
  Pallas kernels: 16.5 us -> 22.7 us
  starting transfers between devices: 38.2 us -> 35 us
  local copies, waits for them, and re-layouts: 2.12 us -> 0.03 us
  waiting for transfers between devices: 42.1 us -> 40.6 us
    pallas_call x17, Pallas kernels: 14.2 us -> 20.4 us  [call(): pl.pallas_call(body, out_shape=outs, grid_spec=pltpu.PrefetchScalarGridSp...]
    ppermute x4, starting transfers between devices: 7.29 us -> 4.55 us  [to_owner(): return lax.ppermute(block, 'section', moves)]
    ppermute x4, waiting for transfers between devices: 3.74 us -> 6.31 us  [to_owner(): return lax.ppermute(block, 'section', moves)]
    ppermute x3, waiting for transfers between devices: 6.07 us -> 4.39 us  [over_chips(): return lax.ppermute(x, 'section', [(s, s ^ 2 * d) for s in range(sections)])]
    ppermute x3, waiting for transfers between devices: 1.4 us -> 0.01 us  [over_cores(): return lax.ppermute(x, 'section', [(s, s ^ 1) for s in range(sections)])]
    reshape x1 -> x0, local copies, waits for them, and re-layouts: 1.06 us -> none  [shards(): order_col, order_row = (order.reshape(panel, 1), order.reshape(1, panel))]
    unnamed x10 -> x8, local copies, waits for them, and re-layouts: 1.06 us -> 0.02 us
  transfers between devices with their start and end apart: 25 -> 25, of which waited for: 16 -> 15; matrix products, arithmetic and copies ran while one was open for 0% -> 0% of each run, Pallas kernels for 9% -> 12%
where the time goes in v8:
time: 99 us; the launch traced here: 99.3 us
  waiting for transfers between devices  40.6 us (41%)
  starting transfers between devices  35 us (35%)
  Pallas kernels  22.7 us (23%)
    ppermute x9, waiting for transfers between devices, over_reps(): return lax.ppermute(x, 'rep', [(r, r ^ d) for r in range(reps)])  26.9 us
    pallas_call x17, Pallas kernels, call(): pl.pallas_call(body, out_shape=outs, grid_spec=pltpu.PrefetchScalarGridSp...  20.4 us
    ppermute x9, starting transfers between devices, over_reps(): return lax.ppermute(x, 'rep', [(r, r ^ d) for r in range(reps)])  14.9 us
    ppermute x6, starting transfers between devices, from_owner(): return lax.ppermute(x, ('section', 'rep'), moves)  11.8 us
    ppermute x4, waiting for transfers between devices, to_owner(): return lax.ppermute(block, 'section', moves)  6.31 us
    ppermute x4, starting transfers between devices, to_owner(): return lax.ppermute(block, 'section', moves)  4.55 us
    ppermute x3, waiting for transfers between devices, over_chips(): return lax.ppermute(x, 'section', [(s, s ^ 2 * d) for s in range(sections)])  4.39 us
    ppermute x3, starting transfers between devices, over_chips(): return lax.ppermute(x, 'section', [(s, s ^ 2 * d) for s in range(sections)])  3.54 us
  transfers between devices with their start and end apart: 25, of which 15 were waited for; matrix products, arithmetic and copies ran while one was open for 0% of the time, Pallas kernels for 12%

profile of v8, /device:TPU:0, one launch (start us, length us, event | category | flops | bytes accessed | tf_op | source)
XLA Modules:
  0.0 99.3 jit_solution(10166735560788512321)
XLA Ops:
  0.6 2.6 %reorder.3.refs_0_ = bf16[1024,128]{1,0:T(8,128)(2,1)S(1)} custom-call(s32[16,128]{1,0:T(8,128)} %bitcast.7, bf16[2048,128]{1,0:T(8,128)(2,1)} %feat_ref.3), custom_call_target="tpu_custom_call" | custom-call | flops 536870912 | bytes 524288 | tf_op jit(solution)/shard_map/reorder/pallas_call | solution.py:59
  3.2 5.3 %collective-permute-start.2 = (bf16[1024,128]{1,0:T(8,128)(2,1)S(1)}, bf16[1024,128]{1,0:T(8,128)(2,1)S(1)}, u32[]{:S(2)}, u32[]{:S(2)}) collective-permute-start(bf16[1024,128]{1,0:T(8,128)(2,1)S(1)} %reorder.3.refs_0_), channel_id=1, source_target_pairs={{0,28},{16,12},{5,25},{21,9},{10,22},{26,6},{15,19},{31,3}} | collective-permute-start | bytes 786440 | tf_op jit(solution)/shard_map/ppermute | solution.py:580
  11.1 2.4 %reorder.2.refs_0_ = bf16[1024,128]{1,0:T(8,128)(2,1)S(1)} custom-call(s32[16,128]{1,0:T(8,128)} %bitcast.8, bf16[2048,128]{1,0:T(8,128)(2,1)} %feat_ref.3), custom_call_target="tpu_custom_call" | custom-call | flops 536870912 | bytes 524288 | tf_op jit(solution)/shard_map/reorder/pallas_call | solution.py:59
  21.7 2.0 %forward.2.refs_2_ = f32[16,128,128]{2,1,0:T(8,128)S(1)} custom-call(s32[2,97]{1,0:T(2,128)S(1)} %entries_of.1.refs_4_.entry_ref, bf16[192,128,128]{2,1,0:T(8,128)(2,1)S(1)} %bitcast.3, bf16[1024,128]{1,0:T(8,128)(2,1)S(1)} %pick.2.refs_0_, bf16[1024,128]{1,0:T(8,128)(2,1)S(1)} %pick.3.refs_1_), custom_call_target="tpu_custom_call" | custom-call | flops 268435456 | bytes 12582912 | tf_op jit(solution)/shard_map/forward/pallas_call | solution.py:59
  23.7 2.6 %forward.3 = (f32[512,128]{1,0:T(8,128)S(1)}, bf16[512,128]{1,0:T(8,128)(2,1)S(1)}, bf16[512,128]{1,0:T(8,128)(2,1)S(1)}, bf16[512,128]{1,0:T(8,128)(2,1)S(1)}) custom-call(s32[2,97]{1,0:T(2,128)S(1)} %entries_of.1.refs_4_.entry_ref, bf16[192,128,128]{2,1,0:T(8,128)(2,1)S(1)} %bitcast.4, bf16[1024,128]{1,0:T(8,128)(2,1)S(1)} %collective-permute-done.3.refs_0_, ...), custom_call_target="tpu_custom_call" | custom-call | flops 268435456 | bytes 12582912 | tf_op jit(solution)/shard_map/forward/pallas_call | solution.py:59
  26.3 3.1 %collective-permute-start.9 = (bf16[512,128]{1,0:T(8,128)(2,1)S(1)}, bf16[512,128]{1,0:T(8,128)(2,1)S(1)}, u32[]{:S(2)}, u32[]{:S(2)}) collective-permute-start(bf16[512,128]{1,0:T(8,128)(2,1)S(1)} %get-tuple-element.31), channel_id=1, source_target_pairs={{0,2},{1,3},{2,0},{3,1},{4,6},{5,7},{6,4},{7,5},{8,10},{9,11},{10,... | collective-permute-start | bytes 393224 | tf_op jit(solution)/shard_map/ppermute | solution.py:571
  30.7 3.5 %collective-permute-done.8.refs_0_ = bf16[512,128]{1,0:T(8,128)(2,1)S(1)} collective-permute-done((bf16[512,128]{1,0:T(8,128)(2,1)S(1)}, bf16[512,128]{1,0:T(8,128)(2,1)S(1)}, u32[]{:S(2)}, u32[]{:S(2)}) %collective-permute-start.8) | collective-permute-done | bytes 131104 | tf_op jit(solution)/shard_map/ppermute | solution.py:571
  34.2 5.9 %collective-permute-done.10.refs_2_ = bf16[512,128]{1,0:T(8,128)(2,1)S(1)} collective-permute-done((bf16[512,128]{1,0:T(8,128)(2,1)S(1)}, bf16[512,128]{1,0:T(8,128)(2,1)S(1)}, u32[]{:S(2)}, u32[]{:S(2)}) %collective-permute-start.10) | collective-permute-done | bytes 131104 | tf_op jit(solution)/shard_map/ppermute | solution.py:571
  40.2 2.7 %collective-permute-start.11 = (bf16[512,128]{1,0:T(8,128)(2,1)S(1)}, bf16[512,128]{1,0:T(8,128)(2,1)S(1)}, u32[]{:S(2)}, u32[]{:S(2)}) collective-permute-start(bf16[512,128]{1,0:T(8,128)(2,1)S(1)} %total_of.1.refs_0_), channel_id=1, source_target_pairs={{0,1},{1,0},{2,3},{3,2},{4,5},{5,4},{6,7},{7,6},{8,9},{9,8},{10,11... | collective-permute-start | bytes 393224 | tf_op jit(solution)/shard_map/ppermute | solution.py:571
  42.9 3.4 %collective-permute-start.13 = (bf16[512,128]{1,0:T(8,128)(2,1)S(1)}, bf16[512,128]{1,0:T(8,128)(2,1)S(1)}, u32[]{:S(2)}, u32[]{:S(2)}) collective-permute-start(bf16[512,128]{1,0:T(8,128)(2,1)S(1)} %total_of.1.refs_0_), channel_id=1, source_target_pairs={{0,3},{1,2},{2,1},{3,0},{4,7},{5,6},{6,5},{7,4},{8,11},{9,10},{10,... | collective-permute-start | bytes 393224 | tf_op jit(solution)/shard_map/ppermute | solution.py:571
  47.3 6.2 %collective-permute-done.13.refs_1_.refs_3_ = bf16[512,128]{1,0:T(8,128)(2,1)S(1)} collective-permute-done((bf16[512,128]{1,0:T(8,128)(2,1)S(1)}, bf16[512,128]{1,0:T(8,128)(2,1)S(1)}, u32[]{:S(2)}, u32[]{:S(2)}) %collective-permute-start.13) | collective-permute-done | bytes 131104 | tf_op jit(solution)/shard_map/ppermute | solution.py:571
  53.5 3.6 %collective-permute-done.12.refs_0_.refs_2_ = bf16[512,128]{1,0:T(8,128)(2,1)S(1)} collective-permute-done((bf16[512,128]{1,0:T(8,128)(2,1)S(1)}, bf16[512,128]{1,0:T(8,128)(2,1)S(1)}, u32[]{:S(2)}, u32[]{:S(2)}) %collective-permute-start.12) | collective-permute-done | bytes 131104 | tf_op jit(solution)/shard_map/ppermute | solution.py:571
  57.6 2.6 %backward.3 = bf16[18,128,128]{2,1,0:T(8,128)(2,1)S(1)} custom-call(s32[2,97]{1,0:T(2,128)S(1)} %entries_of.1.refs_4_.entry_ref, bf16[192,128,128]{2,1,0:T(8,128)(2,1)S(1)} %bitcast.5, bf16[2,128,512]{2,1,0:T(8,128)(2,1)S(1)} %get-tuple-element.33.refs_0_, bf16[2,128,512]{2,1,0:T(8,128)(2,1)S(1)} %up_shares.3.refs_1_, ...), custom_call_target="tpu_custom_call" | custom-call | flops 268435456 | bytes 12582912 | tf_op jit(solution)/shard_map/backward/pallas_call | solution.py:59
  60.3 2.0 %backward.2.kept_ref = f32[16,128,128]{2,1,0:T(8,128)S(1)} custom-call(s32[2,97]{1,0:T(2,128)S(1)} %entries_of.1.refs_4_.entry_ref, bf16[192,128,128]{2,1,0:T(8,128)(2,1)S(1)} %bitcast.6, bf16[2,128,512]{2,1,0:T(8,128)(2,1)S(1)} %get-tuple-element.33.refs_0_, bf16[2,128,512]{2,1,0:T(8,128)(2,1)S(1)} %up_shares.3.refs_1_), custom_call_target="tpu_custom_call" | custom-call | flops 268435456 | bytes 12582912 | tf_op jit(solution)/shard_map/backward/pallas_call | solution.py:59
  62.6 3.4 %collective-permute-start.17 = (bf16[576,128]{1,0:T(8,128)(2,1)S(1)}, bf16[576,128]{1,0:T(8,128)(2,1)S(1)}, u32[]{:S(2)}, u32[]{:S(2)}) collective-permute-start(bf16[576,128]{1,0:T(8,128)(2,1)S(1)} %get-tuple-element.35), channel_id=1, source_target_pairs={{0,24},{4,28},{8,16},{12,20},{16,8},{20,12},{24,0},{28,4},{1,25},{... | collective-permute-start | bytes 442376 | tf_op jit(solution)/shard_map/ppermute | solution.py:565
  67.2 2.0 %collective-permute-done.15.refs_1_ = bf16[576,128]{1,0:T(8,128)(2,1)S(1)} collective-permute-done((bf16[576,128]{1,0:T(8,128)(2,1)S(1)}, bf16[576,128]{1,0:T(8,128)(2,1)S(1)}, u32[]{:S(2)}, u32[]{:S(2)}) %collective-permute-start.15) | collective-permute-done | bytes 147488 | tf_op jit(solution)/shard_map/ppermute | solution.py:565
  69.2 2.4 %collective-permute-done.16.refs_2_ = bf16[576,128]{1,0:T(8,128)(2,1)S(1)} collective-permute-done((bf16[576,128]{1,0:T(8,128)(2,1)S(1)}, bf16[576,128]{1,0:T(8,128)(2,1)S(1)}, u32[]{:S(2)}, u32[]{:S(2)}) %collective-permute-start.16) | collective-permute-done | bytes 147488 | tf_op jit(solution)/shard_map/ppermute | solution.py:565
  73.2 2.9 %collective-permute-start.18 = (bf16[576,128]{1,0:T(8,128)(2,1)S(1)}, bf16[576,128]{1,0:T(8,128)(2,1)S(1)}, u32[]{:S(2)}, u32[]{:S(2)}) collective-permute-start(bf16[576,128]{1,0:T(8,128)(2,1)S(1)} %gather_sum.1._.refs_0_), channel_id=1, source_target_pairs={{0,1},{1,0},{2,3},{3,2},{4,5},{5,4},{6,7},{7,6},{8,9},{9,8},{10,11... | collective-permute-start | bytes 442376 | tf_op jit(solution)/shard_map/ppermute | solution.py:571
  77.6 2.8 %collective-permute-done.20.refs_3_ = bf16[576,128]{1,0:T(8,128)(2,1)S(1)} collective-permute-done((bf16[576,128]{1,0:T(8,128)(2,1)S(1)}, bf16[576,128]{1,0:T(8,128)(2,1)S(1)}, u32[]{:S(2)}, u32[]{:S(2)}) %collective-permute-start.20) | collective-permute-done | bytes 147488 | tf_op jit(solution)/shard_map/ppermute | solution.py:571
  80.4 4.5 %collective-permute-done.19.refs_2_ = bf16[576,128]{1,0:T(8,128)(2,1)S(1)} collective-permute-done((bf16[576,128]{1,0:T(8,128)(2,1)S(1)}, bf16[576,128]{1,0:T(8,128)(2,1)S(1)}, u32[]{:S(2)}, u32[]{:S(2)}) %collective-permute-start.19) | collective-permute-done | bytes 147488 | tf_op jit(solution)/shard_map/ppermute | solution.py:571
  89.7 1.9 %collective-permute-done.24.refs_1_ = bf16[576,128]{1,0:T(8,128)(2,1)S(1)} collective-permute-done((bf16[576,128]{1,0:T(8,128)(2,1)S(1)}, bf16[576,128]{1,0:T(8,128)(2,1)S(1)}, u32[]{:S(2)}, u32[]{:S(2)}) %collective-permute-start.24) | collective-permute-done | bytes 147488 | tf_op jit(solution)/shard_map/ppermute | solution.py:618
  92.9 2.7 %collective-permute-done.21.refs_0_ = bf16[576,128]{1,0:T(8,128)(2,1)S(1)} collective-permute-done((bf16[576,128]{1,0:T(8,128)(2,1)S(1)}, bf16[576,128]{1,0:T(8,128)(2,1)S(1)}, u32[]{:S(2)}, u32[]{:S(2)}) %collective-permute-start.21) | collective-permute-done | bytes 147488 | tf_op jit(solution)/shard_map/ppermute | solution.py:618
  95.7 1.6 %collective-permute-done.22.refs_1_ = bf16[576,128]{1,0:T(8,128)(2,1)S(1)} collective-permute-done((bf16[576,128]{1,0:T(8,128)(2,1)S(1)}, bf16[576,128]{1,0:T(8,128)(2,1)S(1)}, u32[]{:S(2)}, u32[]{:S(2)}) %collective-permute-start.22) | collective-permute-done | bytes 147488 | tf_op jit(solution)/shard_map/ppermute | solution.py:618
  97.3 2.1 %restore.3 = (bf16[2048,128]{1,0:T(8,128)(2,1)}, f32[128,128]{1,0:T(8,128)}) custom-call(bf16[2048,2048]{1,0:T(8,128)(2,1)S(1)} %get-tuple-element.45.hot_ref, bf16[576,128]{1,0:T(8,128)(2,1)S(1)} %collective-permute-done.21.refs_0_, bf16[576,128]{1,0:T(8,128)(2,1)S(1)} %collective-permute-done.22.refs_1_, f32[2048,128]{1,0:T(8,128)S(1)} %get-tuple-element.51.refs_2_, ...), custom_call_target="tpu_custom_call" | custom-call | flops 1073741824 | bytes 1048576 | tf_op jit(solution)/shard_map/restore/pallas_call | solution.py:59
  (54 shorter events, 24.3 us)
Async XLA Ops:
  3.2 13.0 %collective-permute-start.2 = (bf16[1024,128]{1,0:T(8,128)(2,1)S(1)}, bf16[1024,128]{1,0:T(8,128)(2,1)S(1)}, u32[]{:S(2)}, u32[]{:S(2)}) collective-permute-start(bf16[1024,128]{1,0:T(8,128)(2,1)S(1)} %reorder.3.refs_0_), channel_id=1, source_target_pairs={{0,28},{16,12},{5,25},{21,9},{10,22},{26,6},{15,19},{31,3}} | collective-permute-start | bytes 786440 | tf_op jit(solution)/shard_map/ppermute | solution.py:580
  8.5 9.8 %collective-permute-start.1 = (bf16[1024,128]{1,0:T(8,128)(2,1)S(1)}, bf16[1024,128]{1,0:T(8,128)(2,1)S(1)}, u32[]{:S(2)}, u32[]{:S(2)}) collective-permute-start(bf16[1024,128]{1,0:T(8,128)(2,1)S(1)} %reorder.3.refs_0_), channel_id=1, source_target_pairs={{0,20},{16,4},{5,17},{21,1},{10,30},{26,14},{15,27},{31,11}} | collective-permute-start | bytes 786440 | tf_op jit(solution)/shard_map/ppermute | solution.py:580
  9.8 8.5 %collective-permute-start = (bf16[1024,128]{1,0:T(8,128)(2,1)S(1)}, bf16[1024,128]{1,0:T(8,128)(2,1)S(1)}, u32[]{:S(2)}, u32[]{:S(2)}) collective-permute-start(bf16[1024,128]{1,0:T(8,128)(2,1)S(1)} %reorder.3.refs_0_), channel_id=1, source_target_pairs={{0,8},{16,24},{5,13},{21,29},{10,2},{26,18},{15,7},{31,23}} | collective-permute-start | bytes 786440 | tf_op jit(solution)/shard_map/ppermute | solution.py:580
  13.6 5.2 %collective-permute-start.6 = (bf16[1024,128]{1,0:T(8,128)(2,1)S(1)}, bf16[1024,128]{1,0:T(8,128)(2,1)S(1)}, u32[]{:S(2)}, u32[]{:S(2)}) collective-permute-start(bf16[1024,128]{1,0:T(8,128)(2,1)S(1)} %reorder.2.refs_0_), channel_id=1, source_target_pairs={{0,28},{16,12},{5,25},{21,9},{10,22},{26,6},{15,19},{31,3}} | collective-permute-start | bytes 786440 | tf_op jit(solution)/shard_map/ppermute | solution.py:580
  14.9 5.2 %collective-permute-start.5 = (bf16[1024,128]{1,0:T(8,128)(2,1)S(1)}, bf16[1024,128]{1,0:T(8,128)(2,1)S(1)}, u32[]{:S(2)}, u32[]{:S(2)}) collective-permute-start(bf16[1024,128]{1,0:T(8,128)(2,1)S(1)} %reorder.2.refs_0_), channel_id=1, source_target_pairs={{0,20},{16,4},{5,17},{21,1},{10,30},{26,14},{15,27},{31,11}} | collective-permute-start | bytes 786440 | tf_op jit(solution)/shard_map/ppermute | solution.py:580
  16.2 5.3 %collective-permute-start.4 = (bf16[1024,128]{1,0:T(8,128)(2,1)S(1)}, bf16[1024,128]{1,0:T(8,128)(2,1)S(1)}, u32[]{:S(2)}, u32[]{:S(2)}) collective-permute-start(bf16[1024,128]{1,0:T(8,128)(2,1)S(1)} %reorder.2.refs_0_), channel_id=1, source_target_pairs={{0,8},{16,24},{5,13},{21,29},{10,2},{26,18},{15,7},{31,23}} | collective-permute-start | bytes 786440 | tf_op jit(solution)/shard_map/ppermute | solution.py:580
  18.4 5.3 %collective-permute-start.3 = (bf16[1024,128]{1,0:T(8,128)(2,1)S(1)}, bf16[1024,128]{1,0:T(8,128)(2,1)S(1)}, u32[]{:S(2)}, u32[]{:S(2)}) collective-permute-start(bf16[1024,128]{1,0:T(8,128)(2,1)S(1)} %pick.2.refs_0_), channel_id=1, source_target_pairs={{0,4},{4,0},{8,12},{12,8},{16,20},{20,16},{24,28},{28,24},{1,5},{5... | collective-permute-start | bytes 786440 | tf_op jit(solution)/shard_map/ppermute | solution.py:568
  21.6 2.1 %collective-permute-start.7 = (bf16[1024,128]{1,0:T(8,128)(2,1)S(1)}, bf16[1024,128]{1,0:T(8,128)(2,1)S(1)}, u32[]{:S(2)}, u32[]{:S(2)}) collective-permute-start(bf16[1024,128]{1,0:T(8,128)(2,1)S(1)} %pick.3.refs_1_), channel_id=1, source_target_pairs={{0,4},{4,0},{8,12},{12,8},{16,20},{20,16},{24,28},{28,24},{1,5},{5... | collective-permute-start | bytes 786440 | tf_op jit(solution)/shard_map/ppermute | solution.py:568
  26.3 7.9 %collective-permute-start.8 = (bf16[512,128]{1,0:T(8,128)(2,1)S(1)}, bf16[512,128]{1,0:T(8,128)(2,1)S(1)}, u32[]{:S(2)}, u32[]{:S(2)}) collective-permute-start(bf16[512,128]{1,0:T(8,128)(2,1)S(1)} %get-tuple-element.30), channel_id=1, source_target_pairs={{0,1},{1,0},{2,3},{3,2},{4,5},{5,4},{6,7},{7,6},{8,9},{9,8},{10,11... | collective-permute-start | bytes 393224 | tf_op jit(solution)/shard_map/ppermute | solution.py:571
  26.3 7.8 %collective-permute-start.9 = (bf16[512,128]{1,0:T(8,128)(2,1)S(1)}, bf16[512,128]{1,0:T(8,128)(2,1)S(1)}, u32[]{:S(2)}, u32[]{:S(2)}) collective-permute-start(bf16[512,128]{1,0:T(8,128)(2,1)S(1)} %get-tuple-element.31), channel_id=1, source_target_pairs={{0,2},{1,3},{2,0},{3,1},{4,6},{5,7},{6,4},{7,5},{8,10},{9,11},{10,... | collective-permute-start | bytes 393224 | tf_op jit(solution)/shard_map/ppermute | solution.py:571
  29.4 10.7 %collective-permute-start.10 = (bf16[512,128]{1,0:T(8,128)(2,1)S(1)}, bf16[512,128]{1,0:T(8,128)(2,1)S(1)}, u32[]{:S(2)}, u32[]{:S(2)}) collective-permute-start(bf16[512,128]{1,0:T(8,128)(2,1)S(1)} %get-tuple-element.32), channel_id=1, source_target_pairs={{0,3},{1,2},{2,1},{3,0},{4,7},{5,6},{6,5},{7,4},{8,11},{9,10},{10,... | collective-permute-start | bytes 393224 | tf_op jit(solution)/shard_map/ppermute | solution.py:571
  40.2 6.5 %collective-permute-start.11 = (bf16[512,128]{1,0:T(8,128)(2,1)S(1)}, bf16[512,128]{1,0:T(8,128)(2,1)S(1)}, u32[]{:S(2)}, u32[]{:S(2)}) collective-permute-start(bf16[512,128]{1,0:T(8,128)(2,1)S(1)} %total_of.1.refs_0_), channel_id=1, source_target_pairs={{0,1},{1,0},{2,3},{3,2},{4,5},{5,4},{6,7},{7,6},{8,9},{9,8},{10,11... | collective-permute-start | bytes 393224 | tf_op jit(solution)/shard_map/ppermute | solution.py:571
  42.9 10.6 %collective-permute-start.13 = (bf16[512,128]{1,0:T(8,128)(2,1)S(1)}, bf16[512,128]{1,0:T(8,128)(2,1)S(1)}, u32[]{:S(2)}, u32[]{:S(2)}) collective-permute-start(bf16[512,128]{1,0:T(8,128)(2,1)S(1)} %total_of.1.refs_0_), channel_id=1, source_target_pairs={{0,3},{1,2},{2,1},{3,0},{4,7},{5,6},{6,5},{7,4},{8,11},{9,10},{10,... | collective-permute-start | bytes 393224 | tf_op jit(solution)/shard_map/ppermute | solution.py:571
  46.2 10.8 %collective-permute-start.12 = (bf16[512,128]{1,0:T(8,128)(2,1)S(1)}, bf16[512,128]{1,0:T(8,128)(2,1)S(1)}, u32[]{:S(2)}, u32[]{:S(2)}) collective-permute-start(bf16[512,128]{1,0:T(8,128)(2,1)S(1)} %total_of.1.refs_0_), channel_id=1, source_target_pairs={{0,2},{1,3},{2,0},{3,1},{4,6},{5,7},{6,4},{7,5},{8,10},{9,11},{10,... | collective-permute-start | bytes 393224 | tf_op jit(solution)/shard_map/ppermute | solution.py:571
  62.4 6.8 %collective-permute-start.15 = (bf16[576,128]{1,0:T(8,128)(2,1)S(1)}, bf16[576,128]{1,0:T(8,128)(2,1)S(1)}, u32[]{:S(2)}, u32[]{:S(2)}) collective-permute-start(bf16[576,128]{1,0:T(8,128)(2,1)S(1)} %get-tuple-element.42), channel_id=1, source_target_pairs={{0,8},{4,12},{8,0},{12,4},{16,24},{20,28},{24,16},{28,20},{1,9},{5... | collective-permute-start | bytes 442376 | tf_op jit(solution)/shard_map/ppermute | solution.py:565
  62.5 9.1 %collective-permute-start.16 = (bf16[576,128]{1,0:T(8,128)(2,1)S(1)}, bf16[576,128]{1,0:T(8,128)(2,1)S(1)}, u32[]{:S(2)}, u32[]{:S(2)}) collective-permute-start(bf16[576,128]{1,0:T(8,128)(2,1)S(1)} %get-tuple-element.43), channel_id=1, source_target_pairs={{0,16},{4,20},{8,24},{12,28},{16,0},{20,4},{24,8},{28,12},{1,17},{... | collective-permute-start | bytes 442376 | tf_op jit(solution)/shard_map/ppermute | solution.py:565
  62.6 9.0 %collective-permute-start.17 = (bf16[576,128]{1,0:T(8,128)(2,1)S(1)}, bf16[576,128]{1,0:T(8,128)(2,1)S(1)}, u32[]{:S(2)}, u32[]{:S(2)}) collective-permute-start(bf16[576,128]{1,0:T(8,128)(2,1)S(1)} %get-tuple-element.35), channel_id=1, source_target_pairs={{0,24},{4,28},{8,16},{12,20},{16,8},{20,12},{24,0},{28,4},{1,25},{... | collective-permute-start | bytes 442376 | tf_op jit(solution)/shard_map/ppermute | solution.py:565
  71.7 8.7 %collective-permute-start.20 = (bf16[576,128]{1,0:T(8,128)(2,1)S(1)}, bf16[576,128]{1,0:T(8,128)(2,1)S(1)}, u32[]{:S(2)}, u32[]{:S(2)}) collective-permute-start(bf16[576,128]{1,0:T(8,128)(2,1)S(1)} %gather_sum.1._.refs_0_), channel_id=1, source_target_pairs={{0,3},{1,2},{2,1},{3,0},{4,7},{5,6},{6,5},{7,4},{8,11},{9,10},{10,... | collective-permute-start | bytes 442376 | tf_op jit(solution)/shard_map/ppermute | solution.py:571
  73.2 11.7 %collective-permute-start.19 = (bf16[576,128]{1,0:T(8,128)(2,1)S(1)}, bf16[576,128]{1,0:T(8,128)(2,1)S(1)}, u32[]{:S(2)}, u32[]{:S(2)}) collective-permute-start(bf16[576,128]{1,0:T(8,128)(2,1)S(1)} %gather_sum.1._.refs_0_), channel_id=1, source_target_pairs={{0,2},{1,3},{2,0},{3,1},{4,6},{5,7},{6,4},{7,5},{8,10},{9,11},{10,... | collective-permute-start | bytes 442376 | tf_op jit(solution)/shard_map/ppermute | solution.py:571
  73.2 11.7 %collective-permute-start.18 = (bf16[576,128]{1,0:T(8,128)(2,1)S(1)}, bf16[576,128]{1,0:T(8,128)(2,1)S(1)}, u32[]{:S(2)}, u32[]{:S(2)}) collective-permute-start(bf16[576,128]{1,0:T(8,128)(2,1)S(1)} %gather_sum.1._.refs_0_), channel_id=1, source_target_pairs={{0,1},{1,0},{2,3},{3,2},{4,5},{5,4},{6,7},{7,6},{8,9},{9,8},{10,11... | collective-permute-start | bytes 442376 | tf_op jit(solution)/shard_map/ppermute | solution.py:571
  85.2 4.6 %collective-permute-start.23 = (bf16[576,128]{1,0:T(8,128)(2,1)S(1)}, bf16[576,128]{1,0:T(8,128)(2,1)S(1)}, u32[]{:S(2)}, u32[]{:S(2)}) collective-permute-start(bf16[576,128]{1,0:T(8,128)(2,1)S(1)} %get-tuple-element.49), channel_id=1, source_target_pairs={{0,0},{4,4},{8,8},{12,12},{16,20},{20,16},{24,28},{28,24},{1,1},{5... | collective-permute-start | bytes 442376 | tf_op jit(solution)/shard_map/ppermute | solution.py:618
  85.8 5.8 %collective-permute-start.24 = (bf16[576,128]{1,0:T(8,128)(2,1)S(1)}, bf16[576,128]{1,0:T(8,128)(2,1)S(1)}, u32[]{:S(2)}, u32[]{:S(2)}) collective-permute-start(bf16[576,128]{1,0:T(8,128)(2,1)S(1)} %get-tuple-element.50), channel_id=1, source_target_pairs={{0,8},{4,12},{8,0},{12,4},{16,28},{20,24},{24,20},{28,16},{1,9},{5... | collective-permute-start | bytes 442376 | tf_op jit(solution)/shard_map/ppermute | solution.py:618
  87.4 8.3 %collective-permute-start.21 = (bf16[576,128]{1,0:T(8,128)(2,1)S(1)}, bf16[576,128]{1,0:T(8,128)(2,1)S(1)}, u32[]{:S(2)}, u32[]{:S(2)}) collective-permute-start(bf16[576,128]{1,0:T(8,128)(2,1)S(1)} %get-tuple-element.47), channel_id=1, source_target_pairs={{0,20},{4,16},{8,28},{12,24},{16,0},{20,4},{24,8},{28,12},{1,21},{... | collective-permute-start | bytes 442376 | tf_op jit(solution)/shard_map/ppermute | solution.py:618
  88.7 8.6 %collective-permute-start.22 = (bf16[576,128]{1,0:T(8,128)(2,1)S(1)}, bf16[576,128]{1,0:T(8,128)(2,1)S(1)}, u32[]{:S(2)}, u32[]{:S(2)}) collective-permute-start(bf16[576,128]{1,0:T(8,128)(2,1)S(1)} %get-tuple-element.48), channel_id=1, source_target_pairs={{0,28},{4,24},{8,20},{12,16},{16,8},{20,12},{24,0},{28,4},{1,29},{... | collective-permute-start | bytes 442376 | tf_op jit(solution)/shard_map/ppermute | solution.py:618
  (5 other events, 91.8 us)

commit v9 on v8

--- a/solution.py
+++ b/solution.py
@@ -50,26 +50,33 @@
     return pltpu.with_memory_space_constraint(array, pltpu.HBM)
 
 
-def call(body, operands, outs, scalars=(), scratch=(), vmem=(), mib=12, estimate=None, name=None):
-    specs = [
-        pl.BlockSpec(memory_space=pltpu.VMEM) if n in vmem else whole_spec(x)
-        for n, x in enumerate(operands)
-    ]
-    operands = [in_vmem(x) if n in vmem else x for n, x in enumerate(operands)]
-    return pl.pallas_call(
+def call(
+    body, operands, outs, scalars=(), scratch=(), blocked=(), results=(), mib=12, estimate=None, name=None
+):
+    in_place = pl.BlockSpec(memory_space=pltpu.VMEM)
+    many = isinstance(outs, (list, tuple))
+    outs = list(outs) if many else [outs]
+    got = pl.pallas_call(
         body,
-        out_shape=outs,
+        out_shape=[
+            out if n in results else pltpu.VMEM(out.shape, out.dtype) for n, out in enumerate(outs)
+        ],
         grid_spec=pltpu.PrefetchScalarGridSpec(
             num_scalar_prefetch=len(scalars),
             grid=(1,),
-            in_specs=specs,
-            out_specs=jax.tree.map(whole_spec, outs),
+            in_specs=[
+                whole_spec(x) if n in blocked else in_place for n, x in enumerate(operands)
+            ],
+            out_specs=[
+                whole_spec(out) if n in results else in_place for n, out in enumerate(outs)
+            ],
             scratch_shapes=list(scratch),
         ),
         compiler_params=params(mib),
         cost_estimate=estimate or cost(0, MIB),
         name=name,
-    )(*scalars, *operands)
+    )(*scalars, *[x if n in blocked else in_vmem(x) for n, x in enumerate(operands)])
+    return got if many else got[0]
 
 
 def like(array, dtype=None):
@@ -97,6 +104,7 @@
         functools.partial(reorder_body, first=half * rows),
         [in_hbm(order_rows), in_hbm(features)],
         jax.ShapeDtypeStruct((rows, width), BF16),
+        blocked=(0, 1),
         estimate=cost(2 * rows * panel * width, 4 * rows * width),
         name="reorder",
     )
@@ -211,7 +219,6 @@
         outs,
         scalars=(plan,),
         scratch=[pltpu.VMEM((blocks, block, width), BF16), pltpu.VMEM((blocks + 1, block, width), F32)],
-        vmem=(0,),
         estimate=cost(2 * 64 * block * block * width, 12 * MIB),
         name="forward",
     )
@@ -295,7 +302,7 @@
         jax.ShapeDtypeStruct((rows * len(shares), width), BF16),
         jax.ShapeDtypeStruct((8, 128), jnp.int32),
     )
-    return call(finish_body, [weight, *shares], outs, estimate=cost(0, 4 * MIB), name="finish")
+    return call(finish_body, [weight, *shares], outs, results=(0,), estimate=cost(0, 4 * MIB), name="finish")
 
 
 def backward_body(entry_ref, tiles_ref, *refs, slots, keep, shape):
@@ -352,7 +359,6 @@
         jax.ShapeDtypeStruct(out_shape, F32 if keep else BF16),
         scalars=(plan,),
         scratch=[pltpu.VMEM((width, panel), BF16), pltpu.VMEM((blocks + 1, width, block), F32)],
-        vmem=(0,),
         estimate=cost(2 * 64 * block * block * width, 12 * MIB),
         name="backward",
     )
@@ -539,7 +545,7 @@
         body,
         [hot, *parts, *start],
         outs,
-        vmem=(0,),
+        results=(0, 1) if start else (),
         estimate=cost(2 * panel * panel * width, 4 * panel * width),
         name="restore",
     )

time: 99 us -> 99.9 us (level); the launches traced: 99.3 us -> 98.8 us
  Pallas kernels: 22.7 us -> 18.9 us
  waiting for transfers between devices: 40.6 us -> 43 us
  starting transfers between devices: 35 us -> 36 us
    pallas_call x17, Pallas kernels: 20.4 us -> 16.7 us  [call(): pl.pallas_call(body, out_shape=[out if n in results else pltpu.VMEM(out.s...]
    ppermute x3, waiting for transfers between devices: 4.39 us -> 6.06 us  [over_chips(): return lax.ppermute(x, 'section', [(s, s ^ 2 * d) for s in range(sections)])]
  transfers between devices with their start and end apart: 25 -> 25, of which waited for: 15 -> 15; matrix products, arithmetic and copies ran while one was open for 0% -> 0% of each run, Pallas kernels for 12% -> 11%
where the time goes in v9:
time: 99.9 us; the launch traced here: 98.8 us
  waiting for transfers between devices  43 us (43%)
  starting transfers between devices  36 us (36%)
  Pallas kernels  18.9 us (19%)
    ppermute x9, waiting for transfers between devices, over_reps(): return lax.ppermute(x, 'rep', [(r, r ^ d) for r in range(reps)])  27.5 us
    pallas_call x17, Pallas kernels, call(): pl.pallas_call(body, out_shape=[out if n in results else pltpu.VMEM(out.s...  16.7 us
    ppermute x9, starting transfers between devices, over_reps(): return lax.ppermute(x, 'rep', [(r, r ^ d) for r in range(reps)])  15.4 us
    ppermute x6, starting transfers between devices, from_owner(): return lax.ppermute(x, ('section', 'rep'), moves)  11.8 us
    ppermute x4, waiting for transfers between devices, to_owner(): return lax.ppermute(block, 'section', moves)  6.32 us
    ppermute x3, waiting for transfers between devices, over_chips(): return lax.ppermute(x, 'section', [(s, s ^ 2 * d) for s in range(sections)])  6.06 us
    ppermute x4, starting transfers between devices, to_owner(): return lax.ppermute(block, 'section', moves)  4.44 us
    ppermute x3, starting transfers between devices, over_chips(): return lax.ppermute(x, 'section', [(s, s ^ 2 * d) for s in range(sections)])  3.64 us
  transfers between devices with their start and end apart: 25, of which 15 were waited for; matrix products, arithmetic and copies ran while one was open for 0% of the time, Pallas kernels for 11%

profile of v9, /device:TPU:0, one launch (start us, length us, event | category | flops | bytes accessed | tf_op | source)
XLA Modules:
  0.0 98.8 jit_solution(10166735560788512321)
XLA Ops:
  0.6 2.6 %reorder.3.refs_0_ = bf16[1024,128]{1,0:T(8,128)(2,1)S(1)} custom-call(s32[16,128]{1,0:T(8,128)} %bitcast.7, bf16[2048,128]{1,0:T(8,128)(2,1)} %feat_ref.3), custom_call_target="tpu_custom_call" | custom-call | flops 536870912 | bytes 524288 | tf_op jit(solution)/shard_map/reorder/pallas_call | solution.py:59
  3.2 5.3 %collective-permute-start.2 = (bf16[1024,128]{1,0:T(8,128)(2,1)S(1)}, bf16[1024,128]{1,0:T(8,128)(2,1)S(1)}, u32[]{:S(2)}, u32[]{:S(2)}) collective-permute-start(bf16[1024,128]{1,0:T(8,128)(2,1)S(1)} %reorder.3.refs_0_), channel_id=1, source_target_pairs={{0,28},{16,12},{5,25},{21,9},{10,22},{26,6},{15,19},{31,3}} | collective-permute-start | bytes 786440 | tf_op jit(solution)/shard_map/ppermute | solution.py:586
  11.1 2.4 %reorder.2.refs_0_ = bf16[1024,128]{1,0:T(8,128)(2,1)S(1)} custom-call(s32[16,128]{1,0:T(8,128)} %bitcast.8, bf16[2048,128]{1,0:T(8,128)(2,1)} %feat_ref.3), custom_call_target="tpu_custom_call" | custom-call | flops 536870912 | bytes 524288 | tf_op jit(solution)/shard_map/reorder/pallas_call | solution.py:59
  20.0 1.5 %collective-permute-done.4.refs_1_ = bf16[1024,128]{1,0:T(8,128)(2,1)S(1)} collective-permute-done((bf16[1024,128]{1,0:T(8,128)(2,1)S(1)}, bf16[1024,128]{1,0:T(8,128)(2,1)S(1)}, u32[]{:S(2)}, u32[]{:S(2)}) %collective-permute-start.4) | collective-permute-done | bytes 262176 | tf_op jit(solution)/shard_map/ppermute | solution.py:586
  21.7 1.7 %forward.2.refs_2_ = f32[16,128,128]{2,1,0:T(8,128)S(1)} custom-call(s32[2,97]{1,0:T(2,128)S(1)} %entries_of.1.refs_4_.entry_ref, bf16[192,128,128]{2,1,0:T(8,128)(2,1)S(1)} %bitcast.3, bf16[1024,128]{1,0:T(8,128)(2,1)S(1)} %pick.2.refs_0_, bf16[1024,128]{1,0:T(8,128)(2,1)S(1)} %pick.3.refs_1_), custom_call_target="tpu_custom_call" | custom-call | flops 268435456 | bytes 12582912 | tf_op jit(solution)/shard_map/forward/pallas_call | solution.py:59
  24.4 1.8 %collective-permute-start.8 = (bf16[512,128]{1,0:T(8,128)(2,1)S(1)}, bf16[512,128]{1,0:T(8,128)(2,1)S(1)}, u32[]{:S(2)}, u32[]{:S(2)}) collective-permute-start(bf16[512,128]{1,0:T(8,128)(2,1)S(1)} %get-tuple-element.30), channel_id=1, source_target_pairs={{0,1},{1,0},{2,3},{3,2},{4,5},{5,4},{6,7},{7,6},{8,9},{9,8},{10,11... | collective-permute-start | bytes 393224 | tf_op jit(solution)/shard_map/ppermute | solution.py:577
  26.2 3.9 %collective-permute-start.9 = (bf16[512,128]{1,0:T(8,128)(2,1)S(1)}, bf16[512,128]{1,0:T(8,128)(2,1)S(1)}, u32[]{:S(2)}, u32[]{:S(2)}) collective-permute-start(bf16[512,128]{1,0:T(8,128)(2,1)S(1)} %get-tuple-element.31), channel_id=1, source_target_pairs={{0,2},{1,3},{2,0},{3,1},{4,6},{5,7},{6,4},{7,5},{8,10},{9,11},{10,... | collective-permute-start | bytes 393224 | tf_op jit(solution)/shard_map/ppermute | solution.py:577
  30.1 10.0 %collective-permute-done.9.refs_1_ = bf16[512,128]{1,0:T(8,128)(2,1)S(1)} collective-permute-done((bf16[512,128]{1,0:T(8,128)(2,1)S(1)}, bf16[512,128]{1,0:T(8,128)(2,1)S(1)}, u32[]{:S(2)}, u32[]{:S(2)}) %collective-permute-start.9) | collective-permute-done | bytes 131104 | tf_op jit(solution)/shard_map/ppermute | solution.py:577
  40.2 2.5 %collective-permute-start.11 = (bf16[512,128]{1,0:T(8,128)(2,1)S(1)}, bf16[512,128]{1,0:T(8,128)(2,1)S(1)}, u32[]{:S(2)}, u32[]{:S(2)}) collective-permute-start(bf16[512,128]{1,0:T(8,128)(2,1)S(1)} %total_of.1.refs_0_), channel_id=1, source_target_pairs={{0,1},{1,0},{2,3},{3,2},{4,5},{5,4},{6,7},{7,6},{8,9},{9,8},{10,11... | collective-permute-start | bytes 393224 | tf_op jit(solution)/shard_map/ppermute | solution.py:577
  42.7 2.7 %collective-permute-start.13 = (bf16[512,128]{1,0:T(8,128)(2,1)S(1)}, bf16[512,128]{1,0:T(8,128)(2,1)S(1)}, u32[]{:S(2)}, u32[]{:S(2)}) collective-permute-start(bf16[512,128]{1,0:T(8,128)(2,1)S(1)} %total_of.1.refs_0_), channel_id=1, source_target_pairs={{0,3},{1,2},{2,1},{3,0},{4,7},{5,6},{6,5},{7,4},{8,11},{9,10},{10,... | collective-permute-start | bytes 393224 | tf_op jit(solution)/shard_map/ppermute | solution.py:577
  46.6 5.7 %collective-permute-done.13.refs_1_.refs_3_ = bf16[512,128]{1,0:T(8,128)(2,1)S(1)} collective-permute-done((bf16[512,128]{1,0:T(8,128)(2,1)S(1)}, bf16[512,128]{1,0:T(8,128)(2,1)S(1)}, u32[]{:S(2)}, u32[]{:S(2)}) %collective-permute-start.13) | collective-permute-done | bytes 131104 | tf_op jit(solution)/shard_map/ppermute | solution.py:577
  52.3 3.4 %collective-permute-done.12.refs_0_.refs_2_ = bf16[512,128]{1,0:T(8,128)(2,1)S(1)} collective-permute-done((bf16[512,128]{1,0:T(8,128)(2,1)S(1)}, bf16[512,128]{1,0:T(8,128)(2,1)S(1)}, u32[]{:S(2)}, u32[]{:S(2)}) %collective-permute-start.12) | collective-permute-done | bytes 131104 | tf_op jit(solution)/shard_map/ppermute | solution.py:577
  57.7 1.7 %backward.2.kept_ref = f32[16,128,128]{2,1,0:T(8,128)S(1)} custom-call(s32[2,97]{1,0:T(2,128)S(1)} %entries_of.1.refs_4_.entry_ref, bf16[192,128,128]{2,1,0:T(8,128)(2,1)S(1)} %bitcast.6, bf16[2,128,512]{2,1,0:T(8,128)(2,1)S(1)} %get-tuple-element.33.refs_0_, bf16[2,128,512]{2,1,0:T(8,128)(2,1)S(1)} %up_shares.3.refs_1_), custom_call_target="tpu_custom_call" | custom-call | flops 268435456 | bytes 12582912 | tf_op jit(solution)/shard_map/backward/pallas_call | solution.py:59
  59.6 2.1 %collective-permute-start.15 = (bf16[576,128]{1,0:T(8,128)(2,1)S(1)}, bf16[576,128]{1,0:T(8,128)(2,1)S(1)}, u32[]{:S(2)}, u32[]{:S(2)}) collective-permute-start(bf16[576,128]{1,0:T(8,128)(2,1)S(1)} %get-tuple-element.42), channel_id=1, source_target_pairs={{0,8},{4,12},{8,0},{12,4},{16,24},{20,28},{24,16},{28,20},{1,9},{5... | collective-permute-start | bytes 442376 | tf_op jit(solution)/shard_map/ppermute | solution.py:571
  64.4 1.9 %collective-permute-done.15.refs_1_ = bf16[576,128]{1,0:T(8,128)(2,1)S(1)} collective-permute-done((bf16[576,128]{1,0:T(8,128)(2,1)S(1)}, bf16[576,128]{1,0:T(8,128)(2,1)S(1)}, u32[]{:S(2)}, u32[]{:S(2)}) %collective-permute-start.15) | collective-permute-done | bytes 147488 | tf_op jit(solution)/shard_map/ppermute | solution.py:571
  66.3 1.6 %collective-permute-done.16.refs_2_ = bf16[576,128]{1,0:T(8,128)(2,1)S(1)} collective-permute-done((bf16[576,128]{1,0:T(8,128)(2,1)S(1)}, bf16[576,128]{1,0:T(8,128)(2,1)S(1)}, u32[]{:S(2)}, u32[]{:S(2)}) %collective-permute-start.16) | collective-permute-done | bytes 147488 | tf_op jit(solution)/shard_map/ppermute | solution.py:571
  67.9 2.6 %collective-permute-done.17.refs_3_ = bf16[576,128]{1,0:T(8,128)(2,1)S(1)} collective-permute-done((bf16[576,128]{1,0:T(8,128)(2,1)S(1)}, bf16[576,128]{1,0:T(8,128)(2,1)S(1)}, u32[]{:S(2)}, u32[]{:S(2)}) %collective-permute-start.17) | collective-permute-done | bytes 147488 | tf_op jit(solution)/shard_map/ppermute | solution.py:571
  70.6 3.8 %collective-permute-start.20 = (bf16[576,128]{1,0:T(8,128)(2,1)S(1)}, bf16[576,128]{1,0:T(8,128)(2,1)S(1)}, u32[]{:S(2)}, u32[]{:S(2)}) collective-permute-start(bf16[576,128]{1,0:T(8,128)(2,1)S(1)} %gather_sum.1._.refs_0_), channel_id=1, source_target_pairs={{0,3},{1,2},{2,1},{3,0},{4,7},{5,6},{6,5},{7,4},{8,11},{9,10},{10,... | collective-permute-start | bytes 442376 | tf_op jit(solution)/shard_map/ppermute | solution.py:577
  76.5 2.7 %collective-permute-done.20.refs_3_ = bf16[576,128]{1,0:T(8,128)(2,1)S(1)} collective-permute-done((bf16[576,128]{1,0:T(8,128)(2,1)S(1)}, bf16[576,128]{1,0:T(8,128)(2,1)S(1)}, u32[]{:S(2)}, u32[]{:S(2)}) %collective-permute-start.20) | collective-permute-done | bytes 147488 | tf_op jit(solution)/shard_map/ppermute | solution.py:577
  79.2 5.3 %collective-permute-done.19.refs_2_ = bf16[576,128]{1,0:T(8,128)(2,1)S(1)} collective-permute-done((bf16[576,128]{1,0:T(8,128)(2,1)S(1)}, bf16[576,128]{1,0:T(8,128)(2,1)S(1)}, u32[]{:S(2)}, u32[]{:S(2)}) %collective-permute-start.19) | collective-permute-done | bytes 147488 | tf_op jit(solution)/shard_map/ppermute | solution.py:577
  86.7 1.7 %collective-permute-start.21 = (bf16[576,128]{1,0:T(8,128)(2,1)S(1)}, bf16[576,128]{1,0:T(8,128)(2,1)S(1)}, u32[]{:S(2)}, u32[]{:S(2)}) collective-permute-start(bf16[576,128]{1,0:T(8,128)(2,1)S(1)} %get-tuple-element.47), channel_id=1, source_target_pairs={{0,20},{4,16},{8,28},{12,24},{16,0},{20,4},{24,8},{28,12},{1,21},{... | collective-permute-start | bytes 442376 | tf_op jit(solution)/shard_map/ppermute | solution.py:624
  89.2 2.1 %collective-permute-done.24.refs_1_ = bf16[576,128]{1,0:T(8,128)(2,1)S(1)} collective-permute-done((bf16[576,128]{1,0:T(8,128)(2,1)S(1)}, bf16[576,128]{1,0:T(8,128)(2,1)S(1)}, u32[]{:S(2)}, u32[]{:S(2)}) %collective-permute-start.24) | collective-permute-done | bytes 147488 | tf_op jit(solution)/shard_map/ppermute | solution.py:624
  92.5 3.1 %collective-permute-done.21.refs_0_ = bf16[576,128]{1,0:T(8,128)(2,1)S(1)} collective-permute-done((bf16[576,128]{1,0:T(8,128)(2,1)S(1)}, bf16[576,128]{1,0:T(8,128)(2,1)S(1)}, u32[]{:S(2)}, u32[]{:S(2)}) %collective-permute-start.21) | collective-permute-done | bytes 147488 | tf_op jit(solution)/shard_map/ppermute | solution.py:624
  96.8 2.1 %restore.3 = (bf16[2048,128]{1,0:T(8,128)(2,1)}, f32[128,128]{1,0:T(8,128)}) custom-call(bf16[2048,2048]{1,0:T(8,128)(2,1)S(1)} %get-tuple-element.45.hot_ref, bf16[576,128]{1,0:T(8,128)(2,1)S(1)} %collective-permute-done.21.refs_0_, bf16[576,128]{1,0:T(8,128)(2,1)S(1)} %collective-permute-done.22.refs_1_, f32[2048,128]{1,0:T(8,128)S(1)} %get-tuple-element.51.refs_2_, ...), custom_call_target="tpu_custom_call" | custom-call | flops 1073741824 | bytes 1048576 | tf_op jit(solution)/shard_map/restore/pallas_call | solution.py:59
  (54 shorter events, 23.9 us)
Async XLA Ops:
  3.2 13.0 %collective-permute-start.2 = (bf16[1024,128]{1,0:T(8,128)(2,1)S(1)}, bf16[1024,128]{1,0:T(8,128)(2,1)S(1)}, u32[]{:S(2)}, u32[]{:S(2)}) collective-permute-start(bf16[1024,128]{1,0:T(8,128)(2,1)S(1)} %reorder.3.refs_0_), channel_id=1, source_target_pairs={{0,28},{16,12},{5,25},{21,9},{10,22},{26,6},{15,19},{31,3}} | collective-permute-start | bytes 786440 | tf_op jit(solution)/shard_map/ppermute | solution.py:586
  8.5 9.8 %collective-permute-start.1 = (bf16[1024,128]{1,0:T(8,128)(2,1)S(1)}, bf16[1024,128]{1,0:T(8,128)(2,1)S(1)}, u32[]{:S(2)}, u32[]{:S(2)}) collective-permute-start(bf16[1024,128]{1,0:T(8,128)(2,1)S(1)} %reorder.3.refs_0_), channel_id=1, source_target_pairs={{0,20},{16,4},{5,17},{21,1},{10,30},{26,14},{15,27},{31,11}} | collective-permute-start | bytes 786440 | tf_op jit(solution)/shard_map/ppermute | solution.py:586
  9.8 8.5 %collective-permute-start = (bf16[1024,128]{1,0:T(8,128)(2,1)S(1)}, bf16[1024,128]{1,0:T(8,128)(2,1)S(1)}, u32[]{:S(2)}, u32[]{:S(2)}) collective-permute-start(bf16[1024,128]{1,0:T(8,128)(2,1)S(1)} %reorder.3.refs_0_), channel_id=1, source_target_pairs={{0,8},{16,24},{5,13},{21,29},{10,2},{26,18},{15,7},{31,23}} | collective-permute-start | bytes 786440 | tf_op jit(solution)/shard_map/ppermute | solution.py:586
  13.6 5.2 %collective-permute-start.6 = (bf16[1024,128]{1,0:T(8,128)(2,1)S(1)}, bf16[1024,128]{1,0:T(8,128)(2,1)S(1)}, u32[]{:S(2)}, u32[]{:S(2)}) collective-permute-start(bf16[1024,128]{1,0:T(8,128)(2,1)S(1)} %reorder.2.refs_0_), channel_id=1, source_target_pairs={{0,28},{16,12},{5,25},{21,9},{10,22},{26,6},{15,19},{31,3}} | collective-permute-start | bytes 786440 | tf_op jit(solution)/shard_map/ppermute | solution.py:586
  14.9 5.2 %collective-permute-start.5 = (bf16[1024,128]{1,0:T(8,128)(2,1)S(1)}, bf16[1024,128]{1,0:T(8,128)(2,1)S(1)}, u32[]{:S(2)}, u32[]{:S(2)}) collective-permute-start(bf16[1024,128]{1,0:T(8,128)(2,1)S(1)} %reorder.2.refs_0_), channel_id=1, source_target_pairs={{0,20},{16,4},{5,17},{21,1},{10,30},{26,14},{15,27},{31,11}} | collective-permute-start | bytes 786440 | tf_op jit(solution)/shard_map/ppermute | solution.py:586
  16.2 5.3 %collective-permute-start.4 = (bf16[1024,128]{1,0:T(8,128)(2,1)S(1)}, bf16[1024,128]{1,0:T(8,128)(2,1)S(1)}, u32[]{:S(2)}, u32[]{:S(2)}) collective-permute-start(bf16[1024,128]{1,0:T(8,128)(2,1)S(1)} %reorder.2.refs_0_), channel_id=1, source_target_pairs={{0,8},{16,24},{5,13},{21,29},{10,2},{26,18},{15,7},{31,23}} | collective-permute-start | bytes 786440 | tf_op jit(solution)/shard_map/ppermute | solution.py:586
  18.4 4.9 %collective-permute-start.3 = (bf16[1024,128]{1,0:T(8,128)(2,1)S(1)}, bf16[1024,128]{1,0:T(8,128)(2,1)S(1)}, u32[]{:S(2)}, u32[]{:S(2)}) collective-permute-start(bf16[1024,128]{1,0:T(8,128)(2,1)S(1)} %pick.2.refs_0_), channel_id=1, source_target_pairs={{0,4},{4,0},{8,12},{12,8},{16,20},{20,16},{24,28},{28,24},{1,5},{5... | collective-permute-start | bytes 786440 | tf_op jit(solution)/shard_map/ppermute | solution.py:574
  24.4 5.7 %collective-permute-start.8 = (bf16[512,128]{1,0:T(8,128)(2,1)S(1)}, bf16[512,128]{1,0:T(8,128)(2,1)S(1)}, u32[]{:S(2)}, u32[]{:S(2)}) collective-permute-start(bf16[512,128]{1,0:T(8,128)(2,1)S(1)} %get-tuple-element.30), channel_id=1, source_target_pairs={{0,1},{1,0},{2,3},{3,2},{4,5},{5,4},{6,7},{7,6},{8,9},{9,8},{10,11... | collective-permute-start | bytes 393224 | tf_op jit(solution)/shard_map/ppermute | solution.py:577
  26.2 13.9 %collective-permute-start.9 = (bf16[512,128]{1,0:T(8,128)(2,1)S(1)}, bf16[512,128]{1,0:T(8,128)(2,1)S(1)}, u32[]{:S(2)}, u32[]{:S(2)}) collective-permute-start(bf16[512,128]{1,0:T(8,128)(2,1)S(1)} %get-tuple-element.31), channel_id=1, source_target_pairs={{0,2},{1,3},{2,0},{3,1},{4,6},{5,7},{6,4},{7,5},{8,10},{9,11},{10,... | collective-permute-start | bytes 393224 | tf_op jit(solution)/shard_map/ppermute | solution.py:577
  30.1 10.0 %collective-permute-start.10 = (bf16[512,128]{1,0:T(8,128)(2,1)S(1)}, bf16[512,128]{1,0:T(8,128)(2,1)S(1)}, u32[]{:S(2)}, u32[]{:S(2)}) collective-permute-start(bf16[512,128]{1,0:T(8,128)(2,1)S(1)} %get-tuple-element.32), channel_id=1, source_target_pairs={{0,3},{1,2},{2,1},{3,0},{4,7},{5,6},{6,5},{7,4},{8,11},{9,10},{10,... | collective-permute-start | bytes 393224 | tf_op jit(solution)/shard_map/ppermute | solution.py:577
  40.2 5.8 %collective-permute-start.11 = (bf16[512,128]{1,0:T(8,128)(2,1)S(1)}, bf16[512,128]{1,0:T(8,128)(2,1)S(1)}, u32[]{:S(2)}, u32[]{:S(2)}) collective-permute-start(bf16[512,128]{1,0:T(8,128)(2,1)S(1)} %total_of.1.refs_0_), channel_id=1, source_target_pairs={{0,1},{1,0},{2,3},{3,2},{4,5},{5,4},{6,7},{7,6},{8,9},{9,8},{10,11... | collective-permute-start | bytes 393224 | tf_op jit(solution)/shard_map/ppermute | solution.py:577
  42.7 9.5 %collective-permute-start.13 = (bf16[512,128]{1,0:T(8,128)(2,1)S(1)}, bf16[512,128]{1,0:T(8,128)(2,1)S(1)}, u32[]{:S(2)}, u32[]{:S(2)}) collective-permute-start(bf16[512,128]{1,0:T(8,128)(2,1)S(1)} %total_of.1.refs_0_), channel_id=1, source_target_pairs={{0,3},{1,2},{2,1},{3,0},{4,7},{5,6},{6,5},{7,4},{8,11},{9,10},{10,... | collective-permute-start | bytes 393224 | tf_op jit(solution)/shard_map/ppermute | solution.py:577
  45.4 10.2 %collective-permute-start.12 = (bf16[512,128]{1,0:T(8,128)(2,1)S(1)}, bf16[512,128]{1,0:T(8,128)(2,1)S(1)}, u32[]{:S(2)}, u32[]{:S(2)}) collective-permute-start(bf16[512,128]{1,0:T(8,128)(2,1)S(1)} %total_of.1.refs_0_), channel_id=1, source_target_pairs={{0,2},{1,3},{2,0},{3,1},{4,6},{5,7},{6,4},{7,5},{8,10},{9,11},{10,... | collective-permute-start | bytes 393224 | tf_op jit(solution)/shard_map/ppermute | solution.py:577
  57.2 2.2 %collective-permute-start.14 = (bf16[18,128,128]{2,1,0:T(8,128)(2,1)S(1)}, bf16[18,128,128]{2,1,0:T(8,128)(2,1)S(1)}, u32[]{:S(2)}, u32[]{:S(2)}) collective-permute-start(bf16[18,128,128]{2,1,0:T(8,128)(2,1)S(1)} %backward.3), channel_id=1, source_target_pairs={{0,4},{4,0},{8,12},{12,8},{16,20},{20,16},{24,28},{28,24},{1,5},{5... | collective-permute-start | bytes 1769480 | tf_op jit(solution)/shard_map/ppermute | solution.py:574
  59.6 6.8 %collective-permute-start.15 = (bf16[576,128]{1,0:T(8,128)(2,1)S(1)}, bf16[576,128]{1,0:T(8,128)(2,1)S(1)}, u32[]{:S(2)}, u32[]{:S(2)}) collective-permute-start(bf16[576,128]{1,0:T(8,128)(2,1)S(1)} %get-tuple-element.42), channel_id=1, source_target_pairs={{0,8},{4,12},{8,0},{12,4},{16,24},{20,28},{24,16},{28,20},{1,9},{5... | collective-permute-start | bytes 442376 | tf_op jit(solution)/shard_map/ppermute | solution.py:571
  61.6 6.3 %collective-permute-start.16 = (bf16[576,128]{1,0:T(8,128)(2,1)S(1)}, bf16[576,128]{1,0:T(8,128)(2,1)S(1)}, u32[]{:S(2)}, u32[]{:S(2)}) collective-permute-start(bf16[576,128]{1,0:T(8,128)(2,1)S(1)} %get-tuple-element.43), channel_id=1, source_target_pairs={{0,16},{4,20},{8,24},{12,28},{16,0},{20,4},{24,8},{28,12},{1,17},{... | collective-permute-start | bytes 442376 | tf_op jit(solution)/shard_map/ppermute | solution.py:571
  62.0 8.5 %collective-permute-start.17 = (bf16[576,128]{1,0:T(8,128)(2,1)S(1)}, bf16[576,128]{1,0:T(8,128)(2,1)S(1)}, u32[]{:S(2)}, u32[]{:S(2)}) collective-permute-start(bf16[576,128]{1,0:T(8,128)(2,1)S(1)} %get-tuple-element.35), channel_id=1, source_target_pairs={{0,24},{4,28},{8,16},{12,20},{16,8},{20,12},{24,0},{28,4},{1,25},{... | collective-permute-start | bytes 442376 | tf_op jit(solution)/shard_map/ppermute | solution.py:571
  70.6 8.7 %collective-permute-start.20 = (bf16[576,128]{1,0:T(8,128)(2,1)S(1)}, bf16[576,128]{1,0:T(8,128)(2,1)S(1)}, u32[]{:S(2)}, u32[]{:S(2)}) collective-permute-start(bf16[576,128]{1,0:T(8,128)(2,1)S(1)} %gather_sum.1._.refs_0_), channel_id=1, source_target_pairs={{0,3},{1,2},{2,1},{3,0},{4,7},{5,6},{6,5},{7,4},{8,11},{9,10},{10,... | collective-permute-start | bytes 442376 | tf_op jit(solution)/shard_map/ppermute | solution.py:577
  74.4 10.1 %collective-permute-start.19 = (bf16[576,128]{1,0:T(8,128)(2,1)S(1)}, bf16[576,128]{1,0:T(8,128)(2,1)S(1)}, u32[]{:S(2)}, u32[]{:S(2)}) collective-permute-start(bf16[576,128]{1,0:T(8,128)(2,1)S(1)} %gather_sum.1._.refs_0_), channel_id=1, source_target_pairs={{0,2},{1,3},{2,0},{3,1},{4,6},{5,7},{6,4},{7,5},{8,10},{9,11},{10,... | collective-permute-start | bytes 442376 | tf_op jit(solution)/shard_map/ppermute | solution.py:577
  74.4 10.1 %collective-permute-start.18 = (bf16[576,128]{1,0:T(8,128)(2,1)S(1)}, bf16[576,128]{1,0:T(8,128)(2,1)S(1)}, u32[]{:S(2)}, u32[]{:S(2)}) collective-permute-start(bf16[576,128]{1,0:T(8,128)(2,1)S(1)} %gather_sum.1._.refs_0_), channel_id=1, source_target_pairs={{0,1},{1,0},{2,3},{3,2},{4,5},{5,4},{6,7},{7,6},{8,9},{9,8},{10,11... | collective-permute-start | bytes 442376 | tf_op jit(solution)/shard_map/ppermute | solution.py:577
  84.8 4.5 %collective-permute-start.23 = (bf16[576,128]{1,0:T(8,128)(2,1)S(1)}, bf16[576,128]{1,0:T(8,128)(2,1)S(1)}, u32[]{:S(2)}, u32[]{:S(2)}) collective-permute-start(bf16[576,128]{1,0:T(8,128)(2,1)S(1)} %get-tuple-element.49), channel_id=1, source_target_pairs={{0,0},{4,4},{8,8},{12,12},{16,20},{20,16},{24,28},{28,24},{1,1},{5... | collective-permute-start | bytes 442376 | tf_op jit(solution)/shard_map/ppermute | solution.py:624
  85.5 5.8 %collective-permute-start.24 = (bf16[576,128]{1,0:T(8,128)(2,1)S(1)}, bf16[576,128]{1,0:T(8,128)(2,1)S(1)}, u32[]{:S(2)}, u32[]{:S(2)}) collective-permute-start(bf16[576,128]{1,0:T(8,128)(2,1)S(1)} %get-tuple-element.50), channel_id=1, source_target_pairs={{0,8},{4,12},{8,0},{12,4},{16,28},{20,24},{24,20},{28,16},{1,9},{5... | collective-permute-start | bytes 442376 | tf_op jit(solution)/shard_map/ppermute | solution.py:624
  86.7 8.9 %collective-permute-start.21 = (bf16[576,128]{1,0:T(8,128)(2,1)S(1)}, bf16[576,128]{1,0:T(8,128)(2,1)S(1)}, u32[]{:S(2)}, u32[]{:S(2)}) collective-permute-start(bf16[576,128]{1,0:T(8,128)(2,1)S(1)} %get-tuple-element.47), channel_id=1, source_target_pairs={{0,20},{4,16},{8,28},{12,24},{16,0},{20,4},{24,8},{28,12},{1,21},{... | collective-permute-start | bytes 442376 | tf_op jit(solution)/shard_map/ppermute | solution.py:624
  88.4 8.4 %collective-permute-start.22 = (bf16[576,128]{1,0:T(8,128)(2,1)S(1)}, bf16[576,128]{1,0:T(8,128)(2,1)S(1)}, u32[]{:S(2)}, u32[]{:S(2)}) collective-permute-start(bf16[576,128]{1,0:T(8,128)(2,1)S(1)} %get-tuple-element.48), channel_id=1, source_target_pairs={{0,28},{4,24},{8,20},{12,16},{16,8},{20,12},{24,0},{28,4},{1,29},{... | collective-permute-start | bytes 442376 | tf_op jit(solution)/shard_map/ppermute | solution.py:624
  (5 other events, 90.5 us)

commit v10 on v9

--- a/solution.py
+++ b/solution.py
@@ -42,6 +42,11 @@
         self.low = ((section % reps) // 2) ^ (self.rep // 2)
 
 
+def row_spec(array, steps):
+    rest = (0,) * (array.ndim - 1)
+    return pl.BlockSpec((array.shape[0] // steps, *array.shape[1:]), lambda i, *_: (i, *rest))
+
+
 def in_vmem(array):
     return pltpu.with_memory_space_constraint(array, pltpu.VMEM)
 
@@ -51,7 +56,8 @@
 
 
 def call(
-    body, operands, outs, scalars=(), scratch=(), blocked=(), results=(), mib=12, estimate=None, name=None
+    body, operands, outs, scalars=(), scratch=(), blocked=(), results=(), steps=1, mib=12,
+    estimate=None, name=None
 ):
     in_place = pl.BlockSpec(memory_space=pltpu.VMEM)
     many = isinstance(outs, (list, tuple))
@@ -63,12 +69,13 @@
         ],
         grid_spec=pltpu.PrefetchScalarGridSpec(
             num_scalar_prefetch=len(scalars),
-            grid=(1,),
+            grid=(steps,),
             in_specs=[
                 whole_spec(x) if n in blocked else in_place for n, x in enumerate(operands)
             ],
             out_specs=[
-                whole_spec(out) if n in results else in_place for n, out in enumerate(outs)
+                (row_spec(out, steps) if n == 0 else whole_spec(out)) if n in results else in_place
+                for n, out in enumerate(outs)
             ],
             scratch_shapes=list(scratch),
         ),
@@ -83,7 +90,9 @@
     return jax.ShapeDtypeStruct(array.shape, dtype or array.dtype)
 
 
-def reorder_body(order_ref, feat_ref, out_ref, *, first):
+def reorder_body(order_ref, feat_ref, out_ref, *kept, first):
+    if kept:
+        kept[0][...], kept[1][...] = order_ref[...], feat_ref[...]
     panel = feat_ref.shape[0]
     rows = out_ref.shape[0]
     step = order_ref.shape[1]
@@ -97,17 +106,23 @@
         ).astype(BF16)
 
 
-def reorder(order_rows, features, half):
+def reorder(order_rows, features):
     panel, width = features.shape
     rows = panel // HALVES
-    return call(
-        functools.partial(reorder_body, first=half * rows),
-        [in_hbm(order_rows), in_hbm(features)],
-        jax.ShapeDtypeStruct((rows, width), BF16),
-        blocked=(0, 1),
-        estimate=cost(2 * rows * panel * width, 4 * rows * width),
-        name="reorder",
-    )
+    half = jax.ShapeDtypeStruct((rows, width), BF16)
+    halves, kept = [], [in_hbm(order_rows), in_hbm(features)]
+    for h in range(HALVES):
+        got = call(
+            functools.partial(reorder_body, first=h * rows),
+            kept,
+            [half] if h else [half, like(order_rows), like(features)],
+            blocked=() if h else (0, 1),
+            estimate=cost(2 * rows * panel * width, 4 * rows * width),
+            name="reorder",
+        )
+        halves.append(got[0])
+        kept = kept if h else got[1:]
+    return halves
 
 
 def entry_body(rows_ref, cols_ref, live_ref, _, out_ref, *, bits):
@@ -506,19 +521,24 @@
     block = parts[0].shape[1]
     extra = (parts[0].shape[0] - per * block) // 2
     length = per * block
-    grad_ref[...] = start[1][...] if start else jnp.zeros_like(grad_ref)
+    base = pl.program_id(0) * out_ref.shape[0]
+
+    @pl.when(base == 0)
+    def _():
+        grad_ref[...] = start[1][...] if start else jnp.zeros_like(grad_ref)
+        for n, part in enumerate(parts):
+            at = pl.multiple_of((chip ^ (first + n)) * extra, extra)
+            grad_ref[pl.ds(at, extra), :] = sum_of_parts(part, length, extra) * scale
+
     columns, places = [], []
     for n, part in enumerate(parts):
-        u = chip ^ (first + n)
-        at = pl.multiple_of(u * extra, extra)
-        grad_ref[pl.ds(at, extra), :] = sum_of_parts(part, length, extra) * scale
         columns.append(
             jnp.concatenate([part[b * block : (b + 1) * block, :] for b in range(per)], axis=1)
         )
-        places.append(pl.multiple_of(u * length, length))
-    rows = 512
+        places.append(pl.multiple_of((chip ^ (first + n)) * length, length))
+    rows = min(512, out_ref.shape[0])
     for i in range(out_ref.shape[0] // rows):
-        span = slice(i * rows, (i + 1) * rows)
+        span = pl.ds(pl.multiple_of(base + i * rows, rows), rows)
         acc = start[0][span, :] if start else None
         for n, at in enumerate(places):
             term = lax.dot_general(
@@ -528,7 +548,7 @@
                 preferred_element_type=F32,
             )
             acc = term if acc is None else acc + term
-        out_ref[span, :] = acc.astype(out_ref.dtype)
+        out_ref[i * rows : (i + 1) * rows, :] = acc.astype(out_ref.dtype)
 
 
 def restore(hot, parts, first, start, per, scale):
@@ -546,6 +566,7 @@
         [hot, *parts, *start],
         outs,
         results=(0, 1) if start else (),
+        steps=4 if start else 1,
         estimate=cost(2 * panel * panel * width, 4 * panel * width),
         name="restore",
     )
@@ -586,7 +607,7 @@
         return lax.ppermute(x, ("section", "rep"), moves)
 
     order_rows, order_row = order.reshape(panel // block, block), order.reshape(1, panel)
-    owns = [reorder(order_rows, features, h) for h in range(HALVES)]
+    owns = reorder(order_rows, features)
     gots = [[own] + [from_owner(own, d) for d in range(1, chips)] for own in owns]
     bits = (blocks - 1).bit_length()
     plan = entries_of(tile_rows, tile_cols, live, bits, owns[-1][:16])

time: 99.9 us -> 101 us (1.011)
  waiting for transfers between devices: 43 us -> 44.9 us
    ppermute x6, waiting for transfers between devices: 3.04 us -> 4.72 us  [from_owner(): return lax.ppermute(x, ('section', 'rep'), moves)]
    ppermute x3, waiting for transfers between devices: 6.06 us -> 4.48 us  [over_chips(): return lax.ppermute(x, 'section', [(s, s ^ 2 * d) for s in range(sections)])]
    ppermute x9, waiting for transfers between devices: 27.5 us -> 29.1 us  [over_reps(): return lax.ppermute(x, 'rep', [(r, r ^ d) for r in range(reps)])]
  transfers between devices with their start and end apart: 25 -> 25, of which waited for: 15 -> 15; matrix products, arithmetic and copies ran while one was open for 0% -> 0% of each run, Pallas kernels for 11% -> 9%
where the time goes in v10:
time: 101 us
  waiting for transfers between devices  44.9 us (44%)
  starting transfers between devices  35.6 us (35%)
  Pallas kernels  19.2 us (19%)
    ppermute x9, waiting for transfers between devices, over_reps(): return lax.ppermute(x, 'rep', [(r, r ^ d) for r in range(reps)])  29.1 us
    pallas_call x17, Pallas kernels, call(): pl.pallas_call(body, out_shape=[out if n in results else pltpu.VMEM(out.s...  16.9 us
    ppermute x9, starting transfers between devices, over_reps(): return lax.ppermute(x, 'rep', [(r, r ^ d) for r in range(reps)])  15.5 us
    ppermute x6, starting transfers between devices, from_owner(): return lax.ppermute(x, ('section', 'rep'), moves)  11.8 us
    ppermute x4, waiting for transfers between devices, to_owner(): return lax.ppermute(block, 'section', moves)  6.31 us
    ppermute x6, waiting for transfers between devices, from_owner(): return lax.ppermute(x, ('section', 'rep'), moves)  4.72 us
    ppermute x4, starting transfers between devices, to_owner(): return lax.ppermute(block, 'section', moves)  4.54 us
    ppermute x3, waiting for transfers between devices, over_chips(): return lax.ppermute(x, 'section', [(s, s ^ 2 * d) for s in range(sections)])  4.48 us
  transfers between devices with their start and end apart: 25, of which 15 were waited for; matrix products, arithmetic and copies ran while one was open for 0% of the time, Pallas kernels for 9%

profile of v10, /device:TPU:0, one launch (start us, length us, event | category | flops | bytes accessed | tf_op | source)
XLA Modules:
  0.0 100.6 jit_solution(4702245999446084235)
XLA Ops:
  0.6 2.6 %reorder.2 = (bf16[1024,128]{1,0:T(8,128)(2,1)S(1)}, s32[16,128]{1,0:T(8,128)S(1)}, bf16[2048,128]{1,0:T(8,128)(2,1)S(1)}) custom-call(s32[16,128]{1,0:T(8,128)} %bitcast.7, bf16[2048,128]{1,0:T(8,128)(2,1)} %feat_ref.1), custom_call_target="tpu_custom_call" | custom-call | flops 536870912 | bytes 524288 | tf_op jit(solution)/shard_map/reorder/pallas_call | solution.py:65
  4.6 5.3 %collective-permute-start.6 = (bf16[1024,128]{1,0:T(8,128)(2,1)S(1)}, bf16[1024,128]{1,0:T(8,128)(2,1)S(1)}, u32[]{:S(2)}, u32[]{:S(2)}) collective-permute-start(bf16[1024,128]{1,0:T(8,128)(2,1)S(1)} %reorder.3.refs_0_), channel_id=1, source_target_pairs={{0,28},{16,12},{5,25},{21,9},{10,22},{26,6},{15,19},{31,3}} | collective-permute-start | bytes 786440 | tf_op jit(solution)/shard_map/ppermute | solution.py:607
  17.5 1.9 %collective-permute-done.2.refs_3_ = bf16[1024,128]{1,0:T(8,128)(2,1)S(1)} collective-permute-done((bf16[1024,128]{1,0:T(8,128)(2,1)S(1)}, bf16[1024,128]{1,0:T(8,128)(2,1)S(1)}, u32[]{:S(2)}, u32[]{:S(2)}) %collective-permute-start.2) | collective-permute-done | bytes 262176 | tf_op jit(solution)/shard_map/ppermute | solution.py:607
  19.4 2.8 %collective-permute-done.refs_1_ = bf16[1024,128]{1,0:T(8,128)(2,1)S(1)} collective-permute-done((bf16[1024,128]{1,0:T(8,128)(2,1)S(1)}, bf16[1024,128]{1,0:T(8,128)(2,1)S(1)}, u32[]{:S(2)}, u32[]{:S(2)}) %collective-permute-start) | collective-permute-done | bytes 262176 | tf_op jit(solution)/shard_map/ppermute | solution.py:607
  22.3 1.7 %forward.2.refs_2_ = f32[16,128,128]{2,1,0:T(8,128)S(1)} custom-call(s32[2,97]{1,0:T(2,128)S(1)} %entries_of.1.refs_4_.entry_ref, bf16[192,128,128]{2,1,0:T(8,128)(2,1)S(1)} %bitcast.3, bf16[1024,128]{1,0:T(8,128)(2,1)S(1)} %pick.2.refs_0_, bf16[1024,128]{1,0:T(8,128)(2,1)S(1)} %pick.3.refs_1_), custom_call_target="tpu_custom_call" | custom-call | flops 268435456 | bytes 12582912 | tf_op jit(solution)/shard_map/forward/pallas_call | solution.py:65
  25.4 2.7 %collective-permute-start.8 = (bf16[512,128]{1,0:T(8,128)(2,1)S(1)}, bf16[512,128]{1,0:T(8,128)(2,1)S(1)}, u32[]{:S(2)}, u32[]{:S(2)}) collective-permute-start(bf16[512,128]{1,0:T(8,128)(2,1)S(1)} %get-tuple-element.36), channel_id=1, source_target_pairs={{0,1},{1,0},{2,3},{3,2},{4,5},{5,4},{6,7},{7,6},{8,9},{9,8},{10,11... | collective-permute-start | bytes 393224 | tf_op jit(solution)/shard_map/ppermute | solution.py:598
  28.0 2.3 %collective-permute-start.9 = (bf16[512,128]{1,0:T(8,128)(2,1)S(1)}, bf16[512,128]{1,0:T(8,128)(2,1)S(1)}, u32[]{:S(2)}, u32[]{:S(2)}) collective-permute-start(bf16[512,128]{1,0:T(8,128)(2,1)S(1)} %get-tuple-element.37), channel_id=1, source_target_pairs={{0,2},{1,3},{2,0},{3,1},{4,6},{5,7},{6,4},{7,5},{8,10},{9,11},{10,... | collective-permute-start | bytes 393224 | tf_op jit(solution)/shard_map/ppermute | solution.py:598
  31.8 9.0 %collective-permute-done.9.refs_1_ = bf16[512,128]{1,0:T(8,128)(2,1)S(1)} collective-permute-done((bf16[512,128]{1,0:T(8,128)(2,1)S(1)}, bf16[512,128]{1,0:T(8,128)(2,1)S(1)}, u32[]{:S(2)}, u32[]{:S(2)}) %collective-permute-start.9) | collective-permute-done | bytes 131104 | tf_op jit(solution)/shard_map/ppermute | solution.py:598
  40.9 2.9 %collective-permute-start.11 = (bf16[512,128]{1,0:T(8,128)(2,1)S(1)}, bf16[512,128]{1,0:T(8,128)(2,1)S(1)}, u32[]{:S(2)}, u32[]{:S(2)}) collective-permute-start(bf16[512,128]{1,0:T(8,128)(2,1)S(1)} %total_of.1.refs_0_), channel_id=1, source_target_pairs={{0,1},{1,0},{2,3},{3,2},{4,5},{5,4},{6,7},{7,6},{8,9},{9,8},{10,11... | collective-permute-start | bytes 393224 | tf_op jit(solution)/shard_map/ppermute | solution.py:598
  43.8 2.9 %collective-permute-start.13 = (bf16[512,128]{1,0:T(8,128)(2,1)S(1)}, bf16[512,128]{1,0:T(8,128)(2,1)S(1)}, u32[]{:S(2)}, u32[]{:S(2)}) collective-permute-start(bf16[512,128]{1,0:T(8,128)(2,1)S(1)} %total_of.1.refs_0_), channel_id=1, source_target_pairs={{0,3},{1,2},{2,1},{3,0},{4,7},{5,6},{6,5},{7,4},{8,11},{9,10},{10,... | collective-permute-start | bytes 393224 | tf_op jit(solution)/shard_map/ppermute | solution.py:598
  47.7 6.3 %collective-permute-done.13.refs_1_.refs_3_ = bf16[512,128]{1,0:T(8,128)(2,1)S(1)} collective-permute-done((bf16[512,128]{1,0:T(8,128)(2,1)S(1)}, bf16[512,128]{1,0:T(8,128)(2,1)S(1)}, u32[]{:S(2)}, u32[]{:S(2)}) %collective-permute-start.13) | collective-permute-done | bytes 131104 | tf_op jit(solution)/shard_map/ppermute | solution.py:598
  54.0 3.6 %collective-permute-done.12.refs_0_.refs_2_ = bf16[512,128]{1,0:T(8,128)(2,1)S(1)} collective-permute-done((bf16[512,128]{1,0:T(8,128)(2,1)S(1)}, bf16[512,128]{1,0:T(8,128)(2,1)S(1)}, u32[]{:S(2)}, u32[]{:S(2)}) %collective-permute-start.12) | collective-permute-done | bytes 131104 | tf_op jit(solution)/shard_map/ppermute | solution.py:598
  59.5 1.7 %backward.2.kept_ref = f32[16,128,128]{2,1,0:T(8,128)S(1)} custom-call(s32[2,97]{1,0:T(2,128)S(1)} %entries_of.1.refs_4_.entry_ref, bf16[192,128,128]{2,1,0:T(8,128)(2,1)S(1)} %bitcast.6, bf16[2,128,512]{2,1,0:T(8,128)(2,1)S(1)} %get-tuple-element.39.refs_0_, bf16[2,128,512]{2,1,0:T(8,128)(2,1)S(1)} %up_shares.3.refs_1_), custom_call_target="tpu_custom_call" | custom-call | flops 268435456 | bytes 12582912 | tf_op jit(solution)/shard_map/backward/pallas_call | solution.py:65
  62.8 2.4 %collective-permute-start.17 = (bf16[576,128]{1,0:T(8,128)(2,1)S(1)}, bf16[576,128]{1,0:T(8,128)(2,1)S(1)}, u32[]{:S(2)}, u32[]{:S(2)}) collective-permute-start(bf16[576,128]{1,0:T(8,128)(2,1)S(1)} %get-tuple-element.41), channel_id=1, source_target_pairs={{0,24},{4,28},{8,16},{12,20},{16,8},{20,12},{24,0},{28,4},{1,25},{... | collective-permute-start | bytes 442376 | tf_op jit(solution)/shard_map/ppermute | solution.py:592
  66.4 2.0 %collective-permute-done.15.refs_1_ = bf16[576,128]{1,0:T(8,128)(2,1)S(1)} collective-permute-done((bf16[576,128]{1,0:T(8,128)(2,1)S(1)}, bf16[576,128]{1,0:T(8,128)(2,1)S(1)}, u32[]{:S(2)}, u32[]{:S(2)}) %collective-permute-start.15) | collective-permute-done | bytes 147488 | tf_op jit(solution)/shard_map/ppermute | solution.py:592
  68.4 2.5 %collective-permute-done.16.refs_2_ = bf16[576,128]{1,0:T(8,128)(2,1)S(1)} collective-permute-done((bf16[576,128]{1,0:T(8,128)(2,1)S(1)}, bf16[576,128]{1,0:T(8,128)(2,1)S(1)}, u32[]{:S(2)}, u32[]{:S(2)}) %collective-permute-start.16) | collective-permute-done | bytes 147488 | tf_op jit(solution)/shard_map/ppermute | solution.py:592
  71.0 3.0 %collective-permute-start.20 = (bf16[576,128]{1,0:T(8,128)(2,1)S(1)}, bf16[576,128]{1,0:T(8,128)(2,1)S(1)}, u32[]{:S(2)}, u32[]{:S(2)}) collective-permute-start(bf16[576,128]{1,0:T(8,128)(2,1)S(1)} %gather_sum.1._.refs_0_), channel_id=1, source_target_pairs={{0,3},{1,2},{2,1},{3,0},{4,7},{5,6},{6,5},{7,4},{8,11},{9,10},{10,... | collective-permute-start | bytes 442376 | tf_op jit(solution)/shard_map/ppermute | solution.py:598
  74.0 1.4 %collective-permute-start.18 = (bf16[576,128]{1,0:T(8,128)(2,1)S(1)}, bf16[576,128]{1,0:T(8,128)(2,1)S(1)}, u32[]{:S(2)}, u32[]{:S(2)}) collective-permute-start(bf16[576,128]{1,0:T(8,128)(2,1)S(1)} %gather_sum.1._.refs_0_), channel_id=1, source_target_pairs={{0,1},{1,0},{2,3},{3,2},{4,5},{5,4},{6,7},{7,6},{8,9},{9,8},{10,11... | collective-permute-start | bytes 442376 | tf_op jit(solution)/shard_map/ppermute | solution.py:598
  75.5 1.5 %inverse_hot.1 = (bf16[2048,2048]{1,0:T(8,128)(2,1)S(1)}, s32[8,128]{1,0:T(8,128)S(1)}) custom-call(s32[1,2048]{1,0:T(1,128)S(1)} %bitcast.8, bf16[576,128]{1,0:T(8,128)(2,1)S(1)} %gather_sum.1._.refs_0_), custom_call_target="tpu_custom_call" | custom-call | bytes 6291456 | tf_op jit(solution)/shard_map/inverse_hot/pallas_call | solution.py:499
  76.9 2.8 %collective-permute-done.20.refs_3_ = bf16[576,128]{1,0:T(8,128)(2,1)S(1)} collective-permute-done((bf16[576,128]{1,0:T(8,128)(2,1)S(1)}, bf16[576,128]{1,0:T(8,128)(2,1)S(1)}, u32[]{:S(2)}, u32[]{:S(2)}) %collective-permute-start.20) | collective-permute-done | bytes 147488 | tf_op jit(solution)/shard_map/ppermute | solution.py:598
  79.7 5.8 %collective-permute-done.19.refs_2_ = bf16[576,128]{1,0:T(8,128)(2,1)S(1)} collective-permute-done((bf16[576,128]{1,0:T(8,128)(2,1)S(1)}, bf16[576,128]{1,0:T(8,128)(2,1)S(1)}, u32[]{:S(2)}, u32[]{:S(2)}) %collective-permute-start.19) | collective-permute-done | bytes 147488 | tf_op jit(solution)/shard_map/ppermute | solution.py:598
  86.5 1.8 %collective-permute-start.24 = (bf16[576,128]{1,0:T(8,128)(2,1)S(1)}, bf16[576,128]{1,0:T(8,128)(2,1)S(1)}, u32[]{:S(2)}, u32[]{:S(2)}) collective-permute-start(bf16[576,128]{1,0:T(8,128)(2,1)S(1)} %get-tuple-element.56), channel_id=1, source_target_pairs={{0,8},{4,12},{8,0},{12,4},{16,28},{20,24},{24,20},{28,16},{1,9},{5... | collective-permute-start | bytes 442376 | tf_op jit(solution)/shard_map/ppermute | solution.py:645
  92.9 3.7 %collective-permute-done.21.refs_0_ = bf16[576,128]{1,0:T(8,128)(2,1)S(1)} collective-permute-done((bf16[576,128]{1,0:T(8,128)(2,1)S(1)}, bf16[576,128]{1,0:T(8,128)(2,1)S(1)}, u32[]{:S(2)}, u32[]{:S(2)}) %collective-permute-start.21) | collective-permute-done | bytes 147488 | tf_op jit(solution)/shard_map/ppermute | solution.py:645
  97.9 2.7 %restore.3 = (bf16[2048,128]{1,0:T(8,128)(2,1)}, f32[128,128]{1,0:T(8,128)}) custom-call(bf16[2048,2048]{1,0:T(8,128)(2,1)S(1)} %get-tuple-element.51.hot_ref, bf16[576,128]{1,0:T(8,128)(2,1)S(1)} %collective-permute-done.21.refs_0_, bf16[576,128]{1,0:T(8,128)(2,1)S(1)} %collective-permute-done.22.refs_1_, f32[2048,128]{1,0:T(8,128)S(1)} %get-tuple-element.57.refs_2_, ...), custom_call_target="tpu_custom_call" | custom-call | flops 1073741824 | bytes 1048576 | tf_op jit(solution)/shard_map/restore/pallas_call | solution.py:65
  (54 shorter events, 24.5 us)
Async XLA Ops:
  4.6 10.5 %collective-permute-start.6 = (bf16[1024,128]{1,0:T(8,128)(2,1)S(1)}, bf16[1024,128]{1,0:T(8,128)(2,1)S(1)}, u32[]{:S(2)}, u32[]{:S(2)}) collective-permute-start(bf16[1024,128]{1,0:T(8,128)(2,1)S(1)} %reorder.3.refs_0_), channel_id=1, source_target_pairs={{0,28},{16,12},{5,25},{21,9},{10,22},{26,6},{15,19},{31,3}} | collective-permute-start | bytes 786440 | tf_op jit(solution)/shard_map/ppermute | solution.py:607
  9.9 7.4 %collective-permute-start.5 = (bf16[1024,128]{1,0:T(8,128)(2,1)S(1)}, bf16[1024,128]{1,0:T(8,128)(2,1)S(1)}, u32[]{:S(2)}, u32[]{:S(2)}) collective-permute-start(bf16[1024,128]{1,0:T(8,128)(2,1)S(1)} %reorder.3.refs_0_), channel_id=1, source_target_pairs={{0,20},{16,4},{5,17},{21,1},{10,30},{26,14},{15,27},{31,11}} | collective-permute-start | bytes 786440 | tf_op jit(solution)/shard_map/ppermute | solution.py:607
  11.2 6.1 %collective-permute-start.4 = (bf16[1024,128]{1,0:T(8,128)(2,1)S(1)}, bf16[1024,128]{1,0:T(8,128)(2,1)S(1)}, u32[]{:S(2)}, u32[]{:S(2)}) collective-permute-start(bf16[1024,128]{1,0:T(8,128)(2,1)S(1)} %reorder.3.refs_0_), channel_id=1, source_target_pairs={{0,8},{16,24},{5,13},{21,29},{10,2},{26,18},{15,7},{31,23}} | collective-permute-start | bytes 786440 | tf_op jit(solution)/shard_map/ppermute | solution.py:607
  12.5 6.8 %collective-permute-start.2 = (bf16[1024,128]{1,0:T(8,128)(2,1)S(1)}, bf16[1024,128]{1,0:T(8,128)(2,1)S(1)}, u32[]{:S(2)}, u32[]{:S(2)}) collective-permute-start(bf16[1024,128]{1,0:T(8,128)(2,1)S(1)} %get-tuple-element.34.refs_0_), channel_id=1, source_target_pairs={{0,28},{16,12},{5,25},{21,9},{10,22},{26,6},{15,19},{31,3}} | collective-permute-start | bytes 786440 | tf_op jit(solution)/shard_map/ppermute | solution.py:607
  13.8 5.5 %collective-permute-start.1 = (bf16[1024,128]{1,0:T(8,128)(2,1)S(1)}, bf16[1024,128]{1,0:T(8,128)(2,1)S(1)}, u32[]{:S(2)}, u32[]{:S(2)}) collective-permute-start(bf16[1024,128]{1,0:T(8,128)(2,1)S(1)} %get-tuple-element.34.refs_0_), channel_id=1, source_target_pairs={{0,20},{16,4},{5,17},{21,1},{10,30},{26,14},{15,27},{31,11}} | collective-permute-start | bytes 786440 | tf_op jit(solution)/shard_map/ppermute | solution.py:607
  15.2 7.0 %collective-permute-start = (bf16[1024,128]{1,0:T(8,128)(2,1)S(1)}, bf16[1024,128]{1,0:T(8,128)(2,1)S(1)}, u32[]{:S(2)}, u32[]{:S(2)}) collective-permute-start(bf16[1024,128]{1,0:T(8,128)(2,1)S(1)} %get-tuple-element.34.refs_0_), channel_id=1, source_target_pairs={{0,8},{16,24},{5,13},{21,29},{10,2},{26,18},{15,7},{31,23}} | collective-permute-start | bytes 786440 | tf_op jit(solution)/shard_map/ppermute | solution.py:607
  17.4 6.6 %collective-permute-start.7 = (bf16[1024,128]{1,0:T(8,128)(2,1)S(1)}, bf16[1024,128]{1,0:T(8,128)(2,1)S(1)}, u32[]{:S(2)}, u32[]{:S(2)}) collective-permute-start(bf16[1024,128]{1,0:T(8,128)(2,1)S(1)} %pick.3.refs_1_), channel_id=1, source_target_pairs={{0,4},{4,0},{8,12},{12,8},{16,20},{20,16},{24,28},{28,24},{1,5},{5... | collective-permute-start | bytes 786440 | tf_op jit(solution)/shard_map/ppermute | solution.py:595
  25.4 6.5 %collective-permute-start.8 = (bf16[512,128]{1,0:T(8,128)(2,1)S(1)}, bf16[512,128]{1,0:T(8,128)(2,1)S(1)}, u32[]{:S(2)}, u32[]{:S(2)}) collective-permute-start(bf16[512,128]{1,0:T(8,128)(2,1)S(1)} %get-tuple-element.36), channel_id=1, source_target_pairs={{0,1},{1,0},{2,3},{3,2},{4,5},{5,4},{6,7},{7,6},{8,9},{9,8},{10,11... | collective-permute-start | bytes 393224 | tf_op jit(solution)/shard_map/ppermute | solution.py:598
  28.0 12.8 %collective-permute-start.9 = (bf16[512,128]{1,0:T(8,128)(2,1)S(1)}, bf16[512,128]{1,0:T(8,128)(2,1)S(1)}, u32[]{:S(2)}, u32[]{:S(2)}) collective-permute-start(bf16[512,128]{1,0:T(8,128)(2,1)S(1)} %get-tuple-element.37), channel_id=1, source_target_pairs={{0,2},{1,3},{2,0},{3,1},{4,6},{5,7},{6,4},{7,5},{8,10},{9,11},{10,... | collective-permute-start | bytes 393224 | tf_op jit(solution)/shard_map/ppermute | solution.py:598
  30.4 10.5 %collective-permute-start.10 = (bf16[512,128]{1,0:T(8,128)(2,1)S(1)}, bf16[512,128]{1,0:T(8,128)(2,1)S(1)}, u32[]{:S(2)}, u32[]{:S(2)}) collective-permute-start(bf16[512,128]{1,0:T(8,128)(2,1)S(1)} %get-tuple-element.38), channel_id=1, source_target_pairs={{0,3},{1,2},{2,1},{3,0},{4,7},{5,6},{6,5},{7,4},{8,11},{9,10},{10,... | collective-permute-start | bytes 393224 | tf_op jit(solution)/shard_map/ppermute | solution.py:598
  40.9 6.1 %collective-permute-start.11 = (bf16[512,128]{1,0:T(8,128)(2,1)S(1)}, bf16[512,128]{1,0:T(8,128)(2,1)S(1)}, u32[]{:S(2)}, u32[]{:S(2)}) collective-permute-start(bf16[512,128]{1,0:T(8,128)(2,1)S(1)} %total_of.1.refs_0_), channel_id=1, source_target_pairs={{0,1},{1,0},{2,3},{3,2},{4,5},{5,4},{6,7},{7,6},{8,9},{9,8},{10,11... | collective-permute-start | bytes 393224 | tf_op jit(solution)/shard_map/ppermute | solution.py:598
  43.8 10.2 %collective-permute-start.13 = (bf16[512,128]{1,0:T(8,128)(2,1)S(1)}, bf16[512,128]{1,0:T(8,128)(2,1)S(1)}, u32[]{:S(2)}, u32[]{:S(2)}) collective-permute-start(bf16[512,128]{1,0:T(8,128)(2,1)S(1)} %total_of.1.refs_0_), channel_id=1, source_target_pairs={{0,3},{1,2},{2,1},{3,0},{4,7},{5,6},{6,5},{7,4},{8,11},{9,10},{10,... | collective-permute-start | bytes 393224 | tf_op jit(solution)/shard_map/ppermute | solution.py:598
  46.7 10.8 %collective-permute-start.12 = (bf16[512,128]{1,0:T(8,128)(2,1)S(1)}, bf16[512,128]{1,0:T(8,128)(2,1)S(1)}, u32[]{:S(2)}, u32[]{:S(2)}) collective-permute-start(bf16[512,128]{1,0:T(8,128)(2,1)S(1)} %total_of.1.refs_0_), channel_id=1, source_target_pairs={{0,2},{1,3},{2,0},{3,1},{4,6},{5,7},{6,4},{7,5},{8,10},{9,11},{10,... | collective-permute-start | bytes 393224 | tf_op jit(solution)/shard_map/ppermute | solution.py:598
  59.5 2.1 %collective-permute-start.14 = (bf16[18,128,128]{2,1,0:T(8,128)(2,1)S(1)}, bf16[18,128,128]{2,1,0:T(8,128)(2,1)S(1)}, u32[]{:S(2)}, u32[]{:S(2)}) collective-permute-start(bf16[18,128,128]{2,1,0:T(8,128)(2,1)S(1)} %backward.3), channel_id=1, source_target_pairs={{0,4},{4,0},{8,12},{12,8},{16,20},{20,16},{24,28},{28,24},{1,5},{5... | collective-permute-start | bytes 1769480 | tf_op jit(solution)/shard_map/ppermute | solution.py:595
  61.7 6.7 %collective-permute-start.15 = (bf16[576,128]{1,0:T(8,128)(2,1)S(1)}, bf16[576,128]{1,0:T(8,128)(2,1)S(1)}, u32[]{:S(2)}, u32[]{:S(2)}) collective-permute-start(bf16[576,128]{1,0:T(8,128)(2,1)S(1)} %get-tuple-element.48), channel_id=1, source_target_pairs={{0,8},{4,12},{8,0},{12,4},{16,24},{20,28},{24,16},{28,20},{1,9},{5... | collective-permute-start | bytes 442376 | tf_op jit(solution)/shard_map/ppermute | solution.py:592
  61.7 9.2 %collective-permute-start.16 = (bf16[576,128]{1,0:T(8,128)(2,1)S(1)}, bf16[576,128]{1,0:T(8,128)(2,1)S(1)}, u32[]{:S(2)}, u32[]{:S(2)}) collective-permute-start(bf16[576,128]{1,0:T(8,128)(2,1)S(1)} %get-tuple-element.49), channel_id=1, source_target_pairs={{0,16},{4,20},{8,24},{12,28},{16,0},{20,4},{24,8},{28,12},{1,17},{... | collective-permute-start | bytes 442376 | tf_op jit(solution)/shard_map/ppermute | solution.py:592
  62.8 8.1 %collective-permute-start.17 = (bf16[576,128]{1,0:T(8,128)(2,1)S(1)}, bf16[576,128]{1,0:T(8,128)(2,1)S(1)}, u32[]{:S(2)}, u32[]{:S(2)}) collective-permute-start(bf16[576,128]{1,0:T(8,128)(2,1)S(1)} %get-tuple-element.41), channel_id=1, source_target_pairs={{0,24},{4,28},{8,16},{12,20},{16,8},{20,12},{24,0},{28,4},{1,25},{... | collective-permute-start | bytes 442376 | tf_op jit(solution)/shard_map/ppermute | solution.py:592
  71.0 8.7 %collective-permute-start.20 = (bf16[576,128]{1,0:T(8,128)(2,1)S(1)}, bf16[576,128]{1,0:T(8,128)(2,1)S(1)}, u32[]{:S(2)}, u32[]{:S(2)}) collective-permute-start(bf16[576,128]{1,0:T(8,128)(2,1)S(1)} %gather_sum.1._.refs_0_), channel_id=1, source_target_pairs={{0,3},{1,2},{2,1},{3,0},{4,7},{5,6},{6,5},{7,4},{8,11},{9,10},{10,... | collective-permute-start | bytes 442376 | tf_op jit(solution)/shard_map/ppermute | solution.py:598
  74.0 11.5 %collective-permute-start.19 = (bf16[576,128]{1,0:T(8,128)(2,1)S(1)}, bf16[576,128]{1,0:T(8,128)(2,1)S(1)}, u32[]{:S(2)}, u32[]{:S(2)}) collective-permute-start(bf16[576,128]{1,0:T(8,128)(2,1)S(1)} %gather_sum.1._.refs_0_), channel_id=1, source_target_pairs={{0,2},{1,3},{2,0},{3,1},{4,6},{5,7},{6,4},{7,5},{8,10},{9,11},{10,... | collective-permute-start | bytes 442376 | tf_op jit(solution)/shard_map/ppermute | solution.py:598
  74.0 11.5 %collective-permute-start.18 = (bf16[576,128]{1,0:T(8,128)(2,1)S(1)}, bf16[576,128]{1,0:T(8,128)(2,1)S(1)}, u32[]{:S(2)}, u32[]{:S(2)}) collective-permute-start(bf16[576,128]{1,0:T(8,128)(2,1)S(1)} %gather_sum.1._.refs_0_), channel_id=1, source_target_pairs={{0,1},{1,0},{2,3},{3,2},{4,5},{5,4},{6,7},{7,6},{8,9},{9,8},{10,11... | collective-permute-start | bytes 442376 | tf_op jit(solution)/shard_map/ppermute | solution.py:598
  85.8 4.5 %collective-permute-start.23 = (bf16[576,128]{1,0:T(8,128)(2,1)S(1)}, bf16[576,128]{1,0:T(8,128)(2,1)S(1)}, u32[]{:S(2)}, u32[]{:S(2)}) collective-permute-start(bf16[576,128]{1,0:T(8,128)(2,1)S(1)} %get-tuple-element.55), channel_id=1, source_target_pairs={{0,0},{4,4},{8,8},{12,12},{16,20},{20,16},{24,28},{28,24},{1,1},{5... | collective-permute-start | bytes 442376 | tf_op jit(solution)/shard_map/ppermute | solution.py:645
  86.5 5.2 %collective-permute-start.24 = (bf16[576,128]{1,0:T(8,128)(2,1)S(1)}, bf16[576,128]{1,0:T(8,128)(2,1)S(1)}, u32[]{:S(2)}, u32[]{:S(2)}) collective-permute-start(bf16[576,128]{1,0:T(8,128)(2,1)S(1)} %get-tuple-element.56), channel_id=1, source_target_pairs={{0,8},{4,12},{8,0},{12,4},{16,28},{20,24},{24,20},{28,16},{1,9},{5... | collective-permute-start | bytes 442376 | tf_op jit(solution)/shard_map/ppermute | solution.py:645
  88.3 8.4 %collective-permute-start.21 = (bf16[576,128]{1,0:T(8,128)(2,1)S(1)}, bf16[576,128]{1,0:T(8,128)(2,1)S(1)}, u32[]{:S(2)}, u32[]{:S(2)}) collective-permute-start(bf16[576,128]{1,0:T(8,128)(2,1)S(1)} %get-tuple-element.53), channel_id=1, source_target_pairs={{0,20},{4,16},{8,28},{12,24},{16,0},{20,4},{24,8},{28,12},{1,21},{... | collective-permute-start | bytes 442376 | tf_op jit(solution)/shard_map/ppermute | solution.py:645
  89.4 8.5 %collective-permute-start.22 = (bf16[576,128]{1,0:T(8,128)(2,1)S(1)}, bf16[576,128]{1,0:T(8,128)(2,1)S(1)}, u32[]{:S(2)}, u32[]{:S(2)}) collective-permute-start(bf16[576,128]{1,0:T(8,128)(2,1)S(1)} %get-tuple-element.54), channel_id=1, source_target_pairs={{0,28},{4,24},{8,20},{12,16},{16,8},{20,12},{24,0},{28,4},{1,29},{... | collective-permute-start | bytes 442376 | tf_op jit(solution)/shard_map/ppermute | solution.py:645
  (5 other events, 90.6 us)

commit v11 on v9

--- a/solution.py
+++ b/solution.py
@@ -499,7 +499,7 @@
     )(order_row, after)
 
 
-def restore_body(hot_ref, *refs, first, count, per, scale):
+def restore_body(hot_ref, *refs, hops, count, per, scale):
     parts, refs = refs[:count], refs[count:]
     start, (out_ref, grad_ref) = refs[:-2], refs[-2:]
     chip = lax.axis_index("section") // 2
@@ -509,7 +509,7 @@
     grad_ref[...] = start[1][...] if start else jnp.zeros_like(grad_ref)
     columns, places = [], []
     for n, part in enumerate(parts):
-        u = chip ^ (first + n)
+        u = chip ^ hops[n]
         at = pl.multiple_of(u * extra, extra)
         grad_ref[pl.ds(at, extra), :] = sum_of_parts(part, length, extra) * scale
         columns.append(
@@ -531,11 +531,11 @@
         out_ref[span, :] = acc.astype(out_ref.dtype)
 
 
-def restore(hot, parts, first, start, per, scale):
+def restore(hot, parts, hops, start, per, scale):
     panel = hot.shape[0]
     width = parts[0].shape[1]
     body = functools.partial(
-        restore_body, first=first, count=len(parts), per=per, scale=scale
+        restore_body, hops=hops, count=len(parts), per=per, scale=scale
     )
     outs = (
         jax.ShapeDtypeStruct((panel, width), BF16 if start else F32),
@@ -629,8 +629,9 @@
     parts = [to_owner(block, k) for k, block in enumerate(routed)]
     scale = 1.0 / math.sqrt(panel * sections)
     half = chips // 2
-    begun = restore(hot, parts[:half], 0, (), per, scale)
-    feature_grad, weight_grad = restore(hot, parts[half:], half, begun, per, scale)
+    hops = [0, *reversed(range(1, chips))]
+    begun = restore(hot, [parts[k] for k in hops[:half]], hops[:half], (), per, scale)
+    feature_grad, weight_grad = restore(hot, [parts[k] for k in hops[half:]], hops[half:], begun, per, scale)
     return (hidden, weight_grad, feature_grad)
 
 

time: 99.9 us -> 99.1 us (level)
  starting transfers between devices: 36 us -> 34.8 us
  waiting for transfers between devices: 43 us -> 44 us
    ppermute x3, waiting for transfers between devices: 0.01 us -> 1.4 us  [over_cores(): return lax.ppermute(x, 'section', [(s, s ^ 1) for s in range(sections)])]
  transfers between devices with their start and end apart: 25 -> 25, of which waited for: 15 -> 18; matrix products, arithmetic and copies ran while one was open for 0% -> 0% of each run, Pallas kernels for 11% -> 10%
where the time goes in v11:
time: 99.1 us; the launch traced here: 98.1 us
  waiting for transfers between devices  44 us (44%)
  starting transfers between devices  34.8 us (35%)
  Pallas kernels  18.3 us (18%)
    ppermute x9, waiting for transfers between devices, over_reps(): return lax.ppermute(x, 'rep', [(r, r ^ d) for r in range(reps)])  28 us
    pallas_call x17, Pallas kernels, call(): pl.pallas_call(body, out_shape=[out if n in results else pltpu.VMEM(out.s...  16 us
    ppermute x9, starting transfers between devices, over_reps(): return lax.ppermute(x, 'rep', [(r, r ^ d) for r in range(reps)])  14.7 us
    ppermute x6, starting transfers between devices, from_owner(): return lax.ppermute(x, ('section', 'rep'), moves)  11.8 us
    ppermute x3, waiting for transfers between devices, over_chips(): return lax.ppermute(x, 'section', [(s, s ^ 2 * d) for s in range(sections)])  5.79 us
    ppermute x4, waiting for transfers between devices, to_owner(): return lax.ppermute(block, 'section', moves)  5.77 us
    ppermute x4, starting transfers between devices, to_owner(): return lax.ppermute(block, 'section', moves)  4.26 us
    ppermute x3, starting transfers between devices, over_chips(): return lax.ppermute(x, 'section', [(s, s ^ 2 * d) for s in range(sections)])  3.86 us
  transfers between devices with their start and end apart: 25, of which 18 were waited for; matrix products, arithmetic and copies ran while one was open for 0% of the time, Pallas kernels for 10%

profile of v11, /device:TPU:0, one launch (start us, length us, event | category | flops | bytes accessed | tf_op | source)
XLA Modules:
  0.0 98.1 jit_solution(10556850325116754935)
XLA Ops:
  0.6 2.6 %reorder.3.refs_0_ = bf16[1024,128]{1,0:T(8,128)(2,1)S(1)} custom-call(s32[16,128]{1,0:T(8,128)} %bitcast.7, bf16[2048,128]{1,0:T(8,128)(2,1)} %feat_ref.3), custom_call_target="tpu_custom_call" | custom-call | flops 536870912 | bytes 524288 | tf_op jit(solution)/shard_map/reorder/pallas_call | solution.py:59
  3.2 5.3 %collective-permute-start.2 = (bf16[1024,128]{1,0:T(8,128)(2,1)S(1)}, bf16[1024,128]{1,0:T(8,128)(2,1)S(1)}, u32[]{:S(2)}, u32[]{:S(2)}) collective-permute-start(bf16[1024,128]{1,0:T(8,128)(2,1)S(1)} %reorder.3.refs_0_), channel_id=1, source_target_pairs={{0,28},{16,12},{5,25},{21,9},{10,22},{26,6},{15,19},{31,3}} | collective-permute-start | bytes 786440 | tf_op jit(solution)/shard_map/ppermute | solution.py:586
  11.1 2.4 %reorder.2.refs_0_ = bf16[1024,128]{1,0:T(8,128)(2,1)S(1)} custom-call(s32[16,128]{1,0:T(8,128)} %bitcast.8, bf16[2048,128]{1,0:T(8,128)(2,1)} %feat_ref.3), custom_call_target="tpu_custom_call" | custom-call | flops 536870912 | bytes 524288 | tf_op jit(solution)/shard_map/reorder/pallas_call | solution.py:59
  20.0 1.5 %collective-permute-done.4.refs_1_ = bf16[1024,128]{1,0:T(8,128)(2,1)S(1)} collective-permute-done((bf16[1024,128]{1,0:T(8,128)(2,1)S(1)}, bf16[1024,128]{1,0:T(8,128)(2,1)S(1)}, u32[]{:S(2)}, u32[]{:S(2)}) %collective-permute-start.4) | collective-permute-done | bytes 262176 | tf_op jit(solution)/shard_map/ppermute | solution.py:586
  23.2 1.3 %forward.3 = (f32[512,128]{1,0:T(8,128)S(1)}, bf16[512,128]{1,0:T(8,128)(2,1)S(1)}, bf16[512,128]{1,0:T(8,128)(2,1)S(1)}, bf16[512,128]{1,0:T(8,128)(2,1)S(1)}) custom-call(s32[2,97]{1,0:T(2,128)S(1)} %entries_of.1.refs_4_.entry_ref, bf16[192,128,128]{2,1,0:T(8,128)(2,1)S(1)} %bitcast.4, bf16[1024,128]{1,0:T(8,128)(2,1)S(1)} %collective-permute-done.3.refs_0_, ...), custom_call_target="tpu_custom_call" | custom-call | flops 268435456 | bytes 12582912 | tf_op jit(solution)/shard_map/forward/pallas_call | solution.py:59
  25.8 3.3 %collective-permute-start.9 = (bf16[512,128]{1,0:T(8,128)(2,1)S(1)}, bf16[512,128]{1,0:T(8,128)(2,1)S(1)}, u32[]{:S(2)}, u32[]{:S(2)}) collective-permute-start(bf16[512,128]{1,0:T(8,128)(2,1)S(1)} %get-tuple-element.31), channel_id=1, source_target_pairs={{0,2},{1,3},{2,0},{3,1},{4,6},{5,7},{6,4},{7,5},{8,10},{9,11},{10,... | collective-permute-start | bytes 393224 | tf_op jit(solution)/shard_map/ppermute | solution.py:577
  29.3 2.9 %collective-permute-done.8.refs_0_ = bf16[512,128]{1,0:T(8,128)(2,1)S(1)} collective-permute-done((bf16[512,128]{1,0:T(8,128)(2,1)S(1)}, bf16[512,128]{1,0:T(8,128)(2,1)S(1)}, u32[]{:S(2)}, u32[]{:S(2)}) %collective-permute-start.8) | collective-permute-done | bytes 131104 | tf_op jit(solution)/shard_map/ppermute | solution.py:577
  32.2 6.9 %collective-permute-done.9.refs_1_ = bf16[512,128]{1,0:T(8,128)(2,1)S(1)} collective-permute-done((bf16[512,128]{1,0:T(8,128)(2,1)S(1)}, bf16[512,128]{1,0:T(8,128)(2,1)S(1)}, u32[]{:S(2)}, u32[]{:S(2)}) %collective-permute-start.9) | collective-permute-done | bytes 131104 | tf_op jit(solution)/shard_map/ppermute | solution.py:577
  39.2 2.6 %collective-permute-start.11 = (bf16[512,128]{1,0:T(8,128)(2,1)S(1)}, bf16[512,128]{1,0:T(8,128)(2,1)S(1)}, u32[]{:S(2)}, u32[]{:S(2)}) collective-permute-start(bf16[512,128]{1,0:T(8,128)(2,1)S(1)} %total_of.1.refs_0_), channel_id=1, source_target_pairs={{0,1},{1,0},{2,3},{3,2},{4,5},{5,4},{6,7},{7,6},{8,9},{9,8},{10,11... | collective-permute-start | bytes 393224 | tf_op jit(solution)/shard_map/ppermute | solution.py:577
  41.8 2.8 %collective-permute-start.13 = (bf16[512,128]{1,0:T(8,128)(2,1)S(1)}, bf16[512,128]{1,0:T(8,128)(2,1)S(1)}, u32[]{:S(2)}, u32[]{:S(2)}) collective-permute-start(bf16[512,128]{1,0:T(8,128)(2,1)S(1)} %total_of.1.refs_0_), channel_id=1, source_target_pairs={{0,3},{1,2},{2,1},{3,0},{4,7},{5,6},{6,5},{7,4},{8,11},{9,10},{10,... | collective-permute-start | bytes 393224 | tf_op jit(solution)/shard_map/ppermute | solution.py:577
  45.6 5.8 %collective-permute-done.13.refs_1_.refs_3_ = bf16[512,128]{1,0:T(8,128)(2,1)S(1)} collective-permute-done((bf16[512,128]{1,0:T(8,128)(2,1)S(1)}, bf16[512,128]{1,0:T(8,128)(2,1)S(1)}, u32[]{:S(2)}, u32[]{:S(2)}) %collective-permute-start.13) | collective-permute-done | bytes 131104 | tf_op jit(solution)/shard_map/ppermute | solution.py:577
  51.4 3.3 %collective-permute-done.12.refs_0_.refs_2_ = bf16[512,128]{1,0:T(8,128)(2,1)S(1)} collective-permute-done((bf16[512,128]{1,0:T(8,128)(2,1)S(1)}, bf16[512,128]{1,0:T(8,128)(2,1)S(1)}, u32[]{:S(2)}, u32[]{:S(2)}) %collective-permute-start.12) | collective-permute-done | bytes 131104 | tf_op jit(solution)/shard_map/ppermute | solution.py:577
  55.2 1.4 %backward.3 = bf16[18,128,128]{2,1,0:T(8,128)(2,1)S(1)} custom-call(s32[2,97]{1,0:T(2,128)S(1)} %entries_of.1.refs_4_.entry_ref, bf16[192,128,128]{2,1,0:T(8,128)(2,1)S(1)} %bitcast.5, bf16[2,128,512]{2,1,0:T(8,128)(2,1)S(1)} %get-tuple-element.33.refs_0_, bf16[2,128,512]{2,1,0:T(8,128)(2,1)S(1)} %up_shares.3.refs_1_, ...), custom_call_target="tpu_custom_call" | custom-call | flops 268435456 | bytes 12582912 | tf_op jit(solution)/shard_map/backward/pallas_call | solution.py:59
  58.8 2.1 %collective-permute-start.15 = (bf16[576,128]{1,0:T(8,128)(2,1)S(1)}, bf16[576,128]{1,0:T(8,128)(2,1)S(1)}, u32[]{:S(2)}, u32[]{:S(2)}) collective-permute-start(bf16[576,128]{1,0:T(8,128)(2,1)S(1)} %get-tuple-element.42), channel_id=1, source_target_pairs={{0,8},{4,12},{8,0},{12,4},{16,24},{20,28},{24,16},{28,20},{1,9},{5... | collective-permute-start | bytes 442376 | tf_op jit(solution)/shard_map/ppermute | solution.py:571
  63.9 1.6 %collective-permute-done.15.refs_1_ = bf16[576,128]{1,0:T(8,128)(2,1)S(1)} collective-permute-done((bf16[576,128]{1,0:T(8,128)(2,1)S(1)}, bf16[576,128]{1,0:T(8,128)(2,1)S(1)}, u32[]{:S(2)}, u32[]{:S(2)}) %collective-permute-start.15) | collective-permute-done | bytes 147488 | tf_op jit(solution)/shard_map/ppermute | solution.py:571
  65.5 3.0 %collective-permute-done.16.refs_2_ = bf16[576,128]{1,0:T(8,128)(2,1)S(1)} collective-permute-done((bf16[576,128]{1,0:T(8,128)(2,1)S(1)}, bf16[576,128]{1,0:T(8,128)(2,1)S(1)}, u32[]{:S(2)}, u32[]{:S(2)}) %collective-permute-start.16) | collective-permute-done | bytes 147488 | tf_op jit(solution)/shard_map/ppermute | solution.py:571
  69.8 3.2 %collective-permute-start.20 = (bf16[576,128]{1,0:T(8,128)(2,1)S(1)}, bf16[576,128]{1,0:T(8,128)(2,1)S(1)}, u32[]{:S(2)}, u32[]{:S(2)}) collective-permute-start(bf16[576,128]{1,0:T(8,128)(2,1)S(1)} %gather_sum.1._.refs_0_), channel_id=1, source_target_pairs={{0,3},{1,2},{2,1},{3,0},{4,7},{5,6},{6,5},{7,4},{8,11},{9,10},{10,... | collective-permute-start | bytes 442376 | tf_op jit(solution)/shard_map/ppermute | solution.py:577
  74.2 1.5 %inverse_hot.1 = (bf16[2048,2048]{1,0:T(8,128)(2,1)S(1)}, s32[8,128]{1,0:T(8,128)S(1)}) custom-call(s32[1,2048]{1,0:T(1,128)S(1)} %bitcast.9, bf16[576,128]{1,0:T(8,128)(2,1)S(1)} %gather_sum.1._.refs_0_), custom_call_target="tpu_custom_call" | custom-call | bytes 6291456 | tf_op jit(solution)/shard_map/inverse_hot/pallas_call | solution.py:484
  75.7 2.7 %collective-permute-done.20.refs_3_ = bf16[576,128]{1,0:T(8,128)(2,1)S(1)} collective-permute-done((bf16[576,128]{1,0:T(8,128)(2,1)S(1)}, bf16[576,128]{1,0:T(8,128)(2,1)S(1)}, u32[]{:S(2)}, u32[]{:S(2)}) %collective-permute-start.20) | collective-permute-done | bytes 147488 | tf_op jit(solution)/shard_map/ppermute | solution.py:577
  78.4 6.1 %collective-permute-done.19.refs_2_ = bf16[576,128]{1,0:T(8,128)(2,1)S(1)} collective-permute-done((bf16[576,128]{1,0:T(8,128)(2,1)S(1)}, bf16[576,128]{1,0:T(8,128)(2,1)S(1)}, u32[]{:S(2)}, u32[]{:S(2)}) %collective-permute-start.19) | collective-permute-done | bytes 147488 | tf_op jit(solution)/shard_map/ppermute | solution.py:577
  85.4 3.0 %collective-permute-start.24 = (bf16[576,128]{1,0:T(8,128)(2,1)S(1)}, bf16[576,128]{1,0:T(8,128)(2,1)S(1)}, u32[]{:S(2)}, u32[]{:S(2)}) collective-permute-start(bf16[576,128]{1,0:T(8,128)(2,1)S(1)} %get-tuple-element.50), channel_id=1, source_target_pairs={{0,28},{4,24},{8,20},{12,16},{16,8},{20,12},{24,0},{28,4},{1,29},{... | collective-permute-start | bytes 442376 | tf_op jit(solution)/shard_map/ppermute | solution.py:624
  89.0 3.9 %collective-permute-done.24.refs_1_ = bf16[576,128]{1,0:T(8,128)(2,1)S(1)} collective-permute-done((bf16[576,128]{1,0:T(8,128)(2,1)S(1)}, bf16[576,128]{1,0:T(8,128)(2,1)S(1)}, u32[]{:S(2)}, u32[]{:S(2)}) %collective-permute-start.24) | collective-permute-done | bytes 147488 | tf_op jit(solution)/shard_map/ppermute | solution.py:624
  94.2 1.8 %collective-permute-done.21.refs_0_ = bf16[576,128]{1,0:T(8,128)(2,1)S(1)} collective-permute-done((bf16[576,128]{1,0:T(8,128)(2,1)S(1)}, bf16[576,128]{1,0:T(8,128)(2,1)S(1)}, u32[]{:S(2)}, u32[]{:S(2)}) %collective-permute-start.21) | collective-permute-done | bytes 147488 | tf_op jit(solution)/shard_map/ppermute | solution.py:624
  96.1 2.1 %restore.3 = (bf16[2048,128]{1,0:T(8,128)(2,1)}, f32[128,128]{1,0:T(8,128)}) custom-call(bf16[2048,2048]{1,0:T(8,128)(2,1)S(1)} %get-tuple-element.45.hot_ref, bf16[576,128]{1,0:T(8,128)(2,1)S(1)} %collective-permute-done.21.refs_0_, bf16[576,128]{1,0:T(8,128)(2,1)S(1)} %collective-permute-done.22.refs_1_, f32[2048,128]{1,0:T(8,128)S(1)} %get-tuple-element.51.refs_2_, ...), custom_call_target="tpu_custom_call" | custom-call | flops 1073741824 | bytes 1048576 | tf_op jit(solution)/shard_map/restore/pallas_call | solution.py:59
  (54 shorter events, 24.3 us)
Async XLA Ops:
  3.2 13.0 %collective-permute-start.2 = (bf16[1024,128]{1,0:T(8,128)(2,1)S(1)}, bf16[1024,128]{1,0:T(8,128)(2,1)S(1)}, u32[]{:S(2)}, u32[]{:S(2)}) collective-permute-start(bf16[1024,128]{1,0:T(8,128)(2,1)S(1)} %reorder.3.refs_0_), channel_id=1, source_target_pairs={{0,28},{16,12},{5,25},{21,9},{10,22},{26,6},{15,19},{31,3}} | collective-permute-start | bytes 786440 | tf_op jit(solution)/shard_map/ppermute | solution.py:586
  8.5 9.8 %collective-permute-start.1 = (bf16[1024,128]{1,0:T(8,128)(2,1)S(1)}, bf16[1024,128]{1,0:T(8,128)(2,1)S(1)}, u32[]{:S(2)}, u32[]{:S(2)}) collective-permute-start(bf16[1024,128]{1,0:T(8,128)(2,1)S(1)} %reorder.3.refs_0_), channel_id=1, source_target_pairs={{0,20},{16,4},{5,17},{21,1},{10,30},{26,14},{15,27},{31,11}} | collective-permute-start | bytes 786440 | tf_op jit(solution)/shard_map/ppermute | solution.py:586
  9.8 8.5 %collective-permute-start = (bf16[1024,128]{1,0:T(8,128)(2,1)S(1)}, bf16[1024,128]{1,0:T(8,128)(2,1)S(1)}, u32[]{:S(2)}, u32[]{:S(2)}) collective-permute-start(bf16[1024,128]{1,0:T(8,128)(2,1)S(1)} %reorder.3.refs_0_), channel_id=1, source_target_pairs={{0,8},{16,24},{5,13},{21,29},{10,2},{26,18},{15,7},{31,23}} | collective-permute-start | bytes 786440 | tf_op jit(solution)/shard_map/ppermute | solution.py:586
  13.6 5.2 %collective-permute-start.6 = (bf16[1024,128]{1,0:T(8,128)(2,1)S(1)}, bf16[1024,128]{1,0:T(8,128)(2,1)S(1)}, u32[]{:S(2)}, u32[]{:S(2)}) collective-permute-start(bf16[1024,128]{1,0:T(8,128)(2,1)S(1)} %reorder.2.refs_0_), channel_id=1, source_target_pairs={{0,28},{16,12},{5,25},{21,9},{10,22},{26,6},{15,19},{31,3}} | collective-permute-start | bytes 786440 | tf_op jit(solution)/shard_map/ppermute | solution.py:586
  14.9 5.2 %collective-permute-start.5 = (bf16[1024,128]{1,0:T(8,128)(2,1)S(1)}, bf16[1024,128]{1,0:T(8,128)(2,1)S(1)}, u32[]{:S(2)}, u32[]{:S(2)}) collective-permute-start(bf16[1024,128]{1,0:T(8,128)(2,1)S(1)} %reorder.2.refs_0_), channel_id=1, source_target_pairs={{0,20},{16,4},{5,17},{21,1},{10,30},{26,14},{15,27},{31,11}} | collective-permute-start | bytes 786440 | tf_op jit(solution)/shard_map/ppermute | solution.py:586
  16.2 5.3 %collective-permute-start.4 = (bf16[1024,128]{1,0:T(8,128)(2,1)S(1)}, bf16[1024,128]{1,0:T(8,128)(2,1)S(1)}, u32[]{:S(2)}, u32[]{:S(2)}) collective-permute-start(bf16[1024,128]{1,0:T(8,128)(2,1)S(1)} %reorder.2.refs_0_), channel_id=1, source_target_pairs={{0,8},{16,24},{5,13},{21,29},{10,2},{26,18},{15,7},{31,23}} | collective-permute-start | bytes 786440 | tf_op jit(solution)/shard_map/ppermute | solution.py:586
  18.4 4.3 %collective-permute-start.3 = (bf16[1024,128]{1,0:T(8,128)(2,1)S(1)}, bf16[1024,128]{1,0:T(8,128)(2,1)S(1)}, u32[]{:S(2)}, u32[]{:S(2)}) collective-permute-start(bf16[1024,128]{1,0:T(8,128)(2,1)S(1)} %pick.2.refs_0_), channel_id=1, source_target_pairs={{0,4},{4,0},{8,12},{12,8},{16,20},{20,16},{24,28},{28,24},{1,5},{5... | collective-permute-start | bytes 786440 | tf_op jit(solution)/shard_map/ppermute | solution.py:574
  24.5 7.6 %collective-permute-start.8 = (bf16[512,128]{1,0:T(8,128)(2,1)S(1)}, bf16[512,128]{1,0:T(8,128)(2,1)S(1)}, u32[]{:S(2)}, u32[]{:S(2)}) collective-permute-start(bf16[512,128]{1,0:T(8,128)(2,1)S(1)} %get-tuple-element.30), channel_id=1, source_target_pairs={{0,1},{1,0},{2,3},{3,2},{4,5},{5,4},{6,7},{7,6},{8,9},{9,8},{10,11... | collective-permute-start | bytes 393224 | tf_op jit(solution)/shard_map/ppermute | solution.py:577
  25.8 13.3 %collective-permute-start.9 = (bf16[512,128]{1,0:T(8,128)(2,1)S(1)}, bf16[512,128]{1,0:T(8,128)(2,1)S(1)}, u32[]{:S(2)}, u32[]{:S(2)}) collective-permute-start(bf16[512,128]{1,0:T(8,128)(2,1)S(1)} %get-tuple-element.31), channel_id=1, source_target_pairs={{0,2},{1,3},{2,0},{3,1},{4,6},{5,7},{6,4},{7,5},{8,10},{9,11},{10,... | collective-permute-start | bytes 393224 | tf_op jit(solution)/shard_map/ppermute | solution.py:577
  29.1 10.0 %collective-permute-start.10 = (bf16[512,128]{1,0:T(8,128)(2,1)S(1)}, bf16[512,128]{1,0:T(8,128)(2,1)S(1)}, u32[]{:S(2)}, u32[]{:S(2)}) collective-permute-start(bf16[512,128]{1,0:T(8,128)(2,1)S(1)} %get-tuple-element.32), channel_id=1, source_target_pairs={{0,3},{1,2},{2,1},{3,0},{4,7},{5,6},{6,5},{7,4},{8,11},{9,10},{10,... | collective-permute-start | bytes 393224 | tf_op jit(solution)/shard_map/ppermute | solution.py:577
  39.2 5.8 %collective-permute-start.11 = (bf16[512,128]{1,0:T(8,128)(2,1)S(1)}, bf16[512,128]{1,0:T(8,128)(2,1)S(1)}, u32[]{:S(2)}, u32[]{:S(2)}) collective-permute-start(bf16[512,128]{1,0:T(8,128)(2,1)S(1)} %total_of.1.refs_0_), channel_id=1, source_target_pairs={{0,1},{1,0},{2,3},{3,2},{4,5},{5,4},{6,7},{7,6},{8,9},{9,8},{10,11... | collective-permute-start | bytes 393224 | tf_op jit(solution)/shard_map/ppermute | solution.py:577
  41.8 9.6 %collective-permute-start.13 = (bf16[512,128]{1,0:T(8,128)(2,1)S(1)}, bf16[512,128]{1,0:T(8,128)(2,1)S(1)}, u32[]{:S(2)}, u32[]{:S(2)}) collective-permute-start(bf16[512,128]{1,0:T(8,128)(2,1)S(1)} %total_of.1.refs_0_), channel_id=1, source_target_pairs={{0,3},{1,2},{2,1},{3,0},{4,7},{5,6},{6,5},{7,4},{8,11},{9,10},{10,... | collective-permute-start | bytes 393224 | tf_op jit(solution)/shard_map/ppermute | solution.py:577
  44.6 10.1 %collective-permute-start.12 = (bf16[512,128]{1,0:T(8,128)(2,1)S(1)}, bf16[512,128]{1,0:T(8,128)(2,1)S(1)}, u32[]{:S(2)}, u32[]{:S(2)}) collective-permute-start(bf16[512,128]{1,0:T(8,128)(2,1)S(1)} %total_of.1.refs_0_), channel_id=1, source_target_pairs={{0,2},{1,3},{2,0},{3,1},{4,6},{5,7},{6,4},{7,5},{8,10},{9,11},{10,... | collective-permute-start | bytes 393224 | tf_op jit(solution)/shard_map/ppermute | solution.py:577
  56.6 2.1 %collective-permute-start.14 = (bf16[18,128,128]{2,1,0:T(8,128)(2,1)S(1)}, bf16[18,128,128]{2,1,0:T(8,128)(2,1)S(1)}, u32[]{:S(2)}, u32[]{:S(2)}) collective-permute-start(bf16[18,128,128]{2,1,0:T(8,128)(2,1)S(1)} %backward.3), channel_id=1, source_target_pairs={{0,4},{4,0},{8,12},{12,8},{16,20},{20,16},{24,28},{28,24},{1,5},{5... | collective-permute-start | bytes 1769480 | tf_op jit(solution)/shard_map/ppermute | solution.py:574
  58.8 6.7 %collective-permute-start.15 = (bf16[576,128]{1,0:T(8,128)(2,1)S(1)}, bf16[576,128]{1,0:T(8,128)(2,1)S(1)}, u32[]{:S(2)}, u32[]{:S(2)}) collective-permute-start(bf16[576,128]{1,0:T(8,128)(2,1)S(1)} %get-tuple-element.42), channel_id=1, source_target_pairs={{0,8},{4,12},{8,0},{12,4},{16,24},{20,28},{24,16},{28,20},{1,9},{5... | collective-permute-start | bytes 442376 | tf_op jit(solution)/shard_map/ppermute | solution.py:571
  60.8 7.6 %collective-permute-start.16 = (bf16[576,128]{1,0:T(8,128)(2,1)S(1)}, bf16[576,128]{1,0:T(8,128)(2,1)S(1)}, u32[]{:S(2)}, u32[]{:S(2)}) collective-permute-start(bf16[576,128]{1,0:T(8,128)(2,1)S(1)} %get-tuple-element.43), channel_id=1, source_target_pairs={{0,16},{4,20},{8,24},{12,28},{16,0},{20,4},{24,8},{28,12},{1,17},{... | collective-permute-start | bytes 442376 | tf_op jit(solution)/shard_map/ppermute | solution.py:571
  61.5 8.2 %collective-permute-start.17 = (bf16[576,128]{1,0:T(8,128)(2,1)S(1)}, bf16[576,128]{1,0:T(8,128)(2,1)S(1)}, u32[]{:S(2)}, u32[]{:S(2)}) collective-permute-start(bf16[576,128]{1,0:T(8,128)(2,1)S(1)} %get-tuple-element.35), channel_id=1, source_target_pairs={{0,24},{4,28},{8,16},{12,20},{16,8},{20,12},{24,0},{28,4},{1,25},{... | collective-permute-start | bytes 442376 | tf_op jit(solution)/shard_map/ppermute | solution.py:571
  69.8 8.6 %collective-permute-start.20 = (bf16[576,128]{1,0:T(8,128)(2,1)S(1)}, bf16[576,128]{1,0:T(8,128)(2,1)S(1)}, u32[]{:S(2)}, u32[]{:S(2)}) collective-permute-start(bf16[576,128]{1,0:T(8,128)(2,1)S(1)} %gather_sum.1._.refs_0_), channel_id=1, source_target_pairs={{0,3},{1,2},{2,1},{3,0},{4,7},{5,6},{6,5},{7,4},{8,11},{9,10},{10,... | collective-permute-start | bytes 442376 | tf_op jit(solution)/shard_map/ppermute | solution.py:577
  73.0 11.6 %collective-permute-start.19 = (bf16[576,128]{1,0:T(8,128)(2,1)S(1)}, bf16[576,128]{1,0:T(8,128)(2,1)S(1)}, u32[]{:S(2)}, u32[]{:S(2)}) collective-permute-start(bf16[576,128]{1,0:T(8,128)(2,1)S(1)} %gather_sum.1._.refs_0_), channel_id=1, source_target_pairs={{0,2},{1,3},{2,0},{3,1},{4,6},{5,7},{6,4},{7,5},{8,10},{9,11},{10,... | collective-permute-start | bytes 442376 | tf_op jit(solution)/shard_map/ppermute | solution.py:577
  73.0 11.6 %collective-permute-start.18 = (bf16[576,128]{1,0:T(8,128)(2,1)S(1)}, bf16[576,128]{1,0:T(8,128)(2,1)S(1)}, u32[]{:S(2)}, u32[]{:S(2)}) collective-permute-start(bf16[576,128]{1,0:T(8,128)(2,1)S(1)} %gather_sum.1._.refs_0_), channel_id=1, source_target_pairs={{0,1},{1,0},{2,3},{3,2},{4,5},{5,4},{6,7},{7,6},{8,9},{9,8},{10,11... | collective-permute-start | bytes 442376 | tf_op jit(solution)/shard_map/ppermute | solution.py:577
  84.8 4.3 %collective-permute-start.23 = (bf16[576,128]{1,0:T(8,128)(2,1)S(1)}, bf16[576,128]{1,0:T(8,128)(2,1)S(1)}, u32[]{:S(2)}, u32[]{:S(2)}) collective-permute-start(bf16[576,128]{1,0:T(8,128)(2,1)S(1)} %get-tuple-element.49), channel_id=1, source_target_pairs={{0,0},{4,4},{8,8},{12,12},{16,20},{20,16},{24,28},{28,24},{1,1},{5... | collective-permute-start | bytes 442376 | tf_op jit(solution)/shard_map/ppermute | solution.py:624
  85.4 7.5 %collective-permute-start.24 = (bf16[576,128]{1,0:T(8,128)(2,1)S(1)}, bf16[576,128]{1,0:T(8,128)(2,1)S(1)}, u32[]{:S(2)}, u32[]{:S(2)}) collective-permute-start(bf16[576,128]{1,0:T(8,128)(2,1)S(1)} %get-tuple-element.50), channel_id=1, source_target_pairs={{0,28},{4,24},{8,20},{12,16},{16,8},{20,12},{24,0},{28,4},{1,29},{... | collective-permute-start | bytes 442376 | tf_op jit(solution)/shard_map/ppermute | solution.py:624
  88.4 7.6 %collective-permute-start.21 = (bf16[576,128]{1,0:T(8,128)(2,1)S(1)}, bf16[576,128]{1,0:T(8,128)(2,1)S(1)}, u32[]{:S(2)}, u32[]{:S(2)}) collective-permute-start(bf16[576,128]{1,0:T(8,128)(2,1)S(1)} %get-tuple-element.47), channel_id=1, source_target_pairs={{0,20},{4,16},{8,28},{12,24},{16,0},{20,4},{24,8},{28,12},{1,21},{... | collective-permute-start | bytes 442376 | tf_op jit(solution)/shard_map/ppermute | solution.py:624
  88.4 7.6 %collective-permute-start.22 = (bf16[576,128]{1,0:T(8,128)(2,1)S(1)}, bf16[576,128]{1,0:T(8,128)(2,1)S(1)}, u32[]{:S(2)}, u32[]{:S(2)}) collective-permute-start(bf16[576,128]{1,0:T(8,128)(2,1)S(1)} %get-tuple-element.48), channel_id=1, source_target_pairs={{0,8},{4,12},{8,0},{12,4},{16,28},{20,24},{24,20},{28,16},{1,9},{5... | collective-permute-start | bytes 442376 | tf_op jit(solution)/shard_map/ppermute | solution.py:624
  (5 other events, 88.4 us)
